TPU v7x, 32 devices: a whole 2x2x4 slice. The times are simulated.
32 devices in a mesh: groups: 2 (over y), seq: 8 (over z, x), dp: 2 (over core).
Axes of the slice: x: 2, y: 2, z: 4, core: 2. Of those that a mesh axis runs over, the one named last changes fastest.
Arguments:
- x_input: bfloat16 [6144, 4096], P(('groups', 'seq'), 'dp'), parts along dimension 0, may hold values from -6 to 6
- b_input: bfloat16 [6144, 512], P(('groups', 'seq'), 'dp'), parts along dimension 0, may hold values from -6 to 6
- c_input: bfloat16 [6144, 512], P(('groups', 'seq'), 'dp'), parts along dimension 0, may hold values from -6 to 6
- dt_input: float32 [6144, 64], P(('groups', 'seq'), 'dp'), parts along dimension 0, may hold values from -4 to 4
- decay_rate: float32 [64], P('dp'), may hold values from 0 to 1
- gate_input: bfloat16 [6144, 4096], P(('groups', 'seq'), 'dp'), parts along dimension 0, may hold values from -24 to 24
- taps_x: float32 [4, 4096], P(None, 'dp'), may hold values from -3 to 3
- taps_b: float32 [4, 512], P(None, 'dp'), may hold values from -3 to 3
- taps_c: float32 [4, 512], P(None, 'dp'), may hold values from -3 to 3
- norm_gain: float32 [4096], P('dp'), may hold values from 0.5 to 1.5
- doc_lengths: int32 [8], P('groups'), parts along dimension 0, may hold values from 1 to 2304, as said below
Outputs:
- mixed: bfloat16 [6144, 4096], P(('groups', 'seq'), 'dp'), parts along dimension 0
There are 2 independent parts, one for each index of `groups`. A program takes and returns all parts, laid end to end along the dimension named above; an argument that names none is the same for every part. Nothing has to cross between parts.
Inputs may be any that keep to these rules, and one draw needn't show every extreme that they name: `doc_lengths`: the 4 lengths sum to 3072; the second document is the longest, with exactly 2304 tokens.
All inputs are finite; a program needn't handle non-finite values.
Results may differ from a plain program's by a relative error of at most 0.005.
Values may be sent and summed in bfloat16 or wider, within the bound.
No kernel may reach another device: no remote copies, remote signals or barrier semaphores. Data moves between devices by JAX's collectives and lax.ppermute only.
A program may use at most 192 MiB of HBM per device.

v0:
```python
import jax
import jax.numpy as jnp
from jax import lax
from jax.sharding import PartitionSpec as P

STATE = 128
NORM_HEADS = 16
BLOCK = 384


norm_eps = 1e-05


def passed_along(value, axis, steps):
    count = lax.axis_size(axis)
    leading, last = (max(0, -steps), min(count, count - steps))
    return lax.ppermute(value, axis, [(source, source + steps) for source in range(leading, last)])


def entering_2(value, axis, join, neutral):
    count, mine = (lax.axis_size(axis), lax.axis_index(axis))
    pieces = jax.tree.map(lambda part: lax.all_gather(part, axis), value)
    running = jax.tree.map(
        lambda part, zero: jnp.full_like(part, 0) + jnp.asarray(zero, part.dtype), value, neutral
    )

    def lap(position, running):
        longer = join(running, jax.tree.map(lambda part: part[position], pieces))
        return jax.tree.map(lambda new, old: jnp.where(position < mine, new, old), longer, running)

    return lax.fori_loop(0, count - 1, lap, running)


def doc_index(positions, doc_ends):
    return jnp.sum((positions[:, None] >= doc_ends[None, :-1]).astype(jnp.int32), axis=1)


def causal_conv(extended, doc_ext, doc_ids, weight, margin):
    row_count = doc_ids.shape[0]
    running = jnp.zeros((row_count, extended.shape[1]), jnp.float32)
    for offset in range(margin + 1):
        window = extended[offset : offset + row_count]
        same_doc = (doc_ext[offset : offset + row_count] == doc_ids)[:, None]
        running = running + jnp.where(same_doc, window * weight[offset][None, :], 0.0)
    return jax.nn.silu(running).astype(jnp.bfloat16)


def gated_norm(gated_rows, norm_gain, width):
    row_count = gated_rows.shape[0]
    grouped = gated_rows.reshape(row_count, -1, width)
    mean_sq = jnp.mean(grouped * grouped, axis=-1, keepdims=True)
    scaled = (grouped * lax.rsqrt(mean_sq + norm_eps)).reshape(row_count, -1)
    return (scaled * norm_gain[None, :]).astype(jnp.bfloat16)


def combine(earlier, later):
    return (earlier[0] * later[0], later[0][:, None, None] * earlier[1] + later[1])


def block_terms(x_blk, b_blk, c_blk, step_blk, log_blk, doc_blk, prev_doc, per_group, head_dim):
    block_len = x_blk.shape[0]
    heads_dev = step_blk.shape[1]
    subset = 8
    cum_log = jnp.cumsum(log_blk, axis=0)
    row_order = jnp.arange(block_len, dtype=jnp.int32)
    causal = (row_order[None, :] <= row_order[:, None]) & (doc_blk[:, None] == doc_blk[None, :])
    end_weight = (
        jnp.where((doc_blk == doc_blk[-1])[:, None], jnp.exp(cum_log[-1][None, :] - cum_log), 0.0)
        * step_blk
    )
    decay_block = jnp.exp(cum_log[-1]) * (doc_blk[-1] == prev_doc).astype(jnp.float32)
    in_scale = jnp.exp(cum_log) * (doc_blk == prev_doc).astype(jnp.float32)[:, None]
    intra_parts = []
    state_parts = []
    for group_id in range(heads_dev // per_group):
        b_group = b_blk[:, group_id * STATE : (group_id + 1) * STATE]
        c_group = c_blk[:, group_id * STATE : (group_id + 1) * STATE]
        scores = jnp.dot(c_group, b_group.T, preferred_element_type=jnp.float32)
        for sub_id in range(per_group // subset):
            head_low = group_id * per_group + sub_id * subset
            head_high = head_low + subset
            cum_heads = cum_log[:, head_low:head_high].T
            log_gap = cum_heads[:, :, None] - cum_heads[:, None, :]
            weights = (
                jnp.where(causal[None], jnp.exp(jnp.minimum(log_gap, 0.0)), 0.0)
                * step_blk[:, head_low:head_high].T[:, None, :]
                * scores[None]
            ).astype(jnp.bfloat16)
            x_group = x_blk[:, head_low * head_dim : head_high * head_dim].reshape(
                block_len, subset, head_dim
            )
            intra_parts.append(
                jnp.einsum("hts,shp->thp", weights, x_group, preferred_element_type=jnp.float32)
            )
            x_weighted = (
                x_group.astype(jnp.float32) * end_weight[:, head_low:head_high][:, :, None]
            ).astype(jnp.bfloat16)
            state_parts.append(
                jnp.einsum("sn,shp->hnp", b_group, x_weighted, preferred_element_type=jnp.float32)
            )
    return (decay_block, jnp.concatenate(state_parts, 0), jnp.concatenate(intra_parts, 1), in_scale)


def carried_part(c_blk, carry_state, in_scale, per_group):
    state_low = carry_state.astype(jnp.bfloat16)
    pieces = []
    for group_id in range(carry_state.shape[0] // per_group):
        c_group = c_blk[:, group_id * STATE : (group_id + 1) * STATE]
        head_low = group_id * per_group
        pieces.append(
            jnp.einsum(
                "tn,hnp->thp",
                c_group,
                state_low[head_low : head_low + per_group],
                preferred_element_type=jnp.float32,
            )
        )
    return jnp.concatenate(pieces, 1) * in_scale[:, :, None]


def on_device(
    x_input,
    b_input,
    c_input,
    dt_input,
    decay_rate,
    gate_input,
    taps_x,
    taps_b,
    taps_c,
    norm_gain,
    doc_lengths,
):
    tok_rows = x_input.shape[0]
    heads_dev = dt_input.shape[1]
    head_dim = x_input.shape[1] // heads_dev
    groups_dev = b_input.shape[1] // STATE
    per_group = heads_dev // groups_dev
    margin = taps_x.shape[0] - 1
    tail_rows = passed_along(
        (x_input[tok_rows - margin :], b_input[tok_rows - margin :], c_input[tok_rows - margin :]),
        "seq",
        1,
    )
    first_row = lax.axis_index("seq") * tok_rows
    doc_ends = jnp.cumsum(doc_lengths)
    positions = first_row - margin + jnp.arange(tok_rows + margin, dtype=jnp.int32)
    doc_ext = doc_index(positions, doc_ends)
    doc_ids = doc_ext[margin:]

    def convolve(tail_part, values, weight):
        extended = jnp.concatenate([tail_part, values], 0).astype(jnp.float32)
        return causal_conv(extended, doc_ext, doc_ids, weight, margin)

    x_conv = convolve(tail_rows[0], x_input, taps_x)
    b_conv = convolve(tail_rows[1], b_input, taps_b)
    c_conv = convolve(tail_rows[2], c_input, taps_c)
    step_size = jax.nn.softplus(dt_input)
    log_decay = -(step_size * decay_rate[None, :])
    block_id = 0
    row_low = block_id * BLOCK
    prev_doc = doc_ext[margin + row_low - 1]
    block_parts = [
        block_terms(
            x_conv, b_conv, c_conv, step_size, log_decay, doc_ids, prev_doc, per_group, head_dim
        )
    ]
    device_decay = block_parts[0][0]
    device_state = block_parts[0][1]
    unit_decay = jnp.ones_like(device_decay)
    zero_state = jnp.zeros_like(device_state)
    entering = entering_2((device_decay, device_state), "seq", combine, (unit_decay, zero_state))
    carry_state = entering[1]
    block_id = 0
    decay_block, state_block, intra_out, in_scale = block_parts[block_id]
    outputs = intra_out + carried_part(c_conv, carry_state, in_scale, per_group)
    output = outputs.reshape(tok_rows, heads_dev * head_dim)
    gated_rows = output * jax.nn.silu(gate_input.astype(jnp.float32))
    return gated_norm(gated_rows, norm_gain, NORM_HEADS * head_dim)


def solution(mesh):
    placed = (
        P(("groups", "seq"), "dp"),
        P(("groups", "seq"), "dp"),
        P(("groups", "seq"), "dp"),
        P(("groups", "seq"), "dp"),
        P("dp"),
        P(("groups", "seq"), "dp"),
        P(None, "dp"),
        P(None, "dp"),
        P(None, "dp"),
        P("dp"),
        P("groups"),
    )
    return jax.shard_map(
        on_device, mesh=mesh, in_specs=placed, out_specs=P(("groups", "seq"), "dp"), check_vma=False
    )
```

profile of v0, /device:TPU:0, one launch (start us, length us, event | category | flops | bytes accessed | tf_op | source)
XLA Modules:
  0.0 231.5 jit_solution(16446823564188872115)
XLA Ops:
  6.5 0.8 slice.211
  7.3 4.8 %collective-permute-start.1 = (bf16[3,256]{1,0:T(4,128)(2,1)S(1)}, bf16[3,256]{1,0:T(4,128)(2,1)S(1)}, u32[]{:S(2)}, u32[]{:S(2)}) collective-permute-start(bf16[3,256]{1,0:T(4,128)(2,1)S(1)} %slice.211), channel_id=1, source_target_pairs={{0,2},{2,4},{4,6},{6,8},{8,10},{10,12},{12,14},{1,3},{3,5},{5,7},{... | collective-permute-start | bytes 4616 | tf_op jit(solution)/shard_map/ppermute | solution.py:17
  12.2 0.7 slice.221
  12.9 3.4 %collective-permute-start.2 = (bf16[3,256]{1,0:T(4,128)(2,1)S(1)}, bf16[3,256]{1,0:T(4,128)(2,1)S(1)}, u32[]{:S(2)}, u32[]{:S(2)}) collective-permute-start(bf16[3,256]{1,0:T(4,128)(2,1)S(1)} %slice.221), channel_id=1, source_target_pairs={{0,2},{2,4},{4,6},{6,8},{8,10},{10,12},{12,14},{1,3},{3,5},{5,7},{... | collective-permute-start | bytes 4616 | tf_op jit(solution)/shard_map/ppermute | solution.py:17
  16.3 0.8 slice.195
  17.1 3.4 %collective-permute-start = (bf16[3,2048]{1,0:T(4,128)(2,1)S(1)}, bf16[3,2048]{1,0:T(4,128)(2,1)S(1)}, u32[]{:S(2)}, u32[]{:S(2)}) collective-permute-start(bf16[3,2048]{1,0:T(4,128)(2,1)S(1)} %slice.195), channel_id=1, source_target_pairs={{0,2},{2,4},{4,6},{6,8},{8,10},{10,12},{12,14},{1,3},{3,5},{5,7},{... | collective-permute-start | bytes 36872 | tf_op jit(solution)/shard_map/ppermute | solution.py:17
  20.5 0.8 reduce-window.10
  22.1 1.3 compare_convert_fusion
  24.8 0.8 fusion.68
  25.6 0.9 fusion.66
  26.5 0.9 copy_bitcast_fusion
  27.4 0.9 reduce-window.11
  28.8 0.9 exponential_multiply_fusion
  29.7 0.8 fusion.67
  30.6 1.0 maximum_convert_fusion.1
  31.5 1.0 maximum_convert_fusion.2
  33.6 2.9 %multiply_convert_fusion.5 = bf16[384,2048]{1,0:T(8,128)(2,1)S(1)} fusion(f32[387,2048]{1,0:T(8,128)S(1)} %maximum_convert_fusion, f32[2048]{0:T(1024)S(1)} %bitcast.134, f32[2048]{0:T(1024)S(1)} %bitcast.135, f32[2048]{0:T(1024)S(1)} %bitcast.133, f32[2048]{0:T(1024)S(1)} %bitcast.132, pred[384]{0:T(512)(128)(4,1)S(1)} %get-tuple-element.195, ...), kind=kLoop, calls=%fused_computation.27 | loop fusion | flops 11796480 | bytes 14189696 | tf_op jit(solution)/shard_map/convert_element_type | solution.py:45
  38.7 1.0 pad_maximum_fusion
  39.9 17.8 %all-gather.1 = f32[8,1,32]{2,1,0:T(1,128)S(1)} all-gather(f32[1,1,32]{2,1,0:T(1,128)S(1)} %bitcast.147), channel_id=1, replica_groups=mesh['groups'=2,'seq'=8,'dp'=2] {'seq'}, dimensions={0}, use_global_device_ids=true | all-gather | bytes 1152 | tf_op jit(solution)/shard_map/all_gather | solution.py:22
  58.4 2.6 %fusion.22 = f32[384,8,64]{0,2,1:T(8,128)} fusion(bf16[384,8,64]{0,2,1:T(8,128)(2,1)S(1)} %bitcast.129, f32[384,384]{1,0:T(8,128)S(1)} %fusion.50, f32[8,384]{1,0:T(8,128)S(1)} %get-tuple-element.177, f32[8,384]{1,0:T(8,128)S(1)} %get-tuple-element.205, pred[384,384]{1,0:T(8,128)(4,1)S(1)} %fusion.23), kind=kOutput, calls=%fused_computation.40 | convolution fusion | flops 158072832 | bytes 1941504 | tf_op jit(solution)/shard_map/hts,shp->thp/dot_general | solution.py:93
  61.0 2.6 %fusion.21 = f32[384,8,64]{0,2,1:T(8,128)} fusion(bf16[384,8,64]{0,2,1:T(8,128)(2,1)S(1)} %bitcast.127, f32[8,384]{1,0:T(8,128)S(1)} %get-tuple-element.179, f32[8,384]{1,0:T(8,128)S(1)} %get-tuple-element.202, f32[384,384]{1,0:T(8,128)S(1)} %fusion.50, pred[384,384]{1,0:T(8,128)(4,1)S(1)} %fusion.23), kind=kOutput, calls=%fused_computation.39 | convolution fusion | flops 158072832 | bytes 1941504 | tf_op jit(solution)/shard_map/hts,shp->thp/dot_general | solution.py:93
  63.6 2.6 %fusion.20 = f32[384,8,64]{0,2,1:T(8,128)} fusion(bf16[384,8,64]{0,2,1:T(8,128)(2,1)S(1)} %bitcast.125, f32[384,384]{1,0:T(8,128)S(1)} %fusion.46, f32[8,384]{1,0:T(8,128)S(1)} %get-tuple-element.178, f32[8,384]{1,0:T(8,128)S(1)} %get-tuple-element.203, pred[384,384]{1,0:T(8,128)(4,1)S(1)} %fusion.23), kind=kOutput, calls=%fused_computation.38 | convolution fusion | flops 158072832 | bytes 1941504 | tf_op jit(solution)/shard_map/hts,shp->thp/dot_general | solution.py:93
  66.1 2.6 %fusion.19 = f32[384,8,64]{0,2,1:T(8,128)} fusion(bf16[384,8,64]{0,2,1:T(8,128)(2,1)S(1)} %bitcast.123, f32[8,384]{1,0:T(8,128)S(1)} %get-tuple-element.180, f32[8,384]{1,0:T(8,128)S(1)} %get-tuple-element.204, f32[384,384]{1,0:T(8,128)S(1)} %fusion.46, pred[384,384]{1,0:T(8,128)(4,1)S(1)} %fusion.23), kind=kOutput, calls=%fused_computation.37 | convolution fusion | flops 158072832 | bytes 1941504 | tf_op jit(solution)/shard_map/hts,shp->thp/dot_general | solution.py:93
  68.7 95.5 %all-gather.4.cloned.1.call-done = f32[256,128,64]{1,2,0:T(8,128)} async-done(((f32[32,128,64]{1,2,0:T(8,128)}), f32[256,128,64]{1,2,0:T(8,128)}) %all-gather.4.cloned.1.call-update) | async-done | bytes 8388624 | tf_op jit(solution)/shard_map/all_gather | solution.py:22
  164.2 35.0 %while.14 = (s32[]{:T(128)}, f32[32,128,64]{2,1,0:T(8,128)}, s32[]{:T(128)}, f32[8,32]{1,0:T(8,128)S(1)}, f32[8,32,128,64]{2,3,1,0:T(8,128)}, /*index=5*/s32[]{:T(128)}, s32[]{:T(128)}) while((s32[]{:T(128)}, f32[32,128,64]{2,1,0:T(8,128)}, s32[]{:T(128)}, f32[8,32]{1,0:T(8,128)S(1)}, f32[8,32,128,64]{2,3,1,0:T(8,128)}, ...), condition=%wide.region_5.6_spmd.clone, body=%wide.region_4.5_spmd.clone.sunk | while | flops 1048580 | bytes 7340521 | solution.py:31
  164.2 1.3 constant_dynamic-slice_fusion.2
  166.1 1.7 fusion.77
  167.8 1.3 constant_dynamic-slice_fusion.2
  169.8 3.3 %fusion.77 = f32[32,128,64]{2,1,0:T(8,128)} fusion(f32[1,32,128,64]{3,2,1,0:T(8,128)S(1)} %copy.80, f32[32,128,64]{2,1,0:T(8,128)} %get-tuple-element.245, f32[32]{0:T(128)S(1)} %dynamic-slice_bitcast_fusion.2, pred[]{:T(512)S(6)} %compare.3, pred[]{:T(512)S(6)} %lt.22), kind=kLoop, calls=%fused_computation.1.clone.1 | loop fusion | flops 1048576 | bytes 3145858 | tf_op jit(solution)/shard_map/while/body/eval_jaxpr/jit(_where)/select_n | solution.py:29
  173.1 1.3 constant_dynamic-slice_fusion.2
  175.0 3.3 %fusion.77 = f32[32,128,64]{2,1,0:T(8,128)} fusion(f32[1,32,128,64]{3,2,1,0:T(8,128)S(1)} %copy.80, f32[32,128,64]{2,1,0:T(8,128)} %get-tuple-element.245, f32[32]{0:T(128)S(1)} %dynamic-slice_bitcast_fusion.2, pred[]{:T(512)S(6)} %compare.3, pred[]{:T(512)S(6)} %lt.22), kind=kLoop, calls=%fused_computation.1.clone.1 | loop fusion | flops 1048576 | bytes 3145858 | tf_op jit(solution)/shard_map/while/body/eval_jaxpr/jit(_where)/select_n | solution.py:29
  178.3 1.3 constant_dynamic-slice_fusion.2
  180.2 3.3 %fusion.77 = f32[32,128,64]{2,1,0:T(8,128)} fusion(f32[1,32,128,64]{3,2,1,0:T(8,128)S(1)} %copy.80, f32[32,128,64]{2,1,0:T(8,128)} %get-tuple-element.245, f32[32]{0:T(128)S(1)} %dynamic-slice_bitcast_fusion.2, pred[]{:T(512)S(6)} %compare.3, pred[]{:T(512)S(6)} %lt.22), kind=kLoop, calls=%fused_computation.1.clone.1 | loop fusion | flops 1048576 | bytes 3145858 | tf_op jit(solution)/shard_map/while/body/eval_jaxpr/jit(_where)/select_n | solution.py:29
  183.5 1.3 constant_dynamic-slice_fusion.2
  185.4 3.3 %fusion.77 = f32[32,128,64]{2,1,0:T(8,128)} fusion(f32[1,32,128,64]{3,2,1,0:T(8,128)S(1)} %copy.80, f32[32,128,64]{2,1,0:T(8,128)} %get-tuple-element.245, f32[32]{0:T(128)S(1)} %dynamic-slice_bitcast_fusion.2, pred[]{:T(512)S(6)} %compare.3, pred[]{:T(512)S(6)} %lt.22), kind=kLoop, calls=%fused_computation.1.clone.1 | loop fusion | flops 1048576 | bytes 3145858 | tf_op jit(solution)/shard_map/while/body/eval_jaxpr/jit(_where)/select_n | solution.py:29
  188.7 1.3 constant_dynamic-slice_fusion.2
  190.7 3.3 %fusion.77 = f32[32,128,64]{2,1,0:T(8,128)} fusion(f32[1,32,128,64]{3,2,1,0:T(8,128)S(1)} %copy.80, f32[32,128,64]{2,1,0:T(8,128)} %get-tuple-element.245, f32[32]{0:T(128)S(1)} %dynamic-slice_bitcast_fusion.2, pred[]{:T(512)S(6)} %compare.3, pred[]{:T(512)S(6)} %lt.22), kind=kLoop, calls=%fused_computation.1.clone.1 | loop fusion | flops 1048576 | bytes 3145858 | tf_op jit(solution)/shard_map/while/body/eval_jaxpr/jit(_where)/select_n | solution.py:29
  194.0 1.3 constant_dynamic-slice_fusion.2
  195.9 3.3 %fusion.77 = f32[32,128,64]{2,1,0:T(8,128)} fusion(f32[1,32,128,64]{3,2,1,0:T(8,128)S(1)} %copy.80, f32[32,128,64]{2,1,0:T(8,128)} %get-tuple-element.245, f32[32]{0:T(128)S(1)} %dynamic-slice_bitcast_fusion.2, pred[]{:T(512)S(6)} %compare.3, pred[]{:T(512)S(6)} %lt.22), kind=kLoop, calls=%fused_computation.1.clone.1 | loop fusion | flops 1048576 | bytes 3145858 | tf_op jit(solution)/shard_map/while/body/eval_jaxpr/jit(_where)/select_n | solution.py:29
  199.2 2.1 copy.64
  202.7 2.4 %maximum_add_fusion = f32[384,32,64]{0,2,1:T(8,128)} fusion(f32[384,8,64]{0,2,1:T(8,128)S(1)} %copy-done.5, f32[384,8,64]{0,2,1:T(8,128)S(1)} %copy-done.4, f32[384,8,64]{0,2,1:T(8,128)S(1)} %copy-done.3, f32[384,8,64]{0,2,1:T(8,128)S(1)} %copy-done.2, f32[384,16,64]{0,2,1:T(8,128)S(1)} %bitcast.120, f32[384,16,64]{0,2,1:T(8,128)S(1)} %bitcast.119, ...), kind=kLoop, calls=%fused_computation.24 | loop fusion | flops 4718592 | bytes 9486336 | tf_op jit(solution)/shard_map/add | solution.py:176
  205.1 2.4 %copy.65 = f32[384,2048]{1,0:T(8,128)S(1)} copy(f32[384,2048]{0,1:T(8,128)} %bitcast.117) | data formatting | bytes 6291456 | tf_op jit(solution)/shard_map/add | solution.py:176
  207.5 3.9 %fusion.62 = f32[384,2048]{1,0:T(8,128)} fusion(f32[384,2048]{1,0:T(8,128)S(1)} %copy.65, bf16[384,2048]{1,0:T(8,128)(2,1)} %param.18), kind=kLoop, calls=%fused_computation.129 | loop fusion | flops 5505024 | bytes 7864320 | tf_op jit(solution)/shard_map/mul | solution.py:51
  211.4 5.6 %mul.391 = f32[384,2,1024]{2,1,0:T(2,128)} reshape(f32[384,2048]{1,0:T(8,128)} %fusion.62) | data formatting | bytes 6291456 | tf_op jit(solution)/shard_map/mul | solution.py:51
  217.0 2.8 %reduce_sum.19 = f32[384,2]{1,0:T(8,128)S(1)} reduce(f32[384,2,1024]{2,1,0:T(2,128)} %mul.391, f32[]{:T(128)} %constant.56.clone.1), dimensions={2}, to_apply=%region_6.7 | reduce | flops 785664 | bytes 3148804 | tf_op jit(solution)/shard_map/reduce_sum | solution.py:51
  219.8 0.9 mul.392
  220.7 1.4 copy.71
  222.2 2.5 %multiply_convert_fusion.4 = bf16[384,2048]{1,0:T(8,128)(2,1)} fusion(f32[384,2048]{1,0:T(8,128)S(1)} %bitcast.118, f32[2048]{0:T(1024)S(1)} %copy-done.6, f32[384,2048]{1,0:T(8,128)S(1)} %copy.65, bf16[384,2048]{1,0:T(8,128)(2,1)S(1)} %copy-done), kind=kLoop, calls=%fused_computation.26 | loop fusion | flops 7077888 | bytes 9445376 | tf_op jit(solution)/shard_map/convert_element_type | solution.py:53
  (63 shorter events, 10.8 us)
Async XLA Ops:
  6.5 26.6 %copy-start.1 = (bf16[384,2048]{1,0:T(8,128)(2,1)S(1)}, bf16[384,2048]{1,0:T(8,128)(2,1)}, u32[]{:S(2)}) copy-start(bf16[384,2048]{1,0:T(8,128)(2,1)} %param.13) | copy-start | bytes 4718596
  6.5 157.6 %all-gather.4.cloned.1.call-start = ((), (), s32[]{:S(2)}) async-start(), calls=%async_computation | async-start | bytes 9437184 | tf_op jit(solution)/shard_map/all_gather | solution.py:22
  7.3 23.2 %collective-permute-start.1 = (bf16[3,256]{1,0:T(4,128)(2,1)S(1)}, bf16[3,256]{1,0:T(4,128)(2,1)S(1)}, u32[]{:S(2)}, u32[]{:S(2)}) collective-permute-start(bf16[3,256]{1,0:T(4,128)(2,1)S(1)} %slice.211), channel_id=1, source_target_pairs={{0,2},{2,4},{4,6},{6,8},{8,10},{10,12},{12,14},{1,3},{3,5},{5,7},{... | collective-permute-start | bytes 4616 | tf_op jit(solution)/shard_map/ppermute | solution.py:17
  12.9 18.7 %collective-permute-start.2 = (bf16[3,256]{1,0:T(4,128)(2,1)S(1)}, bf16[3,256]{1,0:T(4,128)(2,1)S(1)}, u32[]{:S(2)}, u32[]{:S(2)}) collective-permute-start(bf16[3,256]{1,0:T(4,128)(2,1)S(1)} %slice.221), channel_id=1, source_target_pairs={{0,2},{2,4},{4,6},{6,8},{8,10},{10,12},{12,14},{1,3},{3,5},{5,7},{... | collective-permute-start | bytes 4616 | tf_op jit(solution)/shard_map/ppermute | solution.py:17
  17.1 16.0 %collective-permute-start = (bf16[3,2048]{1,0:T(4,128)(2,1)S(1)}, bf16[3,2048]{1,0:T(4,128)(2,1)S(1)}, u32[]{:S(2)}, u32[]{:S(2)}) collective-permute-start(bf16[3,2048]{1,0:T(4,128)(2,1)S(1)} %slice.195), channel_id=1, source_target_pairs={{0,2},{2,4},{4,6},{6,8},{8,10},{10,12},{12,14},{1,3},{3,5},{5,7},{... | collective-permute-start | bytes 36872 | tf_op jit(solution)/shard_map/ppermute | solution.py:17
  199.2 2.9 %copy-start.2 = (f32[384,8,64]{0,2,1:T(8,128)S(1)}, f32[384,8,64]{0,2,1:T(8,128)}, u32[]{:S(2)}) copy-start(f32[384,8,64]{0,2,1:T(8,128)} %fusion.22) | copy-start | bytes 2359300
  199.2 2.9 %copy-start.3 = (f32[384,8,64]{0,2,1:T(8,128)S(1)}, f32[384,8,64]{0,2,1:T(8,128)}, u32[]{:S(2)}) copy-start(f32[384,8,64]{0,2,1:T(8,128)} %fusion.21) | copy-start | bytes 2359300
  201.3 1.1 copy-start.4
  201.3 1.4 copy-start.5
  220.7 1.5 copy-start
  220.7 1.5 copy-start.6
Sparse Core Ops, SparseCore 0:
  39.9 124.2 all-gather.3
where the time goes:
time: 233 us; the launch traced here: 231 us
  waiting for transfers between devices  95.5 us (41%)
  other arithmetic  45.5 us (20%)
  local copies, waits for them, and re-layouts  33.1 us (14%)
  blocking collectives  17.8 us (8%)
  between operations  15 us (6%)
  matrix products  12.7 us (5%)
  starting transfers between devices  11.7 us (5%)
    all_gather x1, waiting for transfers between devices, entering_2(): pieces = jax.tree.map(lambda part: lax.all_gather(part, axis), value)  95.5 us
    select_n x7, other arithmetic, lap(): jnp.where(position < mine, new, old)  21.5 us
    all_gather x1, blocking collectives, entering_2(): pieces = jax.tree.map(lambda part: lax.all_gather(part, axis), value)  17.8 us
    dynamic_slice x14, local copies, waits for them, and re-layouts, lap(): longer = join(running, jax.tree.map(lambda part: part[position], pieces))  13.3 us
    ppermute x3, starting transfers between devices, passed_along(): lax.ppermute(value, axis, [(source, source + steps) for source in range(l...  11.7 us
    dot_general x4, matrix products, block_terms(): jnp.einsum('hts,shp->thp', weights, x_group, preferred_element_type=jnp.f...  10.3 us
    mul x1, local copies, waits for them, and re-layouts, gated_norm(): mean_sq = jnp.mean(grouped * grouped, axis=-1, keepdims=True)  5.61 us
  transfers between devices with their start and end apart: 4, of which 1 were waited for; matrix products, arithmetic and copies ran while one was open for 10% of the time, Pallas kernels for 0%

commit v1 on v0

v1 whole, which is shorter than its diff:
```python
import functools

import jax
import jax.numpy as jnp
from jax import lax
from jax.experimental import pallas as pl
from jax.experimental.pallas import tpu as pltpu
from jax.sharding import PartitionSpec as P

STATE = 128
NORM_HEADS = 16
SUB = 128
CHUNK = 256
LANES = 128
ROWS = 32
LOG2E = 1.4426950408889634
norm_eps = 1e-05

F32 = jnp.float32
BF16 = jnp.bfloat16
VMEM = pl.BlockSpec(memory_space=pltpu.VMEM)
SMEM = pl.BlockSpec(memory_space=pltpu.SMEM)
ANY = pl.BlockSpec(memory_space=pl.ANY)


def params(mib=48):
    return pltpu.CompilerParams(vmem_limit_bytes=mib << 20)


def cost(flops, moved, transcendentals=0):
    return pl.CostEstimate(flops=flops, bytes_accessed=moved, transcendentals=transcendentals)


def doc_edges(dl_ref):
    edges = [0]
    for i in range(dl_ref.shape[0] - 1):
        edges.append(edges[-1] + dl_ref[i])
    return edges


def doc_start(token, edges):
    start = jnp.zeros_like(token)
    for edge in edges[1:]:
        start = jnp.where(token >= edge, jnp.maximum(start, edge), start)
    return start


def split2(value):
    high = value.astype(BF16)
    return high, (value - high.astype(F32)).astype(BF16)


def split3(value):
    high = value.astype(BF16)
    rest = value - high.astype(F32)
    mid = rest.astype(BF16)
    return high, mid, (rest - mid.astype(F32)).astype(BF16)


def mm(a, b):
    return jnp.dot(a, b, preferred_element_type=F32)


def spread(heads, chunk, width, head_dim):
    row = lax.broadcasted_iota(jnp.int32, (2 * heads, width), 0)
    lane = lax.broadcasted_iota(jnp.int32, (2 * heads, width), 1)
    head = jnp.where(row >= heads, row - heads, row)
    low = (head - chunk * (width // head_dim)) * head_dim
    return jnp.where((lane >= low) & (lane < low + head_dim), 1.0, 0.0).astype(BF16)


def prep_kernel(dl_ref, dt_ref, rate_ref, w_ref, u_ref, u0_ref, col_ref, row_ref, d_ref):
    tok, heads = dt_ref.shape
    row0 = lax.axis_index("seq") * tok
    edges = doc_edges(dl_ref)
    tri = jnp.where(
        lax.broadcasted_iota(jnp.int32, (SUB, SUB), 0) >= lax.broadcasted_iota(jnp.int32, (SUB, SUB), 1), 1.0, 0.0
    ).astype(BF16)
    total = jnp.zeros((1, heads), F32)
    decays = []
    for c in range(tok // SUB):
        rows = pl.ds(c * SUB, SUB)
        first = row0 + c * SUB
        dt = dt_ref[rows, :]
        step = jnp.maximum(dt, 0.0) + jnp.log1p(jnp.exp(-jnp.abs(dt)))
        parts = split3(-(step * rate_ref[...]))
        cum = mm(tri, parts[0]) + (mm(tri, parts[1]) + mm(tri, parts[2]))
        last = cum[SUB - 1 :, :]
        token = first + lax.broadcasted_iota(jnp.int32, (SUB, heads), 0)
        start = doc_start(token, edges)
        last_start = doc_start(jnp.int32(first + SUB - 1), edges)
        within = jnp.where(token >= last_start, 1.0, 0.0)
        w_ref[rows, :] = jnp.concatenate(split2(jnp.exp(last - cum) * step * within), 1)
        u_ref[rows, :] = jnp.concatenate(split2(jnp.exp(cum) * jnp.where(start < first, 1.0, 0.0)), 1)
        u0_ref[rows, :] = jnp.concatenate(split2(jnp.exp(cum + total) * jnp.where(start < row0, 1.0, 0.0)), 1)
        col_ref[rows, :] = cum * LOG2E
        row = (jnp.log(step) - cum) * LOG2E
        padded = jnp.concatenate([row, jnp.zeros((SUB, LANES - heads), F32)], 1)
        row_ref[:, c * SUB : (c + 1) * SUB] = padded.T[:heads]
        decays.append(jnp.exp(last) * jnp.where(last_start < first, 1.0, 0.0))
        total = total + last
    end_start = doc_start(jnp.int32(row0 + tok - 1), edges)
    whole = jnp.exp(total) * jnp.where(end_start < row0, 1.0, 0.0)
    high, mid, low = split3(whole)
    none = jnp.zeros((1, heads), BF16)
    table = [jnp.concatenate([part, none], 1) for part in (high, mid, low)]
    table += [jnp.concatenate(split2(decay), 1) for decay in decays[1:]]
    table += [jnp.concatenate([none, none], 1)] * (8 - len(table))
    d_ref[...] = jnp.concatenate([part.astype(F32) for part in table], 0).astype(BF16)


def prep(doc_lengths, dt_input, rate):
    tok, heads = dt_input.shape
    pair = jax.ShapeDtypeStruct((tok, 2 * heads), BF16)
    return pl.pallas_call(
        prep_kernel,
        out_shape=(
            pair,
            pair,
            pair,
            jax.ShapeDtypeStruct((tok, heads), F32),
            jax.ShapeDtypeStruct((heads, tok), F32),
            jax.ShapeDtypeStruct((8, 2 * heads), BF16),
        ),
        in_specs=[SMEM, VMEM, VMEM],
        out_specs=(VMEM,) * 6,
        compiler_params=params(),
        cost_estimate=cost(tok * SUB * heads * 6, tok * 2048, tok * heads * 6),
        name="prep",
    )(doc_lengths, dt_input, rate)


def convolve(ext_ref, mask_ref, taps, tok, width, put):
    for low in range(0, tok, ROWS):
        total = ext_ref[8 + low : 8 + low + ROWS, :] * taps[-1]
        for back in range(1, len(taps)):
            mask = jnp.concatenate([mask_ref[back - 1, low : low + ROWS, :]] * (width // LANES), 1)
            window = ext_ref[8 + low - back : 8 + low - back + ROWS, :]
            total = total + (window * taps[-1 - back]) * mask
        put(low, (total / (1.0 + jnp.exp(-total))).astype(BF16))


def state_kernel(
    owners,
    dl_ref,
    x_ref,
    b_ref,
    c_ref,
    tail_ref,
    taps_x_ref,
    taps_b_ref,
    taps_c_ref,
    w_ref,
    d_ref,
    xc_ref,
    bc_ref,
    cc_ref,
    h_ref,
    *rest,
):
    sends = rest[:owners]
    ext_ref, mask_ref, bt_ref, xw_ref, out_ref, sem = rest[owners:]
    tok, channels = x_ref.shape
    heads = w_ref.shape[1] // 2
    head_dim = channels // heads
    gn = b_ref.shape[1]
    per_group = channels // (gn // STATE) // CHUNK
    me = lax.axis_index("seq") if sends_apart(owners, channels) else 0
    row0 = lax.axis_index("seq") * tok
    edges = doc_edges(dl_ref)
    taps_len = taps_x_ref.shape[0]
    token = row0 + lax.broadcasted_iota(jnp.int32, (tok, LANES), 0)
    age = token - doc_start(token, edges)
    for back in range(1, taps_len):
        mask_ref[back - 1] = jnp.where(age >= back, 1.0, 0.0)

    def load(values, tail, lanes):
        ext_ref[8:, :] = values.astype(F32)
        ext_ref[:8, :] = tail.astype(F32)

    for ref, taps_ref, to_ref, at in ((b_ref, taps_b_ref, bc_ref, channels), (c_ref, taps_c_ref, cc_ref, channels + gn)):
        load(ref[...], tail_ref[:, at : at + gn], None)
        taps = [taps_ref[i : i + 1, :] for i in range(taps_len)]

        def put(low, value, to_ref=to_ref):
            to_ref[low : low + ROWS, :] = value

        convolve(ext_ref, mask_ref, taps, tok, gn, put)
    for group in range(gn // STATE):
        lanes = slice(group * STATE, (group + 1) * STATE)
        bt_ref[group] = bc_ref[:, lanes].astype(F32).T.astype(BF16)

    def body(k, carry):
        chunk = me ^ k
        lanes = pl.ds(pl.multiple_of(chunk * CHUNK, CHUNK), CHUNK)
        load(x_ref[:, lanes], tail_ref[:, lanes], None)
        taps = [taps_x_ref[i : i + 1, lanes] for i in range(taps_len)]
        one_hot = spread(heads, chunk, CHUNK, head_dim)

        def put(low, value):
            xc_ref[low : low + ROWS, lanes] = value
            weight = mm(w_ref[low : low + ROWS, :], one_hot)
            xw_ref[low : low + ROWS, :] = (value.astype(F32) * weight).astype(BF16)

        convolve(ext_ref, mask_ref, taps, tok, CHUNK, put)
        decay = mm(d_ref[...], one_hot)
        group = chunk // per_group
        state = None
        for c in range(tok // SUB):
            rows = slice(c * SUB, (c + 1) * SUB)
            local = mm(bt_ref[group, :, rows], xw_ref[rows, :])
            if state is None:
                state = local
            else:
                h_ref[c - 1, :, lanes] = state.astype(BF16)
                state = local + decay[2 + c : 3 + c, :] * state
        out_ref[k, :STATE, :] = state.astype(BF16)
        out_ref[k, STATE:, :] = decay.astype(BF16)
        return carry

    lax.fori_loop(0, owners, body, 0)
    copies = [pltpu.make_async_copy(out_ref.at[k], sends[k], sem.at[k]) for k in range(owners)]
    for copy in copies:
        copy.start()
    for copy in copies:
        copy.wait()


def sends_apart(owners, channels):
    return owners == lax.axis_size("seq") and owners * CHUNK == channels and owners & (owners - 1) == 0


def states(doc_lengths, x, b, c, tail, taps_x, taps_b, taps_c, w, d):
    tok, channels = x.shape
    gn = b.shape[1]
    owners = channels // CHUNK
    subs = tok // SUB
    piece = jax.ShapeDtypeStruct((STATE + 8, CHUNK), BF16)
    return pl.pallas_call(
        functools.partial(state_kernel, owners),
        out_shape=(
            jax.ShapeDtypeStruct((tok, channels), BF16),
            jax.ShapeDtypeStruct((tok, gn), BF16),
            jax.ShapeDtypeStruct((tok, gn), BF16),
            jax.ShapeDtypeStruct((subs - 1, STATE, channels), BF16),
        )
        + (piece,) * owners,
        in_specs=[SMEM] + [VMEM] * 9,
        out_specs=(VMEM,) * 4 + (ANY,) * owners,
        scratch_shapes=[
            pltpu.VMEM((tok + 8, CHUNK), F32),
            pltpu.VMEM((taps_x.shape[0] - 1, tok, LANES), F32),
            pltpu.VMEM((gn // STATE, STATE, tok), BF16),
            pltpu.VMEM((tok, CHUNK), BF16),
            pltpu.VMEM((owners, STATE + 8, CHUNK), BF16),
            pltpu.SemaphoreType.DMA((owners,)),
        ],
        compiler_params=params(),
        cost_estimate=cost(tok * STATE * channels * 4, tok * channels * 6, tok * channels * 2),
        name="conv_state",
    )(doc_lengths, x, b, c, tail, taps_x, taps_b, taps_c, w, d)


def scan_kernel(owners, *refs):
    pieces, outs = refs[:owners], refs[owners : 2 * owners]
    in_ref, out_ref, sem_in, sem_out = refs[2 * owners :]
    me = lax.axis_index("seq")
    copies = [pltpu.make_async_copy(pieces[k], in_ref.at[me ^ k], sem_in.at[k]) for k in range(owners)]
    for copy in copies:
        copy.start()
    for copy in copies:
        copy.wait()
    state = jnp.zeros((STATE, CHUNK), F32)
    out_ref[0] = state.astype(BF16)
    for i in range(owners - 1):
        row = in_ref[i, STATE:, :].astype(F32)
        decay = row[0:1] + (row[1:2] + row[2:3])
        state = decay * state + in_ref[i, :STATE, :].astype(F32)
        out_ref[i + 1] = state.astype(BF16)
    copies = [pltpu.make_async_copy(out_ref.at[me ^ k], outs[k], sem_out.at[k]) for k in range(owners)]
    for copy in copies:
        copy.start()
    for copy in copies:
        copy.wait()


def scan_blocks(pieces):
    owners = len(pieces)
    return pl.pallas_call(
        functools.partial(scan_kernel, owners),
        out_shape=(jax.ShapeDtypeStruct((STATE, CHUNK), BF16),) * owners,
        in_specs=[ANY] * owners,
        out_specs=(ANY,) * owners,
        scratch_shapes=[
            pltpu.VMEM((owners, STATE + 8, CHUNK), BF16),
            pltpu.VMEM((owners, STATE, CHUNK), BF16),
            pltpu.SemaphoreType.DMA((owners,)),
            pltpu.SemaphoreType.DMA((owners,)),
        ],
        compiler_params=params(),
        cost_estimate=cost(owners * STATE * CHUNK * 2, owners * STATE * CHUNK * 4),
        name="block_scan",
    )(*pieces)


def intra_kernel(group, heads, head_dim, dl_ref, xc_ref, bc_ref, cc_ref, h_ref, u_ref, col_ref, row_ref, out_ref):
    sub = pl.program_id(0)
    per_group = xc_ref.shape[1] // head_dim
    first = lax.axis_index("seq") * (pl.num_programs(0) * SUB) + sub * SUB
    edges = doc_edges(dl_ref)
    token = first + lax.broadcasted_iota(jnp.int32, (SUB, SUB), 0)
    source = first + lax.broadcasted_iota(jnp.int32, (SUB, SUB), 1)
    keep = (source <= token) & (source >= doc_start(token, edges))
    c_blk = cc_ref[...]
    scores = lax.dot_general(c_blk, bc_ref[...], (((1,), (1,)), ((), ())), preferred_element_type=F32)
    scores = jnp.where(keep, scores, 0.0)
    lane = lax.broadcasted_iota(jnp.int32, (SUB, LANES), 1)
    per_tile = LANES // head_dim
    for tile in range(per_group // per_tile):
        lanes = slice(tile * LANES, (tile + 1) * LANES)
        x_tile = xc_ref[:, lanes].astype(F32)
        left, right = [], []
        for i in range(per_tile):
            head = group * per_group + tile * per_tile + i
            gap = col_ref[:, head : head + 1] + row_ref[head : head + 1, :]
            left.append((jnp.exp2(jnp.minimum(gap, 80.0)) * scores).astype(BF16))
            mine = (lane >= i * head_dim) & (lane < (i + 1) * head_dim)
            right.append(jnp.where(mine, x_tile, 0.0).astype(BF16))
        out_ref[:, lanes] = mm(jnp.concatenate(left, 1), jnp.concatenate(right, 0))

    @pl.when(sub > 0)
    def _():
        for chunk in range(xc_ref.shape[1] // CHUNK):
            lanes = slice(chunk * CHUNK, (chunk + 1) * CHUNK)
            one_hot = spread(heads, group * (xc_ref.shape[1] // CHUNK) + chunk, CHUNK, head_dim)
            out_ref[:, lanes] += mm(c_blk, h_ref[0, :, lanes]) * mm(u_ref[...], one_hot)


def intra(group, doc_lengths, xc, bc, cc, h, u, col, row):
    tok, channels = xc.shape
    heads = col.shape[1]
    head_dim = channels // heads
    groups = bc.shape[1] // STATE
    width = channels // groups
    subs = tok // SUB
    return pl.pallas_call(
        functools.partial(intra_kernel, group, heads, head_dim),
        out_shape=jax.ShapeDtypeStruct((tok, width), F32),
        grid=(subs,),
        in_specs=[
            SMEM,
            pl.BlockSpec((SUB, width), lambda i: (i, group)),
            pl.BlockSpec((SUB, STATE), lambda i: (i, group)),
            pl.BlockSpec((SUB, STATE), lambda i: (i, group)),
            pl.BlockSpec((1, STATE, width), lambda i: (jnp.maximum(i - 1, 0), 0, group)),
            pl.BlockSpec((SUB, 2 * heads), lambda i: (i, 0)),
            pl.BlockSpec((SUB, heads), lambda i: (i, 0)),
            pl.BlockSpec((heads, SUB), lambda i: (0, i)),
        ],
        out_specs=pl.BlockSpec((SUB, width), lambda i: (i, 0)),
        compiler_params=params(),
        cost_estimate=cost(tok * SUB * width * 4, tok * width * 8, tok * SUB * width // head_dim),
        name="intra",
    )(doc_lengths, xc, bc, cc, h, u, col, row)


def final_kernel(owners, heads, head_dim, apart, norm_width, *refs):
    cc_ref, u0_ref, gate_ref, gain_ref = refs[:4]
    groups = cc_ref.shape[1] // STATE
    intra_refs = refs[4 : 4 + groups]
    pieces = refs[4 + groups : 4 + groups + owners]
    out_ref, e_ref, y_ref, sem = refs[4 + groups + owners :]
    me = lax.axis_index("seq") if apart else 0

    @pl.when(pl.program_id(0) == 0)
    def _():
        copies = [pltpu.make_async_copy(pieces[k], e_ref.at[me ^ k], sem.at[k]) for k in range(owners)]
        for copy in copies:
            copy.start()
        for copy in copies:
            copy.wait()

    channels = out_ref.shape[1]
    per_group = owners // groups
    per_norm = norm_width // CHUNK
    for norm in range(channels // norm_width):
        squares = None
        for chunk in range(norm * per_norm, (norm + 1) * per_norm):
            group = chunk // per_group
            lanes = slice(chunk * CHUNK, (chunk + 1) * CHUNK)
            inner = slice((chunk % per_group) * CHUNK, (chunk % per_group + 1) * CHUNK)
            scale = mm(u0_ref[...], spread(heads, chunk, CHUNK, head_dim))
            carried = mm(cc_ref[:, group * STATE : (group + 1) * STATE], e_ref[chunk])
            gate = gate_ref[:, lanes].astype(F32)
            value = (intra_refs[group][:, inner] + carried * scale) * (gate / (1.0 + jnp.exp(-gate)))
            y_ref[:, lanes] = value
            square = value * value
            for part in range(CHUNK // LANES):
                piece = square[:, part * LANES : (part + 1) * LANES]
                squares = piece if squares is None else squares + piece
        factor = lax.rsqrt(jnp.sum(squares, axis=1, keepdims=True) * (1.0 / norm_width) + norm_eps)
        lanes = slice(norm * norm_width, (norm + 1) * norm_width)
        out_ref[:, lanes] = (y_ref[:, lanes] * factor * gain_ref[:, lanes]).astype(BF16)


def final(cc, u0, gate, gain, intra_parts, pieces, head_dim, apart):
    tok, channels = gate.shape
    heads = channels // head_dim
    owners = len(pieces)
    rows = 64
    width = channels // len(intra_parts)
    return pl.pallas_call(
        functools.partial(final_kernel, owners, heads, head_dim, apart, NORM_HEADS * head_dim),
        out_shape=jax.ShapeDtypeStruct((tok, channels), BF16),
        grid=(tok // rows,),
        in_specs=[
            pl.BlockSpec((rows, cc.shape[1]), lambda i: (i, 0)),
            pl.BlockSpec((rows, 2 * heads), lambda i: (i, 0)),
            pl.BlockSpec((rows, channels), lambda i: (i, 0)),
            pl.BlockSpec((1, channels), lambda i: (0, 0)),
        ]
        + [pl.BlockSpec((rows, width), lambda i: (i, 0))] * len(intra_parts)
        + [ANY] * owners,
        out_specs=pl.BlockSpec((rows, channels), lambda i: (i, 0)),
        scratch_shapes=[
            pltpu.VMEM((owners, STATE, CHUNK), BF16),
            pltpu.VMEM((rows, channels), F32),
            pltpu.SemaphoreType.DMA((owners,)),
        ],
        compiler_params=params(),
        cost_estimate=cost(tok * STATE * channels * 2, tok * channels * 8, tok * channels * 2),
        name="final",
    )(cc, u0, gate, gain, *intra_parts, *pieces)


def shifted(value, steps):
    count = lax.axis_size("seq")
    return lax.ppermute(value, "seq", [(i, i + steps) for i in range(count - steps)])


def entering_by_doubling(pieces):
    whole = jnp.concatenate(pieces, 1).astype(F32)
    state, decay = whole[:STATE], whole[STATE] + (whole[STATE + 1] + whole[STATE + 2])
    step = 1
    while step < lax.axis_size("seq"):
        earlier, fell = shifted((state, decay), step)
        state, decay = decay[None, :] * earlier + state, decay * fell
        step *= 2
    entering = shifted(state, 1).astype(BF16)
    return [entering[:, k * CHUNK : (k + 1) * CHUNK] for k in range(len(pieces))]


def exchanged(pieces):
    count = len(pieces)
    return [pieces[0]] + [lax.ppermute(pieces[k], "seq", [(i, i ^ k) for i in range(count)]) for k in range(1, count)]


def on_device(
    x_input,
    b_input,
    c_input,
    dt_input,
    decay_rate,
    gate_input,
    taps_x,
    taps_b,
    taps_c,
    norm_gain,
    doc_lengths,
):
    tok, channels = x_input.shape
    heads = dt_input.shape[1]
    head_dim = channels // heads
    groups = b_input.shape[1] // STATE
    count = lax.axis_size("seq")
    apart = sends_apart(channels // CHUNK, channels)
    ends = jnp.concatenate([x_input[tok - 8 :], b_input[tok - 8 :], c_input[tok - 8 :]], 1)
    tail = lax.ppermute(ends, "seq", [(i, (i + 1) % count) for i in range(count)])
    w, u, u0, col, row, d = prep(doc_lengths, dt_input, decay_rate[None, :])
    xc, bc, cc, h, *pieces = states(doc_lengths, x_input, b_input, c_input, tail, taps_x, taps_b, taps_c, w, d)
    parts = [intra(group, doc_lengths, xc, bc, cc, h, u, col, row) for group in range(groups)]
    if apart:
        entering = exchanged(scan_blocks(exchanged(pieces)))
    else:
        entering = entering_by_doubling(pieces)
    return final(cc, u0, gate_input, norm_gain[None, :], parts, entering, head_dim, apart)


def solution(mesh):
    rows = P(("groups", "seq"), "dp")
    placed = (rows, rows, rows, rows, P("dp"), rows, P(None, "dp"), P(None, "dp"), P(None, "dp"), P("dp"), P("groups"))
    return jax.shard_map(on_device, mesh=mesh, in_specs=placed, out_specs=rows, check_vma=False)
```

time: 233 us -> 64 us (0.27)
  waiting for transfers between devices: 95.5 us -> 6.23 us
  other arithmetic: 45.5 us -> 0.01 us
  local copies, waits for them, and re-layouts: 33.1 us -> 9.77 us
  Pallas kernels: 0 us -> 21.4 us
  blocking collectives: 17.8 us -> 0 us
  between operations: 15 us -> 0.15 us
  starting transfers between devices: 11.7 us -> 26 us
  matrix products: 12.7 us -> 0 us
    all_gather x1 -> x0, waiting for transfers between devices: 95.5 us -> none  [entering_2(): pieces = jax.tree.map(lambda part: lax.all_gather(part, axis), value)]
    select_n x7 -> x0, other arithmetic: 21.5 us -> none  [lap(): jnp.where(position < mine, new, old)]
    pallas_call x0 -> x6, Pallas kernels: none -> 21.4 us  [the longest x1 7.67 us: states(): pl.pallas_call(functools.partial(state_kernel, owners), out_shape=(jax.Sh...]
    all_gather x1 -> x0, blocking collectives: 17.8 us -> none  [entering_2(): pieces = jax.tree.map(lambda part: lax.all_gather(part, axis), value)]
    ppermute x3 -> x15, starting transfers between devices: 11.7 us -> 26 us  [the longest x14 23 us: exchanged(): lax.ppermute(pieces[k], 'seq', [(i, i ^ k) for i in range(count)])]
    dynamic_slice x14 -> x0, local copies, waits for them, and re-layouts: 13.3 us -> none  [lap(): longer = join(running, jax.tree.map(lambda part: part[position], pieces))]
    dot_general x10 -> x0, matrix products: 11.9 us -> none  [the longest x4 10.3 us: block_terms(): jnp.einsum('hts,shp->thp', weights, x_group, preferred_element_type=jnp.f...]
    convert_element_type x7 -> x0, other arithmetic: 9.76 us -> none  [the longest x2 3.54 us: causal_conv(): return jax.nn.silu(running).astype(jnp.bfloat16)]
  transfers between devices with their start and end apart: 4 -> 15, of which waited for: 1 -> 3; matrix products, arithmetic and copies ran while one was open for 10% -> 1% of each run, Pallas kernels for 0% -> 11%
where the time goes in v1:
time: 64 us; the launch traced here: 63.5 us
  starting transfers between devices  26 us (41%)
  Pallas kernels  21.4 us (33%)
  local copies, waits for them, and re-layouts  9.77 us (15%)
  waiting for transfers between devices  6.23 us (10%)
    ppermute x14, starting transfers between devices, exchanged(): lax.ppermute(pieces[k], 'seq', [(i, i ^ k) for i in range(count)])  23 us
    pallas_call x1, Pallas kernels, states(): pl.pallas_call(functools.partial(state_kernel, owners), out_shape=(jax.Sh...  7.67 us
    unnamed x23, local copies, waits for them, and re-layouts  7.63 us
    pallas_call x2, Pallas kernels, intra(): pl.pallas_call(functools.partial(intra_kernel, group, heads, head_dim), o...  6.01 us
    pallas_call x1, Pallas kernels, final(): pl.pallas_call(functools.partial(final_kernel, owners, heads, head_dim, a...  4.9 us
    ppermute x14, waiting for transfers between devices, exchanged(): lax.ppermute(pieces[k], 'seq', [(i, i ^ k) for i in range(count)])  4.55 us
    ppermute x1, starting transfers between devices, on_device(): lax.ppermute(ends, 'seq', [(i, (i + 1) % count) for i in range(count)])  2.94 us
    pallas_call x1, Pallas kernels, scan_blocks(): pl.pallas_call(functools.partial(scan_kernel, owners), out_shape=(jax.Sha...  1.7 us
  transfers between devices with their start and end apart: 15, of which 3 were waited for; matrix products, arithmetic and copies ran while one was open for 1% of the time, Pallas kernels for 11%

profile of v1, /device:TPU:0, one launch (start us, length us, event | category | flops | bytes accessed | tf_op | source)
XLA Modules:
  0.0 63.5 jit_solution(4059933228306541255)
XLA Ops:
  0.0 0.7 %slice.10 = bf16[8,256]{1,0:T(8,128)(2,1)S(1)} slice(bf16[384,256]{1,0:T(8,128)(2,1)} %b_ref.1), slice={[376:384], [0:256]} | slice | bytes 8192 | tf_op jit(solution)/shard_map/slice | solution.py:477
  0.7 0.7 %slice.11 = bf16[8,256]{1,0:T(8,128)(2,1)S(1)} slice(bf16[384,256]{1,0:T(8,128)(2,1)} %c_ref.1), slice={[376:384], [0:256]} | slice | bytes 8192 | tf_op jit(solution)/shard_map/slice | solution.py:477
  1.4 0.8 %slice.9 = bf16[8,2048]{1,0:T(8,128)(2,1)S(1)} slice(bf16[384,2048]{1,0:T(8,128)(2,1)} %x_ref.1), slice={[376:384], [0:2048]} | slice | bytes 65536 | tf_op jit(solution)/shard_map/slice | solution.py:477
  2.1 2.9 %collective-permute-start = (bf16[8,2560]{1,0:T(8,128)(2,1)S(1)}, bf16[8,2560]{1,0:T(8,128)(2,1)S(1)}, u32[]{:S(2)}, u32[]{:S(2)}) collective-permute-start(bf16[8,2560]{1,0:T(8,128)(2,1)S(1)} %pad_maximum_fusion), channel_id=1, source_target_pairs={{0,2},{2,4},{4,6},{6,8},{8,10},{10,12},{12,14},{14,0},{1,3},{3,5},... | collective-permute-start | bytes 122888 | tf_op jit(solution)/shard_map/ppermute | solution.py:478
  5.1 0.9 %copy.12.dt_ref = f32[384,32]{1,0:T(8,128)S(1)} copy(f32[384,32]{0,1:T(8,128)} %param.14) | data formatting | bytes 98304 | tf_op args[3]
  6.0 0.0 copy-start.2
  6.0 0.6 %copy-done.2 = s32[4]{0:T(128)S(1)} copy-done((s32[4]{0:T(128)S(1)}, s32[4]{0:T(128)}, u32[]{:S(2)}) %copy-start.2) | copy-done | bytes 40
  6.7 0.7 %copy-done.5 = f32[32]{0:T(128)S(1)} copy-done((f32[32]{0:T(128)S(1)}, f32[32]{0:T(128)}, u32[]{:S(2)}) %copy-start.5) | copy-done | bytes 152
  7.3 1.1 %prep.1 = (bf16[384,64]{1,0:T(8,128)(2,1)S(1)}, bf16[384,64]{1,0:T(8,128)(2,1)S(1)}, bf16[384,64]{1,0:T(8,128)(2,1)S(1)}, f32[384,32]{1,0:T(8,128)S(1)}, f32[32,...) custom-call(s32[4]{0:T(128)S(1)} %copy-done.2, f32[384,32]{1,0:T(8,128)S(1)} %copy.12.dt_ref, f32[1,32]{1,0:T(1,128)S(1)} %bitcast.3), custom_call_target="tpu_custom_call" | custom-call | flops 9437184 | bytes 786432 | tf_op jit(solution)/shard_map/prep/pallas_call | solution.py:115
  8.4 1.7 %collective-permute-done.tail_ref = bf16[8,2560]{1,0:T(8,128)(2,1)S(1)} collective-permute-done((bf16[8,2560]{1,0:T(8,128)(2,1)S(1)}, bf16[8,2560]{1,0:T(8,128)(2,1)S(1)}, u32[]{:S(2)}, u32[]{:S(2)}) %collective-permute-start) | collective-permute-done | bytes 40992 | tf_op jit(solution)/shard_map/ppermute | solution.py:478
  10.1 1.4 %copy-done.4 = bf16[384,2048]{1,0:T(8,128)(2,1)S(1)} copy-done((bf16[384,2048]{1,0:T(8,128)(2,1)S(1)}, bf16[384,2048]{1,0:T(8,128)(2,1)}, u32[]{:S(2)}) %copy-start.4) | copy-done | bytes 1572888
  11.5 0.9 %copy-done.6 = bf16[384,256]{1,0:T(8,128)(2,1)S(1)} copy-done((bf16[384,256]{1,0:T(8,128)(2,1)S(1)}, bf16[384,256]{1,0:T(8,128)(2,1)}, u32[]{:S(2)}) %copy-start.6) | copy-done | bytes 196632
  12.4 0.9 %copy-done.7 = bf16[384,256]{1,0:T(8,128)(2,1)S(1)} copy-done((bf16[384,256]{1,0:T(8,128)(2,1)S(1)}, bf16[384,256]{1,0:T(8,128)(2,1)}, u32[]{:S(2)}) %copy-start.7) | copy-done | bytes 196632
  13.4 0.8 %copy-done.8 = f32[4,2048]{1,0:T(4,128)S(1)} copy-done((f32[4,2048]{1,0:T(4,128)S(1)}, f32[4,2048]{1,0:T(4,128)}, u32[]{:S(2)}) %copy-start.8) | copy-done | bytes 32792
  14.1 0.7 %copy-done.9 = f32[4,256]{1,0:T(4,128)S(1)} copy-done((f32[4,256]{1,0:T(4,128)S(1)}, f32[4,256]{1,0:T(4,128)}, u32[]{:S(2)}) %copy-start.9) | copy-done | bytes 4120
  14.8 0.7 %copy-done.10 = f32[4,256]{1,0:T(4,128)S(1)} copy-done((f32[4,256]{1,0:T(4,128)S(1)}, f32[4,256]{1,0:T(4,128)}, u32[]{:S(2)}) %copy-start.10) | copy-done | bytes 4120
  15.5 7.7 %conv_state.1 = (bf16[384,2048]{1,0:T(8,128)(2,1)S(1)}, bf16[384,256]{1,0:T(8,128)(2,1)S(1)}, bf16[384,256]{1,0:T(8,128)(2,1)S(1)}, bf16[2,128,2048]{2,1,0:T(8,1...) custom-call(s32[4]{0:T(128)S(1)} %copy-done.2, ...), custom_call_target="tpu_custom_call" | custom-call | flops 402653184 | bytes 4718592 | tf_op jit(solution)/shard_map/conv_state/pallas_call | solution.py:239
  23.2 0.1 collective-permute-start.1
  23.3 1.4 %collective-permute-start.2 = (bf16[136,256]{1,0:T(8,128)(2,1)S(1)}, bf16[136,256]{1,0:T(8,128)(2,1)S(1)}, u32[]{:S(2)}, u32[]{:S(2)}) collective-permute-start(bf16[136,256]{1,0:T(8,128)(2,1)S(1)} %get-tuple-element.43), channel_id=1, source_target_pairs={{0,4},{2,6},{4,0},{6,2},{8,12},{10,14},{12,8},{14,10},{1,5},{3,7},... | collective-permute-start | bytes 208904 | tf_op jit(solution)/shard_map/ppermute | solution.py:455
  24.7 2.0 %collective-permute-start.3 = (bf16[136,256]{1,0:T(8,128)(2,1)S(1)}, bf16[136,256]{1,0:T(8,128)(2,1)S(1)}, u32[]{:S(2)}, u32[]{:S(2)}) collective-permute-start(bf16[136,256]{1,0:T(8,128)(2,1)S(1)} %get-tuple-element.44), channel_id=1, source_target_pairs={{0,6},{2,4},{4,2},{6,0},{8,14},{10,12},{12,10},{14,8},{1,7},{3,5},... | collective-permute-start | bytes 208904 | tf_op jit(solution)/shard_map/ppermute | solution.py:455
  26.7 1.0 %collective-permute-start.4 = (bf16[136,256]{1,0:T(8,128)(2,1)S(1)}, bf16[136,256]{1,0:T(8,128)(2,1)S(1)}, u32[]{:S(2)}, u32[]{:S(2)}) collective-permute-start(bf16[136,256]{1,0:T(8,128)(2,1)S(1)} %get-tuple-element.45), channel_id=1, source_target_pairs={{0,8},{2,10},{4,12},{6,14},{8,0},{10,2},{12,4},{14,6},{1,9},{3,11}... | collective-permute-start | bytes 208904 | tf_op jit(solution)/shard_map/ppermute | solution.py:455
  27.7 1.5 %collective-permute-start.5 = (bf16[136,256]{1,0:T(8,128)(2,1)S(1)}, bf16[136,256]{1,0:T(8,128)(2,1)S(1)}, u32[]{:S(2)}, u32[]{:S(2)}) collective-permute-start(bf16[136,256]{1,0:T(8,128)(2,1)S(1)} %get-tuple-element.46), channel_id=1, source_target_pairs={{0,10},{2,8},{4,14},{6,12},{8,2},{10,0},{12,6},{14,4},{1,11},{3,9}... | collective-permute-start | bytes 208904 | tf_op jit(solution)/shard_map/ppermute | solution.py:455
  29.2 0.0 collective-permute-done.1.refs_1_
  29.2 2.5 %collective-permute-start.6 = (bf16[136,256]{1,0:T(8,128)(2,1)S(1)}, bf16[136,256]{1,0:T(8,128)(2,1)S(1)}, u32[]{:S(2)}, u32[]{:S(2)}) collective-permute-start(bf16[136,256]{1,0:T(8,128)(2,1)S(1)} %get-tuple-element.47), channel_id=1, source_target_pairs={{0,12},{2,14},{4,8},{6,10},{8,4},{10,6},{12,0},{14,2},{1,13},{3,15... | collective-permute-start | bytes 208904 | tf_op jit(solution)/shard_map/ppermute | solution.py:455
  31.7 0.0 collective-permute-done.2.refs_2_
  31.7 2.7 %collective-permute-start.7 = (bf16[136,256]{1,0:T(8,128)(2,1)S(1)}, bf16[136,256]{1,0:T(8,128)(2,1)S(1)}, u32[]{:S(2)}, u32[]{:S(2)}) collective-permute-start(bf16[136,256]{1,0:T(8,128)(2,1)S(1)} %get-tuple-element.48), channel_id=1, source_target_pairs={{0,14},{2,12},{4,10},{6,8},{8,6},{10,4},{12,2},{14,0},{1,15},{3,13... | collective-permute-start | bytes 208904 | tf_op jit(solution)/shard_map/ppermute | solution.py:455
  34.4 0.0 collective-permute-done.3.refs_3_
  34.4 2.5 %collective-permute-done.4.refs_4_ = bf16[136,256]{1,0:T(8,128)(2,1)S(1)} collective-permute-done((bf16[136,256]{1,0:T(8,128)(2,1)S(1)}, bf16[136,256]{1,0:T(8,128)(2,1)S(1)}, u32[]{:S(2)}, u32[]{:S(2)}) %collective-permute-start.4) | collective-permute-done | bytes 69664 | tf_op jit(solution)/shard_map/ppermute | solution.py:455
  36.9 2.1 %collective-permute-done.5.refs_5_ = bf16[136,256]{1,0:T(8,128)(2,1)S(1)} collective-permute-done((bf16[136,256]{1,0:T(8,128)(2,1)S(1)}, bf16[136,256]{1,0:T(8,128)(2,1)S(1)}, u32[]{:S(2)}, u32[]{:S(2)}) %collective-permute-start.5) | collective-permute-done | bytes 69664 | tf_op jit(solution)/shard_map/ppermute | solution.py:455
  38.9 0.0 collective-permute-done.6.refs_6_
  38.9 0.0 collective-permute-done.7.refs_7_
  38.9 1.7 %block_scan.1 = (bf16[128,256]{1,0:T(8,128)(2,1)S(1)}, bf16[128,256]{1,0:T(8,128)(2,1)S(1)}, bf16[128,256]{1,0:T(8,128)(2,1)S(1)}, bf16[128,256]{1,0:T(8,128)(2,...) custom-call(bf16[136,256]{1,0:T(8,128)(2,1)S(1)} %get-tuple-element., ...), custom_call_target="tpu_custom_call" | custom-call | flops 524288 | bytes 1048576 | tf_op jit(solution)/shard_map/block_scan/pallas_call | solution.py:289
  40.6 1.7 %collective-permute-start.8 = (bf16[128,256]{1,0:T(8,128)(2,1)S(1)}, bf16[128,256]{1,0:T(8,128)(2,1)S(1)}, u32[]{:S(2)}, u32[]{:S(2)}) collective-permute-start(bf16[128,256]{1,0:T(8,128)(2,1)S(1)} %get-tuple-element.50), channel_id=1, source_target_pairs={{0,2},{2,0},{4,6},{6,4},{8,10},{10,8},{12,14},{14,12},{1,3},{3,1},... | collective-permute-start | bytes 196616 | tf_op jit(solution)/shard_map/ppermute | solution.py:455
  42.3 2.5 %collective-permute-start.9 = (bf16[128,256]{1,0:T(8,128)(2,1)S(1)}, bf16[128,256]{1,0:T(8,128)(2,1)S(1)}, u32[]{:S(2)}, u32[]{:S(2)}) collective-permute-start(bf16[128,256]{1,0:T(8,128)(2,1)S(1)} %get-tuple-element.51), channel_id=1, source_target_pairs={{0,4},{2,6},{4,0},{6,2},{8,12},{10,14},{12,8},{14,10},{1,5},{3,7},... | collective-permute-start | bytes 196616 | tf_op jit(solution)/shard_map/ppermute | solution.py:455
  44.8 0.0 collective-permute-start.10
  44.8 2.5 %collective-permute-start.11 = (bf16[128,256]{1,0:T(8,128)(2,1)S(1)}, bf16[128,256]{1,0:T(8,128)(2,1)S(1)}, u32[]{:S(2)}, u32[]{:S(2)}) collective-permute-start(bf16[128,256]{1,0:T(8,128)(2,1)S(1)} %get-tuple-element.53), channel_id=1, source_target_pairs={{0,8},{2,10},{4,12},{6,14},{8,0},{10,2},{12,4},{14,6},{1,9},{3,11}... | collective-permute-start | bytes 196616 | tf_op jit(solution)/shard_map/ppermute | solution.py:455
  47.3 1.3 %collective-permute-start.12 = (bf16[128,256]{1,0:T(8,128)(2,1)S(1)}, bf16[128,256]{1,0:T(8,128)(2,1)S(1)}, u32[]{:S(2)}, u32[]{:S(2)}) collective-permute-start(bf16[128,256]{1,0:T(8,128)(2,1)S(1)} %get-tuple-element.54), channel_id=1, source_target_pairs={{0,10},{2,8},{4,14},{6,12},{8,2},{10,0},{12,6},{14,4},{1,11},{3,9}... | collective-permute-start | bytes 196616 | tf_op jit(solution)/shard_map/ppermute | solution.py:455
  48.6 0.0 collective-permute-done.8.refs_7_
  48.6 1.7 %collective-permute-start.13 = (bf16[128,256]{1,0:T(8,128)(2,1)S(1)}, bf16[128,256]{1,0:T(8,128)(2,1)S(1)}, u32[]{:S(2)}, u32[]{:S(2)}) collective-permute-start(bf16[128,256]{1,0:T(8,128)(2,1)S(1)} %get-tuple-element.55), channel_id=1, source_target_pairs={{0,12},{2,14},{4,8},{6,10},{8,4},{10,6},{12,0},{14,2},{1,13},{3,15... | collective-permute-start | bytes 196616 | tf_op jit(solution)/shard_map/ppermute | solution.py:455
  50.3 2.1 %collective-permute-start.14 = (bf16[128,256]{1,0:T(8,128)(2,1)S(1)}, bf16[128,256]{1,0:T(8,128)(2,1)S(1)}, u32[]{:S(2)}, u32[]{:S(2)}) collective-permute-start(bf16[128,256]{1,0:T(8,128)(2,1)S(1)} %get-tuple-element.56), channel_id=1, source_target_pairs={{0,14},{2,12},{4,10},{6,8},{8,6},{10,4},{12,2},{14,0},{1,15},{3,13... | collective-permute-start | bytes 196616 | tf_op jit(solution)/shard_map/ppermute | solution.py:455
  52.5 3.0 %intra.3.refs_5_ = f32[384,1024]{1,0:T(8,128)S(1)} custom-call(s32[4]{0:T(128)S(1)} %copy-done.3, bf16[384,2048]{1,0:T(8,128)(2,1)S(1)} %get-tuple-element.35.xc_ref, bf16[384,256]{1,0:T(8,128)(2,1)S(1)} %get-tuple-element.36.bc_ref, bf16[384,256]{1,0:T(8,128)(2,1)S(1)} %get-tuple-element.33.cc_ref.refs_0_, ...), custom_call_target="tpu_custom_call" | custom-call | flops 201326592 | bytes 3145728 | tf_op jit(solution)/shard_map/intra/pallas_call | solution.py:346
  55.5 0.0 copy-start
  55.5 0.0 copy-start.1
  55.5 3.0 %intra.2.refs_4_ = f32[384,1024]{1,0:T(8,128)S(1)} custom-call(s32[4]{0:T(128)S(1)} %copy-done.3, bf16[384,2048]{1,0:T(8,128)(2,1)S(1)} %get-tuple-element.35.xc_ref, bf16[384,256]{1,0:T(8,128)(2,1)S(1)} %get-tuple-element.36.bc_ref, bf16[384,256]{1,0:T(8,128)(2,1)S(1)} %get-tuple-element.33.cc_ref.refs_0_, ...), custom_call_target="tpu_custom_call" | custom-call | flops 201326592 | bytes 3145728 | tf_op jit(solution)/shard_map/intra/pallas_call | solution.py:346
  58.5 0.0 collective-permute-done.10.refs_9_
  58.5 0.0 collective-permute-done.12.refs_11_
  58.5 0.0 collective-permute-done.13.refs_12_
  58.6 4.9 %final.1 = bf16[384,2048]{1,0:T(8,128)(2,1)} custom-call(bf16[384,256]{1,0:T(8,128)(2,1)S(1)} %get-tuple-element.33.cc_ref.refs_0_, bf16[384,64]{1,0:T(8,128)(2,1)S(1)} %get-tuple-element.34.refs_1_, bf16[384,2048]{1,0:T(8,128)(2,1)S(1)} %copy-done, f32[1,2048]{1,0:T(1,128)S(1)} %bitcast.2, f32[384,1024]{1,0:T(8,128)S(1)} %intra.2.refs_4_, ...), custom_call_target="tpu_custom_call" | custom-call | flops 201326592 | bytes 6291456 | tf_op jit(solution)/shard_map/final/pallas_call | solution.py:412
  (15 shorter events, 0.0 us)
Async XLA Ops:
  2.1 8.0 %collective-permute-start = (bf16[8,2560]{1,0:T(8,128)(2,1)S(1)}, bf16[8,2560]{1,0:T(8,128)(2,1)S(1)}, u32[]{:S(2)}, u32[]{:S(2)}) collective-permute-start(bf16[8,2560]{1,0:T(8,128)(2,1)S(1)} %pad_maximum_fusion), channel_id=1, source_target_pairs={{0,2},{2,4},{4,6},{6,8},{8,10},{10,12},{12,14},{14,0},{1,3},{3,5},... | collective-permute-start | bytes 122888 | tf_op jit(solution)/shard_map/ppermute | solution.py:478
  6.0 0.7 %copy-start.2 = (s32[4]{0:T(128)S(1)}, s32[4]{0:T(128)}, u32[]{:S(2)}) copy-start(s32[4]{0:T(128)} %dl_ref.7) | copy-start | bytes 52
  6.7 0.7 %copy-start.5 = (f32[32]{0:T(128)S(1)}, f32[32]{0:T(128)}, u32[]{:S(2)}) copy-start(f32[32]{0:T(128)} %param.15) | copy-start | bytes 388
  10.1 1.4 %copy-start.4 = (bf16[384,2048]{1,0:T(8,128)(2,1)S(1)}, bf16[384,2048]{1,0:T(8,128)(2,1)}, u32[]{:S(2)}) copy-start(bf16[384,2048]{1,0:T(8,128)(2,1)} %x_ref.1) | copy-start | bytes 4718596
  11.5 0.9 %copy-start.6 = (bf16[384,256]{1,0:T(8,128)(2,1)S(1)}, bf16[384,256]{1,0:T(8,128)(2,1)}, u32[]{:S(2)}) copy-start(bf16[384,256]{1,0:T(8,128)(2,1)} %b_ref.1) | copy-start | bytes 589828
  12.4 0.9 %copy-start.7 = (bf16[384,256]{1,0:T(8,128)(2,1)S(1)}, bf16[384,256]{1,0:T(8,128)(2,1)}, u32[]{:S(2)}) copy-start(bf16[384,256]{1,0:T(8,128)(2,1)} %c_ref.1) | copy-start | bytes 589828
  13.4 0.8 %copy-start.8 = (f32[4,2048]{1,0:T(4,128)S(1)}, f32[4,2048]{1,0:T(4,128)}, u32[]{:S(2)}) copy-start(f32[4,2048]{1,0:T(4,128)} %taps_x_ref.1) | copy-start | bytes 98308
  14.1 0.7 %copy-start.9 = (f32[4,256]{1,0:T(4,128)S(1)}, f32[4,256]{1,0:T(4,128)}, u32[]{:S(2)}) copy-start(f32[4,256]{1,0:T(4,128)} %taps_b_ref.1) | copy-start | bytes 12292
  14.8 0.7 %copy-start.10 = (f32[4,256]{1,0:T(4,128)S(1)}, f32[4,256]{1,0:T(4,128)}, u32[]{:S(2)}) copy-start(f32[4,256]{1,0:T(4,128)} %taps_c_ref.1) | copy-start | bytes 12292
  15.5 37.0 %copy-start.3 = (s32[4]{0:T(128)S(1)}, s32[4]{0:T(128)}, u32[]{:S(2)}) copy-start(s32[4]{0:T(128)} %dl_ref.7) | copy-start | bytes 52
  23.2 6.0 %collective-permute-start.1 = (bf16[136,256]{1,0:T(8,128)(2,1)S(1)}, bf16[136,256]{1,0:T(8,128)(2,1)S(1)}, u32[]{:S(2)}, u32[]{:S(2)}) collective-permute-start(bf16[136,256]{1,0:T(8,128)(2,1)S(1)} %get-tuple-element.42), channel_id=1, source_target_pairs={{0,2},{2,0},{4,6},{6,4},{8,10},{10,8},{12,14},{14,12},{1,3},{3,1},... | collective-permute-start | bytes 208904 | tf_op jit(solution)/shard_map/ppermute | solution.py:455
  23.3 8.4 %collective-permute-start.2 = (bf16[136,256]{1,0:T(8,128)(2,1)S(1)}, bf16[136,256]{1,0:T(8,128)(2,1)S(1)}, u32[]{:S(2)}, u32[]{:S(2)}) collective-permute-start(bf16[136,256]{1,0:T(8,128)(2,1)S(1)} %get-tuple-element.43), channel_id=1, source_target_pairs={{0,4},{2,6},{4,0},{6,2},{8,12},{10,14},{12,8},{14,10},{1,5},{3,7},... | collective-permute-start | bytes 208904 | tf_op jit(solution)/shard_map/ppermute | solution.py:455
  24.7 9.7 %collective-permute-start.3 = (bf16[136,256]{1,0:T(8,128)(2,1)S(1)}, bf16[136,256]{1,0:T(8,128)(2,1)S(1)}, u32[]{:S(2)}, u32[]{:S(2)}) collective-permute-start(bf16[136,256]{1,0:T(8,128)(2,1)S(1)} %get-tuple-element.44), channel_id=1, source_target_pairs={{0,6},{2,4},{4,2},{6,0},{8,14},{10,12},{12,10},{14,8},{1,7},{3,5},... | collective-permute-start | bytes 208904 | tf_op jit(solution)/shard_map/ppermute | solution.py:455
  26.7 10.1 %collective-permute-start.4 = (bf16[136,256]{1,0:T(8,128)(2,1)S(1)}, bf16[136,256]{1,0:T(8,128)(2,1)S(1)}, u32[]{:S(2)}, u32[]{:S(2)}) collective-permute-start(bf16[136,256]{1,0:T(8,128)(2,1)S(1)} %get-tuple-element.45), channel_id=1, source_target_pairs={{0,8},{2,10},{4,12},{6,14},{8,0},{10,2},{12,4},{14,6},{1,9},{3,11}... | collective-permute-start | bytes 208904 | tf_op jit(solution)/shard_map/ppermute | solution.py:455
  27.7 11.2 %collective-permute-start.5 = (bf16[136,256]{1,0:T(8,128)(2,1)S(1)}, bf16[136,256]{1,0:T(8,128)(2,1)S(1)}, u32[]{:S(2)}, u32[]{:S(2)}) collective-permute-start(bf16[136,256]{1,0:T(8,128)(2,1)S(1)} %get-tuple-element.46), channel_id=1, source_target_pairs={{0,10},{2,8},{4,14},{6,12},{8,2},{10,0},{12,6},{14,4},{1,11},{3,9}... | collective-permute-start | bytes 208904 | tf_op jit(solution)/shard_map/ppermute | solution.py:455
  29.2 9.7 %collective-permute-start.6 = (bf16[136,256]{1,0:T(8,128)(2,1)S(1)}, bf16[136,256]{1,0:T(8,128)(2,1)S(1)}, u32[]{:S(2)}, u32[]{:S(2)}) collective-permute-start(bf16[136,256]{1,0:T(8,128)(2,1)S(1)} %get-tuple-element.47), channel_id=1, source_target_pairs={{0,12},{2,14},{4,8},{6,10},{8,4},{10,6},{12,0},{14,2},{1,13},{3,15... | collective-permute-start | bytes 208904 | tf_op jit(solution)/shard_map/ppermute | solution.py:455
  31.7 7.2 %collective-permute-start.7 = (bf16[136,256]{1,0:T(8,128)(2,1)S(1)}, bf16[136,256]{1,0:T(8,128)(2,1)S(1)}, u32[]{:S(2)}, u32[]{:S(2)}) collective-permute-start(bf16[136,256]{1,0:T(8,128)(2,1)S(1)} %get-tuple-element.48), channel_id=1, source_target_pairs={{0,14},{2,12},{4,10},{6,8},{8,6},{10,4},{12,2},{14,0},{1,15},{3,13... | collective-permute-start | bytes 208904 | tf_op jit(solution)/shard_map/ppermute | solution.py:455
  40.6 8.0 %collective-permute-start.8 = (bf16[128,256]{1,0:T(8,128)(2,1)S(1)}, bf16[128,256]{1,0:T(8,128)(2,1)S(1)}, u32[]{:S(2)}, u32[]{:S(2)}) collective-permute-start(bf16[128,256]{1,0:T(8,128)(2,1)S(1)} %get-tuple-element.50), channel_id=1, source_target_pairs={{0,2},{2,0},{4,6},{6,4},{8,10},{10,8},{12,14},{14,12},{1,3},{3,1},... | collective-permute-start | bytes 196616 | tf_op jit(solution)/shard_map/ppermute | solution.py:455
  42.3 8.0 %collective-permute-start.9 = (bf16[128,256]{1,0:T(8,128)(2,1)S(1)}, bf16[128,256]{1,0:T(8,128)(2,1)S(1)}, u32[]{:S(2)}, u32[]{:S(2)}) collective-permute-start(bf16[128,256]{1,0:T(8,128)(2,1)S(1)} %get-tuple-element.51), channel_id=1, source_target_pairs={{0,4},{2,6},{4,0},{6,2},{8,12},{10,14},{12,8},{14,10},{1,5},{3,7},... | collective-permute-start | bytes 196616 | tf_op jit(solution)/shard_map/ppermute | solution.py:455
  44.8 13.7 %collective-permute-start.10 = (bf16[128,256]{1,0:T(8,128)(2,1)S(1)}, bf16[128,256]{1,0:T(8,128)(2,1)S(1)}, u32[]{:S(2)}, u32[]{:S(2)}) collective-permute-start(bf16[128,256]{1,0:T(8,128)(2,1)S(1)} %get-tuple-element.52), channel_id=1, source_target_pairs={{0,6},{2,4},{4,2},{6,0},{8,14},{10,12},{12,10},{14,8},{1,7},{3,5},... | collective-permute-start | bytes 196616 | tf_op jit(solution)/shard_map/ppermute | solution.py:455
  44.8 13.7 %collective-permute-start.11 = (bf16[128,256]{1,0:T(8,128)(2,1)S(1)}, bf16[128,256]{1,0:T(8,128)(2,1)S(1)}, u32[]{:S(2)}, u32[]{:S(2)}) collective-permute-start(bf16[128,256]{1,0:T(8,128)(2,1)S(1)} %get-tuple-element.53), channel_id=1, source_target_pairs={{0,8},{2,10},{4,12},{6,14},{8,0},{10,2},{12,4},{14,6},{1,9},{3,11}... | collective-permute-start | bytes 196616 | tf_op jit(solution)/shard_map/ppermute | solution.py:455
  47.3 11.2 %collective-permute-start.12 = (bf16[128,256]{1,0:T(8,128)(2,1)S(1)}, bf16[128,256]{1,0:T(8,128)(2,1)S(1)}, u32[]{:S(2)}, u32[]{:S(2)}) collective-permute-start(bf16[128,256]{1,0:T(8,128)(2,1)S(1)} %get-tuple-element.54), channel_id=1, source_target_pairs={{0,10},{2,8},{4,14},{6,12},{8,2},{10,0},{12,6},{14,4},{1,11},{3,9}... | collective-permute-start | bytes 196616 | tf_op jit(solution)/shard_map/ppermute | solution.py:455
  48.6 9.9 %collective-permute-start.13 = (bf16[128,256]{1,0:T(8,128)(2,1)S(1)}, bf16[128,256]{1,0:T(8,128)(2,1)S(1)}, u32[]{:S(2)}, u32[]{:S(2)}) collective-permute-start(bf16[128,256]{1,0:T(8,128)(2,1)S(1)} %get-tuple-element.55), channel_id=1, source_target_pairs={{0,12},{2,14},{4,8},{6,10},{8,4},{10,6},{12,0},{14,2},{1,13},{3,15... | collective-permute-start | bytes 196616 | tf_op jit(solution)/shard_map/ppermute | solution.py:455
  50.3 8.2 %collective-permute-start.14 = (bf16[128,256]{1,0:T(8,128)(2,1)S(1)}, bf16[128,256]{1,0:T(8,128)(2,1)S(1)}, u32[]{:S(2)}, u32[]{:S(2)}) collective-permute-start(bf16[128,256]{1,0:T(8,128)(2,1)S(1)} %get-tuple-element.56), channel_id=1, source_target_pairs={{0,14},{2,12},{4,10},{6,8},{8,6},{10,4},{12,2},{14,0},{1,15},{3,13... | collective-permute-start | bytes 196616 | tf_op jit(solution)/shard_map/ppermute | solution.py:455
  55.5 3.1 %copy-start = (bf16[384,2048]{1,0:T(8,128)(2,1)S(1)}, bf16[384,2048]{1,0:T(8,128)(2,1)}, u32[]{:S(2)}) copy-start(bf16[384,2048]{1,0:T(8,128)(2,1)} %refs_2_.1) | copy-start | bytes 4718596
  55.5 3.1 %copy-start.1 = (f32[2048]{0:T(1024)S(1)}, f32[2048]{0:T(1024)}, u32[]{:S(2)}) copy-start(f32[2048]{0:T(1024)} %param.20) | copy-start | bytes 24580

commit v2 on v0

v2 whole, which is shorter than its diff:
```python
import functools

import jax
import jax.numpy as jnp
from jax import lax
from jax.experimental import pallas as pl
from jax.experimental.pallas import tpu as pltpu
from jax.sharding import PartitionSpec as P

STATE = 128
NORM_HEADS = 16
SUB = 128
CHUNK = 256
LANES = 128
ROWS = 32
CLUSTER = 4
LOG2E = 1.4426950408889634
norm_eps = 1e-05

F32 = jnp.float32
BF16 = jnp.bfloat16
VMEM = pl.BlockSpec(memory_space=pltpu.VMEM)
SMEM = pl.BlockSpec(memory_space=pltpu.SMEM)
ANY = pl.BlockSpec(memory_space=pl.ANY)
HBM = pl.BlockSpec(memory_space=pltpu.HBM)


def params(mib=48):
    return pltpu.CompilerParams(vmem_limit_bytes=mib << 20)


def cost(flops, moved, transcendentals=0):
    return pl.CostEstimate(flops=flops, bytes_accessed=moved, transcendentals=transcendentals)


def doc_edges(dl_ref):
    edges = [0]
    for i in range(dl_ref.shape[0] - 1):
        edges.append(edges[-1] + dl_ref[i])
    return edges


def doc_start(token, edges):
    start = jnp.zeros_like(token)
    for edge in edges[1:]:
        start = jnp.where(token >= edge, jnp.maximum(start, edge), start)
    return start


def split2(value):
    high = value.astype(BF16)
    return high, (value - high.astype(F32)).astype(BF16)


def split3(value):
    high = value.astype(BF16)
    rest = value - high.astype(F32)
    mid = rest.astype(BF16)
    return high, mid, (rest - mid.astype(F32)).astype(BF16)


def mm(a, b):
    return jnp.dot(a, b, preferred_element_type=F32)


def silu(value):
    half = 0.5 * value
    return half + half * jnp.tanh(half)


def spread(which, first_head, heads, width, head_dim):
    row = lax.broadcasted_iota(jnp.int32, (2 * LANES, width), 0) & (LANES - 1)
    lane = lax.broadcasted_iota(jnp.int32, (2 * LANES, width), 1)
    low = (row - (which * heads + first_head)) * head_dim
    return jnp.where((lane >= low) & (lane < low + head_dim), 1.0, 0.0).astype(BF16)


def start_all(copies):
    for copy in copies:
        copy.start()


def wait_all(copies):
    for copy in copies:
        copy.wait()


def pack_kernel(x_ref, b_ref, c_ref, out_ref, sem):
    copies, low = [], 0
    for i, ref in enumerate((x_ref, b_ref, c_ref)):
        tok, width = ref.shape
        copies.append(
            pltpu.make_async_copy(ref.at[pl.ds(tok - 8, 8), :], out_ref.at[:, pl.ds(low, width)], sem.at[i])
        )
        low += width
    start_all(copies)
    wait_all(copies)


def pack(x, b, c):
    width = x.shape[1] + b.shape[1] + c.shape[1]
    return pl.pallas_call(
        pack_kernel,
        out_shape=jax.ShapeDtypeStruct((8, width), BF16),
        in_specs=[HBM] * 3,
        out_specs=VMEM,
        scratch_shapes=[pltpu.SemaphoreType.DMA((3,))],
        name="pack",
    )(x, b, c)


def tables(row0, edges, dt_ref, rate_ref, tab_ref, tab32_ref, row_ref, d_ref):
    heads, tok = dt_ref.shape
    upto = jnp.where(
        lax.broadcasted_iota(jnp.int32, (SUB, SUB), 0) <= lax.broadcasted_iota(jnp.int32, (SUB, SUB), 1), 1.0, 0.0
    ).astype(BF16)
    rate = jnp.concatenate([rate_ref[...], jnp.zeros((1, LANES - heads), F32)], 1)
    rate = jnp.broadcast_to(rate, (LANES, LANES)).T[:heads]
    total = jnp.zeros((heads, 1), F32)
    decays = []
    for c in range(tok // SUB):
        span = slice(c * SUB, (c + 1) * SUB)
        first = row0 + c * SUB
        dt = dt_ref[:, span]
        step = jnp.maximum(dt, 0.0) + jnp.log1p(jnp.exp(-jnp.abs(dt)))
        parts = split3(-(step * rate))
        cum = mm(parts[0], upto) + (mm(parts[1], upto) + mm(parts[2], upto))
        last = cum[:, SUB - 1 :]
        token = first + lax.broadcasted_iota(jnp.int32, (heads, SUB), 1)
        start = doc_start(token, edges)
        last_start = doc_start(jnp.int32(first + SUB - 1), edges)
        to_end = jnp.exp(last - cum) * step * jnp.where(token >= last_start, 1.0, 0.0)
        since_sub = jnp.exp(cum) * jnp.where(start < first, 1.0, 0.0)
        since_block = jnp.exp(cum + total) * jnp.where(start < row0, 1.0, 0.0)
        table = jnp.concatenate([to_end, since_sub, since_block, cum * LOG2E], 0).T
        tab32_ref[span, :] = table
        tab_ref[span, :] = jnp.concatenate(split2(table), 1)
        row_ref[:, span] = (jnp.log(step) - cum) * LOG2E
        decays.append(jnp.exp(last) * jnp.where(last_start < first, 1.0, 0.0))
        total = total + last
    end_start = doc_start(jnp.int32(row0 + tok - 1), edges)
    whole = jnp.exp(total) * jnp.where(end_start < row0, 1.0, 0.0)
    columns = [part.astype(F32) for part in split3(whole)] + decays[1:]
    columns.append(jnp.zeros((heads, LANES - len(columns)), F32))
    columns = jnp.concatenate([jnp.concatenate(columns, 1), jnp.zeros((LANES - heads, LANES), F32)], 0)
    d_ref[...] = jnp.concatenate(split2(columns.T[:8]), 1)


def conv_kernel(
    dl_hbm,
    dt_hbm,
    rate_hbm,
    x_hbm,
    b_hbm,
    c_hbm,
    taps_x_hbm,
    taps_b_hbm,
    taps_c_hbm,
    tab_ref,
    tab32_ref,
    row_ref,
    d_ref,
    age_ref,
    taps_ref,
    part_ref,
    xc_ref,
    bc_ref,
    cc_ref,
    dl_ref,
    dt_ref,
    rate_ref,
    in_ref,
    ext_ref,
    mask_ref,
    sem,
    in_sem,
):
    tok, channels = x_hbm.shape
    gn = b_hbm.shape[1]
    taps_len = taps_x_hbm.shape[0]
    row0 = lax.axis_index("seq") * tok
    chunks = channels // CHUNK
    small = [pltpu.make_async_copy(dl_hbm, dl_ref, sem.at[0])]
    small.append(pltpu.make_async_copy(dt_hbm, dt_ref, sem.at[1]))
    small.append(pltpu.make_async_copy(rate_hbm, rate_ref, sem.at[2]))
    low = 0
    for i, ref in enumerate((taps_x_hbm, taps_b_hbm, taps_c_hbm)):
        small.append(pltpu.make_async_copy(ref, taps_ref.at[:, pl.ds(low, ref.shape[1])], sem.at[3 + i]))
        low += ref.shape[1]
    start_all(small)

    def chunk_copy(ref, at, place):
        return pltpu.make_async_copy(ref.at[:, pl.ds(at, CHUNK)], in_ref.at[place], in_sem.at[place])

    for k in range(chunks):
        chunk_copy(x_hbm, k * CHUNK, k).start()
    chunk_copy(b_hbm, 0, chunks).start()
    chunk_copy(c_hbm, 0, chunks + 1).start()
    wait_all(small)
    edges = doc_edges(dl_ref)
    tables(row0, edges, dt_ref, rate_ref, tab_ref, tab32_ref, row_ref, d_ref)
    token = row0 + lax.broadcasted_iota(jnp.int32, (tok, LANES), 0)
    age = token - doc_start(token, edges)
    age_ref[...] = age
    for back in range(1, taps_len):
        mask_ref[back - 1] = jnp.where(age >= back, 1.0, 0.0)
    ext_ref[:8, :] = jnp.zeros((8, CHUNK), F32)

    def convolve(place, lanes, to_ref, to_lanes):
        ext_ref[8:, :] = in_ref[place].astype(F32)
        taps = [taps_ref[i : i + 1, lanes] for i in range(taps_len)]
        for low in range(0, tok, ROWS):
            total = ext_ref[8 + low : 8 + low + ROWS, :] * taps[-1]
            for back in range(1, taps_len):
                mask = jnp.concatenate([mask_ref[back - 1, low : low + ROWS, :]] * (CHUNK // LANES), 1)
                window = ext_ref[8 + low - back : 8 + low - back + ROWS, :]
                total = total + (window * taps[-1 - back]) * mask
            if low == 0:
                part_ref[:, lanes] = total[:8]
            to_ref[low : low + ROWS, to_lanes] = silu(total).astype(BF16)

    def body(k, carry):
        chunk_copy(x_hbm, pl.multiple_of(k * CHUNK, CHUNK), k).wait()
        lanes = pl.ds(pl.multiple_of(k * CHUNK, CHUNK), CHUNK)
        convolve(k, lanes, xc_ref, lanes)
        return carry

    lax.fori_loop(0, chunks, body, 0)
    for i, (ref, to_ref) in enumerate(((b_hbm, bc_ref), (c_hbm, cc_ref))):
        chunk_copy(ref, 0, chunks + i).wait()
        convolve(chunks + i, slice(channels + i * gn, channels + (i + 1) * gn), to_ref, slice(0, gn))


def conv(doc_lengths, dt_t, rate, x, b, c, taps_x, taps_b, taps_c):
    heads, tok = dt_t.shape
    channels, gn = x.shape[1], b.shape[1]
    width = channels + 2 * gn
    places = channels // CHUNK + 2
    taps_len = taps_x.shape[0]
    shape = jax.ShapeDtypeStruct
    return pl.pallas_call(
        conv_kernel,
        out_shape=(
            shape((tok, 2 * LANES), BF16),
            shape((tok, LANES), F32),
            shape((heads, tok), F32),
            shape((8, 2 * LANES), BF16),
            shape((tok, LANES), jnp.int32),
            shape((taps_len, width), F32),
            shape((8, width), F32),
            shape((tok, channels), BF16),
            shape((tok, gn), BF16),
            shape((tok, gn), BF16),
        ),
        in_specs=[HBM] * 9,
        out_specs=(VMEM,) * 10,
        scratch_shapes=[
            pltpu.SMEM(doc_lengths.shape, jnp.int32),
            pltpu.VMEM((heads, tok), F32),
            pltpu.VMEM((1, heads), F32),
            pltpu.VMEM((places, tok, CHUNK), BF16),
            pltpu.VMEM((tok + 8, CHUNK), F32),
            pltpu.VMEM((taps_len - 1, tok, LANES), F32),
            pltpu.SemaphoreType.DMA((6,)),
            pltpu.SemaphoreType.DMA((places,)),
        ],
        compiler_params=params(),
        cost_estimate=cost(tok * width * 16, tok * width * 4, tok * width),
        name="conv",
    )(doc_lengths, dt_t, rate, x, b, c, taps_x, taps_b, taps_c)


def state_kernel(
    tail_ref, part_ref, taps_ref, age_ref, tab_ref, d_ref, xc_in, bc_in, cc_in, xc_ref, bc_ref, cc_ref, h_ref, *rest
):
    sends = rest[:CLUSTER]
    ext_ref, head_ref, bt_ref = rest[CLUSTER:]
    tok, channels = xc_in.shape
    gn = bc_in.shape[1]
    heads = LANES // 4
    head_dim = channels // heads
    owned = channels // CLUSTER
    group_width = channels // (gn // STATE)
    mine = lax.axis_index("seq") % CLUSTER
    taps_len = taps_ref.shape[0]
    width = part_ref.shape[1]

    ext_ref[:8, :] = tail_ref[...].astype(F32)
    ext_ref[8:, :] = jnp.zeros((8, width), F32)
    total = part_ref[...]
    age = jnp.concatenate([age_ref[:8, :]] * (width // LANES), 1)
    for back in range(1, taps_len):
        term = ext_ref[8 - back : 16 - back, :] * taps_ref[taps_len - 1 - back : taps_len - back, :]
        total = total + jnp.where(age >= back, term, 0.0)
    head = silu(total).astype(BF16)
    head_ref[...] = head.astype(F32)
    xc_ref[:8, :] = head[:, :channels]
    bc_ref[:8, :] = head[:, channels : channels + gn]
    cc_ref[:8, :] = head[:, channels + gn :]
    for group in range(gn // STATE):
        lanes = slice(group * STATE, (group + 1) * STATE)
        at = slice(channels + group * STATE, channels + (group + 1) * STATE)
        b_blk = jnp.concatenate([head_ref[:, at], bc_in[:, lanes].astype(F32)[8:]], 0)
        bt_ref[group] = b_blk.T.astype(BF16)

    for k in range(CLUSTER):
        owner = mine ^ k
        for part in range(owned // CHUNK):
            at = owner * owned + part * CHUNK
            lanes = pl.ds(pl.multiple_of(at, CHUNK), CHUNK)
            here = slice(part * CHUNK, (part + 1) * CHUNK)
            one_hot = spread(0, at // head_dim, heads, CHUNK, head_dim)
            decay = mm(d_ref[...], one_hot)
            state = None
            for c in range(tok // SUB):
                rows = slice(c * SUB, (c + 1) * SUB)
                weight = mm(tab_ref[rows, :], one_hot)
                value = xc_in[rows, lanes].astype(F32)
                if c == 0:
                    value = jnp.concatenate([head_ref[:, lanes], value[8:]], 0)
                local = mm(bt_ref[at // group_width, :, rows], (value * weight).astype(BF16))
                if state is None:
                    state = local
                else:
                    h_ref[c - 1, :, lanes] = state.astype(BF16)
                    state = local + decay[2 + c : 3 + c, :] * state
            sends[k][:STATE, here] = state.astype(BF16)
            sends[k][STATE:, here] = decay.astype(BF16)


def states(tail, part, taps, age, tab, d, xc, bc, cc):
    tok, channels = xc.shape
    gn = bc.shape[1]
    width = part.shape[1]
    piece = jax.ShapeDtypeStruct((STATE + 8, channels // CLUSTER), BF16)
    same = [jax.ShapeDtypeStruct(value.shape, value.dtype) for value in (xc, bc, cc)]
    return pl.pallas_call(
        state_kernel,
        out_shape=(*same, jax.ShapeDtypeStruct((tok // SUB - 1, STATE, channels), BF16)) + (piece,) * CLUSTER,
        in_specs=[VMEM] * 9,
        out_specs=(VMEM,) * (4 + CLUSTER),
        scratch_shapes=[
            pltpu.VMEM((16, width), F32),
            pltpu.VMEM((8, width), F32),
            pltpu.VMEM((gn // STATE, STATE, tok), BF16),
        ],
        input_output_aliases={6: 0, 7: 1, 8: 2},
        compiler_params=params(),
        cost_estimate=cost(tok * STATE * channels * 4, tok * channels * 4),
        name="state",
    )(tail, part, taps, age, tab, d, xc, bc, cc)


def scan_kernel(*refs):
    pieces = refs[:CLUSTER]
    local_ref, pre_ref, total_ref = refs[CLUSTER:]
    mine = lax.axis_index("seq") % CLUSTER

    def in_order(values):
        bit = 1
        while bit < CLUSTER:
            odd = (mine & bit) != 0
            values = [jnp.where(odd, values[i ^ bit], values[i]) for i in range(CLUSTER)]
            bit *= 2
        return values

    owned = total_ref.shape[1]
    tables = [ref[STATE:, :].astype(F32) for ref in pieces]
    decays = in_order([row[0:1] + (row[1:2] + row[2:3]) for row in tables])
    pre = jnp.ones((1, owned), F32)
    for i in range(CLUSTER):
        pre_ref[i] = jnp.broadcast_to(pre, (8, owned))
        pre = pre * decays[i]
    pre_ref[CLUSTER] = jnp.broadcast_to(pre, (8, owned))
    for at in range(0, owned, LANES):
        lanes = slice(at, at + LANES)
        for low in range(0, STATE, 64):
            rows = slice(low, low + 64)
            values = in_order([ref[rows, lanes].astype(F32) for ref in pieces])
            local_ref[0, rows, lanes] = jnp.zeros((64, LANES), F32)
            state = values[0]
            for i in range(1, CLUSTER):
                local_ref[i, rows, lanes] = state
                state = decays[i][:, lanes] * state + values[i]
            total_ref[rows, lanes] = state.astype(BF16)


def scan_blocks(pieces):
    owned = pieces[0].shape[1]
    return pl.pallas_call(
        scan_kernel,
        out_shape=(
            jax.ShapeDtypeStruct((CLUSTER, STATE, owned), F32),
            jax.ShapeDtypeStruct((CLUSTER + 1, 8, owned), F32),
            jax.ShapeDtypeStruct((STATE, owned), BF16),
        ),
        in_specs=[VMEM] * CLUSTER,
        out_specs=(VMEM,) * 3,
        compiler_params=params(),
        cost_estimate=cost(CLUSTER * STATE * owned * 2, CLUSTER * STATE * owned * 6),
        name="cluster_scan",
    )(*pieces)


def join_kernel(before_ref, local_ref, pre_ref, *outs):
    index = lax.axis_index("seq")
    mine = index % CLUSTER
    before = jnp.where(index >= CLUSTER, before_ref[...].astype(F32), 0.0)
    for k in range(CLUSTER):
        block = mine ^ k
        outs[k][...] = (local_ref[block] + pre_ref[block][0:1] * before).astype(BF16)


def join(before, local, pre):
    owned = local.shape[2]
    return pl.pallas_call(
        join_kernel,
        out_shape=(jax.ShapeDtypeStruct((STATE, owned), BF16),) * CLUSTER,
        in_specs=[VMEM] * 3,
        out_specs=(VMEM,) * CLUSTER,
        compiler_params=params(),
        cost_estimate=cost(CLUSTER * STATE * owned * 2, CLUSTER * STATE * owned * 6),
        name="join",
    )(before, local, pre)


def group_at(turn, groups):
    return (lax.axis_index("seq") % CLUSTER) // (CLUSTER // groups) ^ turn


def intra_kernel(turn, groups, head_dim, xc_ref, bc_ref, cc_ref, h_ref, tab_ref, tab32_ref, row_ref, age_ref, out_ref):
    sub = pl.program_id(0)
    group = group_at(turn, groups)
    width = xc_ref.shape[1]
    per_group = width // head_dim
    heads = per_group * groups
    back = lax.broadcasted_iota(jnp.int32, (SUB, SUB), 0) - lax.broadcasted_iota(jnp.int32, (SUB, SUB), 1)
    keep = (back >= 0) & (back <= age_ref[...])
    c_blk = cc_ref[...]
    scores = lax.dot_general(c_blk, bc_ref[...], (((1,), (1,)), ((), ())), preferred_element_type=F32)
    scores = jnp.where(keep, scores, 0.0)
    col = pltpu.roll(tab32_ref[...], LANES - (3 * heads + group * per_group), 1)
    lane = lax.broadcasted_iota(jnp.int32, (SUB, LANES), 1)
    per_tile = LANES // head_dim
    for tile in range(per_group // per_tile):
        lanes = slice(tile * LANES, (tile + 1) * LANES)
        x_tile = xc_ref[:, lanes].astype(F32)
        left, right = [], []
        for i in range(per_tile):
            head = tile * per_tile + i
            gap = col[:, head : head + 1] + row_ref[head : head + 1, :]
            left.append((jnp.exp2(jnp.minimum(gap, 80.0)) * scores).astype(BF16))
            mine = (lane >= i * head_dim) & (lane < (i + 1) * head_dim)
            right.append(jnp.where(mine, x_tile, 0.0).astype(BF16))
        out_ref[:, lanes] = mm(jnp.concatenate(left, 1), jnp.concatenate(right, 0))

    @pl.when(sub > 0)
    def _():
        for chunk in range(width // CHUNK):
            lanes = slice(chunk * CHUNK, (chunk + 1) * CHUNK)
            first_head = group * per_group + chunk * (CHUNK // head_dim)
            one_hot = spread(1, first_head, heads, CHUNK, head_dim)
            out_ref[:, lanes] += mm(c_blk, h_ref[0, :, lanes]) * mm(tab_ref[...], one_hot)


def intra(turn, xc, bc, cc, h, tab, tab32, row, age):
    tok, channels = xc.shape
    heads = row.shape[0]
    head_dim = channels // heads
    groups = bc.shape[1] // STATE
    width = channels // groups
    return pl.pallas_call(
        functools.partial(intra_kernel, turn, groups, head_dim),
        out_shape=jax.ShapeDtypeStruct((tok, width), F32),
        grid=(tok // SUB,),
        in_specs=[
            pl.BlockSpec((SUB, width), lambda i: (i, group_at(turn, groups))),
            pl.BlockSpec((SUB, STATE), lambda i: (i, group_at(turn, groups))),
            pl.BlockSpec((SUB, STATE), lambda i: (i, group_at(turn, groups))),
            pl.BlockSpec((1, STATE, width), lambda i: (jnp.maximum(i - 1, 0), 0, group_at(turn, groups))),
            pl.BlockSpec((SUB, 2 * LANES), lambda i: (i, 0)),
            pl.BlockSpec((SUB, LANES), lambda i: (i, 0)),
            pl.BlockSpec((heads // groups, SUB), lambda i: (group_at(turn, groups), i)),
            pl.BlockSpec((SUB, LANES), lambda i: (i, 0)),
        ],
        out_specs=pl.BlockSpec((SUB, width), lambda i: (i, 0)),
        compiler_params=params(),
        cost_estimate=cost(tok * SUB * width * 4, tok * width * 8, tok * SUB * width // head_dim),
        name="intra",
    )(xc, bc, cc, h, tab, tab32, row, age)


def final_kernel(turn, groups, head_dim, *refs):
    cc_ref, tab_ref, gate_ref, gain_ref, part_ref = refs[:5]
    per_group = CLUSTER // groups
    pieces = refs[5 : 5 + per_group]
    out_ref, y_ref = refs[-2:]
    width = gate_ref.shape[1]
    heads = groups * width // head_dim
    group = group_at(turn, groups)
    mine = lax.axis_index("seq") % CLUSTER
    owned = width // per_group
    squares = None
    for k in range(per_group):
        for part in range(owned // CHUNK):
            at = ((mine ^ k) % per_group) * owned + part * CHUNK
            lanes = pl.ds(pl.multiple_of(at, CHUNK), CHUNK)
            scale = mm(tab_ref[...], spread(2, group * (width // head_dim) + at // head_dim, heads, CHUNK, head_dim))
            carried = mm(cc_ref[...], pieces[k][:, part * CHUNK : (part + 1) * CHUNK])
            value = (part_ref[:, lanes] + carried * scale) * silu(gate_ref[:, lanes].astype(F32))
            y_ref[:, lanes] = value
            square = value * value
            for i in range(CHUNK // LANES):
                piece = square[:, i * LANES : (i + 1) * LANES]
                squares = piece if squares is None else squares + piece
    factor = lax.rsqrt(jnp.sum(squares, axis=1, keepdims=True) * (1.0 / width) + norm_eps)
    out_ref[...] = (y_ref[...] * factor * gain_ref[...]).astype(BF16)


def final(turn, cc, tab, gate, gain, part, pieces, head_dim, so_far=None):
    tok, channels = gate.shape
    groups = CLUSTER // len(pieces)
    rows = 64
    width = channels // groups
    operands = (cc, tab, gate, gain, part, *pieces) + (() if so_far is None else (so_far,))
    return pl.pallas_call(
        functools.partial(final_kernel, turn, groups, head_dim),
        out_shape=jax.ShapeDtypeStruct((tok, channels), BF16),
        grid=(tok // rows,),
        in_specs=[
            pl.BlockSpec((rows, STATE), lambda i: (i, group_at(turn, groups))),
            pl.BlockSpec((rows, 2 * LANES), lambda i: (i, 0)),
            pl.BlockSpec((rows, width), lambda i: (i, group_at(turn, groups))),
            pl.BlockSpec((1, width), lambda i: (0, group_at(turn, groups))),
            pl.BlockSpec((rows, width), lambda i: (i, 0)),
        ]
        + [VMEM] * len(pieces)
        + ([] if so_far is None else [ANY]),
        out_specs=pl.BlockSpec((rows, width), lambda i: (i, group_at(turn, groups))),
        scratch_shapes=[pltpu.VMEM((rows, width), F32)],
        input_output_aliases={} if so_far is None else {len(operands) - 1: 0},
        compiler_params=params(),
        cost_estimate=cost(tok * STATE * width * 2, tok * width * 8, tok * width),
        name="final",
    )(*operands)


def moved(value, hop):
    count = lax.axis_size("seq")
    return lax.ppermute(value, "seq", [(i, hop(i)) for i in range(count) if 0 <= hop(i) < count])


def exchanged(pieces, order):
    arrived = {0: pieces[0]}
    for k in order:
        arrived[k] = moved(pieces[k], lambda i, k=k: i ^ k)
    return [arrived[k] for k in range(CLUSTER)]


def before_cluster(total, pre):
    clusters = lax.axis_size("seq") // CLUSTER
    if clusters == 1:
        return jnp.zeros_like(total)
    if clusters == 2:
        return moved(total, lambda i: i ^ CLUSTER)
    shift = lambda value, steps: moved(value, lambda i: i + steps * CLUSTER)
    state, decay = shift((total.astype(F32), pre[CLUSTER, 0]), 1)
    step = 1
    while step < clusters - 1:
        earlier, fell = shift((state, decay), step)
        state, decay = state + decay[None, :] * earlier, decay * fell
        step *= 2
    return state


def tied(values, other):
    *values, _ = lax.optimization_barrier((*values, other))
    return values


def on_device(
    x_input,
    b_input,
    c_input,
    dt_input,
    decay_rate,
    gate_input,
    taps_x,
    taps_b,
    taps_c,
    norm_gain,
    doc_lengths,
):
    channels = x_input.shape[1]
    head_dim = channels // dt_input.shape[1]
    groups = b_input.shape[1] // STATE
    count = lax.axis_size("seq")
    tail = lax.ppermute(pack(x_input, b_input, c_input), "seq", [(i, (i + 1) % count) for i in range(count)])
    tab, tab32, row, d, age, taps, part, xc, bc, cc = conv(
        doc_lengths, dt_input.T, decay_rate[None, :], x_input, b_input, c_input, taps_x, taps_b, taps_c
    )
    xc, bc, cc, h, *pieces = states(tail, part, taps, age, tab, d, xc, bc, cc)
    first = intra(0, xc, bc, cc, h, tab, tab32, row, age)
    local, pre, total = scan_blocks(tied(exchanged(pieces, (3, 2, 1)), first))
    second = intra(1, xc, bc, cc, h, tab, tab32, row, age)
    (before,) = tied([before_cluster(total, pre)], second)
    entering = exchanged(join(before, local, pre), (1, 3, 2))
    share = CLUSTER // groups
    output = None
    for turn, inner in enumerate((first, second)):
        mine = entering[turn * share : (turn + 1) * share]
        output = final(turn, cc, tab, gate_input, norm_gain[None, :], inner, mine, head_dim, output)
    return output


def solution(mesh):
    rows = P(("groups", "seq"), "dp")
    placed = (rows, rows, rows, rows, P("dp"), rows, P(None, "dp"), P(None, "dp"), P(None, "dp"), P("dp"), P("groups"))
    return jax.shard_map(on_device, mesh=mesh, in_specs=placed, out_specs=rows, check_vma=False)
```

time: 233 us -> 45.1 us (0.19)
  waiting for transfers between devices: 95.5 us -> 7.68 us
  other arithmetic: 45.5 us -> 0 us
  local copies, waits for them, and re-layouts: 33.1 us -> 0.83 us
  Pallas kernels: 0 us -> 23.7 us
  blocking collectives: 17.8 us -> 0 us
  between operations: 15 us -> 0.16 us
  matrix products: 12.7 us -> 0 us
    all_gather x1 -> x0, waiting for transfers between devices: 95.5 us -> none  [entering_2(): pieces = jax.tree.map(lambda part: lax.all_gather(part, axis), value)]
    pallas_call x0 -> x9, Pallas kernels: none -> 23.7 us  [the longest x2 7.9 us: final(): pl.pallas_call(functools.partial(final_kernel, turn, groups, head_dim), o...]
    select_n x7 -> x0, other arithmetic: 21.5 us -> none  [lap(): jnp.where(position < mine, new, old)]
    all_gather x1 -> x0, blocking collectives: 17.8 us -> none  [entering_2(): pieces = jax.tree.map(lambda part: lax.all_gather(part, axis), value)]
    dynamic_slice x14 -> x0, local copies, waits for them, and re-layouts: 13.3 us -> none  [lap(): longer = join(running, jax.tree.map(lambda part: part[position], pieces))]
    dot_general x10 -> x0, matrix products: 11.9 us -> none  [the longest x4 10.3 us: block_terms(): jnp.einsum('hts,shp->thp', weights, x_group, preferred_element_type=jnp.f...]
    convert_element_type x7 -> x0, other arithmetic: 9.76 us -> none  [the longest x2 3.54 us: causal_conv(): return jax.nn.silu(running).astype(jnp.bfloat16)]
    ppermute x3 -> x8, waiting for transfers between devices: 0.01 us -> 7.68 us  [the longest x7 7.67 us: moved(): lax.ppermute(value, 'seq', [(i, hop(i)) for i in range(count) if 0 <= hop...]
  transfers between devices with their start and end apart: 4 -> 8, of which waited for: 1 -> 4; matrix products, arithmetic and copies ran while one was open for 10% -> 0% of each run, Pallas kernels for 0% -> 34%
where the time goes in v2:
time: 45.1 us; the launch traced here: 44.9 us
  Pallas kernels  23.7 us (53%)
  starting transfers between devices  12.6 us (28%)
  waiting for transfers between devices  7.68 us (17%)
  local copies, waits for them, and re-layouts  0.83 us (2%)
    ppermute x7, starting transfers between devices, moved(): lax.ppermute(value, 'seq', [(i, hop(i)) for i in range(count) if 0 <= hop...  9.56 us
    pallas_call x2, Pallas kernels, final(): pl.pallas_call(functools.partial(final_kernel, turn, groups, head_dim), o...  7.9 us
    ppermute x7, waiting for transfers between devices, moved(): lax.ppermute(value, 'seq', [(i, hop(i)) for i in range(count) if 0 <= hop...  7.67 us
    pallas_call x2, Pallas kernels, intra(): pl.pallas_call(functools.partial(intra_kernel, turn, groups, head_dim), o...  6.39 us
    pallas_call x1, Pallas kernels, conv(): pl.pallas_call(conv_kernel, out_shape=(shape((tok, 2 * LANES), BF16), sha...  5.13 us
    ppermute x1, starting transfers between devices, on_device(): lax.ppermute(pack(x_input, b_input, c_input), 'seq', [(i, (i + 1) % count...  3 us
    pallas_call x1, Pallas kernels, states(): pl.pallas_call(state_kernel, out_shape=(*same, jax.ShapeDtypeStruct((tok...  2.39 us
    pallas_call x1, Pallas kernels, pack(): pl.pallas_call(pack_kernel, out_shape=jax.ShapeDtypeStruct((8, width), BF...  1.54 us
  transfers between devices with their start and end apart: 8, of which 4 were waited for; matrix products, arithmetic and copies ran while one was open for 0% of the time, Pallas kernels for 34%

profile of v2, /device:TPU:0, one launch (start us, length us, event | category | flops | bytes accessed | tf_op | source)
XLA Modules:
  0.0 44.9 jit_solution(2777166233206018275)
XLA Ops:
  0.0 0.0 copy-start.3
  0.0 0.0 copy-start.2
  0.0 0.0 copy-start
  0.0 0.0 copy-start.9
  0.0 0.0 copy-start.8
  0.0 0.0 copy-start.7
  0.0 0.0 copy-start.5
  0.0 0.0 copy-start.10
  0.0 1.5 %pack.1 = bf16[8,2560]{1,0:T(8,128)(2,1)} custom-call(bf16[384,2048]{1,0:T(8,128)(2,1)} %x_hbm.1, bf16[384,256]{1,0:T(8,128)(2,1)} %b_hbm.1, bf16[384,256]{1,0:T(8,128)(2,1)} %c_hbm.1), custom_call_target="tpu_custom_call" | custom-call | tf_op jit(solution)/shard_map/pack/pallas_call | solution.py:102
  1.6 3.0 %collective-permute-start = (bf16[8,2560]{1,0:T(8,128)(2,1)}, bf16[8,2560]{1,0:T(8,128)(2,1)S(1)}, u32[]{:S(2)}, u32[]{:S(2)}) collective-permute-start(bf16[8,2560]{1,0:T(8,128)(2,1)} %pack.1), channel_id=1, source_target_pairs={{0,2},{2,4},{4,6},{6,8},{8,10},{10,12},{12,14},{14,0},{1,3},{3,5},... | collective-permute-start | bytes 122888 | tf_op jit(solution)/shard_map/ppermute | solution.py:598
  4.6 0.0 copy-done.3
  4.6 0.0 copy-done.2
  4.6 0.0 copy-done
  4.6 0.0 copy-done.9
  4.6 0.0 copy-done.8
  4.6 0.0 copy-done.7
  4.6 0.0 copy-done.5
  4.6 0.0 copy-done.10
  4.7 0.0 copy-start.4
  4.7 0.8 %copy-done.4 = f32[384,32]{0,1:T(8,128)S(1)} copy-done((f32[384,32]{0,1:T(8,128)S(1)}, f32[384,32]{0,1:T(8,128)}, u32[]{:S(2)}) %copy-start.4) | copy-done | bytes 49176
  5.5 5.1 %conv.1 = (bf16[384,256]{1,0:T(8,128)(2,1)S(1)}, f32[384,128]{1,0:T(8,128)S(1)}, f32[32,384]{1,0:T(8,128)S(1)}, bf16[8,256]{1,0:T(8,128)(2,1)S(1)}, s32[384,128]...) custom-call(s32[4]{0:T(128)S(1)} %copy-done.9, ...), custom_call_target="tpu_custom_call" | custom-call | flops 15728640 | bytes 3932160 | tf_op jit(solution)/shard_map/conv/pallas_call | solution.py:241
  10.6 0.0 collective-permute-done.tail_ref
  10.6 2.4 %state.1 = (bf16[384,2048]{1,0:T(8,128)(2,1)S(1)}, bf16[384,256]{1,0:T(8,128)(2,1)S(1)}, bf16[384,256]{1,0:T(8,128)(2,1)S(1)}, bf16[2,128,2048]{2,1,0:T(8,128)(2...) custom-call(bf16[8,2560]{1,0:T(8,128)(2,1)S(1)} %collective-permute-, ...), custom_call_target="tpu_custom_call", output_to_operand_aliasing={{0}: (6, {}), {1}: (7, {}), {2}: (8, {})} | custom-call | flops 402653184 | bytes 3145728 | tf_op jit(solution)/shard_map/state/pallas_call | solution.py:337
  13.0 1.6 %collective-permute-start.1 = (bf16[136,512]{1,0:T(8,128)(2,1)S(1)}, bf16[136,512]{1,0:T(8,128)(2,1)S(1)}, u32[]{:S(2)}, u32[]{:S(2)}) collective-permute-start(bf16[136,512]{1,0:T(8,128)(2,1)S(1)} %get-tuple-element.50), channel_id=1, source_target_pairs={{0,2},{2,0},{4,6},{6,4},{8,10},{10,8},{12,14},{14,12},{1,3},{3,1},... | collective-permute-start | bytes 417800 | tf_op jit(solution)/shard_map/ppermute | solution.py:550
  14.6 1.6 %collective-permute-start.2 = (bf16[136,512]{1,0:T(8,128)(2,1)S(1)}, bf16[136,512]{1,0:T(8,128)(2,1)S(1)}, u32[]{:S(2)}, u32[]{:S(2)}) collective-permute-start(bf16[136,512]{1,0:T(8,128)(2,1)S(1)} %get-tuple-element.51), channel_id=1, source_target_pairs={{0,4},{2,6},{4,0},{6,2},{8,12},{10,14},{12,8},{14,10},{1,5},{3,7},... | collective-permute-start | bytes 417800 | tf_op jit(solution)/shard_map/ppermute | solution.py:550
  16.2 0.4 collective-permute-start.3
  16.6 3.2 %intra.3.refs_4_ = f32[384,1024]{1,0:T(8,128)S(1)} custom-call(bf16[384,2048]{1,0:T(8,128)(2,1)S(1)} %get-tuple-element.44.xc_ref, bf16[384,256]{1,0:T(8,128)(2,1)S(1)} %get-tuple-element.45.bc_ref, bf16[384,256]{1,0:T(8,128)(2,1)S(1)} %get-tuple-element.43.cc_ref.refs_0_, bf16[2,128,2048]{2,1,0:T(8,128)(2,1)S(1)} %get-tuple-element.46.h_ref, ...), custom_call_target="tpu_custom_call" | custom-call | flops 201326592 | bytes 3145728 | tf_op jit(solution)/shard_map/intra/pallas_call | solution.py:472
  19.8 0.0 collective-permute-done.1.refs_1_
  19.8 1.2 %collective-permute-done.2.refs_2_ = bf16[136,512]{1,0:T(8,128)(2,1)S(1)} collective-permute-done((bf16[136,512]{1,0:T(8,128)(2,1)S(1)}, bf16[136,512]{1,0:T(8,128)(2,1)S(1)}, u32[]{:S(2)}, u32[]{:S(2)}) %collective-permute-start.2) | collective-permute-done | bytes 139296 | tf_op jit(solution)/shard_map/ppermute | solution.py:550
  21.0 1.6 %collective-permute-done.3.refs_3_ = bf16[136,512]{1,0:T(8,128)(2,1)S(1)} collective-permute-done((bf16[136,512]{1,0:T(8,128)(2,1)S(1)}, bf16[136,512]{1,0:T(8,128)(2,1)S(1)}, u32[]{:S(2)}, u32[]{:S(2)}) %collective-permute-start.3) | collective-permute-done | bytes 139296 | tf_op jit(solution)/shard_map/ppermute | solution.py:550
  22.6 0.2 cluster_scan.1
  22.8 0.0 copy-start.6
  22.8 2.5 %collective-permute-start.4 = (bf16[128,512]{1,0:T(8,128)(2,1)S(1)}, bf16[128,512]{1,0:T(8,128)(2,1)S(1)}, u32[]{:S(2)}, u32[]{:S(2)}) collective-permute-start(bf16[128,512]{1,0:T(8,128)(2,1)S(1)} %get-tuple-element.57), channel_id=1, source_target_pairs={{0,8},{2,10},{4,12},{6,14},{8,0},{10,2},{12,4},{14,6},{1,9},{3,11}... | collective-permute-start | bytes 393224 | tf_op jit(solution)/shard_map/ppermute | solution.py:550
  25.3 0.0 copy-start.1
  25.3 3.2 %intra.2.refs_4_ = f32[384,1024]{1,0:T(8,128)S(1)} custom-call(bf16[384,2048]{1,0:T(8,128)(2,1)S(1)} %get-tuple-element.44.xc_ref, bf16[384,256]{1,0:T(8,128)(2,1)S(1)} %get-tuple-element.45.bc_ref, bf16[384,256]{1,0:T(8,128)(2,1)S(1)} %get-tuple-element.43.cc_ref.refs_0_, bf16[2,128,2048]{2,1,0:T(8,128)(2,1)S(1)} %get-tuple-element.46.h_ref, ...), custom_call_target="tpu_custom_call" | custom-call | flops 201326592 | bytes 3145728 | tf_op jit(solution)/shard_map/intra/pallas_call | solution.py:472
  28.5 2.4 %collective-permute-done.4.before_ref = bf16[128,512]{1,0:T(8,128)(2,1)S(1)} collective-permute-done((bf16[128,512]{1,0:T(8,128)(2,1)S(1)}, bf16[128,512]{1,0:T(8,128)(2,1)S(1)}, u32[]{:S(2)}, u32[]{:S(2)}) %collective-permute-start.4) | collective-permute-done | bytes 131104 | tf_op jit(solution)/shard_map/ppermute | solution.py:550
  30.8 0.1 join.1
  31.0 0.7 %collective-permute-start.7 = (bf16[128,512]{1,0:T(8,128)(2,1)S(1)}, bf16[128,512]{1,0:T(8,128)(2,1)S(1)}, u32[]{:S(2)}, u32[]{:S(2)}) collective-permute-start(bf16[128,512]{1,0:T(8,128)(2,1)S(1)} %get-tuple-element.64), channel_id=1, source_target_pairs={{0,2},{2,0},{4,6},{6,4},{8,10},{10,8},{12,14},{14,12},{1,3},{3,1},... | collective-permute-start | bytes 393224 | tf_op jit(solution)/shard_map/ppermute | solution.py:550
  31.7 0.3 collective-permute-start.5
  32.0 2.6 %collective-permute-start.6 = (bf16[128,512]{1,0:T(8,128)(2,1)S(1)}, bf16[128,512]{1,0:T(8,128)(2,1)S(1)}, u32[]{:S(2)}, u32[]{:S(2)}) collective-permute-start(bf16[128,512]{1,0:T(8,128)(2,1)S(1)} %get-tuple-element.62), channel_id=1, source_target_pairs={{0,6},{2,4},{4,2},{6,0},{8,14},{10,12},{12,10},{14,8},{1,7},{3,5},... | collective-permute-start | bytes 393224 | tf_op jit(solution)/shard_map/ppermute | solution.py:550
  34.5 2.5 %collective-permute-done.7.refs_6_ = bf16[128,512]{1,0:T(8,128)(2,1)S(1)} collective-permute-done((bf16[128,512]{1,0:T(8,128)(2,1)S(1)}, bf16[128,512]{1,0:T(8,128)(2,1)S(1)}, u32[]{:S(2)}, u32[]{:S(2)}) %collective-permute-start.7) | collective-permute-done | bytes 131104 | tf_op jit(solution)/shard_map/ppermute | solution.py:550
  37.0 0.0 copy-done.6
  37.0 0.0 copy-done.1
  37.0 3.9 %final.2.refs_7_ = bf16[384,2048]{1,0:T(8,128)(2,1)} custom-call(bf16[384,256]{1,0:T(8,128)(2,1)S(1)} %get-tuple-element.43.cc_ref.refs_0_, bf16[384,256]{1,0:T(8,128)(2,1)S(1)} %get-tuple-element.38.tab_ref.refs_1_, bf16[384,2048]{1,0:T(8,128)(2,1)S(1)} %copy-done.1, f32[1,2048]{1,0:T(1,128)S(1)} %bitcast.4, f32[384,1024]{1,0:T(8,128)S(1)} %intra.3.refs_4_, ...), custom_call_target="tpu_custom_call" | custom-call | flops 100663296 | bytes 3145728 | tf_op jit(solution)/shard_map/final/pallas_call | solution.py:526
  41.0 0.0 collective-permute-done.5.refs_5_
  41.0 0.0 collective-permute-done.6.refs_6_
  41.0 4.0 %final.3 = bf16[384,2048]{1,0:T(8,128)(2,1)} custom-call(bf16[384,256]{1,0:T(8,128)(2,1)S(1)} %get-tuple-element.43.cc_ref.refs_0_, bf16[384,256]{1,0:T(8,128)(2,1)S(1)} %get-tuple-element.38.tab_ref.refs_1_, bf16[384,2048]{1,0:T(8,128)(2,1)S(1)} %copy-done.1, f32[1,2048]{1,0:T(1,128)S(1)} %bitcast.5, ...), custom_call_target="tpu_custom_call", output_to_operand_aliasing={{}: (7, {})} | custom-call | flops 100663296 | bytes 3145728 | tf_op jit(solution)/shard_map/final/pallas_call | solution.py:526
Async XLA Ops:
  0.0 4.6 %copy-start.3 = (bf16[384,256]{1,0:T(8,128)(2,1)S(1)}, bf16[384,256]{1,0:T(8,128)(2,1)}, u32[]{:S(2)}) copy-start(bf16[384,256]{1,0:T(8,128)(2,1)} %c_hbm.1) | copy-start | bytes 589828
  0.0 4.6 %copy-start.2 = (bf16[384,256]{1,0:T(8,128)(2,1)S(1)}, bf16[384,256]{1,0:T(8,128)(2,1)}, u32[]{:S(2)}) copy-start(bf16[384,256]{1,0:T(8,128)(2,1)} %b_hbm.1) | copy-start | bytes 589828
  0.0 4.6 %copy-start = (bf16[384,2048]{1,0:T(8,128)(2,1)S(1)}, bf16[384,2048]{1,0:T(8,128)(2,1)}, u32[]{:S(2)}) copy-start(bf16[384,2048]{1,0:T(8,128)(2,1)} %x_hbm.1) | copy-start | bytes 4718596
  0.0 4.6 %copy-start.9 = (s32[4]{0:T(128)S(1)}, s32[4]{0:T(128)}, u32[]{:S(2)}) copy-start(s32[4]{0:T(128)} %dl_hbm.1) | copy-start | bytes 52
  0.0 4.6 %copy-start.8 = (f32[4,256]{1,0:T(4,128)S(1)}, f32[4,256]{1,0:T(4,128)}, u32[]{:S(2)}) copy-start(f32[4,256]{1,0:T(4,128)} %taps_c_hbm.1) | copy-start | bytes 12292
  0.0 4.6 %copy-start.7 = (f32[4,256]{1,0:T(4,128)S(1)}, f32[4,256]{1,0:T(4,128)}, u32[]{:S(2)}) copy-start(f32[4,256]{1,0:T(4,128)} %taps_b_hbm.1) | copy-start | bytes 12292
  0.0 4.6 %copy-start.5 = (f32[4,2048]{1,0:T(4,128)S(1)}, f32[4,2048]{1,0:T(4,128)}, u32[]{:S(2)}) copy-start(f32[4,2048]{1,0:T(4,128)} %taps_x_hbm.1) | copy-start | bytes 98308
  0.0 4.6 %copy-start.10 = (f32[32]{0:T(128)S(1)}, f32[32]{0:T(128)}, u32[]{:S(2)}) copy-start(f32[32]{0:T(128)} %param.15) | copy-start | bytes 388
  1.6 9.0 %collective-permute-start = (bf16[8,2560]{1,0:T(8,128)(2,1)}, bf16[8,2560]{1,0:T(8,128)(2,1)S(1)}, u32[]{:S(2)}, u32[]{:S(2)}) collective-permute-start(bf16[8,2560]{1,0:T(8,128)(2,1)} %pack.1), channel_id=1, source_target_pairs={{0,2},{2,4},{4,6},{6,8},{8,10},{10,12},{12,14},{14,0},{1,3},{3,5},... | collective-permute-start | bytes 122888 | tf_op jit(solution)/shard_map/ppermute | solution.py:598
  4.7 0.8 %copy-start.4 = (f32[384,32]{0,1:T(8,128)S(1)}, f32[384,32]{0,1:T(8,128)}, u32[]{:S(2)}) copy-start(f32[384,32]{0,1:T(8,128)} %param.14) | copy-start | bytes 147460
  13.0 6.8 %collective-permute-start.1 = (bf16[136,512]{1,0:T(8,128)(2,1)S(1)}, bf16[136,512]{1,0:T(8,128)(2,1)S(1)}, u32[]{:S(2)}, u32[]{:S(2)}) collective-permute-start(bf16[136,512]{1,0:T(8,128)(2,1)S(1)} %get-tuple-element.50), channel_id=1, source_target_pairs={{0,2},{2,0},{4,6},{6,4},{8,10},{10,8},{12,14},{14,12},{1,3},{3,1},... | collective-permute-start | bytes 417800 | tf_op jit(solution)/shard_map/ppermute | solution.py:550
  14.6 6.3 %collective-permute-start.2 = (bf16[136,512]{1,0:T(8,128)(2,1)S(1)}, bf16[136,512]{1,0:T(8,128)(2,1)S(1)}, u32[]{:S(2)}, u32[]{:S(2)}) collective-permute-start(bf16[136,512]{1,0:T(8,128)(2,1)S(1)} %get-tuple-element.51), channel_id=1, source_target_pairs={{0,4},{2,6},{4,0},{6,2},{8,12},{10,14},{12,8},{14,10},{1,5},{3,7},... | collective-permute-start | bytes 417800 | tf_op jit(solution)/shard_map/ppermute | solution.py:550
  16.2 6.4 %collective-permute-start.3 = (bf16[136,512]{1,0:T(8,128)(2,1)S(1)}, bf16[136,512]{1,0:T(8,128)(2,1)S(1)}, u32[]{:S(2)}, u32[]{:S(2)}) collective-permute-start(bf16[136,512]{1,0:T(8,128)(2,1)S(1)} %get-tuple-element.52), channel_id=1, source_target_pairs={{0,6},{2,4},{4,2},{6,0},{8,14},{10,12},{12,10},{14,8},{1,7},{3,5},... | collective-permute-start | bytes 417800 | tf_op jit(solution)/shard_map/ppermute | solution.py:550
  22.8 14.2 %copy-start.6 = (f32[2048]{0:T(1024)S(1)}, f32[2048]{0:T(1024)}, u32[]{:S(2)}) copy-start(f32[2048]{0:T(1024)} %param.20) | copy-start | bytes 24580
  22.8 8.0 %collective-permute-start.4 = (bf16[128,512]{1,0:T(8,128)(2,1)S(1)}, bf16[128,512]{1,0:T(8,128)(2,1)S(1)}, u32[]{:S(2)}, u32[]{:S(2)}) collective-permute-start(bf16[128,512]{1,0:T(8,128)(2,1)S(1)} %get-tuple-element.57), channel_id=1, source_target_pairs={{0,8},{2,10},{4,12},{6,14},{8,0},{10,2},{12,4},{14,6},{1,9},{3,11}... | collective-permute-start | bytes 393224 | tf_op jit(solution)/shard_map/ppermute | solution.py:550
  25.3 11.8 %copy-start.1 = (bf16[384,2048]{1,0:T(8,128)(2,1)S(1)}, bf16[384,2048]{1,0:T(8,128)(2,1)}, u32[]{:S(2)}) copy-start(bf16[384,2048]{1,0:T(8,128)(2,1)} %refs_2_.3) | copy-start | bytes 4718596
  31.0 6.0 %collective-permute-start.7 = (bf16[128,512]{1,0:T(8,128)(2,1)S(1)}, bf16[128,512]{1,0:T(8,128)(2,1)S(1)}, u32[]{:S(2)}, u32[]{:S(2)}) collective-permute-start(bf16[128,512]{1,0:T(8,128)(2,1)S(1)} %get-tuple-element.64), channel_id=1, source_target_pairs={{0,2},{2,0},{4,6},{6,4},{8,10},{10,8},{12,14},{14,12},{1,3},{3,1},... | collective-permute-start | bytes 393224 | tf_op jit(solution)/shard_map/ppermute | solution.py:550
  31.7 9.3 %collective-permute-start.5 = (bf16[128,512]{1,0:T(8,128)(2,1)S(1)}, bf16[128,512]{1,0:T(8,128)(2,1)S(1)}, u32[]{:S(2)}, u32[]{:S(2)}) collective-permute-start(bf16[128,512]{1,0:T(8,128)(2,1)S(1)} %get-tuple-element.61), channel_id=1, source_target_pairs={{0,4},{2,6},{4,0},{6,2},{8,12},{10,14},{12,8},{14,10},{1,5},{3,7},... | collective-permute-start | bytes 393224 | tf_op jit(solution)/shard_map/ppermute | solution.py:550
  32.0 9.0 %collective-permute-start.6 = (bf16[128,512]{1,0:T(8,128)(2,1)S(1)}, bf16[128,512]{1,0:T(8,128)(2,1)S(1)}, u32[]{:S(2)}, u32[]{:S(2)}) collective-permute-start(bf16[128,512]{1,0:T(8,128)(2,1)S(1)} %get-tuple-element.62), channel_id=1, source_target_pairs={{0,6},{2,4},{4,2},{6,0},{8,14},{10,12},{12,10},{14,8},{1,7},{3,5},... | collective-permute-start | bytes 393224 | tf_op jit(solution)/shard_map/ppermute | solution.py:550

commit v3 on v2

--- a/solution.py
+++ b/solution.py
@@ -8,7 +8,6 @@
 from jax.sharding import PartitionSpec as P
 
 STATE = 128
-NORM_HEADS = 16
 SUB = 128
 CHUNK = 256
 LANES = 128
@@ -20,12 +19,11 @@
 F32 = jnp.float32
 BF16 = jnp.bfloat16
 VMEM = pl.BlockSpec(memory_space=pltpu.VMEM)
-SMEM = pl.BlockSpec(memory_space=pltpu.SMEM)
 ANY = pl.BlockSpec(memory_space=pl.ANY)
 HBM = pl.BlockSpec(memory_space=pltpu.HBM)
 
 
-def params(mib=48):
+def params(mib=24):
     return pltpu.CompilerParams(vmem_limit_bytes=mib << 20)
 
 
@@ -68,11 +66,10 @@
     return half + half * jnp.tanh(half)
 
 
-def spread(which, first_head, heads, width, head_dim):
-    row = lax.broadcasted_iota(jnp.int32, (2 * LANES, width), 0) & (LANES - 1)
-    lane = lax.broadcasted_iota(jnp.int32, (2 * LANES, width), 1)
-    low = (row - (which * heads + first_head)) * head_dim
-    return jnp.where((lane >= low) & (lane < low + head_dim), 1.0, 0.0).astype(BF16)
+def spread(base, rows, first_head, heads, width, head_dim):
+    row = lax.broadcasted_iota(jnp.int32, (rows, width), 0) - (base + first_head)
+    head = lax.broadcasted_iota(jnp.int32, (rows, width), 1) // head_dim
+    return jnp.where((row == head) | (row == head + heads), 1.0, 0.0).astype(BF16)
 
 
 def start_all(copies):
@@ -85,31 +82,7 @@
         copy.wait()
 
 
-def pack_kernel(x_ref, b_ref, c_ref, out_ref, sem):
-    copies, low = [], 0
-    for i, ref in enumerate((x_ref, b_ref, c_ref)):
-        tok, width = ref.shape
-        copies.append(
-            pltpu.make_async_copy(ref.at[pl.ds(tok - 8, 8), :], out_ref.at[:, pl.ds(low, width)], sem.at[i])
-        )
-        low += width
-    start_all(copies)
-    wait_all(copies)
-
-
-def pack(x, b, c):
-    width = x.shape[1] + b.shape[1] + c.shape[1]
-    return pl.pallas_call(
-        pack_kernel,
-        out_shape=jax.ShapeDtypeStruct((8, width), BF16),
-        in_specs=[HBM] * 3,
-        out_specs=VMEM,
-        scratch_shapes=[pltpu.SemaphoreType.DMA((3,))],
-        name="pack",
-    )(x, b, c)
-
-
-def tables(row0, edges, dt_ref, rate_ref, tab_ref, tab32_ref, row_ref, d_ref):
+def tables(row0, edges, dt_ref, rate_ref, tab_ref, tab0_ref, col_ref, row_ref, d_ref):
     heads, tok = dt_ref.shape
     upto = jnp.where(
         lax.broadcasted_iota(jnp.int32, (SUB, SUB), 0) <= lax.broadcasted_iota(jnp.int32, (SUB, SUB), 1), 1.0, 0.0
@@ -130,11 +103,14 @@
         start = doc_start(token, edges)
         last_start = doc_start(jnp.int32(first + SUB - 1), edges)
         to_end = jnp.exp(last - cum) * step * jnp.where(token >= last_start, 1.0, 0.0)
-        since_sub = jnp.exp(cum) * jnp.where(start < first, 1.0, 0.0)
+        since_sub = jnp.exp(cum) * jnp.where((start < first) & (c > 0), 1.0, 0.0)
         since_block = jnp.exp(cum + total) * jnp.where(start < row0, 1.0, 0.0)
-        table = jnp.concatenate([to_end, since_sub, since_block, cum * LOG2E], 0).T
-        tab32_ref[span, :] = table
-        tab_ref[span, :] = jnp.concatenate(split2(table), 1)
+        first_pair = [part.astype(F32) for part in (*split2(to_end), *split2(since_sub))]
+        second_pair = [part.astype(F32) for part in split2(since_block)] + [cum * LOG2E, jnp.zeros_like(cum)]
+        tab_ref[span, :] = jnp.concatenate(first_pair, 0).T.astype(BF16)
+        second = jnp.concatenate(second_pair, 0).T
+        tab0_ref[span, :] = second[:, : 2 * heads].astype(BF16)
+        col_ref[span, :] = second
         row_ref[:, span] = (jnp.log(step) - cum) * LOG2E
         decays.append(jnp.exp(last) * jnp.where(last_start < first, 1.0, 0.0))
         total = total + last
@@ -143,32 +119,92 @@
     columns = [part.astype(F32) for part in split3(whole)] + decays[1:]
     columns.append(jnp.zeros((heads, LANES - len(columns)), F32))
     columns = jnp.concatenate([jnp.concatenate(columns, 1), jnp.zeros((LANES - heads, LANES), F32)], 0)
-    d_ref[...] = jnp.concatenate(split2(columns.T[:8]), 1)
-
-
-def conv_kernel(
+    halves = [part.astype(F32)[:, :heads] for part in split2(columns.T[:8])]
+    d_ref[...] = jnp.concatenate(halves, 1).astype(BF16)
+
+
+def prep_kernel(
     dl_hbm,
     dt_hbm,
     rate_hbm,
     x_hbm,
     b_hbm,
     c_hbm,
+    ends_ref,
+    tab_ref,
+    tab0_ref,
+    col_ref,
+    row_ref,
+    d_ref,
+    age_ref,
+    dl_ref,
+    dt_ref,
+    rate_ref,
+    sem,
+):
+    tok = x_hbm.shape[0]
+    small = [
+        pltpu.make_async_copy(hbm, ref, sem.at[i])
+        for i, (hbm, ref) in enumerate(((dl_hbm, dl_ref), (dt_hbm, dt_ref), (rate_hbm, rate_ref)))
+    ]
+    start_all(small)
+    ends, low = [], 0
+    for i, ref in enumerate((x_hbm, b_hbm, c_hbm)):
+        width = ref.shape[1]
+        ends.append(
+            pltpu.make_async_copy(ref.at[pl.ds(tok - 8, 8), :], ends_ref.at[:, pl.ds(low, width)], sem.at[3 + i])
+        )
+        low += width
+    start_all(ends)
+    wait_all(small)
+    row0 = lax.axis_index("seq") * tok
+    edges = doc_edges(dl_ref)
+    tables(row0, edges, dt_ref, rate_ref, tab_ref, tab0_ref, col_ref, row_ref, d_ref)
+    token = row0 + lax.broadcasted_iota(jnp.int32, (tok, LANES), 0)
+    age_ref[...] = token - doc_start(token, edges)
+    wait_all(ends)
+
+
+def prep(doc_lengths, dt_t, rate, x, b, c):
+    heads, tok = dt_t.shape
+    shape = jax.ShapeDtypeStruct
+    return pl.pallas_call(
+        prep_kernel,
+        out_shape=(
+            shape((8, x.shape[1] + b.shape[1] + c.shape[1]), BF16),
+            shape((tok, LANES), BF16),
+            shape((tok, 2 * heads), BF16),
+            shape((tok, LANES), F32),
+            shape((heads, tok), F32),
+            shape((8, 2 * heads), BF16),
+            shape((tok, LANES), jnp.int32),
+        ),
+        in_specs=[HBM] * 6,
+        out_specs=(VMEM,) * 7,
+        scratch_shapes=[
+            pltpu.SMEM(doc_lengths.shape, jnp.int32),
+            pltpu.VMEM((heads, tok), F32),
+            pltpu.VMEM((1, heads), F32),
+            pltpu.SemaphoreType.DMA((6,)),
+        ],
+        compiler_params=params(16),
+        name="prep",
+    )(doc_lengths, dt_t, rate, x, b, c)
+
+
+def conv_kernel(
+    age_ref,
+    x_hbm,
+    b_hbm,
+    c_hbm,
     taps_x_hbm,
     taps_b_hbm,
     taps_c_hbm,
-    tab_ref,
-    tab32_ref,
-    row_ref,
-    d_ref,
-    age_ref,
     taps_ref,
     part_ref,
     xc_ref,
     bc_ref,
     cc_ref,
-    dl_ref,
-    dt_ref,
-    rate_ref,
     in_ref,
     ext_ref,
     mask_ref,
@@ -178,14 +214,11 @@
     tok, channels = x_hbm.shape
     gn = b_hbm.shape[1]
     taps_len = taps_x_hbm.shape[0]
-    row0 = lax.axis_index("seq") * tok
     chunks = channels // CHUNK
-    small = [pltpu.make_async_copy(dl_hbm, dl_ref, sem.at[0])]
-    small.append(pltpu.make_async_copy(dt_hbm, dt_ref, sem.at[1]))
-    small.append(pltpu.make_async_copy(rate_hbm, rate_ref, sem.at[2]))
+    small = []
     low = 0
     for i, ref in enumerate((taps_x_hbm, taps_b_hbm, taps_c_hbm)):
-        small.append(pltpu.make_async_copy(ref, taps_ref.at[:, pl.ds(low, ref.shape[1])], sem.at[3 + i]))
+        small.append(pltpu.make_async_copy(ref, taps_ref.at[:, pl.ds(low, ref.shape[1])], sem.at[i]))
         low += ref.shape[1]
     start_all(small)
 
@@ -196,15 +229,10 @@
         chunk_copy(x_hbm, k * CHUNK, k).start()
     chunk_copy(b_hbm, 0, chunks).start()
     chunk_copy(c_hbm, 0, chunks + 1).start()
+    for back in range(1, taps_len):
+        mask_ref[back - 1] = jnp.where(age_ref[...] >= back, 1.0, 0.0)
+    ext_ref[:8, :] = jnp.zeros((8, CHUNK), F32)
     wait_all(small)
-    edges = doc_edges(dl_ref)
-    tables(row0, edges, dt_ref, rate_ref, tab_ref, tab32_ref, row_ref, d_ref)
-    token = row0 + lax.broadcasted_iota(jnp.int32, (tok, LANES), 0)
-    age = token - doc_start(token, edges)
-    age_ref[...] = age
-    for back in range(1, taps_len):
-        mask_ref[back - 1] = jnp.where(age >= back, 1.0, 0.0)
-    ext_ref[:8, :] = jnp.zeros((8, CHUNK), F32)
 
     def convolve(place, lanes, to_ref, to_lanes):
         ext_ref[8:, :] = in_ref[place].astype(F32)
@@ -231,9 +259,9 @@
         convolve(chunks + i, slice(channels + i * gn, channels + (i + 1) * gn), to_ref, slice(0, gn))
 
 
-def conv(doc_lengths, dt_t, rate, x, b, c, taps_x, taps_b, taps_c):
-    heads, tok = dt_t.shape
-    channels, gn = x.shape[1], b.shape[1]
+def conv(age, x, b, c, taps_x, taps_b, taps_c):
+    tok, channels = x.shape
+    gn = b.shape[1]
     width = channels + 2 * gn
     places = channels // CHUNK + 2
     taps_len = taps_x.shape[0]
@@ -241,33 +269,25 @@
     return pl.pallas_call(
         conv_kernel,
         out_shape=(
-            shape((tok, 2 * LANES), BF16),
-            shape((tok, LANES), F32),
-            shape((heads, tok), F32),
-            shape((8, 2 * LANES), BF16),
-            shape((tok, LANES), jnp.int32),
             shape((taps_len, width), F32),
             shape((8, width), F32),
             shape((tok, channels), BF16),
             shape((tok, gn), BF16),
             shape((tok, gn), BF16),
         ),
-        in_specs=[HBM] * 9,
-        out_specs=(VMEM,) * 10,
+        in_specs=[VMEM] + [HBM] * 6,
+        out_specs=(VMEM,) * 5,
         scratch_shapes=[
-            pltpu.SMEM(doc_lengths.shape, jnp.int32),
-            pltpu.VMEM((heads, tok), F32),
-            pltpu.VMEM((1, heads), F32),
             pltpu.VMEM((places, tok, CHUNK), BF16),
             pltpu.VMEM((tok + 8, CHUNK), F32),
             pltpu.VMEM((taps_len - 1, tok, LANES), F32),
-            pltpu.SemaphoreType.DMA((6,)),
+            pltpu.SemaphoreType.DMA((3,)),
             pltpu.SemaphoreType.DMA((places,)),
         ],
-        compiler_params=params(),
+        compiler_params=params(16),
         cost_estimate=cost(tok * width * 16, tok * width * 4, tok * width),
         name="conv",
-    )(doc_lengths, dt_t, rate, x, b, c, taps_x, taps_b, taps_c)
+    )(age, x, b, c, taps_x, taps_b, taps_c)
 
 
 def state_kernel(
@@ -277,7 +297,7 @@
     ext_ref, head_ref, bt_ref = rest[CLUSTER:]
     tok, channels = xc_in.shape
     gn = bc_in.shape[1]
-    heads = LANES // 4
+    heads = d_ref.shape[1] // 2
     head_dim = channels // heads
     owned = channels // CLUSTER
     group_width = channels // (gn // STATE)
@@ -309,12 +329,12 @@
             at = owner * owned + part * CHUNK
             lanes = pl.ds(pl.multiple_of(at, CHUNK), CHUNK)
             here = slice(part * CHUNK, (part + 1) * CHUNK)
-            one_hot = spread(0, at // head_dim, heads, CHUNK, head_dim)
+            one_hot = spread(0, 2 * heads, at // head_dim, heads, CHUNK, head_dim)
             decay = mm(d_ref[...], one_hot)
             state = None
             for c in range(tok // SUB):
                 rows = slice(c * SUB, (c + 1) * SUB)
-                weight = mm(tab_ref[rows, :], one_hot)
+                weight = mm(tab_ref[rows, : 2 * heads], one_hot)
                 value = xc_in[rows, lanes].astype(F32)
                 if c == 0:
                     value = jnp.concatenate([head_ref[:, lanes], value[8:]], 0)
@@ -428,18 +448,42 @@
     return (lax.axis_index("seq") % CLUSTER) // (CLUSTER // groups) ^ turn
 
 
-def intra_kernel(turn, groups, head_dim, xc_ref, bc_ref, cc_ref, h_ref, tab_ref, tab32_ref, row_ref, age_ref, out_ref):
+def intra_kernel(
+    turn,
+    groups,
+    head_dim,
+    xc_ref,
+    bc_ref,
+    cc_ref,
+    h_ref,
+    tab_ref,
+    tab0_ref,
+    col_ref,
+    row_ref,
+    age_ref,
+    gate_ref,
+    part_ref,
+    scale_ref,
+    hot_ref,
+    hot0_ref,
+):
     sub = pl.program_id(0)
     group = group_at(turn, groups)
     width = xc_ref.shape[1]
     per_group = width // head_dim
     heads = per_group * groups
+
+    @pl.when(sub == 0)
+    def _():
+        hot_ref[...] = spread(2 * heads, 4 * heads, group * per_group, heads, width, head_dim)
+        hot0_ref[...] = spread(0, 2 * heads, group * per_group, heads, width, head_dim)
+
     back = lax.broadcasted_iota(jnp.int32, (SUB, SUB), 0) - lax.broadcasted_iota(jnp.int32, (SUB, SUB), 1)
     keep = (back >= 0) & (back <= age_ref[...])
     c_blk = cc_ref[...]
     scores = lax.dot_general(c_blk, bc_ref[...], (((1,), (1,)), ((), ())), preferred_element_type=F32)
     scores = jnp.where(keep, scores, 0.0)
-    col = pltpu.roll(tab32_ref[...], LANES - (3 * heads + group * per_group), 1)
+    col = pltpu.roll(col_ref[...], LANES - (2 * heads + group * per_group), 1)
     lane = lax.broadcasted_iota(jnp.int32, (SUB, LANES), 1)
     per_tile = LANES // head_dim
     for tile in range(per_group // per_tile):
@@ -452,52 +496,50 @@
             left.append((jnp.exp2(jnp.minimum(gap, 80.0)) * scores).astype(BF16))
             mine = (lane >= i * head_dim) & (lane < (i + 1) * head_dim)
             right.append(jnp.where(mine, x_tile, 0.0).astype(BF16))
-        out_ref[:, lanes] = mm(jnp.concatenate(left, 1), jnp.concatenate(right, 0))
-
-    @pl.when(sub > 0)
-    def _():
-        for chunk in range(width // CHUNK):
-            lanes = slice(chunk * CHUNK, (chunk + 1) * CHUNK)
-            first_head = group * per_group + chunk * (CHUNK // head_dim)
-            one_hot = spread(1, first_head, heads, CHUNK, head_dim)
-            out_ref[:, lanes] += mm(c_blk, h_ref[0, :, lanes]) * mm(tab_ref[...], one_hot)
-
-
-def intra(turn, xc, bc, cc, h, tab, tab32, row, age):
+        inner = mm(jnp.concatenate(left, 1), jnp.concatenate(right, 0))
+        inner = inner + mm(c_blk, h_ref[0, :, lanes]) * mm(tab_ref[...], hot_ref[:, lanes])
+        gate = silu(gate_ref[:, lanes].astype(F32))
+        part_ref[:, lanes] = inner * gate
+        scale_ref[:, lanes] = mm(tab0_ref[...], hot0_ref[:, lanes]) * gate
+
+
+def intra(turn, xc, bc, cc, h, tab, tab0, col, row, age, gate):
     tok, channels = xc.shape
     heads = row.shape[0]
     head_dim = channels // heads
     groups = bc.shape[1] // STATE
     width = channels // groups
+    out = jax.ShapeDtypeStruct((tok, width), F32)
     return pl.pallas_call(
         functools.partial(intra_kernel, turn, groups, head_dim),
-        out_shape=jax.ShapeDtypeStruct((tok, width), F32),
+        out_shape=(out, out),
         grid=(tok // SUB,),
         in_specs=[
             pl.BlockSpec((SUB, width), lambda i: (i, group_at(turn, groups))),
             pl.BlockSpec((SUB, STATE), lambda i: (i, group_at(turn, groups))),
             pl.BlockSpec((SUB, STATE), lambda i: (i, group_at(turn, groups))),
             pl.BlockSpec((1, STATE, width), lambda i: (jnp.maximum(i - 1, 0), 0, group_at(turn, groups))),
-            pl.BlockSpec((SUB, 2 * LANES), lambda i: (i, 0)),
+            pl.BlockSpec((SUB, LANES), lambda i: (i, 0)),
+            pl.BlockSpec((SUB, 2 * heads), lambda i: (i, 0)),
             pl.BlockSpec((SUB, LANES), lambda i: (i, 0)),
             pl.BlockSpec((heads // groups, SUB), lambda i: (group_at(turn, groups), i)),
             pl.BlockSpec((SUB, LANES), lambda i: (i, 0)),
+            pl.BlockSpec((SUB, width), lambda i: (i, group_at(turn, groups))),
         ],
-        out_specs=pl.BlockSpec((SUB, width), lambda i: (i, 0)),
-        compiler_params=params(),
-        cost_estimate=cost(tok * SUB * width * 4, tok * width * 8, tok * SUB * width // head_dim),
+        out_specs=(pl.BlockSpec((SUB, width), lambda i: (i, 0)),) * 2,
+        scratch_shapes=[pltpu.VMEM((4 * heads, width), BF16), pltpu.VMEM((2 * heads, width), BF16)],
+        compiler_params=params(16),
+        cost_estimate=cost(tok * SUB * width * 4, tok * width * 12, tok * SUB * width // head_dim),
         name="intra",
-    )(xc, bc, cc, h, tab, tab32, row, age)
-
-
-def final_kernel(turn, groups, head_dim, *refs):
-    cc_ref, tab_ref, gate_ref, gain_ref, part_ref = refs[:5]
+    )(xc, bc, cc, h, tab, tab0, col, row, age, gate)
+
+
+def final_kernel(turn, groups, *refs):
+    cc_ref, gain_ref, part_ref, scale_ref = refs[:4]
     per_group = CLUSTER // groups
-    pieces = refs[5 : 5 + per_group]
+    pieces = refs[4 : 4 + per_group]
     out_ref, y_ref = refs[-2:]
-    width = gate_ref.shape[1]
-    heads = groups * width // head_dim
-    group = group_at(turn, groups)
+    width = part_ref.shape[1]
     mine = lax.axis_index("seq") % CLUSTER
     owned = width // per_group
     squares = None
@@ -505,9 +547,8 @@
         for part in range(owned // CHUNK):
             at = ((mine ^ k) % per_group) * owned + part * CHUNK
             lanes = pl.ds(pl.multiple_of(at, CHUNK), CHUNK)
-            scale = mm(tab_ref[...], spread(2, group * (width // head_dim) + at // head_dim, heads, CHUNK, head_dim))
             carried = mm(cc_ref[...], pieces[k][:, part * CHUNK : (part + 1) * CHUNK])
-            value = (part_ref[:, lanes] + carried * scale) * silu(gate_ref[:, lanes].astype(F32))
+            value = part_ref[:, lanes] + carried * scale_ref[:, lanes]
             y_ref[:, lanes] = value
             square = value * value
             for i in range(CHUNK // LANES):
@@ -517,21 +558,20 @@
     out_ref[...] = (y_ref[...] * factor * gain_ref[...]).astype(BF16)
 
 
-def final(turn, cc, tab, gate, gain, part, pieces, head_dim, so_far=None):
-    tok, channels = gate.shape
+def final(turn, cc, gain, part, scale, pieces, so_far=None):
+    tok, width = part.shape
     groups = CLUSTER // len(pieces)
-    rows = 64
-    width = channels // groups
-    operands = (cc, tab, gate, gain, part, *pieces) + (() if so_far is None else (so_far,))
+    channels = width * groups
+    rows = 128
+    operands = (cc, gain, part, scale, *pieces) + (() if so_far is None else (so_far,))
     return pl.pallas_call(
-        functools.partial(final_kernel, turn, groups, head_dim),
+        functools.partial(final_kernel, turn, groups),
         out_shape=jax.ShapeDtypeStruct((tok, channels), BF16),
         grid=(tok // rows,),
         in_specs=[
             pl.BlockSpec((rows, STATE), lambda i: (i, group_at(turn, groups))),
-            pl.BlockSpec((rows, 2 * LANES), lambda i: (i, 0)),
-            pl.BlockSpec((rows, width), lambda i: (i, group_at(turn, groups))),
             pl.BlockSpec((1, width), lambda i: (0, group_at(turn, groups))),
+            pl.BlockSpec((rows, width), lambda i: (i, 0)),
             pl.BlockSpec((rows, width), lambda i: (i, 0)),
         ]
         + [VMEM] * len(pieces)
@@ -539,8 +579,8 @@
         out_specs=pl.BlockSpec((rows, width), lambda i: (i, group_at(turn, groups))),
         scratch_shapes=[pltpu.VMEM((rows, width), F32)],
         input_output_aliases={} if so_far is None else {len(operands) - 1: 0},
-        compiler_params=params(),
-        cost_estimate=cost(tok * STATE * width * 2, tok * width * 8, tok * width),
+        compiler_params=params(16),
+        cost_estimate=cost(tok * STATE * width * 2, tok * width * 8),
         name="final",
     )(*operands)
 
@@ -591,25 +631,27 @@
     norm_gain,
     doc_lengths,
 ):
-    channels = x_input.shape[1]
-    head_dim = channels // dt_input.shape[1]
     groups = b_input.shape[1] // STATE
     count = lax.axis_size("seq")
-    tail = lax.ppermute(pack(x_input, b_input, c_input), "seq", [(i, (i + 1) % count) for i in range(count)])
-    tab, tab32, row, d, age, taps, part, xc, bc, cc = conv(
-        doc_lengths, dt_input.T, decay_rate[None, :], x_input, b_input, c_input, taps_x, taps_b, taps_c
+    pin = lambda value: pltpu.with_memory_space_constraint(value, pltpu.HBM)
+    x_input, b_input, c_input, doc_lengths = pin(x_input), pin(b_input), pin(c_input), pin(doc_lengths)
+    taps_x, taps_b, taps_c = pin(taps_x), pin(taps_b), pin(taps_c)
+    ends, tab, tab0, col, row, d, age = prep(
+        doc_lengths, pin(dt_input.T), pin(decay_rate[None, :]), x_input, b_input, c_input
     )
+    tail = lax.ppermute(ends, "seq", [(i, (i + 1) % count) for i in range(count)])
+    taps, part, xc, bc, cc = conv(age, x_input, b_input, c_input, taps_x, taps_b, taps_c)
     xc, bc, cc, h, *pieces = states(tail, part, taps, age, tab, d, xc, bc, cc)
-    first = intra(0, xc, bc, cc, h, tab, tab32, row, age)
-    local, pre, total = scan_blocks(tied(exchanged(pieces, (3, 2, 1)), first))
-    second = intra(1, xc, bc, cc, h, tab, tab32, row, age)
-    (before,) = tied([before_cluster(total, pre)], second)
+    first = intra(0, xc, bc, cc, h, tab, tab0, col, row, age, gate_input)
+    local, pre, total = scan_blocks(tied(exchanged(pieces, (3, 2, 1)), first[0]))
+    second = intra(1, xc, bc, cc, h, tab, tab0, col, row, age, gate_input)
+    (before,) = tied([before_cluster(total, pre)], second[0])
     entering = exchanged(join(before, local, pre), (1, 3, 2))
     share = CLUSTER // groups
     output = None
     for turn, inner in enumerate((first, second)):
         mine = entering[turn * share : (turn + 1) * share]
-        output = final(turn, cc, tab, gate_input, norm_gain[None, :], inner, mine, head_dim, output)
+        output = final(turn, cc, norm_gain[None, :], *inner, mine, output)
     return output
 
 

time: 45.1 us -> 40.2 us (0.89)
  Pallas kernels: 23.7 us -> 18.4 us
  waiting for transfers between devices: 7.68 us -> 9.01 us
  local copies, waits for them, and re-layouts: 0.83 us -> 0.01 us
    pallas_call x4, Pallas kernels: 14.6 us -> 10.7 us  [the longest x1 5.08 us: conv(): pl.pallas_call(conv_kernel, out_shape=(shape((taps_len, width), F32), sha...]
    ppermute x7, waiting for transfers between devices: 7.67 us -> 9.01 us  [moved(): lax.ppermute(value, 'seq', [(i, hop(i)) for i in range(count) if 0 <= hop...]
    unnamed x22 -> x4, local copies, waits for them, and re-layouts: 0.83 us -> 0.01 us
    pallas_call x1, Pallas kernels: 2.39 us -> 1.65 us  [states(): pl.pallas_call(state_kernel, out_shape=(*same, jax.ShapeDtypeStruct((tok...]
    pallas_call x2, Pallas kernels: 6.39 us -> 5.69 us  [intra(): pl.pallas_call(functools.partial(intra_kernel, turn, groups, head_dim), o...]
  transfers between devices with their start and end apart: 8 -> 8, of which waited for: 4 -> 5; matrix products, arithmetic and copies ran while one was open for 0% -> 0% of each run, Pallas kernels for 34% -> 32%
where the time goes in v3:
time: 40.2 us; the launch traced here: 40.1 us
  Pallas kernels  18.4 us (46%)
  starting transfers between devices  12.6 us (31%)
  waiting for transfers between devices  9.01 us (22%)
    ppermute x7, starting transfers between devices, moved(): lax.ppermute(value, 'seq', [(i, hop(i)) for i in range(count) if 0 <= hop...  9.56 us
    ppermute x7, waiting for transfers between devices, moved(): lax.ppermute(value, 'seq', [(i, hop(i)) for i in range(count) if 0 <= hop...  9.01 us
    pallas_call x2, Pallas kernels, intra(): pl.pallas_call(functools.partial(intra_kernel, turn, groups, head_dim), o...  5.69 us
    pallas_call x1, Pallas kernels, conv(): pl.pallas_call(conv_kernel, out_shape=(shape((taps_len, width), F32), sha...  5.08 us
    pallas_call x2, Pallas kernels, final(): pl.pallas_call(functools.partial(final_kernel, turn, groups), out_shape=j...  4.2 us
    ppermute x1, starting transfers between devices, on_device(): lax.ppermute(ends, 'seq', [(i, (i + 1) % count) for i in range(count)])  2.99 us
    pallas_call x1, Pallas kernels, states(): pl.pallas_call(state_kernel, out_shape=(*same, jax.ShapeDtypeStruct((tok...  1.65 us
    pallas_call x1, Pallas kernels, prep(): pl.pallas_call(prep_kernel, out_shape=(shape((8, x.shape[1] + b.shape[1]...  1.43 us
  transfers between devices with their start and end apart: 8, of which 5 were waited for; matrix products, arithmetic and copies ran while one was open for 0% of the time, Pallas kernels for 32%

profile of v3, /device:TPU:0, one launch (start us, length us, event | category | flops | bytes accessed | tf_op | source)
XLA Modules:
  0.0 40.1 jit_solution(5751550351385735988)
XLA Ops:
  0.0 1.4 %prep.1 = (bf16[8,2560]{1,0:T(8,128)(2,1)S(1)}, bf16[384,128]{1,0:T(8,128)(2,1)S(1)}, bf16[384,64]{1,0:T(8,128)(2,1)S(1)}, f32[384,128]{1,0:T(8,128)S(1)}, f32[3...) custom-call(s32[4]{0:T(128)} %dl_hbm.1, f32[32,384]{1,0:T(8,128)} %bitcast.5, ...), custom_call_target="tpu_custom_call" | custom-call | tf_op jit(solution)/shard_map/prep/pallas_call | solution.py:171
  1.4 3.0 %collective-permute-start = (bf16[8,2560]{1,0:T(8,128)(2,1)S(1)}, bf16[8,2560]{1,0:T(8,128)(2,1)S(1)}, u32[]{:S(2)}, u32[]{:S(2)}) collective-permute-start(bf16[8,2560]{1,0:T(8,128)(2,1)S(1)} %get-tuple-element.41), channel_id=1, source_target_pairs={{0,2},{2,4},{4,6},{6,8},{8,10},{10,12},{12,14},{14,0},{1,3},{3,5},... | collective-permute-start | bytes 122888 | tf_op jit(solution)/shard_map/ppermute | solution.py:642
  4.4 5.1 %conv.1 = (f32[4,2560]{1,0:T(4,128)S(1)}, f32[8,2560]{1,0:T(8,128)S(1)}, bf16[384,2048]{1,0:T(8,128)(2,1)S(1)}, bf16[384,256]{1,0:T(8,128)(2,1)S(1)}, bf16[384,256]{1,0:T(8,128)(2,1)S(1)}) custom-call(s32[384,128]{1,0:T(8,128)S(1)} %get-tuple-element.42.age_ref, bf16[384,2048]{1,0:T(8,128)(2,1)} %x_hbm.3, bf16[384,256]{1,0:T(8,128)(2,1)} %b_hbm.3, ...), custom_call_target="tpu_custom_call" | custom-call | flops 15728640 | bytes 3932160 | tf_op jit(solution)/shard_map/conv/pallas_call | solution.py:269
  9.5 0.0 copy-start
  9.5 0.0 collective-permute-done.tail_ref
  9.5 1.6 %state.1 = (bf16[384,2048]{1,0:T(8,128)(2,1)S(1)}, bf16[384,256]{1,0:T(8,128)(2,1)S(1)}, bf16[384,256]{1,0:T(8,128)(2,1)S(1)}, bf16[2,128,2048]{2,1,0:T(8,128)(2...) custom-call(bf16[8,2560]{1,0:T(8,128)(2,1)S(1)} %collective-permute-, ...), custom_call_target="tpu_custom_call", output_to_operand_aliasing={{0}: (6, {}), {1}: (7, {}), {2}: (8, {})} | custom-call | flops 402653184 | bytes 3145728 | tf_op jit(solution)/shard_map/state/pallas_call | solution.py:357
  11.2 1.6 %collective-permute-start.1 = (bf16[136,512]{1,0:T(8,128)(2,1)S(1)}, bf16[136,512]{1,0:T(8,128)(2,1)S(1)}, u32[]{:S(2)}, u32[]{:S(2)}) collective-permute-start(bf16[136,512]{1,0:T(8,128)(2,1)S(1)} %get-tuple-element.60), channel_id=1, source_target_pairs={{0,2},{2,0},{4,6},{6,4},{8,10},{10,8},{12,14},{14,12},{1,3},{3,1},... | collective-permute-start | bytes 417800 | tf_op jit(solution)/shard_map/ppermute | solution.py:590
  12.8 1.6 %collective-permute-start.2 = (bf16[136,512]{1,0:T(8,128)(2,1)S(1)}, bf16[136,512]{1,0:T(8,128)(2,1)S(1)}, u32[]{:S(2)}, u32[]{:S(2)}) collective-permute-start(bf16[136,512]{1,0:T(8,128)(2,1)S(1)} %get-tuple-element.61), channel_id=1, source_target_pairs={{0,4},{2,6},{4,0},{6,2},{8,12},{10,14},{12,8},{14,10},{1,5},{3,7},... | collective-permute-start | bytes 417800 | tf_op jit(solution)/shard_map/ppermute | solution.py:590
  14.4 0.4 collective-permute-start.3
  14.7 0.0 copy-done
  14.7 2.8 %intra.3 = (f32[384,1024]{1,0:T(8,128)S(1)}, f32[384,1024]{1,0:T(8,128)S(1)}) custom-call(bf16[384,2048]{1,0:T(8,128)(2,1)S(1)} %get-tuple-element.51.xc_ref, bf16[384,256]{1,0:T(8,128)(2,1)S(1)} %get-tuple-element.52.bc_ref, bf16[384,256]{1,0:T(8,128)(2,1)S(1)} %get-tuple-element.50.cc_ref.refs_0_, bf16[2,128,2048]{2,1,0:T(8,128)(2,1)S(1)} %get-tuple-element.53.h_ref, ...), custom_call_target="tpu_custom_call" | custom-call | flops 201326592 | bytes 4718592 | tf_op jit(solution)/shard_map/intra/pallas_call | solution.py:513
  17.6 0.0 collective-permute-done.1.refs_1_
  17.6 1.5 %collective-permute-done.2.refs_2_ = bf16[136,512]{1,0:T(8,128)(2,1)S(1)} collective-permute-done((bf16[136,512]{1,0:T(8,128)(2,1)S(1)}, bf16[136,512]{1,0:T(8,128)(2,1)S(1)}, u32[]{:S(2)}, u32[]{:S(2)}) %collective-permute-start.2) | collective-permute-done | bytes 139296 | tf_op jit(solution)/shard_map/ppermute | solution.py:590
  19.2 1.6 %collective-permute-done.3.refs_3_ = bf16[136,512]{1,0:T(8,128)(2,1)S(1)} collective-permute-done((bf16[136,512]{1,0:T(8,128)(2,1)S(1)}, bf16[136,512]{1,0:T(8,128)(2,1)S(1)}, u32[]{:S(2)}, u32[]{:S(2)}) %collective-permute-start.3) | collective-permute-done | bytes 139296 | tf_op jit(solution)/shard_map/ppermute | solution.py:590
  20.8 0.2 cluster_scan.1
  21.0 0.0 copy-start.1
  21.0 2.5 %collective-permute-start.4 = (bf16[128,512]{1,0:T(8,128)(2,1)S(1)}, bf16[128,512]{1,0:T(8,128)(2,1)S(1)}, u32[]{:S(2)}, u32[]{:S(2)}) collective-permute-start(bf16[128,512]{1,0:T(8,128)(2,1)S(1)} %get-tuple-element.68), channel_id=1, source_target_pairs={{0,8},{2,10},{4,12},{6,14},{8,0},{10,2},{12,4},{14,6},{1,9},{3,11}... | collective-permute-start | bytes 393224 | tf_op jit(solution)/shard_map/ppermute | solution.py:590
  23.4 2.8 %intra.2 = (f32[384,1024]{1,0:T(8,128)S(1)}, f32[384,1024]{1,0:T(8,128)S(1)}) custom-call(bf16[384,2048]{1,0:T(8,128)(2,1)S(1)} %get-tuple-element.51.xc_ref, bf16[384,256]{1,0:T(8,128)(2,1)S(1)} %get-tuple-element.52.bc_ref, bf16[384,256]{1,0:T(8,128)(2,1)S(1)} %get-tuple-element.50.cc_ref.refs_0_, bf16[2,128,2048]{2,1,0:T(8,128)(2,1)S(1)} %get-tuple-element.53.h_ref, ...), custom_call_target="tpu_custom_call" | custom-call | flops 201326592 | bytes 4718592 | tf_op jit(solution)/shard_map/intra/pallas_call | solution.py:513
  26.3 2.7 %collective-permute-done.4.before_ref = bf16[128,512]{1,0:T(8,128)(2,1)S(1)} collective-permute-done((bf16[128,512]{1,0:T(8,128)(2,1)S(1)}, bf16[128,512]{1,0:T(8,128)(2,1)S(1)}, u32[]{:S(2)}, u32[]{:S(2)}) %collective-permute-start.4) | collective-permute-done | bytes 131104 | tf_op jit(solution)/shard_map/ppermute | solution.py:590
  29.0 0.1 join.1
  29.2 0.7 %collective-permute-start.7 = (bf16[128,512]{1,0:T(8,128)(2,1)S(1)}, bf16[128,512]{1,0:T(8,128)(2,1)S(1)}, u32[]{:S(2)}, u32[]{:S(2)}) collective-permute-start(bf16[128,512]{1,0:T(8,128)(2,1)S(1)} %get-tuple-element.76), channel_id=1, source_target_pairs={{0,2},{2,0},{4,6},{6,4},{8,10},{10,8},{12,14},{14,12},{1,3},{3,1},... | collective-permute-start | bytes 393224 | tf_op jit(solution)/shard_map/ppermute | solution.py:590
  29.9 0.3 collective-permute-start.5
  30.2 2.6 %collective-permute-start.6 = (bf16[128,512]{1,0:T(8,128)(2,1)S(1)}, bf16[128,512]{1,0:T(8,128)(2,1)S(1)}, u32[]{:S(2)}, u32[]{:S(2)}) collective-permute-start(bf16[128,512]{1,0:T(8,128)(2,1)S(1)} %get-tuple-element.73), channel_id=1, source_target_pairs={{0,6},{2,4},{4,2},{6,0},{8,14},{10,12},{12,10},{14,8},{1,7},{3,5},... | collective-permute-start | bytes 393224 | tf_op jit(solution)/shard_map/ppermute | solution.py:590
  32.7 2.5 %collective-permute-done.7.refs_5_ = bf16[128,512]{1,0:T(8,128)(2,1)S(1)} collective-permute-done((bf16[128,512]{1,0:T(8,128)(2,1)S(1)}, bf16[128,512]{1,0:T(8,128)(2,1)S(1)}, u32[]{:S(2)}, u32[]{:S(2)}) %collective-permute-start.7) | collective-permute-done | bytes 131104 | tf_op jit(solution)/shard_map/ppermute | solution.py:590
  35.2 0.0 copy-done.1
  35.2 2.1 %final.2.refs_6_ = bf16[384,2048]{1,0:T(8,128)(2,1)} custom-call(bf16[384,256]{1,0:T(8,128)(2,1)S(1)} %get-tuple-element.50.cc_ref.refs_0_, f32[1,2048]{1,0:T(1,128)S(1)} %bitcast.3, f32[384,1024]{1,0:T(8,128)S(1)} %get-tuple-element.63.refs_2_, f32[384,1024]{1,0:T(8,128)S(1)} %get-tuple-element.74.refs_3_, bf16[128,512]{1,0:T(8,128)(2,1)S(1)} %get-tuple-element.75.refs_4_, ...), custom_call_target="tpu_custom_call" | custom-call | flops 100663296 | bytes 3145728 | tf_op jit(solution)/shard_map/final/pallas_call | solution.py:567
  37.3 0.0 collective-permute-done.5.refs_4_
  37.3 0.6 %collective-permute-done.6.refs_5_ = bf16[128,512]{1,0:T(8,128)(2,1)S(1)} collective-permute-done((bf16[128,512]{1,0:T(8,128)(2,1)S(1)}, bf16[128,512]{1,0:T(8,128)(2,1)S(1)}, u32[]{:S(2)}, u32[]{:S(2)}) %collective-permute-start.6) | collective-permute-done | bytes 131104 | tf_op jit(solution)/shard_map/ppermute | solution.py:590
  38.0 2.1 %final.3 = bf16[384,2048]{1,0:T(8,128)(2,1)} custom-call(bf16[384,256]{1,0:T(8,128)(2,1)S(1)} %get-tuple-element.50.cc_ref.refs_0_, f32[1,2048]{1,0:T(1,128)S(1)} %bitcast.4, f32[384,1024]{1,0:T(8,128)S(1)} %get-tuple-element.57.refs_2_, f32[384,1024]{1,0:T(8,128)S(1)} %get-tuple-element.58.refs_3_, ...), custom_call_target="tpu_custom_call", output_to_operand_aliasing={{}: (6, {})} | custom-call | flops 100663296 | bytes 3145728 | tf_op jit(solution)/shard_map/final/pallas_call | solution.py:567
Async XLA Ops:
  1.4 8.1 %collective-permute-start = (bf16[8,2560]{1,0:T(8,128)(2,1)S(1)}, bf16[8,2560]{1,0:T(8,128)(2,1)S(1)}, u32[]{:S(2)}, u32[]{:S(2)}) collective-permute-start(bf16[8,2560]{1,0:T(8,128)(2,1)S(1)} %get-tuple-element.41), channel_id=1, source_target_pairs={{0,2},{2,4},{4,6},{6,8},{8,10},{10,12},{12,14},{14,0},{1,3},{3,5},... | collective-permute-start | bytes 122888 | tf_op jit(solution)/shard_map/ppermute | solution.py:642
  9.5 5.2 %copy-start = (bf16[384,2048]{1,0:T(8,128)(2,1)S(1)}, bf16[384,2048]{1,0:T(8,128)(2,1)}, u32[]{:S(2)}) copy-start(bf16[384,2048]{1,0:T(8,128)(2,1)} %gate_ref.3) | copy-start | bytes 4718596
  11.2 6.4 %collective-permute-start.1 = (bf16[136,512]{1,0:T(8,128)(2,1)S(1)}, bf16[136,512]{1,0:T(8,128)(2,1)S(1)}, u32[]{:S(2)}, u32[]{:S(2)}) collective-permute-start(bf16[136,512]{1,0:T(8,128)(2,1)S(1)} %get-tuple-element.60), channel_id=1, source_target_pairs={{0,2},{2,0},{4,6},{6,4},{8,10},{10,8},{12,14},{14,12},{1,3},{3,1},... | collective-permute-start | bytes 417800 | tf_op jit(solution)/shard_map/ppermute | solution.py:590
  12.8 6.3 %collective-permute-start.2 = (bf16[136,512]{1,0:T(8,128)(2,1)S(1)}, bf16[136,512]{1,0:T(8,128)(2,1)S(1)}, u32[]{:S(2)}, u32[]{:S(2)}) collective-permute-start(bf16[136,512]{1,0:T(8,128)(2,1)S(1)} %get-tuple-element.61), channel_id=1, source_target_pairs={{0,4},{2,6},{4,0},{6,2},{8,12},{10,14},{12,8},{14,10},{1,5},{3,7},... | collective-permute-start | bytes 417800 | tf_op jit(solution)/shard_map/ppermute | solution.py:590
  14.4 6.4 %collective-permute-start.3 = (bf16[136,512]{1,0:T(8,128)(2,1)S(1)}, bf16[136,512]{1,0:T(8,128)(2,1)S(1)}, u32[]{:S(2)}, u32[]{:S(2)}) collective-permute-start(bf16[136,512]{1,0:T(8,128)(2,1)S(1)} %get-tuple-element.62), channel_id=1, source_target_pairs={{0,6},{2,4},{4,2},{6,0},{8,14},{10,12},{12,10},{14,8},{1,7},{3,5},... | collective-permute-start | bytes 417800 | tf_op jit(solution)/shard_map/ppermute | solution.py:590
  21.0 14.2 %copy-start.1 = (f32[2048]{0:T(1024)S(1)}, f32[2048]{0:T(1024)}, u32[]{:S(2)}) copy-start(f32[2048]{0:T(1024)} %param.20) | copy-start | bytes 24580
  21.0 8.0 %collective-permute-start.4 = (bf16[128,512]{1,0:T(8,128)(2,1)S(1)}, bf16[128,512]{1,0:T(8,128)(2,1)S(1)}, u32[]{:S(2)}, u32[]{:S(2)}) collective-permute-start(bf16[128,512]{1,0:T(8,128)(2,1)S(1)} %get-tuple-element.68), channel_id=1, source_target_pairs={{0,8},{2,10},{4,12},{6,14},{8,0},{10,2},{12,4},{14,6},{1,9},{3,11}... | collective-permute-start | bytes 393224 | tf_op jit(solution)/shard_map/ppermute | solution.py:590
  29.2 6.0 %collective-permute-start.7 = (bf16[128,512]{1,0:T(8,128)(2,1)S(1)}, bf16[128,512]{1,0:T(8,128)(2,1)S(1)}, u32[]{:S(2)}, u32[]{:S(2)}) collective-permute-start(bf16[128,512]{1,0:T(8,128)(2,1)S(1)} %get-tuple-element.76), channel_id=1, source_target_pairs={{0,2},{2,0},{4,6},{6,4},{8,10},{10,8},{12,14},{14,12},{1,3},{3,1},... | collective-permute-start | bytes 393224 | tf_op jit(solution)/shard_map/ppermute | solution.py:590
  29.9 7.5 %collective-permute-start.5 = (bf16[128,512]{1,0:T(8,128)(2,1)S(1)}, bf16[128,512]{1,0:T(8,128)(2,1)S(1)}, u32[]{:S(2)}, u32[]{:S(2)}) collective-permute-start(bf16[128,512]{1,0:T(8,128)(2,1)S(1)} %get-tuple-element.72), channel_id=1, source_target_pairs={{0,4},{2,6},{4,0},{6,2},{8,12},{10,14},{12,8},{14,10},{1,5},{3,7},... | collective-permute-start | bytes 393224 | tf_op jit(solution)/shard_map/ppermute | solution.py:590
  30.2 7.8 %collective-permute-start.6 = (bf16[128,512]{1,0:T(8,128)(2,1)S(1)}, bf16[128,512]{1,0:T(8,128)(2,1)S(1)}, u32[]{:S(2)}, u32[]{:S(2)}) collective-permute-start(bf16[128,512]{1,0:T(8,128)(2,1)S(1)} %get-tuple-element.73), channel_id=1, source_target_pairs={{0,6},{2,4},{4,2},{6,0},{8,14},{10,12},{12,10},{14,8},{1,7},{3,5},... | collective-permute-start | bytes 393224 | tf_op jit(solution)/shard_map/ppermute | solution.py:590

commit v4 on v3

v4 whole, which is shorter than its diff:
```python
import functools

import jax
import jax.numpy as jnp
from jax import lax
from jax.experimental import pallas as pl
from jax.experimental.pallas import tpu as pltpu
from jax.sharding import PartitionSpec as P

STATE = 128
SUB = 128
CHUNK = 256
LANES = 128
ROWS = 32
CLUSTER = 4
LOG2E = 1.4426950408889634
norm_eps = 1e-05

F32 = jnp.float32
BF16 = jnp.bfloat16
VMEM = pl.BlockSpec(memory_space=pltpu.VMEM)
ANY = pl.BlockSpec(memory_space=pl.ANY)
HBM = pl.BlockSpec(memory_space=pltpu.HBM)


def params(mib=24):
    return pltpu.CompilerParams(vmem_limit_bytes=mib << 20)


def cost(flops, moved, transcendentals=0):
    return pl.CostEstimate(flops=flops, bytes_accessed=moved, transcendentals=transcendentals)


def doc_edges(dl_ref):
    edges = [0]
    for i in range(dl_ref.shape[0] - 1):
        edges.append(edges[-1] + dl_ref[i])
    return edges


def doc_start(token, edges):
    start = jnp.zeros_like(token)
    for edge in edges[1:]:
        start = jnp.where(token >= edge, jnp.maximum(start, edge), start)
    return start


def split2(value):
    high = value.astype(BF16)
    return high, (value - high.astype(F32)).astype(BF16)


def split3(value):
    high = value.astype(BF16)
    rest = value - high.astype(F32)
    mid = rest.astype(BF16)
    return high, mid, (rest - mid.astype(F32)).astype(BF16)


def mm(a, b):
    return jnp.dot(a, b, preferred_element_type=F32)


def silu(value):
    half = 0.5 * value
    return half + half * jnp.tanh(half)


def spread(base, rows, first_head, heads, width, head_dim):
    row = lax.broadcasted_iota(jnp.int32, (rows, width), 0) - (base + first_head)
    head = lax.broadcasted_iota(jnp.int32, (rows, width), 1) // head_dim
    return jnp.where((row == head) | (row == head + heads), 1.0, 0.0).astype(BF16)


def start_all(copies):
    for copy in copies:
        copy.start()


def wait_all(copies):
    for copy in copies:
        copy.wait()


def tables(row0, edges, dt_ref, rate_ref, tab_ref, tab0_ref, col_ref, row_ref, d_ref):
    heads, tok = dt_ref.shape
    upto = jnp.where(
        lax.broadcasted_iota(jnp.int32, (SUB, SUB), 0) <= lax.broadcasted_iota(jnp.int32, (SUB, SUB), 1), 1.0, 0.0
    ).astype(BF16)
    rate = jnp.concatenate([rate_ref[...], jnp.zeros((1, LANES - heads), F32)], 1)
    rate = jnp.broadcast_to(rate, (LANES, LANES)).T[:heads]
    total = jnp.zeros((heads, 1), F32)
    decays = []
    for c in range(tok // SUB):
        span = slice(c * SUB, (c + 1) * SUB)
        first = row0 + c * SUB
        dt = dt_ref[:, span]
        step = jnp.maximum(dt, 0.0) + jnp.log1p(jnp.exp(-jnp.abs(dt)))
        parts = split3(-(step * rate))
        cum = mm(parts[0], upto) + (mm(parts[1], upto) + mm(parts[2], upto))
        last = cum[:, SUB - 1 :]
        token = first + lax.broadcasted_iota(jnp.int32, (heads, SUB), 1)
        start = doc_start(token, edges)
        last_start = doc_start(jnp.int32(first + SUB - 1), edges)
        to_end = jnp.exp(last - cum) * step * jnp.where(token >= last_start, 1.0, 0.0)
        since_sub = jnp.exp(cum) * jnp.where((start < first) & (c > 0), 1.0, 0.0)
        since_block = jnp.exp(cum + total) * jnp.where(start < row0, 1.0, 0.0)
        first_pair = [part.astype(F32) for part in (*split2(to_end), *split2(since_sub))]
        second_pair = [part.astype(F32) for part in split2(since_block)] + [cum * LOG2E, jnp.zeros_like(cum)]
        tab_ref[span, :] = jnp.concatenate(first_pair, 0).T.astype(BF16)
        second = jnp.concatenate(second_pair, 0).T
        tab0_ref[span, :] = second[:, : 2 * heads].astype(BF16)
        col_ref[span, :] = second
        row_ref[:, span] = (jnp.log(step) - cum) * LOG2E
        decays.append(jnp.exp(last) * jnp.where(last_start < first, 1.0, 0.0))
        total = total + last
    end_start = doc_start(jnp.int32(row0 + tok - 1), edges)
    whole = jnp.exp(total) * jnp.where(end_start < row0, 1.0, 0.0)
    columns = [part.astype(F32) for part in split3(whole)] + decays[1:]
    columns.append(jnp.zeros((heads, LANES - len(columns)), F32))
    columns = jnp.concatenate([jnp.concatenate(columns, 1), jnp.zeros((LANES - heads, LANES), F32)], 0)
    halves = [part.astype(F32)[:, :heads] for part in split2(columns.T[:8])]
    d_ref[...] = jnp.concatenate(halves, 1).astype(BF16)


def prep_kernel(
    dl_hbm,
    dt_hbm,
    rate_hbm,
    x_hbm,
    b_hbm,
    c_hbm,
    ends_ref,
    tab_ref,
    tab0_ref,
    col_ref,
    row_ref,
    d_ref,
    age_ref,
    dl_ref,
    dt_ref,
    rate_ref,
    sem,
):
    tok = x_hbm.shape[0]
    small = [
        pltpu.make_async_copy(hbm, ref, sem.at[i])
        for i, (hbm, ref) in enumerate(((dl_hbm, dl_ref), (dt_hbm, dt_ref), (rate_hbm, rate_ref)))
    ]
    start_all(small)
    ends, low = [], 0
    for i, ref in enumerate((x_hbm, b_hbm, c_hbm)):
        width = ref.shape[1]
        ends.append(
            pltpu.make_async_copy(ref.at[pl.ds(tok - 8, 8), :], ends_ref.at[:, pl.ds(low, width)], sem.at[3 + i])
        )
        low += width
    start_all(ends)
    wait_all(small)
    row0 = lax.axis_index("seq") * tok
    edges = doc_edges(dl_ref)
    tables(row0, edges, dt_ref, rate_ref, tab_ref, tab0_ref, col_ref, row_ref, d_ref)
    token = row0 + lax.broadcasted_iota(jnp.int32, (tok, LANES), 0)
    age_ref[...] = token - doc_start(token, edges)
    wait_all(ends)


def prep(doc_lengths, dt_t, rate, x, b, c):
    heads, tok = dt_t.shape
    shape = jax.ShapeDtypeStruct
    return pl.pallas_call(
        prep_kernel,
        out_shape=(
            shape((8, x.shape[1] + b.shape[1] + c.shape[1]), BF16),
            shape((tok, LANES), BF16),
            shape((tok, 2 * heads), BF16),
            shape((tok, LANES), F32),
            shape((heads, tok), F32),
            shape((8, 2 * heads), BF16),
            shape((tok, LANES), jnp.int32),
        ),
        in_specs=[HBM] * 6,
        out_specs=(VMEM,) * 7,
        scratch_shapes=[
            pltpu.SMEM(doc_lengths.shape, jnp.int32),
            pltpu.VMEM((heads, tok), F32),
            pltpu.VMEM((1, heads), F32),
            pltpu.SemaphoreType.DMA((6,)),
        ],
        compiler_params=params(16),
        name="prep",
    )(doc_lengths, dt_t, rate, x, b, c)


def place_of(k, owned):
    return pl.multiple_of((lax.axis_index("seq") % CLUSTER ^ k) * owned, owned)


def fill_masks(age_ref, mask_ref):
    for back in range(1, mask_ref.shape[0] + 1):
        mask_ref[back - 1] = jnp.where(age_ref[...] >= back, 1.0, 0.0)


def convolve(ext_ref, mask_ref, taps, emit):
    tok = ext_ref.shape[0] - 8
    repeats = ext_ref.shape[1] // LANES
    for low in range(0, tok, ROWS):
        total = ext_ref[8 + low : 8 + low + ROWS, :] * taps[-1]
        for back in range(1, len(taps)):
            mask = jnp.concatenate([mask_ref[back - 1, low : low + ROWS, :]] * repeats, 1)
            window = ext_ref[8 + low - back : 8 + low - back + ROWS, :]
            total = total + (window * taps[-1 - back]) * mask
        emit(low, total)


def state_of(at, heads, head_dim, bt_ref, tab_ref, d_ref, x_rows, h_put):
    one_hot = spread(0, 2 * heads, at // head_dim, heads, CHUNK, head_dim)
    decay = mm(d_ref[...], one_hot)
    tok = tab_ref.shape[0]
    state = None
    for c in range(tok // SUB):
        rows = slice(c * SUB, (c + 1) * SUB)
        weight = mm(tab_ref[rows, : 2 * heads], one_hot)
        local = mm(bt_ref[:, rows], (x_rows(c) * weight).astype(BF16))
        if state is None:
            state = local
        else:
            h_put(c - 1, state.astype(BF16))
            state = local + decay[2 + c : 3 + c, :] * state
    return state.astype(BF16), decay.astype(BF16)


def conv_kernel(
    age_ref,
    x_hbm,
    b_hbm,
    taps_x_hbm,
    taps_b_hbm,
    taps_x_ref,
    taps_b_ref,
    part_x_ref,
    part_b_ref,
    xc_ref,
    bc_ref,
    in_ref,
    ext_ref,
    mask_ref,
    sem,
    in_sem,
):
    channels = x_hbm.shape[1]
    owned = channels // CLUSTER
    per = owned // CHUNK
    chunks = (CLUSTER - 1) * per
    small = [
        pltpu.make_async_copy(taps_x_hbm, taps_x_ref, sem.at[0]),
        pltpu.make_async_copy(taps_b_hbm, taps_b_ref, sem.at[1]),
    ]
    start_all(small)

    def place(i):
        return pl.multiple_of(place_of(i // per + 1, owned) + (i % per) * CHUNK, CHUNK)

    def fetch(i):
        return pltpu.make_async_copy(x_hbm.at[:, pl.ds(place(i), CHUNK)], in_ref.at[i], in_sem.at[i])

    for i in range(chunks):
        fetch(i).start()
    fetch_b = pltpu.make_async_copy(b_hbm, in_ref.at[chunks], in_sem.at[chunks])
    fetch_b.start()
    fill_masks(age_ref, mask_ref)
    ext_ref[:8, :] = jnp.zeros((8, CHUNK), F32)
    wait_all(small)
    taps_len = taps_x_ref.shape[0]

    def body(i, carry):
        fetch(i).wait()
        k = i // per
        inner = pl.ds(pl.multiple_of((i % per) * CHUNK, CHUNK), CHUNK)
        ext_ref[8:, :] = in_ref[i].astype(F32)

        def emit(low, total):
            if low == 0:
                part_x_ref[k, :, inner] = total[:8]
            xc_ref[k, low : low + ROWS, inner] = silu(total).astype(BF16)

        convolve(ext_ref, mask_ref, [taps_x_ref[j : j + 1, pl.ds(place(i), CHUNK)] for j in range(taps_len)], emit)
        return carry

    lax.fori_loop(0, chunks, body, 0)
    fetch_b.wait()
    ext_ref[8:, :] = in_ref[chunks].astype(F32)

    def emit_b(low, total):
        if low == 0:
            part_b_ref[...] = total[:8]
        bc_ref[low : low + ROWS, :] = silu(total).astype(BF16)

    convolve(ext_ref, mask_ref, [taps_b_ref[j : j + 1, :] for j in range(taps_len)], emit_b)


def conv(age, x, b, taps_x, taps_b):
    tok, channels = x.shape
    gn = b.shape[1]
    owned = channels // CLUSTER
    places = (CLUSTER - 1) * (owned // CHUNK) + 1
    shape = jax.ShapeDtypeStruct
    return pl.pallas_call(
        conv_kernel,
        out_shape=(
            shape(taps_x.shape, F32),
            shape(taps_b.shape, F32),
            shape((CLUSTER - 1, 8, owned), F32),
            shape((8, gn), F32),
            shape((CLUSTER - 1, tok, owned), BF16),
            shape((tok, gn), BF16),
        ),
        in_specs=[VMEM] + [HBM] * 4,
        out_specs=(VMEM,) * 6,
        scratch_shapes=[
            pltpu.VMEM((places, tok, CHUNK), BF16),
            pltpu.VMEM((tok + 8, CHUNK), F32),
            pltpu.VMEM((taps_x.shape[0] - 1, tok, LANES), F32),
            pltpu.SemaphoreType.DMA((2,)),
            pltpu.SemaphoreType.DMA((places,)),
        ],
        compiler_params=params(16),
        cost_estimate=cost(tok * channels * 16, tok * channels * 4, tok * channels),
        name="conv",
    )(age, x, b, taps_x, taps_b)


def state_kernel(
    tail_ref,
    part_x_ref,
    part_b_ref,
    taps_x_ref,
    taps_b_ref,
    age_ref,
    tab_ref,
    d_ref,
    xc_in,
    bc_in,
    xc_ref,
    bc_ref,
    bt_ref,
    h_ref,
    *rest,
):
    sends = rest[: CLUSTER - 1]
    ext_ref, head_ref, head_b_ref = rest[CLUSTER - 1 :]
    pieces, tok, owned = xc_in.shape
    gn = bc_in.shape[1]
    channels = owned * CLUSTER
    heads = d_ref.shape[1] // 2
    head_dim = channels // heads
    taps_len = taps_x_ref.shape[0]
    ext_ref[:8, :] = tail_ref[...].astype(F32)
    ext_ref[8:, :] = jnp.zeros_like(ext_ref[8:, :])

    def head_of(part, lanes, taps, width):
        total = part
        age = jnp.concatenate([age_ref[:8, :]] * (width // LANES), 1)
        for back in range(1, taps_len):
            total = total + jnp.where(age >= back, ext_ref[8 - back : 16 - back, lanes] * taps[-1 - back], 0.0)
        return silu(total).astype(BF16)

    head = head_of(
        part_b_ref[...], slice(channels, channels + gn), [taps_b_ref[j : j + 1, :] for j in range(taps_len)], gn
    )
    bc_ref[:8, :] = head
    head_b_ref[...] = head.astype(F32)
    for group in range(gn // STATE):
        lanes = slice(group * STATE, (group + 1) * STATE)
        b_blk = jnp.concatenate([head_b_ref[:, lanes], bc_in[:, lanes].astype(F32)[8:]], 0)
        bt_ref[group] = b_blk.T.astype(BF16)
    for k in range(pieces):
        at = place_of(k + 1, owned)
        lanes = pl.ds(at, owned)
        head = head_of(part_x_ref[k], lanes, [taps_x_ref[j : j + 1, lanes] for j in range(taps_len)], owned)
        xc_ref[k, :8, :] = head
        head_ref[k] = head.astype(F32)
        for part in range(owned // CHUNK):
            here = slice(part * CHUNK, (part + 1) * CHUNK)

            def x_rows(c):
                value = xc_in[k, c * SUB : (c + 1) * SUB, here].astype(F32)
                return jnp.concatenate([head_ref[k, :, here], value[8:]], 0) if c == 0 else value

            def h_put(c, value):
                h_ref[k, c, :, here] = value

            group = at // (channels // (gn // STATE))
            state, decay = state_of(
                at + part * CHUNK, heads, head_dim, bt_ref.at[group], tab_ref, d_ref, x_rows, h_put
            )
            sends[k][:STATE, here] = state
            sends[k][STATE:, here] = decay


def states(tail, part_x, part_b, taps_x, taps_b, age, tab, d, xc, bc):
    pieces, tok, owned = xc.shape
    gn = bc.shape[1]
    shape = jax.ShapeDtypeStruct
    return pl.pallas_call(
        state_kernel,
        out_shape=(
            shape(xc.shape, BF16),
            shape(bc.shape, BF16),
            shape((gn // STATE, STATE, tok), BF16),
            shape((pieces, tok // SUB - 1, STATE, owned), BF16),
        )
        + (shape((STATE + 8, owned), BF16),) * pieces,
        in_specs=[VMEM] * 10,
        out_specs=(VMEM,) * (4 + pieces),
        scratch_shapes=[
            pltpu.VMEM((16, tail.shape[1]), F32),
            pltpu.VMEM((pieces, 8, owned), F32),
            pltpu.VMEM((8, gn), F32),
        ],
        input_output_aliases={8: 0, 9: 1},
        compiler_params=params(16),
        cost_estimate=cost(tok * STATE * owned * pieces * 4, tok * owned * pieces * 4),
        name="state",
    )(tail, part_x, part_b, taps_x, taps_b, age, tab, d, xc, bc)


def own_kernel(
    tail_ref,
    age_ref,
    tab_ref,
    d_ref,
    bt_ref,
    taps_x_ref,
    x_hbm,
    c_hbm,
    taps_c_hbm,
    xc_ref,
    cc_ref,
    h_ref,
    send_ref,
    in_ref,
    taps_c_ref,
    ext_ref,
    mask_ref,
    sem,
):
    tok, channels = x_hbm.shape
    gn = c_hbm.shape[1]
    owned = channels // CLUSTER
    per = owned // CHUNK
    heads = d_ref.shape[1] // 2
    head_dim = channels // heads
    taps_len = taps_x_ref.shape[0]
    at = place_of(0, owned)
    copies = [
        pltpu.make_async_copy(
            x_hbm.at[:, pl.ds(pl.multiple_of(at + part * CHUNK, CHUNK), CHUNK)], in_ref.at[part], sem.at[part]
        )
        for part in range(per)
    ]
    copies.append(pltpu.make_async_copy(c_hbm, in_ref.at[per], sem.at[per]))
    copies.append(pltpu.make_async_copy(taps_c_hbm, taps_c_ref, sem.at[per + 1]))
    start_all(copies)
    fill_masks(age_ref, mask_ref)
    wait_all(copies)
    for part in range(per + 1):
        here = slice(part * CHUNK, (part + 1) * CHUNK)
        if part < per:
            lanes = pl.ds(pl.multiple_of(at + part * CHUNK, CHUNK), CHUNK)
            taps = [taps_x_ref[j : j + 1, lanes] for j in range(taps_len)]
        else:
            lanes = slice(channels + gn, channels + 2 * gn)
            taps = [taps_c_ref[j : j + 1, :] for j in range(taps_len)]
        ext_ref[:8, :] = tail_ref[:, lanes].astype(F32)
        ext_ref[8:, :] = in_ref[part].astype(F32)

        def emit(low, total):
            value = silu(total).astype(BF16)
            if part < per:
                xc_ref[0, low : low + ROWS, here] = value
            else:
                cc_ref[low : low + ROWS, :] = value

        convolve(ext_ref, mask_ref, taps, emit)
        if part < per:

            def h_put(c, value):
                h_ref[0, c, :, here] = value

            group = at // (channels // (gn // STATE))
            state, decay = state_of(
                at + part * CHUNK,
                heads,
                head_dim,
                bt_ref.at[group],
                tab_ref,
                d_ref,
                lambda c: xc_ref[0, c * SUB : (c + 1) * SUB, here].astype(F32),
                h_put,
            )
            send_ref[:STATE, here] = state
            send_ref[STATE:, here] = decay


def own(tail, age, tab, d, bt, taps_x, x, c, taps_c):
    tok, channels = x.shape
    gn = c.shape[1]
    owned = channels // CLUSTER
    places = owned // CHUNK + 1
    shape = jax.ShapeDtypeStruct
    return pl.pallas_call(
        own_kernel,
        out_shape=(
            shape((1, tok, owned), BF16),
            shape((tok, gn), BF16),
            shape((1, tok // SUB - 1, STATE, owned), BF16),
            shape((STATE + 8, owned), BF16),
        ),
        in_specs=[VMEM] * 6 + [HBM] * 3,
        out_specs=(VMEM,) * 4,
        scratch_shapes=[
            pltpu.VMEM((places, tok, CHUNK), BF16),
            pltpu.VMEM(taps_c.shape, F32),
            pltpu.VMEM((tok + 8, CHUNK), F32),
            pltpu.VMEM((taps_c.shape[0] - 1, tok, LANES), F32),
            pltpu.SemaphoreType.DMA((places + 1,)),
        ],
        compiler_params=params(16),
        cost_estimate=cost(tok * owned * 16 + tok * STATE * owned * 4, tok * owned * 8, tok * owned),
        name="own",
    )(tail, age, tab, d, bt, taps_x, x, c, taps_c)


def scan_kernel(*refs):
    pieces = refs[:CLUSTER]
    local_ref, pre_ref, total_ref = refs[CLUSTER:]
    mine = lax.axis_index("seq") % CLUSTER

    def in_order(values):
        bit = 1
        while bit < CLUSTER:
            odd = (mine & bit) != 0
            values = [jnp.where(odd, values[i ^ bit], values[i]) for i in range(CLUSTER)]
            bit *= 2
        return values

    owned = total_ref.shape[1]
    tables = [ref[STATE:, :].astype(F32) for ref in pieces]
    decays = in_order([row[0:1] + (row[1:2] + row[2:3]) for row in tables])
    pre = jnp.ones((1, owned), F32)
    for i in range(CLUSTER):
        pre_ref[i] = jnp.broadcast_to(pre, (8, owned))
        pre = pre * decays[i]
    pre_ref[CLUSTER] = jnp.broadcast_to(pre, (8, owned))
    for at in range(0, owned, LANES):
        lanes = slice(at, at + LANES)
        for low in range(0, STATE, 64):
            rows = slice(low, low + 64)
            values = in_order([ref[rows, lanes].astype(F32) for ref in pieces])
            local_ref[0, rows, lanes] = jnp.zeros((64, LANES), F32)
            state = values[0]
            for i in range(1, CLUSTER):
                local_ref[i, rows, lanes] = state
                state = decays[i][:, lanes] * state + values[i]
            total_ref[rows, lanes] = state.astype(BF16)


def scan_blocks(pieces):
    owned = pieces[0].shape[1]
    return pl.pallas_call(
        scan_kernel,
        out_shape=(
            jax.ShapeDtypeStruct((CLUSTER, STATE, owned), F32),
            jax.ShapeDtypeStruct((CLUSTER + 1, 8, owned), F32),
            jax.ShapeDtypeStruct((STATE, owned), BF16),
        ),
        in_specs=[VMEM] * CLUSTER,
        out_specs=(VMEM,) * 3,
        compiler_params=params(),
        cost_estimate=cost(CLUSTER * STATE * owned * 2, CLUSTER * STATE * owned * 6),
        name="cluster_scan",
    )(*pieces)


def join_kernel(before_ref, local_ref, pre_ref, *outs):
    index = lax.axis_index("seq")
    mine = index % CLUSTER
    before = jnp.where(index >= CLUSTER, before_ref[...].astype(F32), 0.0)
    for k in range(CLUSTER):
        block = mine ^ k
        outs[k][...] = (local_ref[block] + pre_ref[block][0:1] * before).astype(BF16)


def join(before, local, pre):
    owned = local.shape[2]
    return pl.pallas_call(
        join_kernel,
        out_shape=(jax.ShapeDtypeStruct((STATE, owned), BF16),) * CLUSTER,
        in_specs=[VMEM] * 3,
        out_specs=(VMEM,) * CLUSTER,
        compiler_params=params(),
        cost_estimate=cost(CLUSTER * STATE * owned * 2, CLUSTER * STATE * owned * 6),
        name="join",
    )(before, local, pre)


def group_at(turn, groups):
    return (lax.axis_index("seq") % CLUSTER) // (CLUSTER // groups) ^ turn


def intra_kernel(pieces, heads, head_dim, *refs):
    bc_ref, cc_ref, tab_ref, tab0_ref, col_ref, row_ref, age_ref = refs[:7]
    count = len(pieces)
    xs, hs, gates = refs[7 : 7 + count], refs[7 + count : 7 + 2 * count], refs[7 + 2 * count : 7 + 3 * count]
    parts, scales = refs[7 + 3 * count : 7 + 4 * count], refs[7 + 4 * count : 7 + 5 * count]
    hot_ref, hot0_ref = refs[7 + 5 * count :]
    owned = parts[0].shape[1]
    per_piece = owned // head_dim
    mine = lax.axis_index("seq") % CLUSTER

    @pl.when(pl.program_id(0) == 0)
    def _():
        for p, k in enumerate(pieces):
            hot_ref[p] = spread(2 * heads, 4 * heads, (mine ^ k) * per_piece, heads, owned, head_dim)
            hot0_ref[p] = spread(0, 2 * heads, (mine ^ k) * per_piece, heads, owned, head_dim)

    back = lax.broadcasted_iota(jnp.int32, (SUB, SUB), 0) - lax.broadcasted_iota(jnp.int32, (SUB, SUB), 1)
    keep = (back >= 0) & (back <= age_ref[...])
    c_blk = cc_ref[...]
    scores = lax.dot_general(c_blk, bc_ref[...], (((1,), (1,)), ((), ())), preferred_element_type=F32)
    scores = jnp.where(keep, scores, 0.0)
    lane = lax.broadcasted_iota(jnp.int32, (SUB, LANES), 1)
    per_tile = LANES // head_dim
    for p, k in enumerate(pieces):
        first = (mine ^ k) * per_piece
        col = pltpu.roll(col_ref[...], LANES - (2 * heads + first), 1)
        row = row_ref[pl.ds(pl.multiple_of(first, per_piece), per_piece), :]
        for tile in range(owned // LANES):
            lanes = slice(tile * LANES, (tile + 1) * LANES)
            x_tile = xs[p][0, :, lanes].astype(F32)
            left, right = [], []
            for i in range(per_tile):
                head = tile * per_tile + i
                gap = col[:, head : head + 1] + row[head : head + 1, :]
                left.append((jnp.exp2(jnp.minimum(gap, 80.0)) * scores).astype(BF16))
                here = (lane >= i * head_dim) & (lane < (i + 1) * head_dim)
                right.append(jnp.where(here, x_tile, 0.0).astype(BF16))
            inner = mm(jnp.concatenate(left, 1), jnp.concatenate(right, 0))
            inner = inner + mm(c_blk, hs[p][0, 0, :, lanes]) * mm(tab_ref[...], hot_ref[p, :, lanes])
            gate = silu(gates[p][:, lanes].astype(F32))
            parts[p][:, lanes] = inner * gate
            scales[p][:, lanes] = mm(tab0_ref[...], hot0_ref[p, :, lanes]) * gate


def intra(turn, pieces, bc, cc, tab, tab0, col, row, age, xs, hs, gate):
    tok, gn = bc.shape
    heads = row.shape[0]
    channels = gate.shape[1]
    head_dim = channels // heads
    groups = gn // STATE
    owned = channels // CLUSTER
    count = len(pieces)
    out = jax.ShapeDtypeStruct((tok, owned), F32)

    def piece_spec(block, index):
        return [pl.BlockSpec(block, functools.partial(index, k)) for k in pieces]

    return pl.pallas_call(
        functools.partial(intra_kernel, pieces, heads, head_dim),
        out_shape=(out,) * (2 * count),
        grid=(tok // SUB,),
        in_specs=[
            pl.BlockSpec((SUB, STATE), lambda i: (i, group_at(turn, groups))),
            pl.BlockSpec((SUB, STATE), lambda i: (i, group_at(turn, groups))),
            pl.BlockSpec((SUB, tab.shape[1]), lambda i: (i, 0)),
            pl.BlockSpec((SUB, tab0.shape[1]), lambda i: (i, 0)),
            pl.BlockSpec((SUB, LANES), lambda i: (i, 0)),
            pl.BlockSpec((heads, SUB), lambda i: (0, i)),
            pl.BlockSpec((SUB, LANES), lambda i: (i, 0)),
        ]
        + piece_spec((1, SUB, owned), lambda k, i: (max(k - 1, 0), i, 0))
        + piece_spec((1, 1, STATE, owned), lambda k, i: (max(k - 1, 0), jnp.maximum(i - 1, 0), 0, 0))
        + piece_spec((SUB, owned), lambda k, i: (i, lax.axis_index("seq") % CLUSTER ^ k)),
        out_specs=(pl.BlockSpec((SUB, owned), lambda i: (i, 0)),) * (2 * count),
        scratch_shapes=[pltpu.VMEM((count, 4 * heads, owned), BF16), pltpu.VMEM((count, 2 * heads, owned), BF16)],
        compiler_params=params(16),
        cost_estimate=cost(tok * SUB * owned * count * 4, tok * owned * count * 12, tok * SUB * owned * count // head_dim),
        name="intra",
    )(bc, cc, tab, tab0, col, row, age, *xs, *hs, *([gate] * count))


def final_kernel(groups, *refs):
    cc_ref, gain_ref = refs[:2]
    parts, scales, pieces = (refs[2 + i * CLUSTER : 2 + (i + 1) * CLUSTER] for i in range(3))
    out_hbm, y_ref, put_ref, sem = refs[2 + 3 * CLUSTER :]
    tok, owned = parts[0].shape
    share = CLUSTER // groups
    rows = y_ref.shape[1]
    copies = []
    for turn in range(groups):
        group = group_at(turn, groups)
        c_lanes = pl.ds(pl.multiple_of(group * STATE, STATE), STATE)
        for low in range(0, tok, rows):
            span = slice(low, low + rows)
            c_blk = cc_ref[span, c_lanes]
            squares = None
            for i in range(share):
                k = turn * share + i
                for at in range(0, owned, CHUNK):
                    lanes = slice(at, at + CHUNK)
                    value = parts[k][span, lanes] + mm(c_blk, pieces[k][:, lanes]) * scales[k][span, lanes]
                    y_ref[i, :, lanes] = value
                    square = value * value
                    for j in range(0, CHUNK, LANES):
                        piece = square[:, j : j + LANES]
                        squares = piece if squares is None else squares + piece
            factor = lax.rsqrt(jnp.sum(squares, axis=1, keepdims=True) * (1.0 / (share * owned)) + norm_eps)
            for i in range(share):
                k = turn * share + i
                columns = pl.ds(place_of(k, owned), owned)
                put_ref[k, span, :] = (y_ref[i] * factor * gain_ref[:, columns]).astype(BF16)
                copy = pltpu.make_async_copy(
                    put_ref.at[k, span, :], out_hbm.at[span, columns], sem.at[k, low // rows]
                )
                copy.start()
                copies.append(copy)
    wait_all(copies)


def final(cc, gain, parts, scales, pieces):
    tok, owned = parts[0].shape
    groups = cc.shape[1] // STATE
    rows = 64
    return pl.pallas_call(
        functools.partial(final_kernel, groups),
        out_shape=jax.ShapeDtypeStruct((tok, owned * CLUSTER), BF16),
        in_specs=[VMEM] * (2 + 3 * CLUSTER),
        out_specs=ANY,
        scratch_shapes=[
            pltpu.VMEM((CLUSTER // groups, rows, owned), F32),
            pltpu.VMEM((CLUSTER, tok, owned), BF16),
            pltpu.SemaphoreType.DMA((CLUSTER, tok // rows)),
        ],
        compiler_params=params(16),
        cost_estimate=cost(tok * STATE * owned * CLUSTER * 2, tok * owned * CLUSTER * 8),
        name="final",
    )(cc, gain, *parts, *scales, *pieces)


def moved(value, hop):
    count = lax.axis_size("seq")
    return lax.ppermute(value, "seq", [(i, hop(i)) for i in range(count) if 0 <= hop(i) < count])


def exchanged(pieces, order):
    arrived = {0: pieces[0]}
    for k in order:
        arrived[k] = moved(pieces[k], lambda i, k=k: i ^ k)
    return [arrived[k] for k in range(CLUSTER)]


def before_cluster(total, pre):
    clusters = lax.axis_size("seq") // CLUSTER
    if clusters == 1:
        return jnp.zeros_like(total)
    if clusters == 2:
        return moved(total, lambda i: i ^ CLUSTER)
    shift = lambda value, steps: moved(value, lambda i: i + steps * CLUSTER)
    state, decay = shift((total.astype(F32), pre[CLUSTER, 0]), 1)
    step = 1
    while step < clusters - 1:
        earlier, fell = shift((state, decay), step)
        state, decay = state + decay[None, :] * earlier, decay * fell
        step *= 2
    return state


def tied(values, other):
    *values, _ = lax.optimization_barrier((*values, other))
    return values


def on_device(
    x_input,
    b_input,
    c_input,
    dt_input,
    decay_rate,
    gate_input,
    taps_x,
    taps_b,
    taps_c,
    norm_gain,
    doc_lengths,
):
    groups = b_input.shape[1] // STATE
    count = lax.axis_size("seq")
    pin = lambda value: pltpu.with_memory_space_constraint(value, pltpu.HBM)
    x_input, b_input, c_input, doc_lengths = pin(x_input), pin(b_input), pin(c_input), pin(doc_lengths)
    taps_x, taps_b, taps_c = pin(taps_x), pin(taps_b), pin(taps_c)
    ends, tab, tab0, col, row, d, age = prep(
        doc_lengths, pin(dt_input.T), pin(decay_rate[None, :]), x_input, b_input, c_input
    )
    tail = lax.ppermute(ends, "seq", [(i, (i + 1) % count) for i in range(count)])
    taps_x, taps_b, part_x, part_b, xc, bc = conv(age, x_input, b_input, taps_x, taps_b)
    xc, bc, bt, h, *sends = states(tail, part_x, part_b, taps_x, taps_b, age, tab, d, xc, bc)
    own_x, cc, own_h, own_send = own(tail, age, tab, d, bt, taps_x, x_input, c_input, taps_c)
    shared = (bc, cc, tab, tab0, col, row, age)
    share = CLUSTER // groups

    def inner(turn):
        pieces = tuple(range(turn * share, (turn + 1) * share))
        xs, hs = ([mine if k == 0 else other for k in pieces] for mine, other in ((own_x, xc), (own_h, h)))
        return intra(turn, pieces, *shared, xs, hs, gate_input)

    first = inner(0)
    arrived = tied(exchanged([own_send, *sends], (3, 2, 1)), first[0])
    local, pre, total = scan_blocks(arrived)
    later = [inner(turn) for turn in range(1, groups)]
    (before,) = tied([before_cluster(total, pre)], later[-1][0])
    entering = exchanged(join(before, local, pre), (3, 2, 1))
    parts = [part for turn in (first, *later) for part in turn[:share]]
    scales = [part for turn in (first, *later) for part in turn[share:]]
    return final(cc, norm_gain[None, :], parts, scales, entering)


def solution(mesh):
    rows = P(("groups", "seq"), "dp")
    placed = (rows, rows, rows, rows, P("dp"), rows, P(None, "dp"), P(None, "dp"), P(None, "dp"), P("dp"), P("groups"))
    return jax.shard_map(on_device, mesh=mesh, in_specs=placed, out_specs=rows, check_vma=False)
```

time: 40.2 us -> 37.5 us (0.933)
  Pallas kernels: 18.4 us -> 16.8 us
  starting transfers between devices: 12.6 us -> 11.6 us
    ppermute x7, waiting for transfers between devices: 9.01 us -> 7.35 us  [moved(): lax.ppermute(value, 'seq', [(i, hop(i)) for i in range(count) if 0 <= hop...]
    pallas_call x6, Pallas kernels: 16.6 us -> 15 us  [the longest x2 5.64 us: intra(): pl.pallas_call(functools.partial(intra_kernel, pieces, heads, head_dim),...]
    ppermute x1, waiting for transfers between devices: 0.01 us -> 1.42 us  [on_device(): lax.ppermute(ends, 'seq', [(i, (i + 1) % count) for i in range(count)])]
    ppermute x7, starting transfers between devices: 9.56 us -> 8.63 us  [moved(): lax.ppermute(value, 'seq', [(i, hop(i)) for i in range(count) if 0 <= hop...]
where the time goes in v4:
time: 37.5 us; the launch traced here: 37.3 us
  Pallas kernels  16.8 us (45%)
  starting transfers between devices  11.6 us (31%)
  waiting for transfers between devices  8.78 us (23%)
    ppermute x7, starting transfers between devices, moved(): lax.ppermute(value, 'seq', [(i, hop(i)) for i in range(count) if 0 <= hop...  8.63 us
    ppermute x7, waiting for transfers between devices, moved(): lax.ppermute(value, 'seq', [(i, hop(i)) for i in range(count) if 0 <= hop...  7.35 us
    pallas_call x2, Pallas kernels, intra(): pl.pallas_call(functools.partial(intra_kernel, pieces, heads, head_dim),...  5.64 us
    pallas_call x1, Pallas kernels, conv(): pl.pallas_call(conv_kernel, out_shape=(shape(taps_x.shape, F32), shape(ta...  3.59 us
    ppermute x1, starting transfers between devices, on_device(): lax.ppermute(ends, 'seq', [(i, (i + 1) % count) for i in range(count)])  2.99 us
    pallas_call x1, Pallas kernels, own(): pl.pallas_call(own_kernel, out_shape=(shape((1, tok, owned), BF16), shape...  2.61 us
    pallas_call x1, Pallas kernels, final(): pl.pallas_call(functools.partial(final_kernel, groups), out_shape=jax.Sha...  1.92 us
    pallas_call x1, Pallas kernels, prep(): pl.pallas_call(prep_kernel, out_shape=(shape((8, x.shape[1] + b.shape[1]...  1.43 us
  transfers between devices with their start and end apart: 8, of which 5 were waited for; matrix products, arithmetic and copies ran while one was open for 0% of the time, Pallas kernels for 32%

profile of v4, /device:TPU:0, one launch (start us, length us, event | category | flops | bytes accessed | tf_op | source)
XLA Modules:
  0.0 37.3 jit_solution(10487189734562562935)
XLA Ops:
  0.0 1.4 %prep.1 = (bf16[8,2560]{1,0:T(8,128)(2,1)S(1)}, bf16[384,128]{1,0:T(8,128)(2,1)S(1)}, bf16[384,64]{1,0:T(8,128)(2,1)S(1)}, f32[384,128]{1,0:T(8,128)S(1)}, f32[3...) custom-call(s32[4]{0:T(128)} %dl_hbm.1, f32[32,384]{1,0:T(8,128)} %bitcast.4, ...), custom_call_target="tpu_custom_call" | custom-call | tf_op jit(solution)/shard_map/prep/pallas_call | solution.py:171
  1.4 3.0 %collective-permute-start = (bf16[8,2560]{1,0:T(8,128)(2,1)S(1)}, bf16[8,2560]{1,0:T(8,128)(2,1)S(1)}, u32[]{:S(2)}, u32[]{:S(2)}) collective-permute-start(bf16[8,2560]{1,0:T(8,128)(2,1)S(1)} %get-tuple-element.49), channel_id=1, source_target_pairs={{0,2},{2,4},{4,6},{6,8},{8,10},{10,12},{12,14},{14,0},{1,3},{3,5},... | collective-permute-start | bytes 122888 | tf_op jit(solution)/shard_map/ppermute | solution.py:805
  4.4 3.6 %conv.1 = (f32[4,2048]{1,0:T(4,128)S(1)}, f32[4,256]{1,0:T(4,128)S(1)}, f32[3,8,512]{2,1,0:T(8,128)S(1)}, f32[8,256]{1,0:T(8,128)S(1)}, bf16[3,384,512]{2,1,0:T(8,128)(2,1)S(1)}, /*index=5*/bf16[384,256]{1,0:T(8,128)(2,1)S(1)}) custom-call(s32[384,128]{1,0:T(8,128)S(1)} %get-tuple-element.50.age_ref.refs_6_, bf16[384,2048]{1,0:T(8,128)(2,1)} %x_hbm.5, ...), custom_call_target="tpu_custom_call" | custom-call | flops 12582912 | bytes 3145728 | tf_op jit(solution)/shard_map/conv/pallas_call | solution.py:308
  8.0 1.4 %collective-permute-done.tail_ref = bf16[8,2560]{1,0:T(8,128)(2,1)S(1)} collective-permute-done((bf16[8,2560]{1,0:T(8,128)(2,1)S(1)}, bf16[8,2560]{1,0:T(8,128)(2,1)S(1)}, u32[]{:S(2)}, u32[]{:S(2)}) %collective-permute-start) | collective-permute-done | bytes 40992 | tf_op jit(solution)/shard_map/ppermute | solution.py:805
  9.4 1.3 %state.1 = (bf16[3,384,512]{2,1,0:T(8,128)(2,1)S(1)}, bf16[384,256]{1,0:T(8,128)(2,1)S(1)}, bf16[2,128,384]{2,1,0:T(8,128)(2,1)S(1)}, bf16[3,2,128,512]{3,2,1,0:...) custom-call(bf16[8,2560]{1,0:T(8,128)(2,1)S(1)} %collective-permute-, ...), custom_call_target="tpu_custom_call", output_to_operand_aliasing={{0}: (8, {}), {1}: (9, {})} | custom-call | flops 301989888 | bytes 2359296 | tf_op jit(solution)/shard_map/state/pallas_call | solution.py:405
  10.7 0.0 copy-start
  10.7 0.2 collective-permute-start.1
  10.9 1.6 %collective-permute-start.2 = (bf16[136,512]{1,0:T(8,128)(2,1)S(1)}, bf16[136,512]{1,0:T(8,128)(2,1)S(1)}, u32[]{:S(2)}, u32[]{:S(2)}) collective-permute-start(bf16[136,512]{1,0:T(8,128)(2,1)S(1)} %get-tuple-element.79), channel_id=1, source_target_pairs={{0,4},{2,6},{4,0},{6,2},{8,12},{10,14},{12,8},{14,10},{1,5},{3,7},... | collective-permute-start | bytes 417800 | tf_op jit(solution)/shard_map/ppermute | solution.py:753
  12.5 1.8 %collective-permute-start.3 = (bf16[136,512]{1,0:T(8,128)(2,1)S(1)}, bf16[136,512]{1,0:T(8,128)(2,1)S(1)}, u32[]{:S(2)}, u32[]{:S(2)}) collective-permute-start(bf16[136,512]{1,0:T(8,128)(2,1)S(1)} %get-tuple-element.80), channel_id=1, source_target_pairs={{0,6},{2,4},{4,2},{6,0},{8,14},{10,12},{12,10},{14,8},{1,7},{3,5},... | collective-permute-start | bytes 417800 | tf_op jit(solution)/shard_map/ppermute | solution.py:753
  14.3 2.6 %own.1 = (bf16[1,384,512]{2,1,0:T(8,128)(2,1)S(1)}, bf16[384,256]{1,0:T(8,128)(2,1)S(1)}, bf16[1,2,128,512]{3,2,1,0:T(8,128)(2,1)S(1)}, bf16[136,512]{1,0:T(8,128)(2,1)S(1)}) custom-call(bf16[8,2560]{1,0:T(8,128)(2,1)S(1)} %collective-permute-done.tail_ref, s32[384,128]{1,0:T(8,128)S(1)} %get-tuple-element.50.age_ref.refs_6_, ...), custom_call_target="tpu_custom_call" | custom-call | flops 103809024 | bytes 1572864 | tf_op jit(solution)/shard_map/own/pallas_call | solution.py:512
  16.9 0.0 copy-done
  16.9 2.9 %intra.2 = (f32[384,512]{1,0:T(8,128)S(1)}, f32[384,512]{1,0:T(8,128)S(1)}, f32[384,512]{1,0:T(8,128)S(1)}, f32[384,512]{1,0:T(8,128)S(1)}) custom-call(bf16[384,256]{1,0:T(8,128)(2,1)S(1)} %get-tuple-element.61.refs_0_, bf16[384,256]{1,0:T(8,128)(2,1)S(1)} %get-tuple-element.60.refs_1_.refs_0_, bf16[384,128]{1,0:T(8,128)(2,1)S(1)} %get-tuple-element.51.tab_ref.refs_2_, ...), custom_call_target="tpu_custom_call" | custom-call | flops 201326592 | bytes 4718592 | tf_op jit(solution)/shard_map/intra/pallas_call | solution.py:669
  19.8 0.0 collective-permute-done.1.refs_1_
  19.8 0.0 collective-permute-done.2.refs_2_
  19.8 0.0 collective-permute-done.3.refs_3_
  19.8 0.2 cluster_scan.1
  20.0 0.0 copy-start.1
  20.0 1.5 %collective-permute-start.4 = (bf16[128,512]{1,0:T(8,128)(2,1)S(1)}, bf16[128,512]{1,0:T(8,128)(2,1)S(1)}, u32[]{:S(2)}, u32[]{:S(2)}) collective-permute-start(bf16[128,512]{1,0:T(8,128)(2,1)S(1)} %get-tuple-element.85), channel_id=1, source_target_pairs={{0,8},{2,10},{4,12},{6,14},{8,0},{10,2},{12,4},{14,6},{1,9},{3,11}... | collective-permute-start | bytes 393224 | tf_op jit(solution)/shard_map/ppermute | solution.py:753
  21.6 2.8 %intra.3 = (f32[384,512]{1,0:T(8,128)S(1)}, f32[384,512]{1,0:T(8,128)S(1)}, f32[384,512]{1,0:T(8,128)S(1)}, f32[384,512]{1,0:T(8,128)S(1)}) custom-call(bf16[384,256]{1,0:T(8,128)(2,1)S(1)} %get-tuple-element.61.refs_0_, bf16[384,256]{1,0:T(8,128)(2,1)S(1)} %get-tuple-element.60.refs_1_.refs_0_, bf16[384,128]{1,0:T(8,128)(2,1)S(1)} %get-tuple-element.51.tab_ref.refs_2_, ...), custom_call_target="tpu_custom_call" | custom-call | flops 201326592 | bytes 4718592 | tf_op jit(solution)/shard_map/intra/pallas_call | solution.py:669
  24.3 3.0 %collective-permute-done.4.before_ref = bf16[128,512]{1,0:T(8,128)(2,1)S(1)} collective-permute-done((bf16[128,512]{1,0:T(8,128)(2,1)S(1)}, bf16[128,512]{1,0:T(8,128)(2,1)S(1)}, u32[]{:S(2)}, u32[]{:S(2)}) %collective-permute-start.4) | collective-permute-done | bytes 131104 | tf_op jit(solution)/shard_map/ppermute | solution.py:753
  27.3 0.1 join.1
  27.5 0.8 %collective-permute-start.5 = (bf16[128,512]{1,0:T(8,128)(2,1)S(1)}, bf16[128,512]{1,0:T(8,128)(2,1)S(1)}, u32[]{:S(2)}, u32[]{:S(2)}) collective-permute-start(bf16[128,512]{1,0:T(8,128)(2,1)S(1)} %get-tuple-element.90), channel_id=1, source_target_pairs={{0,2},{2,0},{4,6},{6,4},{8,10},{10,8},{12,14},{14,12},{1,3},{3,1},... | collective-permute-start | bytes 393224 | tf_op jit(solution)/shard_map/ppermute | solution.py:753
  28.2 0.0 collective-permute-start.6
  28.3 2.8 %collective-permute-start.7 = (bf16[128,512]{1,0:T(8,128)(2,1)S(1)}, bf16[128,512]{1,0:T(8,128)(2,1)S(1)}, u32[]{:S(2)}, u32[]{:S(2)}) collective-permute-start(bf16[128,512]{1,0:T(8,128)(2,1)S(1)} %get-tuple-element.92), channel_id=1, source_target_pairs={{0,6},{2,4},{4,2},{6,0},{8,14},{10,12},{12,10},{14,8},{1,7},{3,5},... | collective-permute-start | bytes 393224 | tf_op jit(solution)/shard_map/ppermute | solution.py:753
  31.0 1.5 %collective-permute-done.5.refs_11_ = bf16[128,512]{1,0:T(8,128)(2,1)S(1)} collective-permute-done((bf16[128,512]{1,0:T(8,128)(2,1)S(1)}, bf16[128,512]{1,0:T(8,128)(2,1)S(1)}, u32[]{:S(2)}, u32[]{:S(2)}) %collective-permute-start.5) | collective-permute-done | bytes 131104 | tf_op jit(solution)/shard_map/ppermute | solution.py:753
  32.5 0.7 %collective-permute-done.6.refs_12_ = bf16[128,512]{1,0:T(8,128)(2,1)S(1)} collective-permute-done((bf16[128,512]{1,0:T(8,128)(2,1)S(1)}, bf16[128,512]{1,0:T(8,128)(2,1)S(1)}, u32[]{:S(2)}, u32[]{:S(2)}) %collective-permute-start.6) | collective-permute-done | bytes 131104 | tf_op jit(solution)/shard_map/ppermute | solution.py:753
  33.2 2.1 %collective-permute-done.7.refs_13_ = bf16[128,512]{1,0:T(8,128)(2,1)S(1)} collective-permute-done((bf16[128,512]{1,0:T(8,128)(2,1)S(1)}, bf16[128,512]{1,0:T(8,128)(2,1)S(1)}, u32[]{:S(2)}, u32[]{:S(2)}) %collective-permute-start.7) | collective-permute-done | bytes 131104 | tf_op jit(solution)/shard_map/ppermute | solution.py:753
  35.4 0.0 copy-done.1
  35.4 1.9 %final.1 = bf16[384,2048]{1,0:T(8,128)(2,1)} custom-call(bf16[384,256]{1,0:T(8,128)(2,1)S(1)} %get-tuple-element.60.refs_1_.refs_0_, f32[1,2048]{1,0:T(1,128)S(1)} %bitcast.3, f32[384,512]{1,0:T(8,128)S(1)} %get-tuple-element.69.refs_2_, f32[384,512]{1,0:T(8,128)S(1)} %get-tuple-element.70.refs_3_, f32[384,512]{1,0:T(8,128)S(1)} %get-tuple-element.71.refs_4_, ...), custom_call_target="tpu_custom_call" | custom-call | flops 201326592 | bytes 6291456 | tf_op jit(solution)/shard_map/final/pallas_call | solution.py:735
Async XLA Ops:
  1.4 8.0 %collective-permute-start = (bf16[8,2560]{1,0:T(8,128)(2,1)S(1)}, bf16[8,2560]{1,0:T(8,128)(2,1)S(1)}, u32[]{:S(2)}, u32[]{:S(2)}) collective-permute-start(bf16[8,2560]{1,0:T(8,128)(2,1)S(1)} %get-tuple-element.49), channel_id=1, source_target_pairs={{0,2},{2,4},{4,6},{6,8},{8,10},{10,12},{12,14},{14,0},{1,3},{3,5},... | collective-permute-start | bytes 122888 | tf_op jit(solution)/shard_map/ppermute | solution.py:805
  10.7 6.2 %copy-start = (bf16[384,2048]{1,0:T(8,128)(2,1)S(1)}, bf16[384,2048]{1,0:T(8,128)(2,1)}, u32[]{:S(2)}) copy-start(bf16[384,2048]{1,0:T(8,128)(2,1)} %refs_12_.3) | copy-start | bytes 4718596
  10.7 9.1 %collective-permute-start.1 = (bf16[136,512]{1,0:T(8,128)(2,1)S(1)}, bf16[136,512]{1,0:T(8,128)(2,1)S(1)}, u32[]{:S(2)}, u32[]{:S(2)}) collective-permute-start(bf16[136,512]{1,0:T(8,128)(2,1)S(1)} %get-tuple-element.78), channel_id=1, source_target_pairs={{0,2},{2,0},{4,6},{6,4},{8,10},{10,8},{12,14},{14,12},{1,3},{3,1},... | collective-permute-start | bytes 417800 | tf_op jit(solution)/shard_map/ppermute | solution.py:753
  10.9 8.9 %collective-permute-start.2 = (bf16[136,512]{1,0:T(8,128)(2,1)S(1)}, bf16[136,512]{1,0:T(8,128)(2,1)S(1)}, u32[]{:S(2)}, u32[]{:S(2)}) collective-permute-start(bf16[136,512]{1,0:T(8,128)(2,1)S(1)} %get-tuple-element.79), channel_id=1, source_target_pairs={{0,4},{2,6},{4,0},{6,2},{8,12},{10,14},{12,8},{14,10},{1,5},{3,7},... | collective-permute-start | bytes 417800 | tf_op jit(solution)/shard_map/ppermute | solution.py:753
  12.5 7.3 %collective-permute-start.3 = (bf16[136,512]{1,0:T(8,128)(2,1)S(1)}, bf16[136,512]{1,0:T(8,128)(2,1)S(1)}, u32[]{:S(2)}, u32[]{:S(2)}) collective-permute-start(bf16[136,512]{1,0:T(8,128)(2,1)S(1)} %get-tuple-element.80), channel_id=1, source_target_pairs={{0,6},{2,4},{4,2},{6,0},{8,14},{10,12},{12,10},{14,8},{1,7},{3,5},... | collective-permute-start | bytes 417800 | tf_op jit(solution)/shard_map/ppermute | solution.py:753
  20.0 15.3 %copy-start.1 = (f32[2048]{0:T(1024)S(1)}, f32[2048]{0:T(1024)}, u32[]{:S(2)}) copy-start(f32[2048]{0:T(1024)} %param.20) | copy-start | bytes 24580
  20.0 7.3 %collective-permute-start.4 = (bf16[128,512]{1,0:T(8,128)(2,1)S(1)}, bf16[128,512]{1,0:T(8,128)(2,1)S(1)}, u32[]{:S(2)}, u32[]{:S(2)}) collective-permute-start(bf16[128,512]{1,0:T(8,128)(2,1)S(1)} %get-tuple-element.85), channel_id=1, source_target_pairs={{0,8},{2,10},{4,12},{6,14},{8,0},{10,2},{12,4},{14,6},{1,9},{3,11}... | collective-permute-start | bytes 393224 | tf_op jit(solution)/shard_map/ppermute | solution.py:753
  27.5 5.1 %collective-permute-start.5 = (bf16[128,512]{1,0:T(8,128)(2,1)S(1)}, bf16[128,512]{1,0:T(8,128)(2,1)S(1)}, u32[]{:S(2)}, u32[]{:S(2)}) collective-permute-start(bf16[128,512]{1,0:T(8,128)(2,1)S(1)} %get-tuple-element.90), channel_id=1, source_target_pairs={{0,2},{2,0},{4,6},{6,4},{8,10},{10,8},{12,14},{14,12},{1,3},{3,1},... | collective-permute-start | bytes 393224 | tf_op jit(solution)/shard_map/ppermute | solution.py:753
  28.2 5.0 %collective-permute-start.6 = (bf16[128,512]{1,0:T(8,128)(2,1)S(1)}, bf16[128,512]{1,0:T(8,128)(2,1)S(1)}, u32[]{:S(2)}, u32[]{:S(2)}) collective-permute-start(bf16[128,512]{1,0:T(8,128)(2,1)S(1)} %get-tuple-element.91), channel_id=1, source_target_pairs={{0,4},{2,6},{4,0},{6,2},{8,12},{10,14},{12,8},{14,10},{1,5},{3,7},... | collective-permute-start | bytes 393224 | tf_op jit(solution)/shard_map/ppermute | solution.py:753
  28.3 7.1 %collective-permute-start.7 = (bf16[128,512]{1,0:T(8,128)(2,1)S(1)}, bf16[128,512]{1,0:T(8,128)(2,1)S(1)}, u32[]{:S(2)}, u32[]{:S(2)}) collective-permute-start(bf16[128,512]{1,0:T(8,128)(2,1)S(1)} %get-tuple-element.92), channel_id=1, source_target_pairs={{0,6},{2,4},{4,2},{6,0},{8,14},{10,12},{12,10},{14,8},{1,7},{3,5},... | collective-permute-start | bytes 393224 | tf_op jit(solution)/shard_map/ppermute | solution.py:753

commit v5 on v4

--- a/solution.py
+++ b/solution.py
@@ -13,6 +13,7 @@
 LANES = 128
 ROWS = 32
 CLUSTER = 4
+EARLY = 2
 LOG2E = 1.4426950408889634
 norm_eps = 1e-05
 
@@ -123,73 +124,22 @@
     d_ref[...] = jnp.concatenate(halves, 1).astype(BF16)
 
 
-def prep_kernel(
-    dl_hbm,
-    dt_hbm,
-    rate_hbm,
-    x_hbm,
-    b_hbm,
-    c_hbm,
-    ends_ref,
-    tab_ref,
-    tab0_ref,
-    col_ref,
-    row_ref,
-    d_ref,
-    age_ref,
-    dl_ref,
-    dt_ref,
-    rate_ref,
-    sem,
-):
-    tok = x_hbm.shape[0]
-    small = [
-        pltpu.make_async_copy(hbm, ref, sem.at[i])
-        for i, (hbm, ref) in enumerate(((dl_hbm, dl_ref), (dt_hbm, dt_ref), (rate_hbm, rate_ref)))
-    ]
-    start_all(small)
-    ends, low = [], 0
-    for i, ref in enumerate((x_hbm, b_hbm, c_hbm)):
-        width = ref.shape[1]
-        ends.append(
-            pltpu.make_async_copy(ref.at[pl.ds(tok - 8, 8), :], ends_ref.at[:, pl.ds(low, width)], sem.at[3 + i])
-        )
-        low += width
-    start_all(ends)
-    wait_all(small)
-    row0 = lax.axis_index("seq") * tok
-    edges = doc_edges(dl_ref)
-    tables(row0, edges, dt_ref, rate_ref, tab_ref, tab0_ref, col_ref, row_ref, d_ref)
-    token = row0 + lax.broadcasted_iota(jnp.int32, (tok, LANES), 0)
-    age_ref[...] = token - doc_start(token, edges)
-    wait_all(ends)
-
-
-def prep(doc_lengths, dt_t, rate, x, b, c):
-    heads, tok = dt_t.shape
-    shape = jax.ShapeDtypeStruct
-    return pl.pallas_call(
-        prep_kernel,
-        out_shape=(
-            shape((8, x.shape[1] + b.shape[1] + c.shape[1]), BF16),
-            shape((tok, LANES), BF16),
-            shape((tok, 2 * heads), BF16),
-            shape((tok, LANES), F32),
-            shape((heads, tok), F32),
-            shape((8, 2 * heads), BF16),
-            shape((tok, LANES), jnp.int32),
-        ),
-        in_specs=[HBM] * 6,
-        out_specs=(VMEM,) * 7,
-        scratch_shapes=[
-            pltpu.SMEM(doc_lengths.shape, jnp.int32),
-            pltpu.VMEM((heads, tok), F32),
-            pltpu.VMEM((1, heads), F32),
-            pltpu.SemaphoreType.DMA((6,)),
-        ],
+def pack_kernel(x_ref, b_ref, c_ref, out_ref):
+    out_ref[...] = jnp.concatenate([x_ref[...], b_ref[...], c_ref[...]], 1)
+
+
+def pack(x, b, c):
+    tiles = x.shape[0] // 8
+    widths = [value.shape[1] for value in (x, b, c)]
+    return pl.pallas_call(
+        pack_kernel,
+        out_shape=jax.ShapeDtypeStruct((8, sum(widths)), BF16),
+        grid=(1,),
+        in_specs=[pl.BlockSpec((8, width), lambda i: (tiles - 1, 0)) for width in widths],
+        out_specs=pl.BlockSpec((8, sum(widths)), lambda i: (0, 0)),
         compiler_params=params(16),
-        name="prep",
-    )(doc_lengths, dt_t, rate, x, b, c)
+        name="pack",
+    )(x, b, c)
 
 
 def place_of(k, owned):
@@ -221,40 +171,56 @@
     for c in range(tok // SUB):
         rows = slice(c * SUB, (c + 1) * SUB)
         weight = mm(tab_ref[rows, : 2 * heads], one_hot)
+        if c == 0:
+            head_weight = weight[:8]
         local = mm(bt_ref[:, rows], (x_rows(c) * weight).astype(BF16))
         if state is None:
             state = local
         else:
-            h_put(c - 1, state.astype(BF16))
+            h_put(c - 1, state)
             state = local + decay[2 + c : 3 + c, :] * state
-    return state.astype(BF16), decay.astype(BF16)
+    return state, decay, head_weight
 
 
 def conv_kernel(
-    age_ref,
+    dl_hbm,
+    dt_hbm,
+    rate_hbm,
     x_hbm,
     b_hbm,
     taps_x_hbm,
     taps_b_hbm,
+    tab_ref,
+    tab0_ref,
+    col_ref,
+    row_ref,
+    d_ref,
+    age_ref,
     taps_x_ref,
     taps_b_ref,
     part_x_ref,
     part_b_ref,
     xc_ref,
     bc_ref,
+    dl_ref,
+    dt_ref,
+    rate_ref,
     in_ref,
     ext_ref,
     mask_ref,
     sem,
     in_sem,
 ):
-    channels = x_hbm.shape[1]
+    tok, channels = x_hbm.shape
     owned = channels // CLUSTER
     per = owned // CHUNK
-    chunks = (CLUSTER - 1) * per
+    chunks = EARLY * per
     small = [
-        pltpu.make_async_copy(taps_x_hbm, taps_x_ref, sem.at[0]),
-        pltpu.make_async_copy(taps_b_hbm, taps_b_ref, sem.at[1]),
+        pltpu.make_async_copy(dl_hbm, dl_ref, sem.at[0]),
+        pltpu.make_async_copy(dt_hbm, dt_ref, sem.at[1]),
+        pltpu.make_async_copy(rate_hbm, rate_ref, sem.at[2]),
+        pltpu.make_async_copy(taps_x_hbm, taps_x_ref, sem.at[3]),
+        pltpu.make_async_copy(taps_b_hbm, taps_b_ref, sem.at[4]),
     ]
     start_all(small)
 
@@ -268,9 +234,14 @@
         fetch(i).start()
     fetch_b = pltpu.make_async_copy(b_hbm, in_ref.at[chunks], in_sem.at[chunks])
     fetch_b.start()
-    fill_masks(age_ref, mask_ref)
     ext_ref[:8, :] = jnp.zeros((8, CHUNK), F32)
     wait_all(small)
+    row0 = lax.axis_index("seq") * tok
+    edges = doc_edges(dl_ref)
+    tables(row0, edges, dt_ref, rate_ref, tab_ref, tab0_ref, col_ref, row_ref, d_ref)
+    token = row0 + lax.broadcasted_iota(jnp.int32, (tok, LANES), 0)
+    age_ref[...] = token - doc_start(token, edges)
+    fill_masks(age_ref, mask_ref)
     taps_len = taps_x_ref.shape[0]
 
     def body(i, carry):
@@ -299,61 +270,122 @@
     convolve(ext_ref, mask_ref, [taps_b_ref[j : j + 1, :] for j in range(taps_len)], emit_b)
 
 
-def conv(age, x, b, taps_x, taps_b):
+def conv(doc_lengths, dt_t, rate, x, b, taps_x, taps_b):
+    heads = dt_t.shape[0]
     tok, channels = x.shape
     gn = b.shape[1]
     owned = channels // CLUSTER
-    places = (CLUSTER - 1) * (owned // CHUNK) + 1
+    places = EARLY * (owned // CHUNK) + 1
     shape = jax.ShapeDtypeStruct
     return pl.pallas_call(
         conv_kernel,
         out_shape=(
+            shape((tok, LANES), BF16),
+            shape((tok, 2 * heads), BF16),
+            shape((tok, LANES), F32),
+            shape((heads, tok), F32),
+            shape((8, 2 * heads), BF16),
+            shape((tok, LANES), jnp.int32),
             shape(taps_x.shape, F32),
             shape(taps_b.shape, F32),
-            shape((CLUSTER - 1, 8, owned), F32),
+            shape((EARLY, 8, owned), F32),
             shape((8, gn), F32),
-            shape((CLUSTER - 1, tok, owned), BF16),
+            shape((EARLY, tok, owned), BF16),
             shape((tok, gn), BF16),
         ),
-        in_specs=[VMEM] + [HBM] * 4,
-        out_specs=(VMEM,) * 6,
+        in_specs=[HBM] * 7,
+        out_specs=(VMEM,) * 12,
         scratch_shapes=[
+            pltpu.SMEM(doc_lengths.shape, jnp.int32),
+            pltpu.VMEM((heads, tok), F32),
+            pltpu.VMEM((1, heads), F32),
             pltpu.VMEM((places, tok, CHUNK), BF16),
             pltpu.VMEM((tok + 8, CHUNK), F32),
             pltpu.VMEM((taps_x.shape[0] - 1, tok, LANES), F32),
-            pltpu.SemaphoreType.DMA((2,)),
+            pltpu.SemaphoreType.DMA((5,)),
             pltpu.SemaphoreType.DMA((places,)),
         ],
         compiler_params=params(16),
         cost_estimate=cost(tok * channels * 16, tok * channels * 4, tok * channels),
         name="conv",
-    )(age, x, b, taps_x, taps_b)
-
-
-def state_kernel(
+    )(doc_lengths, dt_t, rate, x, b, taps_x, taps_b)
+
+
+def state_kernel(tab_ref, d_ref, xc_ref, bc_ref, s_ref, h_ref, decay_ref, weight_ref, bt_ref):
+    pieces, tok, owned = xc_ref.shape
+    gn = bc_ref.shape[1]
+    channels = owned * CLUSTER
+    heads = d_ref.shape[1] // 2
+    for group in range(gn // STATE):
+        b_blk = bc_ref[:, group * STATE : (group + 1) * STATE].astype(F32)[8:]
+        bt_ref[group] = jnp.concatenate([jnp.zeros((8, STATE), F32), b_blk], 0).T.astype(BF16)
+    for k in range(pieces):
+        at = place_of(k + 1, owned)
+        group = at // (channels // (gn // STATE))
+        for part in range(owned // CHUNK):
+            here = slice(part * CHUNK, (part + 1) * CHUNK)
+
+            def h_put(c, value):
+                h_ref[k, c, :, here] = value
+
+            state, decay, weight = state_of(
+                at + part * CHUNK,
+                heads,
+                channels // heads,
+                bt_ref.at[group],
+                tab_ref,
+                d_ref,
+                lambda c: xc_ref[k, c * SUB : (c + 1) * SUB, here].astype(F32),
+                h_put,
+            )
+            s_ref[k, :, here] = state
+            decay_ref[k, :, here] = decay
+            weight_ref[k, :, here] = weight
+
+
+def states(tab, d, xc, bc):
+    pieces, tok, owned = xc.shape
+    gn = bc.shape[1]
+    row = jax.ShapeDtypeStruct((pieces, 8, owned), F32)
+    return pl.pallas_call(
+        state_kernel,
+        out_shape=(
+            jax.ShapeDtypeStruct((pieces, STATE, owned), F32),
+            jax.ShapeDtypeStruct((pieces, tok // SUB - 1, STATE, owned), F32),
+            row,
+            row,
+        ),
+        in_specs=[VMEM] * 4,
+        out_specs=(VMEM,) * 4,
+        scratch_shapes=[pltpu.VMEM((gn // STATE, STATE, tok), BF16)],
+        compiler_params=params(16),
+        cost_estimate=cost(tok * STATE * owned * pieces * 4, tok * owned * pieces * 4),
+        name="state",
+    )(tab, d, xc, bc)
+
+
+def head_kernel(
     tail_ref,
     part_x_ref,
     part_b_ref,
     taps_x_ref,
     taps_b_ref,
     age_ref,
-    tab_ref,
-    d_ref,
+    s_ref,
+    decay_ref,
+    weight_ref,
     xc_in,
     bc_in,
     xc_ref,
     bc_ref,
-    bt_ref,
-    h_ref,
+    extra_ref,
     *rest,
 ):
-    sends = rest[: CLUSTER - 1]
-    ext_ref, head_ref, head_b_ref = rest[CLUSTER - 1 :]
-    pieces, tok, owned = xc_in.shape
+    pieces, _, owned = s_ref.shape
+    sends = rest[:pieces]
+    ext_ref, bt_ref, xw_ref = rest[pieces:]
     gn = bc_in.shape[1]
     channels = owned * CLUSTER
-    heads = d_ref.shape[1] // 2
-    head_dim = channels // heads
     taps_len = taps_x_ref.shape[0]
     ext_ref[:8, :] = tail_ref[...].astype(F32)
     ext_ref[8:, :] = jnp.zeros_like(ext_ref[8:, :])
@@ -369,102 +401,75 @@
         part_b_ref[...], slice(channels, channels + gn), [taps_b_ref[j : j + 1, :] for j in range(taps_len)], gn
     )
     bc_ref[:8, :] = head
-    head_b_ref[...] = head.astype(F32)
     for group in range(gn // STATE):
-        lanes = slice(group * STATE, (group + 1) * STATE)
-        b_blk = jnp.concatenate([head_b_ref[:, lanes], bc_in[:, lanes].astype(F32)[8:]], 0)
-        bt_ref[group] = b_blk.T.astype(BF16)
+        rows = head[:, group * STATE : (group + 1) * STATE].astype(F32)
+        bt_ref[group] = jnp.concatenate([rows, jnp.zeros((LANES - 8, STATE), F32)], 0).T.astype(BF16)
+    xw_ref[...] = jnp.zeros_like(xw_ref)
     for k in range(pieces):
         at = place_of(k + 1, owned)
         lanes = pl.ds(at, owned)
         head = head_of(part_x_ref[k], lanes, [taps_x_ref[j : j + 1, lanes] for j in range(taps_len)], owned)
         xc_ref[k, :8, :] = head
-        head_ref[k] = head.astype(F32)
-        for part in range(owned // CHUNK):
-            here = slice(part * CHUNK, (part + 1) * CHUNK)
-
-            def x_rows(c):
-                value = xc_in[k, c * SUB : (c + 1) * SUB, here].astype(F32)
-                return jnp.concatenate([head_ref[k, :, here], value[8:]], 0) if c == 0 else value
-
-            def h_put(c, value):
-                h_ref[k, c, :, here] = value
-
-            group = at // (channels // (gn // STATE))
-            state, decay = state_of(
-                at + part * CHUNK, heads, head_dim, bt_ref.at[group], tab_ref, d_ref, x_rows, h_put
-            )
-            sends[k][:STATE, here] = state
-            sends[k][STATE:, here] = decay
-
-
-def states(tail, part_x, part_b, taps_x, taps_b, age, tab, d, xc, bc):
-    pieces, tok, owned = xc.shape
+        xw_ref[:8, :] = head.astype(F32) * weight_ref[k]
+        extra = mm(bt_ref[at // (channels // (gn // STATE))], xw_ref[...].astype(BF16))
+        extra_ref[k] = extra
+        decay = decay_ref[k]
+        rest_of_block = decay[3:4, :]
+        for c in range(4, 3 + xc_in.shape[1] // SUB - 1):
+            rest_of_block = rest_of_block * decay[c : c + 1, :]
+        sends[k][:STATE, :] = (s_ref[k] + rest_of_block * extra).astype(BF16)
+        sends[k][STATE:, :] = decay.astype(BF16)
+
+
+def with_head(tail, part_x, part_b, taps_x, taps_b, age, state, decay, weight, xc, bc):
+    pieces, _, owned = xc.shape
     gn = bc.shape[1]
     shape = jax.ShapeDtypeStruct
     return pl.pallas_call(
-        state_kernel,
-        out_shape=(
-            shape(xc.shape, BF16),
-            shape(bc.shape, BF16),
-            shape((gn // STATE, STATE, tok), BF16),
-            shape((pieces, tok // SUB - 1, STATE, owned), BF16),
-        )
+        head_kernel,
+        out_shape=(shape(xc.shape, BF16), shape(bc.shape, BF16), shape(state.shape, F32))
         + (shape((STATE + 8, owned), BF16),) * pieces,
-        in_specs=[VMEM] * 10,
-        out_specs=(VMEM,) * (4 + pieces),
+        in_specs=[VMEM] * 11,
+        out_specs=(VMEM,) * (3 + pieces),
         scratch_shapes=[
             pltpu.VMEM((16, tail.shape[1]), F32),
-            pltpu.VMEM((pieces, 8, owned), F32),
-            pltpu.VMEM((8, gn), F32),
+            pltpu.VMEM((gn // STATE, STATE, LANES), BF16),
+            pltpu.VMEM((LANES, owned), F32),
         ],
-        input_output_aliases={8: 0, 9: 1},
+        input_output_aliases={9: 0, 10: 1},
         compiler_params=params(16),
-        cost_estimate=cost(tok * STATE * owned * pieces * 4, tok * owned * pieces * 4),
-        name="state",
-    )(tail, part_x, part_b, taps_x, taps_b, age, tab, d, xc, bc)
-
-
-def own_kernel(
-    tail_ref,
-    age_ref,
-    tab_ref,
-    d_ref,
-    bt_ref,
-    taps_x_ref,
-    x_hbm,
-    c_hbm,
-    taps_c_hbm,
-    xc_ref,
-    cc_ref,
-    h_ref,
-    send_ref,
-    in_ref,
-    taps_c_ref,
-    ext_ref,
-    mask_ref,
-    sem,
-):
-    tok, channels = x_hbm.shape
-    gn = c_hbm.shape[1]
+        cost_estimate=cost(STATE * LANES * owned * pieces * 2, STATE * owned * pieces * 10),
+        name="head",
+    )(tail, part_x, part_b, taps_x, taps_b, age, state, decay, weight, xc, bc)
+
+
+def late_kernel(k, with_c, *refs):
+    tail_ref, age_ref, tab_ref, d_ref, bc_ref, taps_x_ref, x_ref = refs[:7]
+    refs = refs[7:]
+    if with_c:
+        c_ref, taps_c_ref, others_ref, extra_ref, decay_ref, cc_ref, early_ref = refs[:7]
+        refs = refs[7:]
+    xc_ref, h_ref, send_ref, bt_ref, ext_ref, mask_ref = refs
+    tok, channels = x_ref.shape
     owned = channels // CLUSTER
+    gn = bc_ref.shape[1]
     per = owned // CHUNK
     heads = d_ref.shape[1] // 2
     head_dim = channels // heads
     taps_len = taps_x_ref.shape[0]
-    at = place_of(0, owned)
-    copies = [
-        pltpu.make_async_copy(
-            x_hbm.at[:, pl.ds(pl.multiple_of(at + part * CHUNK, CHUNK), CHUNK)], in_ref.at[part], sem.at[part]
-        )
-        for part in range(per)
-    ]
-    copies.append(pltpu.make_async_copy(c_hbm, in_ref.at[per], sem.at[per]))
-    copies.append(pltpu.make_async_copy(taps_c_hbm, taps_c_ref, sem.at[per + 1]))
-    start_all(copies)
+    at = place_of(k, owned)
     fill_masks(age_ref, mask_ref)
-    wait_all(copies)
-    for part in range(per + 1):
+    group = at // (channels // (gn // STATE))
+    b_blk = bc_ref[:, pl.ds(pl.multiple_of(group * STATE, STATE), STATE)]
+    bt_ref[...] = b_blk.astype(F32).T.astype(BF16)
+    if with_c:
+        for i in range(EARLY):
+            extra = extra_ref[i]
+            for c in range(tok // SUB - 1):
+                if c > 0:
+                    extra = extra * decay_ref[i, 2 + c : 3 + c, :]
+                early_ref[i, c] = (others_ref[i, c] + extra).astype(BF16)
+    for part in range(per + with_c):
         here = slice(part * CHUNK, (part + 1) * CHUNK)
         if part < per:
             lanes = pl.ds(pl.multiple_of(at + part * CHUNK, CHUNK), CHUNK)
@@ -473,7 +478,7 @@
             lanes = slice(channels + gn, channels + 2 * gn)
             taps = [taps_c_ref[j : j + 1, :] for j in range(taps_len)]
         ext_ref[:8, :] = tail_ref[:, lanes].astype(F32)
-        ext_ref[8:, :] = in_ref[part].astype(F32)
+        ext_ref[8:, :] = (x_ref[:, lanes] if part < per else c_ref[...]).astype(F32)
 
         def emit(low, total):
             value = silu(total).astype(BF16)
@@ -486,55 +491,71 @@
         if part < per:
 
             def h_put(c, value):
-                h_ref[0, c, :, here] = value
-
-            group = at // (channels // (gn // STATE))
-            state, decay = state_of(
+                h_ref[0, c, :, here] = value.astype(BF16)
+
+            state, decay, _ = state_of(
                 at + part * CHUNK,
                 heads,
                 head_dim,
-                bt_ref.at[group],
+                bt_ref,
                 tab_ref,
                 d_ref,
                 lambda c: xc_ref[0, c * SUB : (c + 1) * SUB, here].astype(F32),
                 h_put,
             )
-            send_ref[:STATE, here] = state
-            send_ref[STATE:, here] = decay
-
-
-def own(tail, age, tab, d, bt, taps_x, x, c, taps_c):
+            send_ref[:STATE, here] = state.astype(BF16)
+            send_ref[STATE:, here] = decay.astype(BF16)
+
+
+def late(k, tail, age, tab, d, bc, taps_x, x, with_c=()):
     tok, channels = x.shape
-    gn = c.shape[1]
     owned = channels // CLUSTER
-    places = owned // CHUNK + 1
+    gn = bc.shape[1]
+    subs = tok // SUB - 1
     shape = jax.ShapeDtypeStruct
-    return pl.pallas_call(
-        own_kernel,
+    extra_out = (shape((tok, gn), BF16), shape((EARLY, subs, STATE, owned), BF16)) if with_c else ()
+    return pl.pallas_call(
+        functools.partial(late_kernel, k, bool(with_c)),
         out_shape=(
+            *extra_out,
             shape((1, tok, owned), BF16),
-            shape((tok, gn), BF16),
-            shape((1, tok // SUB - 1, STATE, owned), BF16),
+            shape((1, subs, STATE, owned), BF16),
             shape((STATE + 8, owned), BF16),
         ),
-        in_specs=[VMEM] * 6 + [HBM] * 3,
-        out_specs=(VMEM,) * 4,
+        in_specs=[VMEM] * (7 + len(with_c)),
+        out_specs=(VMEM,) * (3 + len(extra_out)),
         scratch_shapes=[
-            pltpu.VMEM((places, tok, CHUNK), BF16),
-            pltpu.VMEM(taps_c.shape, F32),
+            pltpu.VMEM((STATE, tok), BF16),
             pltpu.VMEM((tok + 8, CHUNK), F32),
-            pltpu.VMEM((taps_c.shape[0] - 1, tok, LANES), F32),
-            pltpu.SemaphoreType.DMA((places + 1,)),
+            pltpu.VMEM((taps_x.shape[0] - 1, tok, LANES), F32),
         ],
         compiler_params=params(16),
         cost_estimate=cost(tok * owned * 16 + tok * STATE * owned * 4, tok * owned * 8, tok * owned),
-        name="own",
-    )(tail, age, tab, d, bt, taps_x, x, c, taps_c)
+        name="own" if with_c else "late",
+    )(tail, age, tab, d, bc, taps_x, x, *with_c)
+
+
+def collect_kernel(*refs):
+    *pieces, out_ref = refs
+    for k, ref in enumerate(pieces):
+        out_ref[k] = ref[...]
+
+
+def collect(pieces):
+    return pl.pallas_call(
+        collect_kernel,
+        out_shape=jax.ShapeDtypeStruct((len(pieces), *pieces[0].shape), BF16),
+        in_specs=[VMEM] * len(pieces),
+        out_specs=VMEM,
+        compiler_params=params(16),
+        cost_estimate=cost(0, 4 * len(pieces) * pieces[0].size),
+        name="collect",
+    )(*pieces)
 
 
 def scan_kernel(*refs):
-    pieces = refs[:CLUSTER]
-    local_ref, pre_ref, total_ref = refs[CLUSTER:]
+    first_ref, *last, local_ref, pre_ref, total_ref = refs
+    pieces = [first_ref.at[k] for k in range(first_ref.shape[0])] + last
     mine = lax.axis_index("seq") % CLUSTER
 
     def in_order(values):
@@ -567,6 +588,7 @@
 
 
 def scan_blocks(pieces):
+    operands = (collect(pieces[: 1 + EARLY]), *pieces[1 + EARLY :])
     owned = pieces[0].shape[1]
     return pl.pallas_call(
         scan_kernel,
@@ -575,12 +597,12 @@
             jax.ShapeDtypeStruct((CLUSTER + 1, 8, owned), F32),
             jax.ShapeDtypeStruct((STATE, owned), BF16),
         ),
-        in_specs=[VMEM] * CLUSTER,
+        in_specs=[VMEM] * len(operands),
         out_specs=(VMEM,) * 3,
         compiler_params=params(),
         cost_estimate=cost(CLUSTER * STATE * owned * 2, CLUSTER * STATE * owned * 6),
         name="cluster_scan",
-    )(*pieces)
+    )(*operands)
 
 
 def join_kernel(before_ref, local_ref, pre_ref, *outs):
@@ -653,6 +675,10 @@
             scales[p][:, lanes] = mm(tab0_ref[...], hot0_ref[p, :, lanes]) * gate
 
 
+def early_index(k):
+    return k - 1 if 1 <= k <= EARLY else 0
+
+
 def intra(turn, pieces, bc, cc, tab, tab0, col, row, age, xs, hs, gate):
     tok, gn = bc.shape
     heads = row.shape[0]
@@ -679,8 +705,8 @@
             pl.BlockSpec((heads, SUB), lambda i: (0, i)),
             pl.BlockSpec((SUB, LANES), lambda i: (i, 0)),
         ]
-        + piece_spec((1, SUB, owned), lambda k, i: (max(k - 1, 0), i, 0))
-        + piece_spec((1, 1, STATE, owned), lambda k, i: (max(k - 1, 0), jnp.maximum(i - 1, 0), 0, 0))
+        + piece_spec((1, SUB, owned), lambda k, i: (early_index(k), i, 0))
+        + piece_spec((1, 1, STATE, owned), lambda k, i: (early_index(k), jnp.maximum(i - 1, 0), 0, 0))
         + piece_spec((SUB, owned), lambda k, i: (i, lax.axis_index("seq") % CLUSTER ^ k)),
         out_specs=(pl.BlockSpec((SUB, owned), lambda i: (i, 0)),) * (2 * count),
         scratch_shapes=[pltpu.VMEM((count, 4 * heads, owned), BF16), pltpu.VMEM((count, 2 * heads, owned), BF16)],
@@ -690,62 +716,60 @@
     )(bc, cc, tab, tab0, col, row, age, *xs, *hs, *([gate] * count))
 
 
-def final_kernel(groups, *refs):
+def final_kernel(turn, groups, *refs):
     cc_ref, gain_ref = refs[:2]
-    parts, scales, pieces = (refs[2 + i * CLUSTER : 2 + (i + 1) * CLUSTER] for i in range(3))
-    out_hbm, y_ref, put_ref, sem = refs[2 + 3 * CLUSTER :]
+    share = CLUSTER // groups
+    parts, scales, pieces = (refs[2 + i * share : 2 + (i + 1) * share] for i in range(3))
+    out_hbm, y_ref, put_ref, sem = refs[-4:]
     tok, owned = parts[0].shape
-    share = CLUSTER // groups
     rows = y_ref.shape[1]
     copies = []
-    for turn in range(groups):
-        group = group_at(turn, groups)
-        c_lanes = pl.ds(pl.multiple_of(group * STATE, STATE), STATE)
-        for low in range(0, tok, rows):
-            span = slice(low, low + rows)
-            c_blk = cc_ref[span, c_lanes]
-            squares = None
-            for i in range(share):
-                k = turn * share + i
-                for at in range(0, owned, CHUNK):
-                    lanes = slice(at, at + CHUNK)
-                    value = parts[k][span, lanes] + mm(c_blk, pieces[k][:, lanes]) * scales[k][span, lanes]
-                    y_ref[i, :, lanes] = value
-                    square = value * value
-                    for j in range(0, CHUNK, LANES):
-                        piece = square[:, j : j + LANES]
-                        squares = piece if squares is None else squares + piece
-            factor = lax.rsqrt(jnp.sum(squares, axis=1, keepdims=True) * (1.0 / (share * owned)) + norm_eps)
-            for i in range(share):
-                k = turn * share + i
-                columns = pl.ds(place_of(k, owned), owned)
-                put_ref[k, span, :] = (y_ref[i] * factor * gain_ref[:, columns]).astype(BF16)
-                copy = pltpu.make_async_copy(
-                    put_ref.at[k, span, :], out_hbm.at[span, columns], sem.at[k, low // rows]
-                )
-                copy.start()
-                copies.append(copy)
+    c_lanes = pl.ds(pl.multiple_of(group_at(turn, groups) * STATE, STATE), STATE)
+    columns = [pl.ds(place_of(turn * share + i, owned), owned) for i in range(share)]
+    for low in range(0, tok, rows):
+        span = slice(low, low + rows)
+        c_blk = cc_ref[span, c_lanes]
+        squares = None
+        for i in range(share):
+            for at in range(0, owned, CHUNK):
+                lanes = slice(at, at + CHUNK)
+                value = parts[i][span, lanes] + mm(c_blk, pieces[i][:, lanes]) * scales[i][span, lanes]
+                y_ref[i, :, lanes] = value
+                square = value * value
+                for j in range(0, CHUNK, LANES):
+                    piece = square[:, j : j + LANES]
+                    squares = piece if squares is None else squares + piece
+        factor = lax.rsqrt(jnp.sum(squares, axis=1, keepdims=True) * (1.0 / (share * owned)) + norm_eps)
+        for i in range(share):
+            put_ref[i, span, :] = (y_ref[i] * factor * gain_ref[:, columns[i]]).astype(BF16)
+            copies.append(
+                pltpu.make_async_copy(put_ref.at[i, span, :], out_hbm.at[span, columns[i]], sem.at[i, low // rows])
+            )
+            copies[-1].start()
     wait_all(copies)
 
 
-def final(cc, gain, parts, scales, pieces):
+def final(turn, cc, gain, parts, scales, pieces, so_far):
     tok, owned = parts[0].shape
     groups = cc.shape[1] // STATE
+    share = CLUSTER // groups
     rows = 64
-    return pl.pallas_call(
-        functools.partial(final_kernel, groups),
+    operands = (cc, gain, *parts, *scales, *pieces) + (() if so_far is None else (so_far,))
+    return pl.pallas_call(
+        functools.partial(final_kernel, turn, groups),
         out_shape=jax.ShapeDtypeStruct((tok, owned * CLUSTER), BF16),
-        in_specs=[VMEM] * (2 + 3 * CLUSTER),
+        in_specs=[VMEM] * (2 + 3 * share) + ([] if so_far is None else [ANY]),
         out_specs=ANY,
         scratch_shapes=[
-            pltpu.VMEM((CLUSTER // groups, rows, owned), F32),
-            pltpu.VMEM((CLUSTER, tok, owned), BF16),
-            pltpu.SemaphoreType.DMA((CLUSTER, tok // rows)),
+            pltpu.VMEM((share, rows, owned), F32),
+            pltpu.VMEM((share, tok, owned), BF16),
+            pltpu.SemaphoreType.DMA((share, tok // rows)),
         ],
+        input_output_aliases={} if so_far is None else {len(operands) - 1: 0},
         compiler_params=params(16),
-        cost_estimate=cost(tok * STATE * owned * CLUSTER * 2, tok * owned * CLUSTER * 8),
+        cost_estimate=cost(tok * STATE * owned * share * 2, tok * owned * share * 8),
         name="final",
-    )(cc, gain, *parts, *scales, *pieces)
+    )(*operands)
 
 
 def moved(value, hop):
@@ -797,32 +821,41 @@
     groups = b_input.shape[1] // STATE
     count = lax.axis_size("seq")
     pin = lambda value: pltpu.with_memory_space_constraint(value, pltpu.HBM)
+    raw_x, raw_c, raw_taps_c = x_input, c_input, taps_c
     x_input, b_input, c_input, doc_lengths = pin(x_input), pin(b_input), pin(c_input), pin(doc_lengths)
-    taps_x, taps_b, taps_c = pin(taps_x), pin(taps_b), pin(taps_c)
-    ends, tab, tab0, col, row, d, age = prep(
-        doc_lengths, pin(dt_input.T), pin(decay_rate[None, :]), x_input, b_input, c_input
+    taps_x, taps_b = pin(taps_x), pin(taps_b)
+    tail = lax.ppermute(pack(x_input, b_input, c_input), "seq", [(i, (i + 1) % count) for i in range(count)])
+    tab, tab0, col, row, d, age, taps_x, taps_b, part_x, part_b, xc, bc = conv(
+        doc_lengths, pin(dt_input.T), pin(decay_rate[None, :]), x_input, b_input, taps_x, taps_b
     )
-    tail = lax.ppermute(ends, "seq", [(i, (i + 1) % count) for i in range(count)])
-    taps_x, taps_b, part_x, part_b, xc, bc = conv(age, x_input, b_input, taps_x, taps_b)
-    xc, bc, bt, h, *sends = states(tail, part_x, part_b, taps_x, taps_b, age, tab, d, xc, bc)
-    own_x, cc, own_h, own_send = own(tail, age, tab, d, bt, taps_x, x_input, c_input, taps_c)
-    shared = (bc, cc, tab, tab0, col, row, age)
+    state, others, decay, weight = states(tab, d, xc, bc)
+    xc, bc, extra, *sends = with_head(tail, part_x, part_b, taps_x, taps_b, age, state, decay, weight, xc, bc)
+    known = (tail, age, tab, d, bc, taps_x, raw_x)
+    xs, hs = [None] + [xc] * EARLY, [None] * (1 + EARLY)
+    for k in range(1 + EARLY, CLUSTER):
+        late_x, late_h, late_send = late(k, *known)
+        xs.append(late_x)
+        hs.append(late_h)
+        sends.append(late_send)
+    cc, early_h, xs[0], hs[0], own_send = late(0, *known, (raw_c, raw_taps_c, others, extra, decay))
+    hs[1 : 1 + EARLY] = [early_h] * EARLY
+    shared = (bc, cc, tab, tab0, col, row)
     share = CLUSTER // groups
 
-    def inner(turn):
+    def inner(turn, age):
         pieces = tuple(range(turn * share, (turn + 1) * share))
-        xs, hs = ([mine if k == 0 else other for k in pieces] for mine, other in ((own_x, xc), (own_h, h)))
-        return intra(turn, pieces, *shared, xs, hs, gate_input)
-
-    first = inner(0)
-    arrived = tied(exchanged([own_send, *sends], (3, 2, 1)), first[0])
-    local, pre, total = scan_blocks(arrived)
-    later = [inner(turn) for turn in range(1, groups)]
-    (before,) = tied([before_cluster(total, pre)], later[-1][0])
-    entering = exchanged(join(before, local, pre), (3, 2, 1))
-    parts = [part for turn in (first, *later) for part in turn[:share]]
-    scales = [part for turn in (first, *later) for part in turn[share:]]
-    return final(cc, norm_gain[None, :], parts, scales, entering)
+        return intra(turn, pieces, *shared, age, [xs[k] for k in pieces], [hs[k] for k in pieces], gate_input)
+
+    local, pre, total = scan_blocks(exchanged([own_send, *sends], (1, 2, 3)))
+    first = inner(0, *tied([age], total))
+    joined = join(*tied([before_cluster(total, pre)], first[0]), local, pre)
+    later = [inner(turn, *tied([age], joined[0])) for turn in range(1, groups)]
+    entering = exchanged(joined, (1, 2, 3))
+    output = None
+    for turn, found in enumerate((first, *later)):
+        mine = entering[turn * share : (turn + 1) * share]
+        output = final(turn, cc, norm_gain[None, :], found[:share], found[share:], mine, output)
+    return output
 
 
 def solution(mesh):

time: 37.5 us -> 36.8 us (0.981)
  waiting for transfers between devices: 8.78 us -> 7.42 us
  starting transfers between devices: 11.6 us -> 12 us
    ppermute x1, waiting for transfers between devices: 1.42 us -> 0.51 us  [on_device(): lax.ppermute(pack(x_input, b_input, c_input), 'seq', [(i, (i + 1) % count...]
    ppermute x7, waiting for transfers between devices: 7.35 us -> 6.91 us  [moved(): lax.ppermute(value, 'seq', [(i, hop(i)) for i in range(count) if 0 <= hop...]
    ppermute x7, starting transfers between devices: 8.63 us -> 9.05 us  [moved(): lax.ppermute(value, 'seq', [(i, hop(i)) for i in range(count) if 0 <= hop...]
    pallas_call x5 -> x9, Pallas kernels: 10.8 us -> 11.1 us  [the longest x1 3.59 us: conv(): pl.pallas_call(conv_kernel, out_shape=(shape((tok, LANES), BF16), shape((...]
  transfers between devices with their start and end apart: 8 -> 8, of which waited for: 5 -> 6; matrix products, arithmetic and copies ran while one was open for 0% -> 0% of each run, Pallas kernels for 32% -> 39%
where the time goes in v5:
time: 36.8 us; the launch traced here: 36.6 us
  Pallas kernels  17 us (46%)
  starting transfers between devices  12 us (33%)
  waiting for transfers between devices  7.42 us (20%)
    ppermute x7, starting transfers between devices, moved(): lax.ppermute(value, 'seq', [(i, hop(i)) for i in range(count) if 0 <= hop...  9.05 us
    ppermute x7, waiting for transfers between devices, moved(): lax.ppermute(value, 'seq', [(i, hop(i)) for i in range(count) if 0 <= hop...  6.91 us
    pallas_call x2, Pallas kernels, intra(): pl.pallas_call(functools.partial(intra_kernel, pieces, heads, head_dim),...  5.59 us
    pallas_call x1, Pallas kernels, conv(): pl.pallas_call(conv_kernel, out_shape=(shape((tok, LANES), BF16), shape((...  3.59 us
    ppermute x1, starting transfers between devices, on_device(): lax.ppermute(pack(x_input, b_input, c_input), 'seq', [(i, (i + 1) % count...  2.94 us
    pallas_call x2, Pallas kernels, late(): pl.pallas_call(functools.partial(late_kernel, k, bool(with_c)), out_shape...  2.8 us
    pallas_call x2, Pallas kernels, final(): pl.pallas_call(functools.partial(final_kernel, turn, groups), out_shape=j...  2.68 us
    pallas_call x1, Pallas kernels, states(): pl.pallas_call(state_kernel, out_shape=(jax.ShapeDtypeStruct((pieces, STA...  0.89 us
  transfers between devices with their start and end apart: 8, of which 6 were waited for; matrix products, arithmetic and copies ran while one was open for 0% of the time, Pallas kernels for 39%

profile of v5, /device:TPU:0, one launch (start us, length us, event | category | flops | bytes accessed | tf_op | source)
XLA Modules:
  0.0 36.6 jit_solution(5450622393453236242)
XLA Ops:
  0.0 0.8 %pack.1 = bf16[8,2560]{1,0:T(8,128)(2,1)S(1)} custom-call(bf16[384,2048]{1,0:T(8,128)(2,1)} %refs_6_.3, bf16[384,256]{1,0:T(8,128)(2,1)} %b_hbm.1, bf16[384,256]{1,0:T(8,128)(2,1)} %refs_7_.1), custom_call_target="tpu_custom_call" | custom-call | tf_op jit(solution)/shard_map/pack/pallas_call | solution.py:134
  0.8 2.9 %collective-permute-start = (bf16[8,2560]{1,0:T(8,128)(2,1)S(1)}, bf16[8,2560]{1,0:T(8,128)(2,1)S(1)}, u32[]{:S(2)}, u32[]{:S(2)}) collective-permute-start(bf16[8,2560]{1,0:T(8,128)(2,1)S(1)} %pack.1), channel_id=1, source_target_pairs={{0,2},{2,4},{4,6},{6,8},{8,10},{10,12},{12,14},{14,0},{1,3},{3,5},... | collective-permute-start | bytes 122888 | tf_op jit(solution)/shard_map/ppermute | solution.py:827
  3.7 3.6 %conv.1 = (bf16[384,128]{1,0:T(8,128)(2,1)S(1)}, bf16[384,64]{1,0:T(8,128)(2,1)S(1)}, f32[384,128]{1,0:T(8,128)S(1)}, f32[32,384]{1,0:T(8,128)S(1)}, bf16[8,64]{...) custom-call(s32[4]{0:T(128)} %dl_hbm.1, ...), custom_call_target="tpu_custom_call" | custom-call | flops 12582912 | bytes 3145728 | tf_op jit(solution)/shard_map/conv/pallas_call | solution.py:280
  7.3 0.0 copy-start
  7.3 0.9 %state.1 = (f32[2,128,512]{2,1,0:T(8,128)S(1)}, f32[2,2,128,512]{3,2,1,0:T(8,128)S(1)}, f32[2,8,512]{2,1,0:T(8,128)S(1)}, f32[2,8,512]{2,1,0:T(8,128)S(1)}) custom-call(bf16[384,128]{1,0:T(8,128)(2,1)S(1)} %get-tuple-element.53.tab_ref.refs_2_, bf16[8,64]{1,0:T(8,128)(2,1)S(1)} %get-tuple-element.54.d_ref.refs_3_, ...), custom_call_target="tpu_custom_call" | custom-call | flops 201326592 | bytes 1572864 | tf_op jit(solution)/shard_map/state/pallas_call | solution.py:350
  8.2 0.5 %collective-permute-done.tail_ref.refs_0_ = bf16[8,2560]{1,0:T(8,128)(2,1)S(1)} collective-permute-done((bf16[8,2560]{1,0:T(8,128)(2,1)S(1)}, bf16[8,2560]{1,0:T(8,128)(2,1)S(1)}, u32[]{:S(2)}, u32[]{:S(2)}) %collective-permute-start) | collective-permute-done | bytes 40992 | tf_op jit(solution)/shard_map/ppermute | solution.py:827
  8.7 0.0 copy-start.2
  8.7 0.0 copy-start.4
  8.7 0.3 head.1
  9.1 1.1 %collective-permute-start.1 = (bf16[136,512]{1,0:T(8,128)(2,1)S(1)}, bf16[136,512]{1,0:T(8,128)(2,1)S(1)}, u32[]{:S(2)}, u32[]{:S(2)}) collective-permute-start(bf16[136,512]{1,0:T(8,128)(2,1)S(1)} %get-tuple-element.72), channel_id=1, source_target_pairs={{0,2},{2,0},{4,6},{6,4},{8,10},{10,8},{12,14},{14,12},{1,3},{3,1},... | collective-permute-start | bytes 417800 | tf_op jit(solution)/shard_map/ppermute | solution.py:777
  10.2 1.6 %collective-permute-start.2 = (bf16[136,512]{1,0:T(8,128)(2,1)S(1)}, bf16[136,512]{1,0:T(8,128)(2,1)S(1)}, u32[]{:S(2)}, u32[]{:S(2)}) collective-permute-start(bf16[136,512]{1,0:T(8,128)(2,1)S(1)} %get-tuple-element.73), channel_id=1, source_target_pairs={{0,4},{2,6},{4,0},{6,2},{8,12},{10,14},{12,8},{14,10},{1,5},{3,7},... | collective-permute-start | bytes 417800 | tf_op jit(solution)/shard_map/ppermute | solution.py:777
  11.8 0.0 copy-done
  11.8 1.1 %late.1 = (bf16[1,384,512]{2,1,0:T(8,128)(2,1)S(1)}, bf16[1,2,128,512]{3,2,1,0:T(8,128)(2,1)S(1)}, bf16[136,512]{1,0:T(8,128)(2,1)S(1)}) custom-call(bf16[8,2560]{1,0:T(8,128)(2,1)S(1)} %collective-permute-done.tail_ref.refs_0_, s32[384,128]{1,0:T(8,128)S(1)} %get-tuple-element.86.age_ref.refs_1_.refs_6_, ...), custom_call_target="tpu_custom_call" | custom-call | flops 103809024 | bytes 1572864 | tf_op jit(solution)/shard_map/late/pallas_call | solution.py:517
  12.9 0.9 %collective-permute-start.3 = (bf16[136,512]{1,0:T(8,128)(2,1)S(1)}, bf16[136,512]{1,0:T(8,128)(2,1)S(1)}, u32[]{:S(2)}, u32[]{:S(2)}) collective-permute-start(bf16[136,512]{1,0:T(8,128)(2,1)S(1)} %get-tuple-element.74), channel_id=1, source_target_pairs={{0,6},{2,4},{4,2},{6,0},{8,14},{10,12},{12,10},{14,8},{1,7},{3,5},... | collective-permute-start | bytes 417800 | tf_op jit(solution)/shard_map/ppermute | solution.py:777
  13.8 0.0 copy-done.2
  13.8 0.0 copy-done.4
  13.8 0.0 copy-start.1
  13.8 1.7 %own.1 = (bf16[384,256]{1,0:T(8,128)(2,1)S(1)}, bf16[2,2,128,512]{3,2,1,0:T(8,128)(2,1)S(1)}, bf16[1,384,512]{2,1,0:T(8,128)(2,1)S(1)}, bf16[1,2,128,512]{3,2,1,0:T(8,128)(2,1)S(1)}, bf16[136,512]{1,0:T(8,128)(2,1)S(1)}) custom-call(bf16[8,2560]{1,0:T(8,128)(2,1)S(1)} %collective-permute-done.tail_ref.refs_0_, ...), custom_call_target="tpu_custom_call" | custom-call | flops 103809024 | bytes 1572864 | tf_op jit(solution)/shard_map/own/pallas_call | solution.py:517
  15.5 0.0 collective-permute-done.1.refs_1_
  15.5 0.5 %collective-permute-done.2.refs_2_ = bf16[136,512]{1,0:T(8,128)(2,1)S(1)} collective-permute-done((bf16[136,512]{1,0:T(8,128)(2,1)S(1)}, bf16[136,512]{1,0:T(8,128)(2,1)S(1)}, u32[]{:S(2)}, u32[]{:S(2)}) %collective-permute-start.2) | collective-permute-done | bytes 139296 | tf_op jit(solution)/shard_map/ppermute | solution.py:777
  16.1 2.8 %collective-permute-done.3.refs_1_ = bf16[136,512]{1,0:T(8,128)(2,1)S(1)} collective-permute-done((bf16[136,512]{1,0:T(8,128)(2,1)S(1)}, bf16[136,512]{1,0:T(8,128)(2,1)S(1)}, u32[]{:S(2)}, u32[]{:S(2)}) %collective-permute-start.3) | collective-permute-done | bytes 139296 | tf_op jit(solution)/shard_map/ppermute | solution.py:777
  18.9 0.2 cluster_scan.1
  19.2 1.9 %collective-permute-start.4 = (bf16[128,512]{1,0:T(8,128)(2,1)S(1)}, bf16[128,512]{1,0:T(8,128)(2,1)S(1)}, u32[]{:S(2)}, u32[]{:S(2)}) collective-permute-start(bf16[128,512]{1,0:T(8,128)(2,1)S(1)} %get-tuple-element.75), channel_id=1, source_target_pairs={{0,8},{2,10},{4,12},{6,14},{8,0},{10,2},{12,4},{14,6},{1,9},{3,11}... | collective-permute-start | bytes 393224 | tf_op jit(solution)/shard_map/ppermute | solution.py:777
  21.0 0.0 copy-done.1
  21.0 2.8 %intra.2 = (f32[384,512]{1,0:T(8,128)S(1)}, f32[384,512]{1,0:T(8,128)S(1)}, f32[384,512]{1,0:T(8,128)S(1)}, f32[384,512]{1,0:T(8,128)S(1)}) custom-call(bf16[384,256]{1,0:T(8,128)(2,1)S(1)} %get-tuple-element.64.refs_4_.refs_0_, bf16[384,256]{1,0:T(8,128)(2,1)S(1)} %get-tuple-element.67.refs_1_.refs_0_, ...), custom_call_target="tpu_custom_call" | custom-call | flops 201326592 | bytes 4718592 | tf_op jit(solution)/shard_map/intra/pallas_call | solution.py:695
  23.8 2.8 %collective-permute-done.4.before_ref = bf16[128,512]{1,0:T(8,128)(2,1)S(1)} collective-permute-done((bf16[128,512]{1,0:T(8,128)(2,1)S(1)}, bf16[128,512]{1,0:T(8,128)(2,1)S(1)}, u32[]{:S(2)}, u32[]{:S(2)}) %collective-permute-start.4) | collective-permute-done | bytes 131104 | tf_op jit(solution)/shard_map/ppermute | solution.py:777
  26.7 0.1 join.1
  26.8 1.3 %collective-permute-start.7 = (bf16[128,512]{1,0:T(8,128)(2,1)S(1)}, bf16[128,512]{1,0:T(8,128)(2,1)S(1)}, u32[]{:S(2)}, u32[]{:S(2)}) collective-permute-start(bf16[128,512]{1,0:T(8,128)(2,1)S(1)} %get-tuple-element.98), channel_id=1, source_target_pairs={{0,2},{2,0},{4,6},{6,4},{8,10},{10,8},{12,14},{14,12},{1,3},{3,1},... | collective-permute-start | bytes 393224 | tf_op jit(solution)/shard_map/ppermute | solution.py:777
  28.1 0.0 collective-permute-start.5
  28.1 2.2 %collective-permute-start.6 = (bf16[128,512]{1,0:T(8,128)(2,1)S(1)}, bf16[128,512]{1,0:T(8,128)(2,1)S(1)}, u32[]{:S(2)}, u32[]{:S(2)}) collective-permute-start(bf16[128,512]{1,0:T(8,128)(2,1)S(1)} %get-tuple-element.94), channel_id=1, source_target_pairs={{0,6},{2,4},{4,2},{6,0},{8,14},{10,12},{12,10},{14,8},{1,7},{3,5},... | collective-permute-start | bytes 393224 | tf_op jit(solution)/shard_map/ppermute | solution.py:777
  30.4 0.0 copy-start.3
  30.4 2.8 %intra.3 = (f32[384,512]{1,0:T(8,128)S(1)}, f32[384,512]{1,0:T(8,128)S(1)}, f32[384,512]{1,0:T(8,128)S(1)}, f32[384,512]{1,0:T(8,128)S(1)}) custom-call(bf16[384,256]{1,0:T(8,128)(2,1)S(1)} %get-tuple-element.64.refs_4_.refs_0_, bf16[384,256]{1,0:T(8,128)(2,1)S(1)} %get-tuple-element.67.refs_1_.refs_0_, ...), custom_call_target="tpu_custom_call" | custom-call | flops 201326592 | bytes 4718592 | tf_op jit(solution)/shard_map/intra/pallas_call | solution.py:695
  33.2 0.1 collective-permute-done.7.refs_7_
  33.2 0.0 copy-done.3
  33.2 1.3 %final.2.refs_8_ = bf16[384,2048]{1,0:T(8,128)(2,1)} custom-call(bf16[384,256]{1,0:T(8,128)(2,1)S(1)} %get-tuple-element.67.refs_1_.refs_0_, f32[1,2048]{1,0:T(1,128)S(1)} %bitcast.3, f32[384,512]{1,0:T(8,128)S(1)} %get-tuple-element.81.refs_2_, f32[384,512]{1,0:T(8,128)S(1)} %get-tuple-element.95.refs_3_, f32[384,512]{1,0:T(8,128)S(1)} %get-tuple-element.96.refs_4_, ...), custom_call_target="tpu_custom_call" | custom-call | flops 100663296 | bytes 3145728 | tf_op jit(solution)/shard_map/final/pallas_call | solution.py:758
  34.6 0.0 collective-permute-done.5.refs_6_
  34.6 0.6 %collective-permute-done.6.refs_7_ = bf16[128,512]{1,0:T(8,128)(2,1)S(1)} collective-permute-done((bf16[128,512]{1,0:T(8,128)(2,1)S(1)}, bf16[128,512]{1,0:T(8,128)(2,1)S(1)}, u32[]{:S(2)}, u32[]{:S(2)}) %collective-permute-start.6) | collective-permute-done | bytes 131104 | tf_op jit(solution)/shard_map/ppermute | solution.py:777
  35.2 1.3 %final.3 = bf16[384,2048]{1,0:T(8,128)(2,1)} custom-call(bf16[384,256]{1,0:T(8,128)(2,1)S(1)} %get-tuple-element.67.refs_1_.refs_0_, f32[1,2048]{1,0:T(1,128)S(1)} %bitcast.4, f32[384,512]{1,0:T(8,128)S(1)} %get-tuple-element.89.refs_2_, f32[384,512]{1,0:T(8,128)S(1)} %get-tuple-element.90.refs_3_, ...), custom_call_target="tpu_custom_call", output_to_operand_aliasing={{}: (8, {})} | custom-call | flops 100663296 | bytes 3145728 | tf_op jit(solution)/shard_map/final/pallas_call | solution.py:758
  (1 shorter events, 0.0 us)
Async XLA Ops:
  0.8 8.0 %collective-permute-start = (bf16[8,2560]{1,0:T(8,128)(2,1)S(1)}, bf16[8,2560]{1,0:T(8,128)(2,1)S(1)}, u32[]{:S(2)}, u32[]{:S(2)}) collective-permute-start(bf16[8,2560]{1,0:T(8,128)(2,1)S(1)} %pack.1), channel_id=1, source_target_pairs={{0,2},{2,4},{4,6},{6,8},{8,10},{10,12},{12,14},{14,0},{1,3},{3,5},... | collective-permute-start | bytes 122888 | tf_op jit(solution)/shard_map/ppermute | solution.py:827
  7.3 4.5 %copy-start = (bf16[384,2048]{1,0:T(8,128)(2,1)S(1)}, bf16[384,2048]{1,0:T(8,128)(2,1)}, u32[]{:S(2)}) copy-start(bf16[384,2048]{1,0:T(8,128)(2,1)} %refs_6_.3) | copy-start | bytes 4718596
  8.7 5.1 %copy-start.2 = (bf16[384,256]{1,0:T(8,128)(2,1)S(1)}, bf16[384,256]{1,0:T(8,128)(2,1)}, u32[]{:S(2)}) copy-start(bf16[384,256]{1,0:T(8,128)(2,1)} %refs_7_.1) | copy-start | bytes 589828
  8.7 5.1 %copy-start.4 = (f32[4,256]{1,0:T(4,128)S(1)}, f32[4,256]{1,0:T(4,128)}, u32[]{:S(2)}) copy-start(f32[4,256]{1,0:T(4,128)} %refs_8_.1) | copy-start | bytes 12292
  9.1 6.4 %collective-permute-start.1 = (bf16[136,512]{1,0:T(8,128)(2,1)S(1)}, bf16[136,512]{1,0:T(8,128)(2,1)S(1)}, u32[]{:S(2)}, u32[]{:S(2)}) collective-permute-start(bf16[136,512]{1,0:T(8,128)(2,1)S(1)} %get-tuple-element.72), channel_id=1, source_target_pairs={{0,2},{2,0},{4,6},{6,4},{8,10},{10,8},{12,14},{14,12},{1,3},{3,1},... | collective-permute-start | bytes 417800 | tf_op jit(solution)/shard_map/ppermute | solution.py:777
  10.2 5.9 %collective-permute-start.2 = (bf16[136,512]{1,0:T(8,128)(2,1)S(1)}, bf16[136,512]{1,0:T(8,128)(2,1)S(1)}, u32[]{:S(2)}, u32[]{:S(2)}) collective-permute-start(bf16[136,512]{1,0:T(8,128)(2,1)S(1)} %get-tuple-element.73), channel_id=1, source_target_pairs={{0,4},{2,6},{4,0},{6,2},{8,12},{10,14},{12,8},{14,10},{1,5},{3,7},... | collective-permute-start | bytes 417800 | tf_op jit(solution)/shard_map/ppermute | solution.py:777
  12.9 6.0 %collective-permute-start.3 = (bf16[136,512]{1,0:T(8,128)(2,1)S(1)}, bf16[136,512]{1,0:T(8,128)(2,1)S(1)}, u32[]{:S(2)}, u32[]{:S(2)}) collective-permute-start(bf16[136,512]{1,0:T(8,128)(2,1)S(1)} %get-tuple-element.74), channel_id=1, source_target_pairs={{0,6},{2,4},{4,2},{6,0},{8,14},{10,12},{12,10},{14,8},{1,7},{3,5},... | collective-permute-start | bytes 417800 | tf_op jit(solution)/shard_map/ppermute | solution.py:777
  13.8 7.2 %copy-start.1 = (bf16[384,2048]{1,0:T(8,128)(2,1)S(1)}, bf16[384,2048]{1,0:T(8,128)(2,1)}, u32[]{:S(2)}) copy-start(bf16[384,2048]{1,0:T(8,128)(2,1)} %refs_12_.3) | copy-start | bytes 4718596
  19.2 7.5 %collective-permute-start.4 = (bf16[128,512]{1,0:T(8,128)(2,1)S(1)}, bf16[128,512]{1,0:T(8,128)(2,1)S(1)}, u32[]{:S(2)}, u32[]{:S(2)}) collective-permute-start(bf16[128,512]{1,0:T(8,128)(2,1)S(1)} %get-tuple-element.75), channel_id=1, source_target_pairs={{0,8},{2,10},{4,12},{6,14},{8,0},{10,2},{12,4},{14,6},{1,9},{3,11}... | collective-permute-start | bytes 393224 | tf_op jit(solution)/shard_map/ppermute | solution.py:777
  26.8 6.4 %collective-permute-start.7 = (bf16[128,512]{1,0:T(8,128)(2,1)S(1)}, bf16[128,512]{1,0:T(8,128)(2,1)S(1)}, u32[]{:S(2)}, u32[]{:S(2)}) collective-permute-start(bf16[128,512]{1,0:T(8,128)(2,1)S(1)} %get-tuple-element.98), channel_id=1, source_target_pairs={{0,2},{2,0},{4,6},{6,4},{8,10},{10,8},{12,14},{14,12},{1,3},{3,1},... | collective-permute-start | bytes 393224 | tf_op jit(solution)/shard_map/ppermute | solution.py:777
  28.1 6.5 %collective-permute-start.5 = (bf16[128,512]{1,0:T(8,128)(2,1)S(1)}, bf16[128,512]{1,0:T(8,128)(2,1)S(1)}, u32[]{:S(2)}, u32[]{:S(2)}) collective-permute-start(bf16[128,512]{1,0:T(8,128)(2,1)S(1)} %get-tuple-element.93), channel_id=1, source_target_pairs={{0,4},{2,6},{4,0},{6,2},{8,12},{10,14},{12,8},{14,10},{1,5},{3,7},... | collective-permute-start | bytes 393224 | tf_op jit(solution)/shard_map/ppermute | solution.py:777
  28.1 7.1 %collective-permute-start.6 = (bf16[128,512]{1,0:T(8,128)(2,1)S(1)}, bf16[128,512]{1,0:T(8,128)(2,1)S(1)}, u32[]{:S(2)}, u32[]{:S(2)}) collective-permute-start(bf16[128,512]{1,0:T(8,128)(2,1)S(1)} %get-tuple-element.94), channel_id=1, source_target_pairs={{0,6},{2,4},{4,2},{6,0},{8,14},{10,12},{12,10},{14,8},{1,7},{3,5},... | collective-permute-start | bytes 393224 | tf_op jit(solution)/shard_map/ppermute | solution.py:777
  30.4 2.9 %copy-start.3 = (f32[2048]{0:T(1024)S(1)}, f32[2048]{0:T(1024)}, u32[]{:S(2)}) copy-start(f32[2048]{0:T(1024)} %param.20) | copy-start | bytes 24580

commit v6 on v5

--- a/solution.py
+++ b/solution.py
@@ -125,7 +125,8 @@
 
 
 def pack_kernel(x_ref, b_ref, c_ref, out_ref):
-    out_ref[...] = jnp.concatenate([x_ref[...], b_ref[...], c_ref[...]], 1)
+    rows = [ref[...].astype(F32)[4:] for ref in (x_ref, b_ref, c_ref)]
+    out_ref[...] = jnp.concatenate(rows, 1).astype(BF16)
 
 
 def pack(x, b, c):
@@ -133,10 +134,10 @@
     widths = [value.shape[1] for value in (x, b, c)]
     return pl.pallas_call(
         pack_kernel,
-        out_shape=jax.ShapeDtypeStruct((8, sum(widths)), BF16),
+        out_shape=jax.ShapeDtypeStruct((4, sum(widths)), BF16),
         grid=(1,),
         in_specs=[pl.BlockSpec((8, width), lambda i: (tiles - 1, 0)) for width in widths],
-        out_specs=pl.BlockSpec((8, sum(widths)), lambda i: (0, 0)),
+        out_specs=pl.BlockSpec((4, sum(widths)), lambda i: (0, 0)),
         compiler_params=params(16),
         name="pack",
     )(x, b, c)
@@ -182,85 +183,71 @@
     return state, decay, head_weight
 
 
+def put_piece(send_ref, low, state):
+    for tile in range(state.shape[1] // LANES):
+        at = low * STATE + tile * STATE
+        send_ref[at : at + STATE, :] = state[:, tile * LANES : (tile + 1) * LANES].astype(BF16)
+
+
+def put_decay(send_ref, decay):
+    tiles = decay.shape[1] // LANES
+    rows = [decay[:2, tile * LANES : (tile + 1) * LANES] for tile in range(tiles)]
+    send_ref[tiles * STATE :, :] = jnp.concatenate(rows, 0).astype(BF16)
+
+
+def piece_shape(owned):
+    return jax.ShapeDtypeStruct((owned // LANES * (STATE + 2), LANES), BF16)
+
+
 def conv_kernel(
-    dl_hbm,
-    dt_hbm,
-    rate_hbm,
-    x_hbm,
-    b_hbm,
-    taps_x_hbm,
-    taps_b_hbm,
+    dl_ref,
+    dt_ref,
+    rate_ref,
+    x_ref,
+    b_ref,
+    taps_x_ref,
+    taps_b_ref,
     tab_ref,
     tab0_ref,
     col_ref,
     row_ref,
     d_ref,
     age_ref,
-    taps_x_ref,
-    taps_b_ref,
     part_x_ref,
     part_b_ref,
     xc_ref,
     bc_ref,
-    dl_ref,
-    dt_ref,
-    rate_ref,
-    in_ref,
     ext_ref,
     mask_ref,
-    sem,
-    in_sem,
 ):
-    tok, channels = x_hbm.shape
+    tok, channels = x_ref.shape
     owned = channels // CLUSTER
     per = owned // CHUNK
-    chunks = EARLY * per
-    small = [
-        pltpu.make_async_copy(dl_hbm, dl_ref, sem.at[0]),
-        pltpu.make_async_copy(dt_hbm, dt_ref, sem.at[1]),
-        pltpu.make_async_copy(rate_hbm, rate_ref, sem.at[2]),
-        pltpu.make_async_copy(taps_x_hbm, taps_x_ref, sem.at[3]),
-        pltpu.make_async_copy(taps_b_hbm, taps_b_ref, sem.at[4]),
-    ]
-    start_all(small)
-
-    def place(i):
-        return pl.multiple_of(place_of(i // per + 1, owned) + (i % per) * CHUNK, CHUNK)
-
-    def fetch(i):
-        return pltpu.make_async_copy(x_hbm.at[:, pl.ds(place(i), CHUNK)], in_ref.at[i], in_sem.at[i])
-
-    for i in range(chunks):
-        fetch(i).start()
-    fetch_b = pltpu.make_async_copy(b_hbm, in_ref.at[chunks], in_sem.at[chunks])
-    fetch_b.start()
-    ext_ref[:8, :] = jnp.zeros((8, CHUNK), F32)
-    wait_all(small)
     row0 = lax.axis_index("seq") * tok
     edges = doc_edges(dl_ref)
     tables(row0, edges, dt_ref, rate_ref, tab_ref, tab0_ref, col_ref, row_ref, d_ref)
     token = row0 + lax.broadcasted_iota(jnp.int32, (tok, LANES), 0)
     age_ref[...] = token - doc_start(token, edges)
     fill_masks(age_ref, mask_ref)
+    ext_ref[:8, :] = jnp.zeros((8, CHUNK), F32)
     taps_len = taps_x_ref.shape[0]
 
     def body(i, carry):
-        fetch(i).wait()
         k = i // per
+        lanes = pl.ds(pl.multiple_of(place_of(k + 1, owned) + (i % per) * CHUNK, CHUNK), CHUNK)
         inner = pl.ds(pl.multiple_of((i % per) * CHUNK, CHUNK), CHUNK)
-        ext_ref[8:, :] = in_ref[i].astype(F32)
+        ext_ref[8:, :] = x_ref[:, lanes].astype(F32)
 
         def emit(low, total):
             if low == 0:
                 part_x_ref[k, :, inner] = total[:8]
             xc_ref[k, low : low + ROWS, inner] = silu(total).astype(BF16)
 
-        convolve(ext_ref, mask_ref, [taps_x_ref[j : j + 1, pl.ds(place(i), CHUNK)] for j in range(taps_len)], emit)
+        convolve(ext_ref, mask_ref, [taps_x_ref[j : j + 1, lanes] for j in range(taps_len)], emit)
         return carry
 
-    lax.fori_loop(0, chunks, body, 0)
-    fetch_b.wait()
-    ext_ref[8:, :] = in_ref[chunks].astype(F32)
+    lax.fori_loop(0, EARLY * per, body, 0)
+    ext_ref[8:, :] = b_ref[...].astype(F32)
 
     def emit_b(low, total):
         if low == 0:
@@ -275,7 +262,6 @@
     tok, channels = x.shape
     gn = b.shape[1]
     owned = channels // CLUSTER
-    places = EARLY * (owned // CHUNK) + 1
     shape = jax.ShapeDtypeStruct
     return pl.pallas_call(
         conv_kernel,
@@ -286,24 +272,16 @@
             shape((heads, tok), F32),
             shape((8, 2 * heads), BF16),
             shape((tok, LANES), jnp.int32),
-            shape(taps_x.shape, F32),
-            shape(taps_b.shape, F32),
             shape((EARLY, 8, owned), F32),
             shape((8, gn), F32),
             shape((EARLY, tok, owned), BF16),
             shape((tok, gn), BF16),
         ),
-        in_specs=[HBM] * 7,
-        out_specs=(VMEM,) * 12,
+        in_specs=[pl.BlockSpec(memory_space=pltpu.SMEM)] + [VMEM] * 6,
+        out_specs=(VMEM,) * 10,
         scratch_shapes=[
-            pltpu.SMEM(doc_lengths.shape, jnp.int32),
-            pltpu.VMEM((heads, tok), F32),
-            pltpu.VMEM((1, heads), F32),
-            pltpu.VMEM((places, tok, CHUNK), BF16),
             pltpu.VMEM((tok + 8, CHUNK), F32),
             pltpu.VMEM((taps_x.shape[0] - 1, tok, LANES), F32),
-            pltpu.SemaphoreType.DMA((5,)),
-            pltpu.SemaphoreType.DMA((places,)),
         ],
         compiler_params=params(16),
         cost_estimate=cost(tok * channels * 16, tok * channels * 4, tok * channels),
@@ -387,7 +365,7 @@
     gn = bc_in.shape[1]
     channels = owned * CLUSTER
     taps_len = taps_x_ref.shape[0]
-    ext_ref[:8, :] = tail_ref[...].astype(F32)
+    ext_ref[4:8, :] = tail_ref[...].astype(F32)
     ext_ref[8:, :] = jnp.zeros_like(ext_ref[8:, :])
 
     def head_of(part, lanes, taps, width):
@@ -417,8 +395,8 @@
         rest_of_block = decay[3:4, :]
         for c in range(4, 3 + xc_in.shape[1] // SUB - 1):
             rest_of_block = rest_of_block * decay[c : c + 1, :]
-        sends[k][:STATE, :] = (s_ref[k] + rest_of_block * extra).astype(BF16)
-        sends[k][STATE:, :] = decay.astype(BF16)
+        put_piece(sends[k], 0, s_ref[k] + rest_of_block * extra)
+        put_decay(sends[k], decay)
 
 
 def with_head(tail, part_x, part_b, taps_x, taps_b, age, state, decay, weight, xc, bc):
@@ -428,7 +406,7 @@
     return pl.pallas_call(
         head_kernel,
         out_shape=(shape(xc.shape, BF16), shape(bc.shape, BF16), shape(state.shape, F32))
-        + (shape((STATE + 8, owned), BF16),) * pieces,
+        + (piece_shape(owned),) * pieces,
         in_specs=[VMEM] * 11,
         out_specs=(VMEM,) * (3 + pieces),
         scratch_shapes=[
@@ -469,6 +447,7 @@
                 if c > 0:
                     extra = extra * decay_ref[i, 2 + c : 3 + c, :]
                 early_ref[i, c] = (others_ref[i, c] + extra).astype(BF16)
+    decays = []
     for part in range(per + with_c):
         here = slice(part * CHUNK, (part + 1) * CHUNK)
         if part < per:
@@ -477,7 +456,7 @@
         else:
             lanes = slice(channels + gn, channels + 2 * gn)
             taps = [taps_c_ref[j : j + 1, :] for j in range(taps_len)]
-        ext_ref[:8, :] = tail_ref[:, lanes].astype(F32)
+        ext_ref[4:8, :] = tail_ref[:, lanes].astype(F32)
         ext_ref[8:, :] = (x_ref[:, lanes] if part < per else c_ref[...]).astype(F32)
 
         def emit(low, total):
@@ -503,8 +482,9 @@
                 lambda c: xc_ref[0, c * SUB : (c + 1) * SUB, here].astype(F32),
                 h_put,
             )
-            send_ref[:STATE, here] = state.astype(BF16)
-            send_ref[STATE:, here] = decay.astype(BF16)
+            put_piece(send_ref, part * (CHUNK // LANES), state)
+            decays.append(decay)
+    put_decay(send_ref, jnp.concatenate(decays, 1))
 
 
 def late(k, tail, age, tab, d, bc, taps_x, x, with_c=()):
@@ -520,7 +500,7 @@
             *extra_out,
             shape((1, tok, owned), BF16),
             shape((1, subs, STATE, owned), BF16),
-            shape((STATE + 8, owned), BF16),
+            piece_shape(owned),
         ),
         in_specs=[VMEM] * (7 + len(with_c)),
         out_specs=(VMEM,) * (3 + len(extra_out)),
@@ -567,8 +547,11 @@
         return values
 
     owned = total_ref.shape[1]
-    tables = [ref[STATE:, :].astype(F32) for ref in pieces]
-    decays = in_order([row[0:1] + (row[1:2] + row[2:3]) for row in tables])
+    tiles = owned // LANES
+    rows = [ref[tiles * STATE :, :].astype(F32) for ref in pieces]
+    decays = in_order(
+        [jnp.concatenate([row[2 * t : 2 * t + 1] + row[2 * t + 1 : 2 * t + 2] for t in range(tiles)], 1) for row in rows]
+    )
     pre = jnp.ones((1, owned), F32)
     for i in range(CLUSTER):
         pre_ref[i] = jnp.broadcast_to(pre, (8, owned))
@@ -578,7 +561,8 @@
         lanes = slice(at, at + LANES)
         for low in range(0, STATE, 64):
             rows = slice(low, low + 64)
-            values = in_order([ref[rows, lanes].astype(F32) for ref in pieces])
+            at_rows = slice(at + low, at + low + 64)
+            values = in_order([ref[at_rows, :].astype(F32) for ref in pieces])
             local_ref[0, rows, lanes] = jnp.zeros((64, LANES), F32)
             state = values[0]
             for i in range(1, CLUSTER):
@@ -589,7 +573,7 @@
 
 def scan_blocks(pieces):
     operands = (collect(pieces[: 1 + EARLY]), *pieces[1 + EARLY :])
-    owned = pieces[0].shape[1]
+    owned = pieces[0].shape[0] // (STATE + 2) * LANES
     return pl.pallas_call(
         scan_kernel,
         out_shape=(
@@ -821,23 +805,21 @@
     groups = b_input.shape[1] // STATE
     count = lax.axis_size("seq")
     pin = lambda value: pltpu.with_memory_space_constraint(value, pltpu.HBM)
-    raw_x, raw_c, raw_taps_c = x_input, c_input, taps_c
-    x_input, b_input, c_input, doc_lengths = pin(x_input), pin(b_input), pin(c_input), pin(doc_lengths)
-    taps_x, taps_b = pin(taps_x), pin(taps_b)
-    tail = lax.ppermute(pack(x_input, b_input, c_input), "seq", [(i, (i + 1) % count) for i in range(count)])
-    tab, tab0, col, row, d, age, taps_x, taps_b, part_x, part_b, xc, bc = conv(
-        doc_lengths, pin(dt_input.T), pin(decay_rate[None, :]), x_input, b_input, taps_x, taps_b
+    ends = pack(pin(x_input), pin(b_input), pin(c_input))
+    tail = lax.ppermute(ends, "seq", [(i, (i + 1) % count) for i in range(count)])
+    tab, tab0, col, row, d, age, part_x, part_b, xc, bc = conv(
+        doc_lengths, dt_input.T, decay_rate[None, :], x_input, b_input, taps_x, taps_b
     )
     state, others, decay, weight = states(tab, d, xc, bc)
     xc, bc, extra, *sends = with_head(tail, part_x, part_b, taps_x, taps_b, age, state, decay, weight, xc, bc)
-    known = (tail, age, tab, d, bc, taps_x, raw_x)
+    known = (tail, age, tab, d, bc, taps_x, x_input)
     xs, hs = [None] + [xc] * EARLY, [None] * (1 + EARLY)
     for k in range(1 + EARLY, CLUSTER):
         late_x, late_h, late_send = late(k, *known)
         xs.append(late_x)
         hs.append(late_h)
         sends.append(late_send)
-    cc, early_h, xs[0], hs[0], own_send = late(0, *known, (raw_c, raw_taps_c, others, extra, decay))
+    cc, early_h, xs[0], hs[0], own_send = late(0, *known, (c_input, taps_c, others, extra, decay))
     hs[1 : 1 + EARLY] = [early_h] * EARLY
     shared = (bc, cc, tab, tab0, col, row)
     share = CLUSTER // groups

time: 36.8 us -> 36.2 us (0.984)
    pallas_call x1, Pallas kernels: 3.59 us -> 2.99 us  [conv(): pl.pallas_call(conv_kernel, out_shape=(shape((tok, LANES), BF16), shape((...]
    ppermute x7, waiting for transfers between devices: 6.91 us -> 6.39 us  [moved(): lax.ppermute(value, 'seq', [(i, hop(i)) for i in range(count) if 0 <= hop...]
  transfers between devices with their start and end apart: 8 -> 8, of which waited for: 6 -> 5; matrix products, arithmetic and copies ran while one was open for 0% -> 0% of each run, Pallas kernels for 39% -> 38%
where the time goes in v6:
time: 36.2 us; the launch traced here: 36 us
  Pallas kernels  16.7 us (46%)
  starting transfers between devices  11.9 us (33%)
  waiting for transfers between devices  7.24 us (20%)
    ppermute x7, starting transfers between devices, moved(): lax.ppermute(value, 'seq', [(i, hop(i)) for i in range(count) if 0 <= hop...  8.91 us
    ppermute x7, waiting for transfers between devices, moved(): lax.ppermute(value, 'seq', [(i, hop(i)) for i in range(count) if 0 <= hop...  6.39 us
    pallas_call x2, Pallas kernels, intra(): pl.pallas_call(functools.partial(intra_kernel, pieces, heads, head_dim),...  5.66 us
    pallas_call x1, Pallas kernels, conv(): pl.pallas_call(conv_kernel, out_shape=(shape((tok, LANES), BF16), shape((...  2.99 us
    ppermute x1, starting transfers between devices, on_device(): lax.ppermute(ends, 'seq', [(i, (i + 1) % count) for i in range(count)])  2.95 us
    pallas_call x2, Pallas kernels, final(): pl.pallas_call(functools.partial(final_kernel, turn, groups), out_shape=j...  2.79 us
    pallas_call x2, Pallas kernels, late(): pl.pallas_call(functools.partial(late_kernel, k, bool(with_c)), out_shape...  2.78 us
    pallas_call x1, Pallas kernels, pack(): pl.pallas_call(pack_kernel, out_shape=jax.ShapeDtypeStruct((4, sum(widths...  0.91 us
  transfers between devices with their start and end apart: 8, of which 5 were waited for; matrix products, arithmetic and copies ran while one was open for 0% of the time, Pallas kernels for 38%

profile of v6, /device:TPU:0, one launch (start us, length us, event | category | flops | bytes accessed | tf_op | source)
XLA Modules:
  0.0 36.0 jit_solution(18281445359506493307)
XLA Ops:
  0.0 0.0 copy-start
  0.0 0.0 copy-start.3
  0.0 0.0 copy-start.4
  0.0 0.0 copy-start.7
  0.0 0.0 copy-start.9
  0.0 0.0 copy-start.10
  0.0 0.0 copy-start.5
  0.0 0.9 %pack.1 = bf16[4,2560]{1,0:T(4,128)(2,1)S(1)} custom-call(bf16[384,2048]{1,0:T(8,128)(2,1)} %refs_6_.3, bf16[384,256]{1,0:T(8,128)(2,1)} %b_ref.3, bf16[384,256]{1,0:T(8,128)(2,1)} %refs_7_.1), custom_call_target="tpu_custom_call" | custom-call | tf_op jit(solution)/shard_map/pack/pallas_call | solution.py:135
  0.9 3.0 %collective-permute-start = (bf16[4,2560]{1,0:T(4,128)(2,1)S(1)}, bf16[4,2560]{1,0:T(4,128)(2,1)S(1)}, u32[]{:S(2)}, u32[]{:S(2)}) collective-permute-start(bf16[4,2560]{1,0:T(4,128)(2,1)S(1)} %pack.1), channel_id=1, source_target_pairs={{0,2},{2,4},{4,6},{6,8},{8,10},{10,12},{12,14},{14,0},{1,3},{3,5},... | collective-permute-start | bytes 61448 | tf_op jit(solution)/shard_map/ppermute | solution.py:809
  3.9 0.0 copy-done
  3.9 0.0 copy-done.3
  3.9 0.0 copy-done.4
  3.9 0.0 copy-done.7
  3.9 0.0 copy-done.9
  3.9 0.0 copy-done.10
  3.9 0.0 copy-done.5
  3.9 3.0 %conv.1 = (bf16[384,128]{1,0:T(8,128)(2,1)S(1)}, bf16[384,64]{1,0:T(8,128)(2,1)S(1)}, f32[384,128]{1,0:T(8,128)S(1)}, f32[32,384]{1,0:T(8,128)S(1)}, bf16[8,64]{...) custom-call(s32[4]{0:T(128)S(1)} %copy-done.9, ...), custom_call_target="tpu_custom_call" | custom-call | flops 12582912 | bytes 3145728 | tf_op jit(solution)/shard_map/conv/pallas_call | solution.py:266
  6.9 0.9 %state.1 = (f32[2,128,512]{2,1,0:T(8,128)S(1)}, f32[2,2,128,512]{3,2,1,0:T(8,128)S(1)}, f32[2,8,512]{2,1,0:T(8,128)S(1)}, f32[2,8,512]{2,1,0:T(8,128)S(1)}) custom-call(bf16[384,128]{1,0:T(8,128)(2,1)S(1)} %get-tuple-element.51.tab_ref.refs_2_, bf16[8,64]{1,0:T(8,128)(2,1)S(1)} %get-tuple-element.52.d_ref.refs_3_, ...), custom_call_target="tpu_custom_call" | custom-call | flops 201326592 | bytes 1572864 | tf_op jit(solution)/shard_map/state/pallas_call | solution.py:328
  7.8 0.9 %collective-permute-done.tail_ref.refs_0_ = bf16[4,2560]{1,0:T(4,128)(2,1)S(1)} collective-permute-done((bf16[4,2560]{1,0:T(4,128)(2,1)S(1)}, bf16[4,2560]{1,0:T(4,128)(2,1)S(1)}, u32[]{:S(2)}, u32[]{:S(2)}) %collective-permute-start) | collective-permute-done | bytes 20512 | tf_op jit(solution)/shard_map/ppermute | solution.py:809
  8.7 0.0 copy-start.2
  8.7 0.0 copy-start.8
  8.7 0.3 head.1
  9.0 0.8 %collective-permute-start.1 = (bf16[520,128]{1,0:T(8,128)(2,1)S(1)}, bf16[520,128]{1,0:T(8,128)(2,1)S(1)}, u32[]{:S(2)}, u32[]{:S(2)}) collective-permute-start(bf16[520,128]{1,0:T(8,128)(2,1)S(1)} %get-tuple-element.68), channel_id=1, source_target_pairs={{0,2},{2,0},{4,6},{6,4},{8,10},{10,8},{12,14},{14,12},{1,3},{3,1},... | collective-permute-start | bytes 399368 | tf_op jit(solution)/shard_map/ppermute | solution.py:761
  9.8 1.6 %collective-permute-start.2 = (bf16[520,128]{1,0:T(8,128)(2,1)S(1)}, bf16[520,128]{1,0:T(8,128)(2,1)S(1)}, u32[]{:S(2)}, u32[]{:S(2)}) collective-permute-start(bf16[520,128]{1,0:T(8,128)(2,1)S(1)} %get-tuple-element.69), channel_id=1, source_target_pairs={{0,4},{2,6},{4,0},{6,2},{8,12},{10,14},{12,8},{14,10},{1,5},{3,7},... | collective-permute-start | bytes 399368 | tf_op jit(solution)/shard_map/ppermute | solution.py:761
  11.4 1.1 %late.1 = (bf16[1,384,512]{2,1,0:T(8,128)(2,1)S(1)}, bf16[1,2,128,512]{3,2,1,0:T(8,128)(2,1)S(1)}, bf16[520,128]{1,0:T(8,128)(2,1)S(1)}) custom-call(bf16[4,2560]{1,0:T(4,128)(2,1)S(1)} %collective-permute-done.tail_ref.refs_0_, s32[384,128]{1,0:T(8,128)S(1)} %get-tuple-element.82.age_ref.refs_1_.refs_6_, ...), custom_call_target="tpu_custom_call" | custom-call | flops 103809024 | bytes 1572864 | tf_op jit(solution)/shard_map/late/pallas_call | solution.py:497
  12.5 1.3 %collective-permute-start.3 = (bf16[520,128]{1,0:T(8,128)(2,1)S(1)}, bf16[520,128]{1,0:T(8,128)(2,1)S(1)}, u32[]{:S(2)}, u32[]{:S(2)}) collective-permute-start(bf16[520,128]{1,0:T(8,128)(2,1)S(1)} %get-tuple-element.70), channel_id=1, source_target_pairs={{0,6},{2,4},{4,2},{6,0},{8,14},{10,12},{12,10},{14,8},{1,7},{3,5},... | collective-permute-start | bytes 399368 | tf_op jit(solution)/shard_map/ppermute | solution.py:761
  13.8 0.0 copy-done.2
  13.8 0.0 copy-done.8
  13.8 1.6 %own.1 = (bf16[384,256]{1,0:T(8,128)(2,1)S(1)}, bf16[2,2,128,512]{3,2,1,0:T(8,128)(2,1)S(1)}, bf16[1,384,512]{2,1,0:T(8,128)(2,1)S(1)}, bf16[1,2,128,512]{3,2,1,0:T(8,128)(2,1)S(1)}, bf16[520,128]{1,0:T(8,128)(2,1)S(1)}) custom-call(bf16[4,2560]{1,0:T(4,128)(2,1)S(1)} %collective-permute-done.tail_ref.refs_0_, ...), custom_call_target="tpu_custom_call" | custom-call | flops 103809024 | bytes 1572864 | tf_op jit(solution)/shard_map/own/pallas_call | solution.py:497
  15.4 0.0 collective-permute-done.1.refs_1_
  15.5 0.1 collective-permute-done.2.refs_2_
  15.6 2.9 %collective-permute-done.3.refs_1_ = bf16[520,128]{1,0:T(8,128)(2,1)S(1)} collective-permute-done((bf16[520,128]{1,0:T(8,128)(2,1)S(1)}, bf16[520,128]{1,0:T(8,128)(2,1)S(1)}, u32[]{:S(2)}, u32[]{:S(2)}) %collective-permute-start.3) | collective-permute-done | bytes 133152 | tf_op jit(solution)/shard_map/ppermute | solution.py:761
  18.5 0.2 cluster_scan.1
  18.7 1.7 %collective-permute-start.4 = (bf16[128,512]{1,0:T(8,128)(2,1)S(1)}, bf16[128,512]{1,0:T(8,128)(2,1)S(1)}, u32[]{:S(2)}, u32[]{:S(2)}) collective-permute-start(bf16[128,512]{1,0:T(8,128)(2,1)S(1)} %get-tuple-element.71), channel_id=1, source_target_pairs={{0,8},{2,10},{4,12},{6,14},{8,0},{10,2},{12,4},{14,6},{1,9},{3,11}... | collective-permute-start | bytes 393224 | tf_op jit(solution)/shard_map/ppermute | solution.py:761
  20.5 0.0 copy-done.1
  20.5 2.8 %intra.2 = (f32[384,512]{1,0:T(8,128)S(1)}, f32[384,512]{1,0:T(8,128)S(1)}, f32[384,512]{1,0:T(8,128)S(1)}, f32[384,512]{1,0:T(8,128)S(1)}) custom-call(bf16[384,256]{1,0:T(8,128)(2,1)S(1)} %get-tuple-element.60.refs_4_.refs_0_, bf16[384,256]{1,0:T(8,128)(2,1)S(1)} %get-tuple-element.63.refs_1_.refs_0_, ...), custom_call_target="tpu_custom_call" | custom-call | flops 201326592 | bytes 4718592 | tf_op jit(solution)/shard_map/intra/pallas_call | solution.py:679
  23.3 2.9 %collective-permute-done.4.before_ref = bf16[128,512]{1,0:T(8,128)(2,1)S(1)} collective-permute-done((bf16[128,512]{1,0:T(8,128)(2,1)S(1)}, bf16[128,512]{1,0:T(8,128)(2,1)S(1)}, u32[]{:S(2)}, u32[]{:S(2)}) %collective-permute-start.4) | collective-permute-done | bytes 131104 | tf_op jit(solution)/shard_map/ppermute | solution.py:761
  26.2 0.1 join.1
  26.3 1.2 %collective-permute-start.7 = (bf16[128,512]{1,0:T(8,128)(2,1)S(1)}, bf16[128,512]{1,0:T(8,128)(2,1)S(1)}, u32[]{:S(2)}, u32[]{:S(2)}) collective-permute-start(bf16[128,512]{1,0:T(8,128)(2,1)S(1)} %get-tuple-element.94), channel_id=1, source_target_pairs={{0,2},{2,0},{4,6},{6,4},{8,10},{10,8},{12,14},{14,12},{1,3},{3,1},... | collective-permute-start | bytes 393224 | tf_op jit(solution)/shard_map/ppermute | solution.py:761
  27.5 0.0 collective-permute-start.5
  27.5 2.4 %collective-permute-start.6 = (bf16[128,512]{1,0:T(8,128)(2,1)S(1)}, bf16[128,512]{1,0:T(8,128)(2,1)S(1)}, u32[]{:S(2)}, u32[]{:S(2)}) collective-permute-start(bf16[128,512]{1,0:T(8,128)(2,1)S(1)} %get-tuple-element.90), channel_id=1, source_target_pairs={{0,6},{2,4},{4,2},{6,0},{8,14},{10,12},{12,10},{14,8},{1,7},{3,5},... | collective-permute-start | bytes 393224 | tf_op jit(solution)/shard_map/ppermute | solution.py:761
  29.9 2.8 %intra.3 = (f32[384,512]{1,0:T(8,128)S(1)}, f32[384,512]{1,0:T(8,128)S(1)}, f32[384,512]{1,0:T(8,128)S(1)}, f32[384,512]{1,0:T(8,128)S(1)}) custom-call(bf16[384,256]{1,0:T(8,128)(2,1)S(1)} %get-tuple-element.60.refs_4_.refs_0_, bf16[384,256]{1,0:T(8,128)(2,1)S(1)} %get-tuple-element.63.refs_1_.refs_0_, ...), custom_call_target="tpu_custom_call" | custom-call | flops 201326592 | bytes 4718592 | tf_op jit(solution)/shard_map/intra/pallas_call | solution.py:679
  32.7 0.0 collective-permute-done.7.refs_7_
  32.8 0.0 copy-done.6
  32.8 1.4 %final.2.refs_8_ = bf16[384,2048]{1,0:T(8,128)(2,1)} custom-call(bf16[384,256]{1,0:T(8,128)(2,1)S(1)} %get-tuple-element.63.refs_1_.refs_0_, f32[1,2048]{1,0:T(1,128)S(1)} %bitcast.4, f32[384,512]{1,0:T(8,128)S(1)} %get-tuple-element.77.refs_2_, f32[384,512]{1,0:T(8,128)S(1)} %get-tuple-element.91.refs_3_, f32[384,512]{1,0:T(8,128)S(1)} %get-tuple-element.92.refs_4_, ...), custom_call_target="tpu_custom_call" | custom-call | flops 100663296 | bytes 3145728 | tf_op jit(solution)/shard_map/final/pallas_call | solution.py:742
  34.2 0.0 collective-permute-done.5.refs_6_
  34.2 0.4 %collective-permute-done.6.refs_7_ = bf16[128,512]{1,0:T(8,128)(2,1)S(1)} collective-permute-done((bf16[128,512]{1,0:T(8,128)(2,1)S(1)}, bf16[128,512]{1,0:T(8,128)(2,1)S(1)}, u32[]{:S(2)}, u32[]{:S(2)}) %collective-permute-start.6) | collective-permute-done | bytes 131104 | tf_op jit(solution)/shard_map/ppermute | solution.py:761
  34.6 1.4 %final.3 = bf16[384,2048]{1,0:T(8,128)(2,1)} custom-call(bf16[384,256]{1,0:T(8,128)(2,1)S(1)} %get-tuple-element.63.refs_1_.refs_0_, f32[1,2048]{1,0:T(1,128)S(1)} %bitcast.5, f32[384,512]{1,0:T(8,128)S(1)} %get-tuple-element.85.refs_2_, f32[384,512]{1,0:T(8,128)S(1)} %get-tuple-element.86.refs_3_, ...), custom_call_target="tpu_custom_call", output_to_operand_aliasing={{}: (8, {})} | custom-call | flops 100663296 | bytes 3145728 | tf_op jit(solution)/shard_map/final/pallas_call | solution.py:742
  (3 shorter events, 0.0 us)
Async XLA Ops:
  0.0 3.9 %copy-start = (bf16[384,2048]{1,0:T(8,128)(2,1)S(1)}, bf16[384,2048]{1,0:T(8,128)(2,1)}, u32[]{:S(2)}) copy-start(bf16[384,2048]{1,0:T(8,128)(2,1)} %refs_6_.3) | copy-start | bytes 4718596
  0.0 3.9 %copy-start.3 = (bf16[384,256]{1,0:T(8,128)(2,1)S(1)}, bf16[384,256]{1,0:T(8,128)(2,1)}, u32[]{:S(2)}) copy-start(bf16[384,256]{1,0:T(8,128)(2,1)} %b_ref.3) | copy-start | bytes 589828
  0.0 3.9 %copy-start.4 = (f32[4,2048]{1,0:T(4,128)S(1)}, f32[4,2048]{1,0:T(4,128)}, u32[]{:S(2)}) copy-start(f32[4,2048]{1,0:T(4,128)} %refs_5_.3) | copy-start | bytes 98308
  0.0 3.9 %copy-start.7 = (f32[4,256]{1,0:T(4,128)S(1)}, f32[4,256]{1,0:T(4,128)}, u32[]{:S(2)}) copy-start(f32[4,256]{1,0:T(4,128)} %taps_b_ref.3) | copy-start | bytes 12292
  0.0 3.9 %copy-start.9 = (s32[4]{0:T(128)S(1)}, s32[4]{0:T(128)}, u32[]{:S(2)}) copy-start(s32[4]{0:T(128)} %dl_ref.1) | copy-start | bytes 52
  0.0 3.9 %copy-start.10 = (f32[32]{0:T(128)S(1)}, f32[32]{0:T(128)}, u32[]{:S(2)}) copy-start(f32[32]{0:T(128)} %param.15) | copy-start | bytes 388
  0.0 3.9 %copy-start.5 = (f32[384,32]{0,1:T(8,128)S(1)}, f32[384,32]{0,1:T(8,128)}, u32[]{:S(2)}) copy-start(f32[384,32]{0,1:T(8,128)} %param.14) | copy-start | bytes 147460
  0.9 7.7 %collective-permute-start = (bf16[4,2560]{1,0:T(4,128)(2,1)S(1)}, bf16[4,2560]{1,0:T(4,128)(2,1)S(1)}, u32[]{:S(2)}, u32[]{:S(2)}) collective-permute-start(bf16[4,2560]{1,0:T(4,128)(2,1)S(1)} %pack.1), channel_id=1, source_target_pairs={{0,2},{2,4},{4,6},{6,8},{8,10},{10,12},{12,14},{14,0},{1,3},{3,5},... | collective-permute-start | bytes 61448 | tf_op jit(solution)/shard_map/ppermute | solution.py:809
  8.7 5.1 %copy-start.2 = (bf16[384,256]{1,0:T(8,128)(2,1)S(1)}, bf16[384,256]{1,0:T(8,128)(2,1)}, u32[]{:S(2)}) copy-start(bf16[384,256]{1,0:T(8,128)(2,1)} %refs_7_.1) | copy-start | bytes 589828
  8.7 5.1 %copy-start.8 = (f32[4,256]{1,0:T(4,128)S(1)}, f32[4,256]{1,0:T(4,128)}, u32[]{:S(2)}) copy-start(f32[4,256]{1,0:T(4,128)} %refs_8_.1) | copy-start | bytes 12292
  9.0 6.4 %collective-permute-start.1 = (bf16[520,128]{1,0:T(8,128)(2,1)S(1)}, bf16[520,128]{1,0:T(8,128)(2,1)S(1)}, u32[]{:S(2)}, u32[]{:S(2)}) collective-permute-start(bf16[520,128]{1,0:T(8,128)(2,1)S(1)} %get-tuple-element.68), channel_id=1, source_target_pairs={{0,2},{2,0},{4,6},{6,4},{8,10},{10,8},{12,14},{14,12},{1,3},{3,1},... | collective-permute-start | bytes 399368 | tf_op jit(solution)/shard_map/ppermute | solution.py:761
  9.8 5.7 %collective-permute-start.2 = (bf16[520,128]{1,0:T(8,128)(2,1)S(1)}, bf16[520,128]{1,0:T(8,128)(2,1)S(1)}, u32[]{:S(2)}, u32[]{:S(2)}) collective-permute-start(bf16[520,128]{1,0:T(8,128)(2,1)S(1)} %get-tuple-element.69), channel_id=1, source_target_pairs={{0,4},{2,6},{4,0},{6,2},{8,12},{10,14},{12,8},{14,10},{1,5},{3,7},... | collective-permute-start | bytes 399368 | tf_op jit(solution)/shard_map/ppermute | solution.py:761
  12.5 6.0 %collective-permute-start.3 = (bf16[520,128]{1,0:T(8,128)(2,1)S(1)}, bf16[520,128]{1,0:T(8,128)(2,1)S(1)}, u32[]{:S(2)}, u32[]{:S(2)}) collective-permute-start(bf16[520,128]{1,0:T(8,128)(2,1)S(1)} %get-tuple-element.70), channel_id=1, source_target_pairs={{0,6},{2,4},{4,2},{6,0},{8,14},{10,12},{12,10},{14,8},{1,7},{3,5},... | collective-permute-start | bytes 399368 | tf_op jit(solution)/shard_map/ppermute | solution.py:761
  13.8 6.7 %copy-start.1 = (bf16[384,2048]{1,0:T(8,128)(2,1)S(1)}, bf16[384,2048]{1,0:T(8,128)(2,1)}, u32[]{:S(2)}) copy-start(bf16[384,2048]{1,0:T(8,128)(2,1)} %refs_12_.3) | copy-start | bytes 4718596
  18.7 7.5 %collective-permute-start.4 = (bf16[128,512]{1,0:T(8,128)(2,1)S(1)}, bf16[128,512]{1,0:T(8,128)(2,1)S(1)}, u32[]{:S(2)}, u32[]{:S(2)}) collective-permute-start(bf16[128,512]{1,0:T(8,128)(2,1)S(1)} %get-tuple-element.71), channel_id=1, source_target_pairs={{0,8},{2,10},{4,12},{6,14},{8,0},{10,2},{12,4},{14,6},{1,9},{3,11}... | collective-permute-start | bytes 393224 | tf_op jit(solution)/shard_map/ppermute | solution.py:761
  26.3 6.4 %collective-permute-start.7 = (bf16[128,512]{1,0:T(8,128)(2,1)S(1)}, bf16[128,512]{1,0:T(8,128)(2,1)S(1)}, u32[]{:S(2)}, u32[]{:S(2)}) collective-permute-start(bf16[128,512]{1,0:T(8,128)(2,1)S(1)} %get-tuple-element.94), channel_id=1, source_target_pairs={{0,2},{2,0},{4,6},{6,4},{8,10},{10,8},{12,14},{14,12},{1,3},{3,1},... | collective-permute-start | bytes 393224 | tf_op jit(solution)/shard_map/ppermute | solution.py:761
  27.5 6.7 %collective-permute-start.5 = (bf16[128,512]{1,0:T(8,128)(2,1)S(1)}, bf16[128,512]{1,0:T(8,128)(2,1)S(1)}, u32[]{:S(2)}, u32[]{:S(2)}) collective-permute-start(bf16[128,512]{1,0:T(8,128)(2,1)S(1)} %get-tuple-element.89), channel_id=1, source_target_pairs={{0,4},{2,6},{4,0},{6,2},{8,12},{10,14},{12,8},{14,10},{1,5},{3,7},... | collective-permute-start | bytes 393224 | tf_op jit(solution)/shard_map/ppermute | solution.py:761
  27.5 7.1 %collective-permute-start.6 = (bf16[128,512]{1,0:T(8,128)(2,1)S(1)}, bf16[128,512]{1,0:T(8,128)(2,1)S(1)}, u32[]{:S(2)}, u32[]{:S(2)}) collective-permute-start(bf16[128,512]{1,0:T(8,128)(2,1)S(1)} %get-tuple-element.90), channel_id=1, source_target_pairs={{0,6},{2,4},{4,2},{6,0},{8,14},{10,12},{12,10},{14,8},{1,7},{3,5},... | collective-permute-start | bytes 393224 | tf_op jit(solution)/shard_map/ppermute | solution.py:761
  29.9 2.9 %copy-start.6 = (f32[2048]{0:T(1024)S(1)}, f32[2048]{0:T(1024)}, u32[]{:S(2)}) copy-start(f32[2048]{0:T(1024)} %param.20) | copy-start | bytes 24580

commit v7 on v6

--- a/solution.py
+++ b/solution.py
@@ -83,36 +83,35 @@
         copy.wait()
 
 
-def tables(row0, edges, dt_ref, rate_ref, tab_ref, tab0_ref, col_ref, row_ref, d_ref):
+def steps_of(row0, edges, dt_ref, rate_ref):
     heads, tok = dt_ref.shape
     upto = jnp.where(
         lax.broadcasted_iota(jnp.int32, (SUB, SUB), 0) <= lax.broadcasted_iota(jnp.int32, (SUB, SUB), 1), 1.0, 0.0
     ).astype(BF16)
     rate = jnp.concatenate([rate_ref[...], jnp.zeros((1, LANES - heads), F32)], 1)
     rate = jnp.broadcast_to(rate, (LANES, LANES)).T[:heads]
-    total = jnp.zeros((heads, 1), F32)
-    decays = []
+    found = []
     for c in range(tok // SUB):
         span = slice(c * SUB, (c + 1) * SUB)
-        first = row0 + c * SUB
         dt = dt_ref[:, span]
         step = jnp.maximum(dt, 0.0) + jnp.log1p(jnp.exp(-jnp.abs(dt)))
         parts = split3(-(step * rate))
         cum = mm(parts[0], upto) + (mm(parts[1], upto) + mm(parts[2], upto))
+        token = row0 + c * SUB + lax.broadcasted_iota(jnp.int32, (heads, SUB), 1)
+        found.append((span, row0 + c * SUB, step, cum, token))
+    return found
+
+
+def end_tables(row0, edges, dt_ref, rate_ref, tab_ref, d_ref):
+    heads, tok = dt_ref.shape
+    total = jnp.zeros((heads, 1), F32)
+    decays = []
+    for span, first, step, cum, token in steps_of(row0, edges, dt_ref, rate_ref):
         last = cum[:, SUB - 1 :]
-        token = first + lax.broadcasted_iota(jnp.int32, (heads, SUB), 1)
-        start = doc_start(token, edges)
         last_start = doc_start(jnp.int32(first + SUB - 1), edges)
         to_end = jnp.exp(last - cum) * step * jnp.where(token >= last_start, 1.0, 0.0)
-        since_sub = jnp.exp(cum) * jnp.where((start < first) & (c > 0), 1.0, 0.0)
-        since_block = jnp.exp(cum + total) * jnp.where(start < row0, 1.0, 0.0)
-        first_pair = [part.astype(F32) for part in (*split2(to_end), *split2(since_sub))]
-        second_pair = [part.astype(F32) for part in split2(since_block)] + [cum * LOG2E, jnp.zeros_like(cum)]
-        tab_ref[span, :] = jnp.concatenate(first_pair, 0).T.astype(BF16)
-        second = jnp.concatenate(second_pair, 0).T
-        tab0_ref[span, :] = second[:, : 2 * heads].astype(BF16)
-        col_ref[span, :] = second
-        row_ref[:, span] = (jnp.log(step) - cum) * LOG2E
+        pair = [part.astype(F32) for part in split2(to_end)] + [jnp.zeros((LANES - 2 * heads, SUB), F32)]
+        tab_ref[span, :] = jnp.concatenate(pair, 0).T[:, : 2 * heads].astype(BF16)
         decays.append(jnp.exp(last) * jnp.where(last_start < first, 1.0, 0.0))
         total = total + last
     end_start = doc_start(jnp.int32(row0 + tok - 1), edges)
@@ -122,6 +121,21 @@
     columns = jnp.concatenate([jnp.concatenate(columns, 1), jnp.zeros((LANES - heads, LANES), F32)], 0)
     halves = [part.astype(F32)[:, :heads] for part in split2(columns.T[:8])]
     d_ref[...] = jnp.concatenate(halves, 1).astype(BF16)
+
+
+def inner_tables(row0, edges, dt_ref, rate_ref, tab_ref, col_ref, row_ref):
+    heads = dt_ref.shape[0]
+    total = jnp.zeros((heads, 1), F32)
+    for span, first, step, cum, token in steps_of(row0, edges, dt_ref, rate_ref):
+        start = doc_start(token, edges)
+        since_sub = jnp.exp(cum) * jnp.where((start < first) & (first > row0), 1.0, 0.0)
+        since_block = jnp.exp(cum + total) * jnp.where(start < row0, 1.0, 0.0)
+        pairs = [part.astype(F32) for part in (*split2(since_block), *split2(since_sub))]
+        tab_ref[span, :] = jnp.concatenate(pairs, 0).T.astype(BF16)
+        zero = jnp.zeros_like(cum)
+        col_ref[span, :] = jnp.concatenate([zero, zero, cum * LOG2E, zero], 0).T
+        row_ref[:, span] = (jnp.log(step) - cum) * LOG2E
+        total = total + cum[:, SUB - 1 :]
 
 
 def pack_kernel(x_ref, b_ref, c_ref, out_ref):
@@ -171,7 +185,7 @@
     state = None
     for c in range(tok // SUB):
         rows = slice(c * SUB, (c + 1) * SUB)
-        weight = mm(tab_ref[rows, : 2 * heads], one_hot)
+        weight = mm(tab_ref[rows, :], one_hot)
         if c == 0:
             head_weight = weight[:8]
         local = mm(bt_ref[:, rows], (x_rows(c) * weight).astype(BF16))
@@ -208,9 +222,6 @@
     taps_x_ref,
     taps_b_ref,
     tab_ref,
-    tab0_ref,
-    col_ref,
-    row_ref,
     d_ref,
     age_ref,
     part_x_ref,
@@ -225,7 +236,7 @@
     per = owned // CHUNK
     row0 = lax.axis_index("seq") * tok
     edges = doc_edges(dl_ref)
-    tables(row0, edges, dt_ref, rate_ref, tab_ref, tab0_ref, col_ref, row_ref, d_ref)
+    end_tables(row0, edges, dt_ref, rate_ref, tab_ref, d_ref)
     token = row0 + lax.broadcasted_iota(jnp.int32, (tok, LANES), 0)
     age_ref[...] = token - doc_start(token, edges)
     fill_masks(age_ref, mask_ref)
@@ -266,10 +277,7 @@
     return pl.pallas_call(
         conv_kernel,
         out_shape=(
-            shape((tok, LANES), BF16),
             shape((tok, 2 * heads), BF16),
-            shape((tok, LANES), F32),
-            shape((heads, tok), F32),
             shape((8, 2 * heads), BF16),
             shape((tok, LANES), jnp.int32),
             shape((EARLY, 8, owned), F32),
@@ -278,7 +286,7 @@
             shape((tok, gn), BF16),
         ),
         in_specs=[pl.BlockSpec(memory_space=pltpu.SMEM)] + [VMEM] * 6,
-        out_specs=(VMEM,) * 10,
+        out_specs=(VMEM,) * 7,
         scratch_shapes=[
             pltpu.VMEM((tok + 8, CHUNK), F32),
             pltpu.VMEM((taps_x.shape[0] - 1, tok, LANES), F32),
@@ -425,8 +433,9 @@
     tail_ref, age_ref, tab_ref, d_ref, bc_ref, taps_x_ref, x_ref = refs[:7]
     refs = refs[7:]
     if with_c:
-        c_ref, taps_c_ref, others_ref, extra_ref, decay_ref, cc_ref, early_ref = refs[:7]
-        refs = refs[7:]
+        c_ref, taps_c_ref, others_ref, extra_ref, decay_ref, dt_ref, rate_ref, dl_ref = refs[:8]
+        cc_ref, early_ref, inner_ref, col_ref, row_ref = refs[8:13]
+        refs = refs[13:]
     xc_ref, h_ref, send_ref, bt_ref, ext_ref, mask_ref = refs
     tok, channels = x_ref.shape
     owned = channels // CLUSTER
@@ -441,6 +450,8 @@
     b_blk = bc_ref[:, pl.ds(pl.multiple_of(group * STATE, STATE), STATE)]
     bt_ref[...] = b_blk.astype(F32).T.astype(BF16)
     if with_c:
+        row0 = lax.axis_index("seq") * tok
+        inner_tables(row0, doc_edges(dl_ref), dt_ref, rate_ref, inner_ref, col_ref, row_ref)
         for i in range(EARLY):
             extra = extra_ref[i]
             for c in range(tok // SUB - 1):
@@ -493,7 +504,16 @@
     gn = bc.shape[1]
     subs = tok // SUB - 1
     shape = jax.ShapeDtypeStruct
-    extra_out = (shape((tok, gn), BF16), shape((EARLY, subs, STATE, owned), BF16)) if with_c else ()
+    heads = d.shape[1] // 2
+    extra_out = (
+        shape((tok, gn), BF16),
+        shape((EARLY, subs, STATE, owned), BF16),
+        shape((tok, LANES), BF16),
+        shape((tok, LANES), F32),
+        shape((heads, tok), F32),
+    )
+    if not with_c:
+        extra_out = ()
     return pl.pallas_call(
         functools.partial(late_kernel, k, bool(with_c)),
         out_shape=(
@@ -502,7 +522,7 @@
             shape((1, subs, STATE, owned), BF16),
             piece_shape(owned),
         ),
-        in_specs=[VMEM] * (7 + len(with_c)),
+        in_specs=[VMEM] * 7 + ([VMEM] * (len(with_c) - 1) + [pl.BlockSpec(memory_space=pltpu.SMEM)] if with_c else []),
         out_specs=(VMEM,) * (3 + len(extra_out)),
         scratch_shapes=[
             pltpu.VMEM((STATE, tok), BF16),
@@ -616,11 +636,11 @@
 
 
 def intra_kernel(pieces, heads, head_dim, *refs):
-    bc_ref, cc_ref, tab_ref, tab0_ref, col_ref, row_ref, age_ref = refs[:7]
+    bc_ref, cc_ref, tab_ref, col_ref, row_ref, age_ref = refs[:6]
+    refs = refs[6:]
     count = len(pieces)
-    xs, hs, gates = refs[7 : 7 + count], refs[7 + count : 7 + 2 * count], refs[7 + 2 * count : 7 + 3 * count]
-    parts, scales = refs[7 + 3 * count : 7 + 4 * count], refs[7 + 4 * count : 7 + 5 * count]
-    hot_ref, hot0_ref = refs[7 + 5 * count :]
+    xs, hs, gates, parts, scales = (refs[i * count : (i + 1) * count] for i in range(5))
+    hot_ref, hot0_ref = refs[5 * count :]
     owned = parts[0].shape[1]
     per_piece = owned // head_dim
     mine = lax.axis_index("seq") % CLUSTER
@@ -656,14 +676,14 @@
             inner = inner + mm(c_blk, hs[p][0, 0, :, lanes]) * mm(tab_ref[...], hot_ref[p, :, lanes])
             gate = silu(gates[p][:, lanes].astype(F32))
             parts[p][:, lanes] = inner * gate
-            scales[p][:, lanes] = mm(tab0_ref[...], hot0_ref[p, :, lanes]) * gate
+            scales[p][:, lanes] = mm(tab_ref[:, : 2 * heads], hot0_ref[p, :, lanes]) * gate
 
 
 def early_index(k):
     return k - 1 if 1 <= k <= EARLY else 0
 
 
-def intra(turn, pieces, bc, cc, tab, tab0, col, row, age, xs, hs, gate):
+def intra(turn, pieces, bc, cc, tab, col, row, age, xs, hs, gate):
     tok, gn = bc.shape
     heads = row.shape[0]
     channels = gate.shape[1]
@@ -684,7 +704,6 @@
             pl.BlockSpec((SUB, STATE), lambda i: (i, group_at(turn, groups))),
             pl.BlockSpec((SUB, STATE), lambda i: (i, group_at(turn, groups))),
             pl.BlockSpec((SUB, tab.shape[1]), lambda i: (i, 0)),
-            pl.BlockSpec((SUB, tab0.shape[1]), lambda i: (i, 0)),
             pl.BlockSpec((SUB, LANES), lambda i: (i, 0)),
             pl.BlockSpec((heads, SUB), lambda i: (0, i)),
             pl.BlockSpec((SUB, LANES), lambda i: (i, 0)),
@@ -697,7 +716,7 @@
         compiler_params=params(16),
         cost_estimate=cost(tok * SUB * owned * count * 4, tok * owned * count * 12, tok * SUB * owned * count // head_dim),
         name="intra",
-    )(bc, cc, tab, tab0, col, row, age, *xs, *hs, *([gate] * count))
+    )(bc, cc, tab, col, row, age, *xs, *hs, *([gate] * count))
 
 
 def final_kernel(turn, groups, *refs):
@@ -807,9 +826,8 @@
     pin = lambda value: pltpu.with_memory_space_constraint(value, pltpu.HBM)
     ends = pack(pin(x_input), pin(b_input), pin(c_input))
     tail = lax.ppermute(ends, "seq", [(i, (i + 1) % count) for i in range(count)])
-    tab, tab0, col, row, d, age, part_x, part_b, xc, bc = conv(
-        doc_lengths, dt_input.T, decay_rate[None, :], x_input, b_input, taps_x, taps_b
-    )
+    rates = (dt_input.T, decay_rate[None, :])
+    tab, d, age, part_x, part_b, xc, bc = conv(doc_lengths, *rates, x_input, b_input, taps_x, taps_b)
     state, others, decay, weight = states(tab, d, xc, bc)
     xc, bc, extra, *sends = with_head(tail, part_x, part_b, taps_x, taps_b, age, state, decay, weight, xc, bc)
     known = (tail, age, tab, d, bc, taps_x, x_input)
@@ -819,9 +837,11 @@
         xs.append(late_x)
         hs.append(late_h)
         sends.append(late_send)
-    cc, early_h, xs[0], hs[0], own_send = late(0, *known, (c_input, taps_c, others, extra, decay))
+    cc, early_h, inner_tab, col, row, xs[0], hs[0], own_send = late(
+        0, *known, (c_input, taps_c, others, extra, decay, *rates, doc_lengths)
+    )
     hs[1 : 1 + EARLY] = [early_h] * EARLY
-    shared = (bc, cc, tab, tab0, col, row)
+    shared = (bc, cc, inner_tab, col, row)
     share = CLUSTER // groups
 
     def inner(turn, age):

time: 36.2 us -> 36.2 us (level)
  Pallas kernels: 16.7 us -> 17.4 us
  waiting for transfers between devices: 7.24 us -> 6.6 us
    ppermute x7, waiting for transfers between devices: 6.39 us -> 5.71 us  [moved(): lax.ppermute(value, 'seq', [(i, hop(i)) for i in range(count) if 0 <= hop...]
    pallas_call x2, Pallas kernels: 2.78 us -> 3.45 us  [late(): pl.pallas_call(functools.partial(late_kernel, k, bool(with_c)), out_shape...]
  transfers between devices with their start and end apart: 8 -> 8, of which waited for: 5 -> 4; matrix products, arithmetic and copies ran while one was open for 0% -> 0% of each run, Pallas kernels for 38% -> 40%
where the time goes in v7:
time: 36.2 us; the launch traced here: 36.1 us
  Pallas kernels  17.4 us (48%)
  starting transfers between devices  11.9 us (33%)
  waiting for transfers between devices  6.6 us (18%)
    ppermute x7, starting transfers between devices, moved(): lax.ppermute(value, 'seq', [(i, hop(i)) for i in range(count) if 0 <= hop...  8.92 us
    ppermute x7, waiting for transfers between devices, moved(): lax.ppermute(value, 'seq', [(i, hop(i)) for i in range(count) if 0 <= hop...  5.71 us
    pallas_call x2, Pallas kernels, intra(): pl.pallas_call(functools.partial(intra_kernel, pieces, heads, head_dim),...  5.67 us
    pallas_call x2, Pallas kernels, late(): pl.pallas_call(functools.partial(late_kernel, k, bool(with_c)), out_shape...  3.45 us
    pallas_call x1, Pallas kernels, conv(): pl.pallas_call(conv_kernel, out_shape=(shape((tok, 2 * heads), BF16), sha...  2.96 us
    ppermute x1, starting transfers between devices, on_device(): lax.ppermute(ends, 'seq', [(i, (i + 1) % count) for i in range(count)])  2.95 us
    pallas_call x2, Pallas kernels, final(): pl.pallas_call(functools.partial(final_kernel, turn, groups), out_shape=j...  2.79 us
    pallas_call x1, Pallas kernels, pack(): pl.pallas_call(pack_kernel, out_shape=jax.ShapeDtypeStruct((4, sum(widths...  0.91 us
  transfers between devices with their start and end apart: 8, of which 4 were waited for; matrix products, arithmetic and copies ran while one was open for 0% of the time, Pallas kernels for 40%

profile of v7, /device:TPU:0, one launch (start us, length us, event | category | flops | bytes accessed | tf_op | source)
XLA Modules:
  0.0 36.1 jit_solution(908728114514653817)
XLA Ops:
  0.0 0.0 copy-start
  0.0 0.0 copy-start.3
  0.0 0.0 copy-start.4
  0.0 0.0 copy-start.7
  0.0 0.0 copy-start.10
  0.0 0.0 copy-start.5
  0.0 0.9 %pack.1 = bf16[4,2560]{1,0:T(4,128)(2,1)S(1)} custom-call(bf16[384,2048]{1,0:T(8,128)(2,1)} %refs_6_.3, bf16[384,256]{1,0:T(8,128)(2,1)} %b_ref.3, bf16[384,256]{1,0:T(8,128)(2,1)} %refs_7_.1), custom_call_target="tpu_custom_call" | custom-call | tf_op jit(solution)/shard_map/pack/pallas_call | solution.py:149
  0.9 3.0 %collective-permute-start = (bf16[4,2560]{1,0:T(4,128)(2,1)S(1)}, bf16[4,2560]{1,0:T(4,128)(2,1)S(1)}, u32[]{:S(2)}, u32[]{:S(2)}) collective-permute-start(bf16[4,2560]{1,0:T(4,128)(2,1)S(1)} %pack.1), channel_id=1, source_target_pairs={{0,2},{2,4},{4,6},{6,8},{8,10},{10,12},{12,14},{14,0},{1,3},{3,5},... | collective-permute-start | bytes 61448 | tf_op jit(solution)/shard_map/ppermute | solution.py:828
  3.9 0.0 copy-done
  3.9 0.0 copy-done.3
  3.9 0.0 copy-done.4
  3.9 0.0 copy-done.9
  3.9 0.0 copy-done.7
  3.9 0.0 copy-done.10
  3.9 0.0 copy-done.5
  3.9 3.0 %conv.1 = (bf16[384,64]{1,0:T(8,128)(2,1)S(1)}, bf16[8,64]{1,0:T(8,128)(2,1)S(1)}, s32[384,128]{1,0:T(8,128)S(1)}, f32[2,8,512]{2,1,0:T(8,128)S(1)}, f32[8,256]{...) custom-call(s32[4]{0:T(128)S(1)} %copy-done.9, f32[32,384]{1,0:T(8,128)S(1)} %bitcast.3, ...), custom_call_target="tpu_custom_call" | custom-call | flops 12582912 | bytes 3145728 | tf_op jit(solution)/shard_map/conv/pallas_call | solution.py:277
  6.9 0.9 %state.1 = (f32[2,128,512]{2,1,0:T(8,128)S(1)}, f32[2,2,128,512]{3,2,1,0:T(8,128)S(1)}, f32[2,8,512]{2,1,0:T(8,128)S(1)}, f32[2,8,512]{2,1,0:T(8,128)S(1)}) custom-call(bf16[384,64]{1,0:T(8,128)(2,1)S(1)} %get-tuple-element.51.tab_ref.refs_2_, bf16[8,64]{1,0:T(8,128)(2,1)S(1)} %get-tuple-element.52.d_ref.refs_3_, ...), custom_call_target="tpu_custom_call" | custom-call | flops 201326592 | bytes 1572864 | tf_op jit(solution)/shard_map/state/pallas_call | solution.py:336
  7.8 0.9 %collective-permute-done.tail_ref.refs_0_ = bf16[4,2560]{1,0:T(4,128)(2,1)S(1)} collective-permute-done((bf16[4,2560]{1,0:T(4,128)(2,1)S(1)}, bf16[4,2560]{1,0:T(4,128)(2,1)S(1)}, u32[]{:S(2)}, u32[]{:S(2)}) %collective-permute-start) | collective-permute-done | bytes 20512 | tf_op jit(solution)/shard_map/ppermute | solution.py:828
  8.7 0.0 copy-start.2
  8.7 0.0 copy-start.8
  8.7 0.3 head.1
  9.0 0.8 %collective-permute-start.1 = (bf16[520,128]{1,0:T(8,128)(2,1)S(1)}, bf16[520,128]{1,0:T(8,128)(2,1)S(1)}, u32[]{:S(2)}, u32[]{:S(2)}) collective-permute-start(bf16[520,128]{1,0:T(8,128)(2,1)S(1)} %get-tuple-element.68), channel_id=1, source_target_pairs={{0,2},{2,0},{4,6},{6,4},{8,10},{10,8},{12,14},{14,12},{1,3},{3,1},... | collective-permute-start | bytes 399368 | tf_op jit(solution)/shard_map/ppermute | solution.py:780
  9.8 1.6 %collective-permute-start.2 = (bf16[520,128]{1,0:T(8,128)(2,1)S(1)}, bf16[520,128]{1,0:T(8,128)(2,1)S(1)}, u32[]{:S(2)}, u32[]{:S(2)}) collective-permute-start(bf16[520,128]{1,0:T(8,128)(2,1)S(1)} %get-tuple-element.69), channel_id=1, source_target_pairs={{0,4},{2,6},{4,0},{6,2},{8,12},{10,14},{12,8},{14,10},{1,5},{3,7},... | collective-permute-start | bytes 399368 | tf_op jit(solution)/shard_map/ppermute | solution.py:780
  11.4 1.1 %late.1 = (bf16[1,384,512]{2,1,0:T(8,128)(2,1)S(1)}, bf16[1,2,128,512]{3,2,1,0:T(8,128)(2,1)S(1)}, bf16[520,128]{1,0:T(8,128)(2,1)S(1)}) custom-call(bf16[4,2560]{1,0:T(4,128)(2,1)S(1)} %collective-permute-done.tail_ref.refs_0_, s32[384,128]{1,0:T(8,128)S(1)} %get-tuple-element.82.age_ref.refs_1_.refs_5_, ...), custom_call_target="tpu_custom_call" | custom-call | flops 103809024 | bytes 1572864 | tf_op jit(solution)/shard_map/late/pallas_call | solution.py:517
  12.5 1.3 %collective-permute-start.3 = (bf16[520,128]{1,0:T(8,128)(2,1)S(1)}, bf16[520,128]{1,0:T(8,128)(2,1)S(1)}, u32[]{:S(2)}, u32[]{:S(2)}) collective-permute-start(bf16[520,128]{1,0:T(8,128)(2,1)S(1)} %get-tuple-element.70), channel_id=1, source_target_pairs={{0,6},{2,4},{4,2},{6,0},{8,14},{10,12},{12,10},{14,8},{1,7},{3,5},... | collective-permute-start | bytes 399368 | tf_op jit(solution)/shard_map/ppermute | solution.py:780
  13.8 0.0 copy-done.2
  13.8 0.0 copy-done.8
  13.8 0.0 copy-start.1
  13.8 2.3 %own.1 = (bf16[384,256]{1,0:T(8,128)(2,1)S(1)}, bf16[2,2,128,512]{3,2,1,0:T(8,128)(2,1)S(1)}, bf16[384,128]{1,0:T(8,128)(2,1)S(1)}, f32[384,128]{1,0:T(8,128)S(1...) custom-call(bf16[4,2560]{1,0:T(4,128)(2,1)S(1)} %collective-permute-, ...), custom_call_target="tpu_custom_call" | custom-call | flops 103809024 | bytes 1572864 | tf_op jit(solution)/shard_map/own/pallas_call | solution.py:517
  16.1 0.0 collective-permute-done.1.refs_1_
  16.1 0.0 collective-permute-done.2.refs_2_
  16.2 2.3 %collective-permute-done.3.refs_1_ = bf16[520,128]{1,0:T(8,128)(2,1)S(1)} collective-permute-done((bf16[520,128]{1,0:T(8,128)(2,1)S(1)}, bf16[520,128]{1,0:T(8,128)(2,1)S(1)}, u32[]{:S(2)}, u32[]{:S(2)}) %collective-permute-start.3) | collective-permute-done | bytes 133152 | tf_op jit(solution)/shard_map/ppermute | solution.py:780
  18.5 0.2 cluster_scan.1
  18.7 1.7 %collective-permute-start.4 = (bf16[128,512]{1,0:T(8,128)(2,1)S(1)}, bf16[128,512]{1,0:T(8,128)(2,1)S(1)}, u32[]{:S(2)}, u32[]{:S(2)}) collective-permute-start(bf16[128,512]{1,0:T(8,128)(2,1)S(1)} %get-tuple-element.71), channel_id=1, source_target_pairs={{0,8},{2,10},{4,12},{6,14},{8,0},{10,2},{12,4},{14,6},{1,9},{3,11}... | collective-permute-start | bytes 393224 | tf_op jit(solution)/shard_map/ppermute | solution.py:780
  20.4 0.0 copy-done.1
  20.4 2.8 %intra.2 = (f32[384,512]{1,0:T(8,128)S(1)}, f32[384,512]{1,0:T(8,128)S(1)}, f32[384,512]{1,0:T(8,128)S(1)}, f32[384,512]{1,0:T(8,128)S(1)}) custom-call(bf16[384,256]{1,0:T(8,128)(2,1)S(1)} %get-tuple-element.60.refs_4_.refs_0_, bf16[384,256]{1,0:T(8,128)(2,1)S(1)} %get-tuple-element.63.refs_1_.refs_0_, bf16[384,128]{1,0:T(8,128)(2,1)S(1)} %get-tuple-element.64.refs_2_, ...), custom_call_target="tpu_custom_call" | custom-call | flops 201326592 | bytes 4718592 | tf_op jit(solution)/shard_map/intra/pallas_call | solution.py:699
  23.3 2.9 %collective-permute-done.4.before_ref = bf16[128,512]{1,0:T(8,128)(2,1)S(1)} collective-permute-done((bf16[128,512]{1,0:T(8,128)(2,1)S(1)}, bf16[128,512]{1,0:T(8,128)(2,1)S(1)}, u32[]{:S(2)}, u32[]{:S(2)}) %collective-permute-start.4) | collective-permute-done | bytes 131104 | tf_op jit(solution)/shard_map/ppermute | solution.py:780
  26.2 0.1 join.1
  26.3 1.1 %collective-permute-start.7 = (bf16[128,512]{1,0:T(8,128)(2,1)S(1)}, bf16[128,512]{1,0:T(8,128)(2,1)S(1)}, u32[]{:S(2)}, u32[]{:S(2)}) collective-permute-start(bf16[128,512]{1,0:T(8,128)(2,1)S(1)} %get-tuple-element.94), channel_id=1, source_target_pairs={{0,2},{2,0},{4,6},{6,4},{8,10},{10,8},{12,14},{14,12},{1,3},{3,1},... | collective-permute-start | bytes 393224 | tf_op jit(solution)/shard_map/ppermute | solution.py:780
  27.5 0.0 collective-permute-start.5
  27.5 2.4 %collective-permute-start.6 = (bf16[128,512]{1,0:T(8,128)(2,1)S(1)}, bf16[128,512]{1,0:T(8,128)(2,1)S(1)}, u32[]{:S(2)}, u32[]{:S(2)}) collective-permute-start(bf16[128,512]{1,0:T(8,128)(2,1)S(1)} %get-tuple-element.90), channel_id=1, source_target_pairs={{0,6},{2,4},{4,2},{6,0},{8,14},{10,12},{12,10},{14,8},{1,7},{3,5},... | collective-permute-start | bytes 393224 | tf_op jit(solution)/shard_map/ppermute | solution.py:780
  29.9 2.8 %intra.3 = (f32[384,512]{1,0:T(8,128)S(1)}, f32[384,512]{1,0:T(8,128)S(1)}, f32[384,512]{1,0:T(8,128)S(1)}, f32[384,512]{1,0:T(8,128)S(1)}) custom-call(bf16[384,256]{1,0:T(8,128)(2,1)S(1)} %get-tuple-element.60.refs_4_.refs_0_, bf16[384,256]{1,0:T(8,128)(2,1)S(1)} %get-tuple-element.63.refs_1_.refs_0_, bf16[384,128]{1,0:T(8,128)(2,1)S(1)} %get-tuple-element.64.refs_2_, ...), custom_call_target="tpu_custom_call" | custom-call | flops 201326592 | bytes 4718592 | tf_op jit(solution)/shard_map/intra/pallas_call | solution.py:699
  32.7 0.0 collective-permute-done.7.refs_7_
  32.8 0.0 copy-done.6
  32.8 1.4 %final.2.refs_8_ = bf16[384,2048]{1,0:T(8,128)(2,1)} custom-call(bf16[384,256]{1,0:T(8,128)(2,1)S(1)} %get-tuple-element.63.refs_1_.refs_0_, f32[1,2048]{1,0:T(1,128)S(1)} %bitcast.5, f32[384,512]{1,0:T(8,128)S(1)} %get-tuple-element.77.refs_2_, f32[384,512]{1,0:T(8,128)S(1)} %get-tuple-element.91.refs_3_, f32[384,512]{1,0:T(8,128)S(1)} %get-tuple-element.92.refs_4_, ...), custom_call_target="tpu_custom_call" | custom-call | flops 100663296 | bytes 3145728 | tf_op jit(solution)/shard_map/final/pallas_call | solution.py:761
  34.2 0.0 collective-permute-done.5.refs_6_
  34.2 0.5 %collective-permute-done.6.refs_7_ = bf16[128,512]{1,0:T(8,128)(2,1)S(1)} collective-permute-done((bf16[128,512]{1,0:T(8,128)(2,1)S(1)}, bf16[128,512]{1,0:T(8,128)(2,1)S(1)}, u32[]{:S(2)}, u32[]{:S(2)}) %collective-permute-start.6) | collective-permute-done | bytes 131104 | tf_op jit(solution)/shard_map/ppermute | solution.py:780
  34.6 1.4 %final.3 = bf16[384,2048]{1,0:T(8,128)(2,1)} custom-call(bf16[384,256]{1,0:T(8,128)(2,1)S(1)} %get-tuple-element.63.refs_1_.refs_0_, f32[1,2048]{1,0:T(1,128)S(1)} %bitcast.6, f32[384,512]{1,0:T(8,128)S(1)} %get-tuple-element.85.refs_2_, f32[384,512]{1,0:T(8,128)S(1)} %get-tuple-element.86.refs_3_, ...), custom_call_target="tpu_custom_call", output_to_operand_aliasing={{}: (8, {})} | custom-call | flops 100663296 | bytes 3145728 | tf_op jit(solution)/shard_map/final/pallas_call | solution.py:761
  (3 shorter events, 0.0 us)
Async XLA Ops:
  0.0 3.9 %copy-start = (bf16[384,2048]{1,0:T(8,128)(2,1)S(1)}, bf16[384,2048]{1,0:T(8,128)(2,1)}, u32[]{:S(2)}) copy-start(bf16[384,2048]{1,0:T(8,128)(2,1)} %refs_6_.3) | copy-start | bytes 4718596
  0.0 3.9 %copy-start.3 = (bf16[384,256]{1,0:T(8,128)(2,1)S(1)}, bf16[384,256]{1,0:T(8,128)(2,1)}, u32[]{:S(2)}) copy-start(bf16[384,256]{1,0:T(8,128)(2,1)} %b_ref.3) | copy-start | bytes 589828
  0.0 3.9 %copy-start.4 = (f32[4,2048]{1,0:T(4,128)S(1)}, f32[4,2048]{1,0:T(4,128)}, u32[]{:S(2)}) copy-start(f32[4,2048]{1,0:T(4,128)} %refs_5_.3) | copy-start | bytes 98308
  0.0 3.9 %copy-start.9 = (s32[4]{0:T(128)S(1)}, s32[4]{0:T(128)}, u32[]{:S(2)}) copy-start(s32[4]{0:T(128)} %refs_14_.1) | copy-start | bytes 52
  0.0 3.9 %copy-start.7 = (f32[4,256]{1,0:T(4,128)S(1)}, f32[4,256]{1,0:T(4,128)}, u32[]{:S(2)}) copy-start(f32[4,256]{1,0:T(4,128)} %taps_b_ref.3) | copy-start | bytes 12292
  0.0 3.9 %copy-start.10 = (f32[32]{0:T(128)S(1)}, f32[32]{0:T(128)}, u32[]{:S(2)}) copy-start(f32[32]{0:T(128)} %param.15) | copy-start | bytes 388
  0.0 3.9 %copy-start.5 = (f32[384,32]{0,1:T(8,128)S(1)}, f32[384,32]{0,1:T(8,128)}, u32[]{:S(2)}) copy-start(f32[384,32]{0,1:T(8,128)} %param.14) | copy-start | bytes 147460
  0.9 7.7 %collective-permute-start = (bf16[4,2560]{1,0:T(4,128)(2,1)S(1)}, bf16[4,2560]{1,0:T(4,128)(2,1)S(1)}, u32[]{:S(2)}, u32[]{:S(2)}) collective-permute-start(bf16[4,2560]{1,0:T(4,128)(2,1)S(1)} %pack.1), channel_id=1, source_target_pairs={{0,2},{2,4},{4,6},{6,8},{8,10},{10,12},{12,14},{14,0},{1,3},{3,5},... | collective-permute-start | bytes 61448 | tf_op jit(solution)/shard_map/ppermute | solution.py:828
  8.7 5.1 %copy-start.2 = (bf16[384,256]{1,0:T(8,128)(2,1)S(1)}, bf16[384,256]{1,0:T(8,128)(2,1)}, u32[]{:S(2)}) copy-start(bf16[384,256]{1,0:T(8,128)(2,1)} %refs_7_.1) | copy-start | bytes 589828
  8.7 5.1 %copy-start.8 = (f32[4,256]{1,0:T(4,128)S(1)}, f32[4,256]{1,0:T(4,128)}, u32[]{:S(2)}) copy-start(f32[4,256]{1,0:T(4,128)} %refs_8_.1) | copy-start | bytes 12292
  9.0 7.1 %collective-permute-start.1 = (bf16[520,128]{1,0:T(8,128)(2,1)S(1)}, bf16[520,128]{1,0:T(8,128)(2,1)S(1)}, u32[]{:S(2)}, u32[]{:S(2)}) collective-permute-start(bf16[520,128]{1,0:T(8,128)(2,1)S(1)} %get-tuple-element.68), channel_id=1, source_target_pairs={{0,2},{2,0},{4,6},{6,4},{8,10},{10,8},{12,14},{14,12},{1,3},{3,1},... | collective-permute-start | bytes 399368 | tf_op jit(solution)/shard_map/ppermute | solution.py:780
  9.8 6.4 %collective-permute-start.2 = (bf16[520,128]{1,0:T(8,128)(2,1)S(1)}, bf16[520,128]{1,0:T(8,128)(2,1)S(1)}, u32[]{:S(2)}, u32[]{:S(2)}) collective-permute-start(bf16[520,128]{1,0:T(8,128)(2,1)S(1)} %get-tuple-element.69), channel_id=1, source_target_pairs={{0,4},{2,6},{4,0},{6,2},{8,12},{10,14},{12,8},{14,10},{1,5},{3,7},... | collective-permute-start | bytes 399368 | tf_op jit(solution)/shard_map/ppermute | solution.py:780
  12.5 6.0 %collective-permute-start.3 = (bf16[520,128]{1,0:T(8,128)(2,1)S(1)}, bf16[520,128]{1,0:T(8,128)(2,1)S(1)}, u32[]{:S(2)}, u32[]{:S(2)}) collective-permute-start(bf16[520,128]{1,0:T(8,128)(2,1)S(1)} %get-tuple-element.70), channel_id=1, source_target_pairs={{0,6},{2,4},{4,2},{6,0},{8,14},{10,12},{12,10},{14,8},{1,7},{3,5},... | collective-permute-start | bytes 399368 | tf_op jit(solution)/shard_map/ppermute | solution.py:780
  13.8 6.6 %copy-start.1 = (bf16[384,2048]{1,0:T(8,128)(2,1)S(1)}, bf16[384,2048]{1,0:T(8,128)(2,1)}, u32[]{:S(2)}) copy-start(bf16[384,2048]{1,0:T(8,128)(2,1)} %refs_11_.3) | copy-start | bytes 4718596
  18.7 7.5 %collective-permute-start.4 = (bf16[128,512]{1,0:T(8,128)(2,1)S(1)}, bf16[128,512]{1,0:T(8,128)(2,1)S(1)}, u32[]{:S(2)}, u32[]{:S(2)}) collective-permute-start(bf16[128,512]{1,0:T(8,128)(2,1)S(1)} %get-tuple-element.71), channel_id=1, source_target_pairs={{0,8},{2,10},{4,12},{6,14},{8,0},{10,2},{12,4},{14,6},{1,9},{3,11}... | collective-permute-start | bytes 393224 | tf_op jit(solution)/shard_map/ppermute | solution.py:780
  26.3 6.4 %collective-permute-start.7 = (bf16[128,512]{1,0:T(8,128)(2,1)S(1)}, bf16[128,512]{1,0:T(8,128)(2,1)S(1)}, u32[]{:S(2)}, u32[]{:S(2)}) collective-permute-start(bf16[128,512]{1,0:T(8,128)(2,1)S(1)} %get-tuple-element.94), channel_id=1, source_target_pairs={{0,2},{2,0},{4,6},{6,4},{8,10},{10,8},{12,14},{14,12},{1,3},{3,1},... | collective-permute-start | bytes 393224 | tf_op jit(solution)/shard_map/ppermute | solution.py:780
  27.5 6.7 %collective-permute-start.5 = (bf16[128,512]{1,0:T(8,128)(2,1)S(1)}, bf16[128,512]{1,0:T(8,128)(2,1)S(1)}, u32[]{:S(2)}, u32[]{:S(2)}) collective-permute-start(bf16[128,512]{1,0:T(8,128)(2,1)S(1)} %get-tuple-element.89), channel_id=1, source_target_pairs={{0,4},{2,6},{4,0},{6,2},{8,12},{10,14},{12,8},{14,10},{1,5},{3,7},... | collective-permute-start | bytes 393224 | tf_op jit(solution)/shard_map/ppermute | solution.py:780
  27.5 7.2 %collective-permute-start.6 = (bf16[128,512]{1,0:T(8,128)(2,1)S(1)}, bf16[128,512]{1,0:T(8,128)(2,1)S(1)}, u32[]{:S(2)}, u32[]{:S(2)}) collective-permute-start(bf16[128,512]{1,0:T(8,128)(2,1)S(1)} %get-tuple-element.90), channel_id=1, source_target_pairs={{0,6},{2,4},{4,2},{6,0},{8,14},{10,12},{12,10},{14,8},{1,7},{3,5},... | collective-permute-start | bytes 393224 | tf_op jit(solution)/shard_map/ppermute | solution.py:780
  29.9 2.9 %copy-start.6 = (f32[2048]{0:T(1024)S(1)}, f32[2048]{0:T(1024)}, u32[]{:S(2)}) copy-start(f32[2048]{0:T(1024)} %param.20) | copy-start | bytes 24580

commit v8 on v7

--- a/solution.py
+++ b/solution.py
@@ -13,7 +13,7 @@
 LANES = 128
 ROWS = 32
 CLUSTER = 4
-EARLY = 2
+EARLY = 3
 LOG2E = 1.4426950408889634
 norm_eps = 1e-05
 
@@ -33,17 +33,22 @@
 
 
 def doc_edges(dl_ref):
-    edges = [0]
-    for i in range(dl_ref.shape[0] - 1):
-        edges.append(edges[-1] + dl_ref[i])
+    lengths = dl_ref[...]
+    edges = [lengths[:, :1]]
+    for i in range(1, lengths.shape[1] - 1):
+        edges.append(edges[-1] + lengths[:, i : i + 1])
     return edges
 
 
 def doc_start(token, edges):
     start = jnp.zeros_like(token)
-    for edge in edges[1:]:
+    for edge in edges:
         start = jnp.where(token >= edge, jnp.maximum(start, edge), start)
     return start
+
+
+def one(value):
+    return jnp.full((1, 1), value, jnp.int32)
 
 
 def split2(value):
@@ -108,13 +113,13 @@
     decays = []
     for span, first, step, cum, token in steps_of(row0, edges, dt_ref, rate_ref):
         last = cum[:, SUB - 1 :]
-        last_start = doc_start(jnp.int32(first + SUB - 1), edges)
+        last_start = doc_start(one(first + SUB - 1), edges)
         to_end = jnp.exp(last - cum) * step * jnp.where(token >= last_start, 1.0, 0.0)
         pair = [part.astype(F32) for part in split2(to_end)] + [jnp.zeros((LANES - 2 * heads, SUB), F32)]
         tab_ref[span, :] = jnp.concatenate(pair, 0).T[:, : 2 * heads].astype(BF16)
         decays.append(jnp.exp(last) * jnp.where(last_start < first, 1.0, 0.0))
         total = total + last
-    end_start = doc_start(jnp.int32(row0 + tok - 1), edges)
+    end_start = doc_start(one(row0 + tok - 1), edges)
     whole = jnp.exp(total) * jnp.where(end_start < row0, 1.0, 0.0)
     columns = [part.astype(F32) for part in split3(whole)] + decays[1:]
     columns.append(jnp.zeros((heads, LANES - len(columns)), F32))
@@ -285,7 +290,7 @@
             shape((EARLY, tok, owned), BF16),
             shape((tok, gn), BF16),
         ),
-        in_specs=[pl.BlockSpec(memory_space=pltpu.SMEM)] + [VMEM] * 6,
+        in_specs=[VMEM] * 7,
         out_specs=(VMEM,) * 7,
         scratch_shapes=[
             pltpu.VMEM((tok + 8, CHUNK), F32),
@@ -522,7 +527,7 @@
             shape((1, subs, STATE, owned), BF16),
             piece_shape(owned),
         ),
-        in_specs=[VMEM] * 7 + ([VMEM] * (len(with_c) - 1) + [pl.BlockSpec(memory_space=pltpu.SMEM)] if with_c else []),
+        in_specs=[VMEM] * (7 + len(with_c)),
         out_specs=(VMEM,) * (3 + len(extra_out)),
         scratch_shapes=[
             pltpu.VMEM((STATE, tok), BF16),
@@ -827,7 +832,8 @@
     ends = pack(pin(x_input), pin(b_input), pin(c_input))
     tail = lax.ppermute(ends, "seq", [(i, (i + 1) % count) for i in range(count)])
     rates = (dt_input.T, decay_rate[None, :])
-    tab, d, age, part_x, part_b, xc, bc = conv(doc_lengths, *rates, x_input, b_input, taps_x, taps_b)
+    lengths = doc_lengths[None, :]
+    tab, d, age, part_x, part_b, xc, bc = conv(lengths, *rates, x_input, b_input, taps_x, taps_b)
     state, others, decay, weight = states(tab, d, xc, bc)
     xc, bc, extra, *sends = with_head(tail, part_x, part_b, taps_x, taps_b, age, state, decay, weight, xc, bc)
     known = (tail, age, tab, d, bc, taps_x, x_input)
@@ -838,7 +844,7 @@
         hs.append(late_h)
         sends.append(late_send)
     cc, early_h, inner_tab, col, row, xs[0], hs[0], own_send = late(
-        0, *known, (c_input, taps_c, others, extra, decay, *rates, doc_lengths)
+        0, *known, (c_input, taps_c, others, extra, decay, *rates, lengths)
     )
     hs[1 : 1 + EARLY] = [early_h] * EARLY
     shared = (bc, cc, inner_tab, col, row)

time: 36.2 us -> 36.5 us (level)
  Pallas kernels: 17.4 us -> 16.3 us
  waiting for transfers between devices: 6.6 us -> 7.59 us
    ppermute x7, waiting for transfers between devices: 5.71 us -> 7.31 us  [moved(): lax.ppermute(value, 'seq', [(i, hop(i)) for i in range(count) if 0 <= hop...]
    pallas_call x2 -> x1, Pallas kernels: 3.45 us -> 1.86 us  [late(): pl.pallas_call(functools.partial(late_kernel, k, bool(with_c)), out_shape...]
    ppermute x1, waiting for transfers between devices: 0.89 us -> 0.28 us  [on_device(): lax.ppermute(ends, 'seq', [(i, (i + 1) % count) for i in range(count)])]
    ppermute x7, starting transfers between devices: 8.92 us -> 9.29 us  [moved(): lax.ppermute(value, 'seq', [(i, hop(i)) for i in range(count) if 0 <= hop...]
  transfers between devices with their start and end apart: 8 -> 8, of which waited for: 4 -> 6; matrix products, arithmetic and copies ran while one was open for 0% -> 0% of each run, Pallas kernels for 40% -> 36%
where the time goes in v8:
time: 36.5 us; the launch traced here: 36.4 us
  Pallas kernels  16.3 us (45%)
  starting transfers between devices  12.2 us (33%)
  waiting for transfers between devices  7.59 us (21%)
    ppermute x7, starting transfers between devices, moved(): lax.ppermute(value, 'seq', [(i, hop(i)) for i in range(count) if 0 <= hop...  9.29 us
    ppermute x7, waiting for transfers between devices, moved(): lax.ppermute(value, 'seq', [(i, hop(i)) for i in range(count) if 0 <= hop...  7.31 us
    pallas_call x2, Pallas kernels, intra(): pl.pallas_call(functools.partial(intra_kernel, pieces, heads, head_dim),...  5.61 us
    pallas_call x1, Pallas kernels, conv(): pl.pallas_call(conv_kernel, out_shape=(shape((tok, 2 * heads), BF16), sha...  3.19 us
    ppermute x1, starting transfers between devices, on_device(): lax.ppermute(ends, 'seq', [(i, (i + 1) % count) for i in range(count)])  2.95 us
    pallas_call x2, Pallas kernels, final(): pl.pallas_call(functools.partial(final_kernel, turn, groups), out_shape=j...  2.76 us
    pallas_call x1, Pallas kernels, late(): pl.pallas_call(functools.partial(late_kernel, k, bool(with_c)), out_shape...  1.86 us
    pallas_call x1, Pallas kernels, states(): pl.pallas_call(state_kernel, out_shape=(jax.ShapeDtypeStruct((pieces, STA...  1.25 us
  transfers between devices with their start and end apart: 8, of which 6 were waited for; matrix products, arithmetic and copies ran while one was open for 0% of the time, Pallas kernels for 36%

profile of v8, /device:TPU:0, one launch (start us, length us, event | category | flops | bytes accessed | tf_op | source)
XLA Modules:
  0.0 36.4 jit_solution(365898222237026685)
XLA Ops:
  0.0 0.0 copy-start.1
  0.0 0.0 copy-start.3
  0.0 0.0 copy-start.4
  0.0 0.0 copy-start.7
  0.0 0.0 copy-start.10
  0.0 0.0 copy-start.5
  0.0 0.9 %pack.1 = bf16[4,2560]{1,0:T(4,128)(2,1)S(1)} custom-call(bf16[384,2048]{1,0:T(8,128)(2,1)} %refs_6_.1, bf16[384,256]{1,0:T(8,128)(2,1)} %b_ref.3, bf16[384,256]{1,0:T(8,128)(2,1)} %refs_7_.1), custom_call_target="tpu_custom_call" | custom-call | tf_op jit(solution)/shard_map/pack/pallas_call | solution.py:154
  0.9 3.0 %collective-permute-start = (bf16[4,2560]{1,0:T(4,128)(2,1)S(1)}, bf16[4,2560]{1,0:T(4,128)(2,1)S(1)}, u32[]{:S(2)}, u32[]{:S(2)}) collective-permute-start(bf16[4,2560]{1,0:T(4,128)(2,1)S(1)} %pack.1), channel_id=1, source_target_pairs={{0,2},{2,4},{4,6},{6,8},{8,10},{10,12},{12,14},{14,0},{1,3},{3,5},... | collective-permute-start | bytes 61448 | tf_op jit(solution)/shard_map/ppermute | solution.py:833
  3.9 0.0 copy-done.1
  3.9 0.0 copy-done.3
  3.9 0.0 copy-done.4
  3.9 0.0 copy-done.7
  3.9 0.0 copy-done.9
  3.9 0.0 copy-done.10
  3.9 0.0 copy-done.5
  3.9 3.2 %conv.1 = (bf16[384,64]{1,0:T(8,128)(2,1)S(1)}, bf16[8,64]{1,0:T(8,128)(2,1)S(1)}, s32[384,128]{1,0:T(8,128)S(1)}, f32[3,8,512]{2,1,0:T(8,128)S(1)}, f32[8,256]{...) custom-call(s32[1,4]{1,0:T(1,128)S(1)} %bitcast.8, f32[32,384]{1,0:T(8,128)S(1)} %bitcast.4, ...), custom_call_target="tpu_custom_call" | custom-call | flops 12582912 | bytes 3145728 | tf_op jit(solution)/shard_map/conv/pallas_call | solution.py:282
  7.1 1.3 %state.1 = (f32[3,128,512]{2,1,0:T(8,128)S(1)}, f32[3,2,128,512]{3,2,1,0:T(8,128)S(1)}, f32[3,8,512]{2,1,0:T(8,128)S(1)}, f32[3,8,512]{2,1,0:T(8,128)S(1)}) custom-call(bf16[384,64]{1,0:T(8,128)(2,1)S(1)} %get-tuple-element.49.tab_ref.refs_2_, bf16[8,64]{1,0:T(8,128)(2,1)S(1)} %get-tuple-element.50.d_ref.refs_3_, ...), custom_call_target="tpu_custom_call" | custom-call | flops 301989888 | bytes 2359296 | tf_op jit(solution)/shard_map/state/pallas_call | solution.py:341
  8.4 0.0 copy-start.2
  8.4 0.0 copy-start.8
  8.4 0.3 collective-permute-done.tail_ref.refs_0_
  8.7 0.4 head.1
  9.1 1.4 %collective-permute-start.1 = (bf16[520,128]{1,0:T(8,128)(2,1)S(1)}, bf16[520,128]{1,0:T(8,128)(2,1)S(1)}, u32[]{:S(2)}, u32[]{:S(2)}) collective-permute-start(bf16[520,128]{1,0:T(8,128)(2,1)S(1)} %get-tuple-element.66), channel_id=1, source_target_pairs={{0,2},{2,0},{4,6},{6,4},{8,10},{10,8},{12,14},{14,12},{1,3},{3,1},... | collective-permute-start | bytes 399368 | tf_op jit(solution)/shard_map/ppermute | solution.py:785
  10.4 1.6 %collective-permute-start.2 = (bf16[520,128]{1,0:T(8,128)(2,1)S(1)}, bf16[520,128]{1,0:T(8,128)(2,1)S(1)}, u32[]{:S(2)}, u32[]{:S(2)}) collective-permute-start(bf16[520,128]{1,0:T(8,128)(2,1)S(1)} %get-tuple-element.67), channel_id=1, source_target_pairs={{0,4},{2,6},{4,0},{6,2},{8,12},{10,14},{12,8},{14,10},{1,5},{3,7},... | collective-permute-start | bytes 399368 | tf_op jit(solution)/shard_map/ppermute | solution.py:785
  12.0 0.6 %collective-permute-start.3 = (bf16[520,128]{1,0:T(8,128)(2,1)S(1)}, bf16[520,128]{1,0:T(8,128)(2,1)S(1)}, u32[]{:S(2)}, u32[]{:S(2)}) collective-permute-start(bf16[520,128]{1,0:T(8,128)(2,1)S(1)} %get-tuple-element.68), channel_id=1, source_target_pairs={{0,6},{2,4},{4,2},{6,0},{8,14},{10,12},{12,10},{14,8},{1,7},{3,5},... | collective-permute-start | bytes 399368 | tf_op jit(solution)/shard_map/ppermute | solution.py:785
  12.6 0.0 copy-done.2
  12.6 0.0 copy-done.8
  12.6 1.9 %own.1 = (bf16[384,256]{1,0:T(8,128)(2,1)S(1)}, bf16[3,2,128,512]{3,2,1,0:T(8,128)(2,1)S(1)}, bf16[384,128]{1,0:T(8,128)(2,1)S(1)}, f32[384,128]{1,0:T(8,128)S(1...) custom-call(bf16[4,2560]{1,0:T(4,128)(2,1)S(1)} %collective-permute-, ...), custom_call_target="tpu_custom_call" | custom-call | flops 103809024 | bytes 1572864 | tf_op jit(solution)/shard_map/own/pallas_call | solution.py:522
  14.5 0.0 copy-start
  14.5 0.0 collective-permute-done.1.refs_1_
  14.5 2.1 %collective-permute-done.2.refs_2_ = bf16[520,128]{1,0:T(8,128)(2,1)S(1)} collective-permute-done((bf16[520,128]{1,0:T(8,128)(2,1)S(1)}, bf16[520,128]{1,0:T(8,128)(2,1)S(1)}, u32[]{:S(2)}, u32[]{:S(2)}) %collective-permute-start.2) | collective-permute-done | bytes 133152 | tf_op jit(solution)/shard_map/ppermute | solution.py:785
  16.6 1.9 %collective-permute-done.3.refs_3_ = bf16[520,128]{1,0:T(8,128)(2,1)S(1)} collective-permute-done((bf16[520,128]{1,0:T(8,128)(2,1)S(1)}, bf16[520,128]{1,0:T(8,128)(2,1)S(1)}, u32[]{:S(2)}, u32[]{:S(2)}) %collective-permute-start.3) | collective-permute-done | bytes 133152 | tf_op jit(solution)/shard_map/ppermute | solution.py:785
  18.5 0.2 cluster_scan.1
  18.7 2.2 %collective-permute-start.4 = (bf16[128,512]{1,0:T(8,128)(2,1)S(1)}, bf16[128,512]{1,0:T(8,128)(2,1)S(1)}, u32[]{:S(2)}, u32[]{:S(2)}) collective-permute-start(bf16[128,512]{1,0:T(8,128)(2,1)S(1)} %get-tuple-element.69), channel_id=1, source_target_pairs={{0,8},{2,10},{4,12},{6,14},{8,0},{10,2},{12,4},{14,6},{1,9},{3,11}... | collective-permute-start | bytes 393224 | tf_op jit(solution)/shard_map/ppermute | solution.py:785
  20.9 0.0 copy-done
  20.9 2.8 %intra.2 = (f32[384,512]{1,0:T(8,128)S(1)}, f32[384,512]{1,0:T(8,128)S(1)}, f32[384,512]{1,0:T(8,128)S(1)}, f32[384,512]{1,0:T(8,128)S(1)}) custom-call(bf16[384,256]{1,0:T(8,128)(2,1)S(1)} %get-tuple-element.58.refs_4_.refs_0_, bf16[384,256]{1,0:T(8,128)(2,1)S(1)} %get-tuple-element.61.refs_1_.refs_0_, bf16[384,128]{1,0:T(8,128)(2,1)S(1)} %get-tuple-element.62.refs_2_, ...), custom_call_target="tpu_custom_call" | custom-call | flops 201326592 | bytes 4718592 | tf_op jit(solution)/shard_map/intra/pallas_call | solution.py:704
  23.7 2.7 %collective-permute-done.4.before_ref = bf16[128,512]{1,0:T(8,128)(2,1)S(1)} collective-permute-done((bf16[128,512]{1,0:T(8,128)(2,1)S(1)}, bf16[128,512]{1,0:T(8,128)(2,1)S(1)}, u32[]{:S(2)}, u32[]{:S(2)}) %collective-permute-start.4) | collective-permute-done | bytes 131104 | tf_op jit(solution)/shard_map/ppermute | solution.py:785
  26.4 0.1 join.1
  26.5 0.7 %collective-permute-start.7 = (bf16[128,512]{1,0:T(8,128)(2,1)S(1)}, bf16[128,512]{1,0:T(8,128)(2,1)S(1)}, u32[]{:S(2)}, u32[]{:S(2)}) collective-permute-start(bf16[128,512]{1,0:T(8,128)(2,1)S(1)} %get-tuple-element.90), channel_id=1, source_target_pairs={{0,2},{2,0},{4,6},{6,4},{8,10},{10,8},{12,14},{14,12},{1,3},{3,1},... | collective-permute-start | bytes 393224 | tf_op jit(solution)/shard_map/ppermute | solution.py:785
  27.3 0.3 collective-permute-start.5
  27.5 2.6 %collective-permute-start.6 = (bf16[128,512]{1,0:T(8,128)(2,1)S(1)}, bf16[128,512]{1,0:T(8,128)(2,1)S(1)}, u32[]{:S(2)}, u32[]{:S(2)}) collective-permute-start(bf16[128,512]{1,0:T(8,128)(2,1)S(1)} %get-tuple-element.86), channel_id=1, source_target_pairs={{0,6},{2,4},{4,2},{6,0},{8,14},{10,12},{12,10},{14,8},{1,7},{3,5},... | collective-permute-start | bytes 393224 | tf_op jit(solution)/shard_map/ppermute | solution.py:785
  30.1 0.0 copy-start.6
  30.1 2.8 %intra.3 = (f32[384,512]{1,0:T(8,128)S(1)}, f32[384,512]{1,0:T(8,128)S(1)}, f32[384,512]{1,0:T(8,128)S(1)}, f32[384,512]{1,0:T(8,128)S(1)}) custom-call(bf16[384,256]{1,0:T(8,128)(2,1)S(1)} %get-tuple-element.58.refs_4_.refs_0_, bf16[384,256]{1,0:T(8,128)(2,1)S(1)} %get-tuple-element.61.refs_1_.refs_0_, bf16[384,128]{1,0:T(8,128)(2,1)S(1)} %get-tuple-element.62.refs_2_, ...), custom_call_target="tpu_custom_call" | custom-call | flops 201326592 | bytes 4718592 | tf_op jit(solution)/shard_map/intra/pallas_call | solution.py:704
  32.9 0.1 collective-permute-done.7.refs_7_
  33.0 0.0 copy-done.6
  33.0 1.4 %final.2.refs_8_ = bf16[384,2048]{1,0:T(8,128)(2,1)} custom-call(bf16[384,256]{1,0:T(8,128)(2,1)S(1)} %get-tuple-element.61.refs_1_.refs_0_, f32[1,2048]{1,0:T(1,128)S(1)} %bitcast.6, f32[384,512]{1,0:T(8,128)S(1)} %get-tuple-element.75.refs_2_, f32[384,512]{1,0:T(8,128)S(1)} %get-tuple-element.87.refs_3_, f32[384,512]{1,0:T(8,128)S(1)} %get-tuple-element.88.refs_4_, ...), custom_call_target="tpu_custom_call" | custom-call | flops 100663296 | bytes 3145728 | tf_op jit(solution)/shard_map/final/pallas_call | solution.py:766
  34.4 0.0 collective-permute-done.5.refs_6_
  34.4 0.6 %collective-permute-done.6.refs_7_ = bf16[128,512]{1,0:T(8,128)(2,1)S(1)} collective-permute-done((bf16[128,512]{1,0:T(8,128)(2,1)S(1)}, bf16[128,512]{1,0:T(8,128)(2,1)S(1)}, u32[]{:S(2)}, u32[]{:S(2)}) %collective-permute-start.6) | collective-permute-done | bytes 131104 | tf_op jit(solution)/shard_map/ppermute | solution.py:785
  35.0 1.4 %final.3 = bf16[384,2048]{1,0:T(8,128)(2,1)} custom-call(bf16[384,256]{1,0:T(8,128)(2,1)S(1)} %get-tuple-element.61.refs_1_.refs_0_, f32[1,2048]{1,0:T(1,128)S(1)} %bitcast.7, f32[384,512]{1,0:T(8,128)S(1)} %get-tuple-element.81.refs_2_, f32[384,512]{1,0:T(8,128)S(1)} %get-tuple-element.82.refs_3_, ...), custom_call_target="tpu_custom_call", output_to_operand_aliasing={{}: (8, {})} | custom-call | flops 100663296 | bytes 3145728 | tf_op jit(solution)/shard_map/final/pallas_call | solution.py:766
  (2 shorter events, 0.0 us)
Async XLA Ops:
  0.0 3.9 %copy-start.1 = (bf16[384,2048]{1,0:T(8,128)(2,1)S(1)}, bf16[384,2048]{1,0:T(8,128)(2,1)}, u32[]{:S(2)}) copy-start(bf16[384,2048]{1,0:T(8,128)(2,1)} %refs_6_.1) | copy-start | bytes 4718596
  0.0 3.9 %copy-start.3 = (bf16[384,256]{1,0:T(8,128)(2,1)S(1)}, bf16[384,256]{1,0:T(8,128)(2,1)}, u32[]{:S(2)}) copy-start(bf16[384,256]{1,0:T(8,128)(2,1)} %b_ref.3) | copy-start | bytes 589828
  0.0 3.9 %copy-start.4 = (f32[4,2048]{1,0:T(4,128)S(1)}, f32[4,2048]{1,0:T(4,128)}, u32[]{:S(2)}) copy-start(f32[4,2048]{1,0:T(4,128)} %refs_5_.1) | copy-start | bytes 98308
  0.0 3.9 %copy-start.7 = (f32[4,256]{1,0:T(4,128)S(1)}, f32[4,256]{1,0:T(4,128)}, u32[]{:S(2)}) copy-start(f32[4,256]{1,0:T(4,128)} %taps_b_ref.3) | copy-start | bytes 12292
  0.0 3.9 %copy-start.9 = (s32[4]{0:T(128)S(1)}, s32[4]{0:T(128)}, u32[]{:S(2)}) copy-start(s32[4]{0:T(128)} %param.21) | copy-start | bytes 52
  0.0 3.9 %copy-start.10 = (f32[32]{0:T(128)S(1)}, f32[32]{0:T(128)}, u32[]{:S(2)}) copy-start(f32[32]{0:T(128)} %param.15) | copy-start | bytes 388
  0.0 3.9 %copy-start.5 = (f32[384,32]{0,1:T(8,128)S(1)}, f32[384,32]{0,1:T(8,128)}, u32[]{:S(2)}) copy-start(f32[384,32]{0,1:T(8,128)} %param.14) | copy-start | bytes 147460
  0.9 7.7 %collective-permute-start = (bf16[4,2560]{1,0:T(4,128)(2,1)S(1)}, bf16[4,2560]{1,0:T(4,128)(2,1)S(1)}, u32[]{:S(2)}, u32[]{:S(2)}) collective-permute-start(bf16[4,2560]{1,0:T(4,128)(2,1)S(1)} %pack.1), channel_id=1, source_target_pairs={{0,2},{2,4},{4,6},{6,8},{8,10},{10,12},{12,14},{14,0},{1,3},{3,5},... | collective-permute-start | bytes 61448 | tf_op jit(solution)/shard_map/ppermute | solution.py:833
  8.4 4.2 %copy-start.2 = (bf16[384,256]{1,0:T(8,128)(2,1)S(1)}, bf16[384,256]{1,0:T(8,128)(2,1)}, u32[]{:S(2)}) copy-start(bf16[384,256]{1,0:T(8,128)(2,1)} %refs_7_.1) | copy-start | bytes 589828
  8.4 4.2 %copy-start.8 = (f32[4,256]{1,0:T(4,128)S(1)}, f32[4,256]{1,0:T(4,128)}, u32[]{:S(2)}) copy-start(f32[4,256]{1,0:T(4,128)} %refs_8_.1) | copy-start | bytes 12292
  9.1 5.4 %collective-permute-start.1 = (bf16[520,128]{1,0:T(8,128)(2,1)S(1)}, bf16[520,128]{1,0:T(8,128)(2,1)S(1)}, u32[]{:S(2)}, u32[]{:S(2)}) collective-permute-start(bf16[520,128]{1,0:T(8,128)(2,1)S(1)} %get-tuple-element.66), channel_id=1, source_target_pairs={{0,2},{2,0},{4,6},{6,4},{8,10},{10,8},{12,14},{14,12},{1,3},{3,1},... | collective-permute-start | bytes 399368 | tf_op jit(solution)/shard_map/ppermute | solution.py:785
  10.4 6.1 %collective-permute-start.2 = (bf16[520,128]{1,0:T(8,128)(2,1)S(1)}, bf16[520,128]{1,0:T(8,128)(2,1)S(1)}, u32[]{:S(2)}, u32[]{:S(2)}) collective-permute-start(bf16[520,128]{1,0:T(8,128)(2,1)S(1)} %get-tuple-element.67), channel_id=1, source_target_pairs={{0,4},{2,6},{4,0},{6,2},{8,12},{10,14},{12,8},{14,10},{1,5},{3,7},... | collective-permute-start | bytes 399368 | tf_op jit(solution)/shard_map/ppermute | solution.py:785
  12.0 6.4 %collective-permute-start.3 = (bf16[520,128]{1,0:T(8,128)(2,1)S(1)}, bf16[520,128]{1,0:T(8,128)(2,1)S(1)}, u32[]{:S(2)}, u32[]{:S(2)}) collective-permute-start(bf16[520,128]{1,0:T(8,128)(2,1)S(1)} %get-tuple-element.68), channel_id=1, source_target_pairs={{0,6},{2,4},{4,2},{6,0},{8,14},{10,12},{12,10},{14,8},{1,7},{3,5},... | collective-permute-start | bytes 399368 | tf_op jit(solution)/shard_map/ppermute | solution.py:785
  14.5 6.4 %copy-start = (bf16[384,2048]{1,0:T(8,128)(2,1)S(1)}, bf16[384,2048]{1,0:T(8,128)(2,1)}, u32[]{:S(2)}) copy-start(bf16[384,2048]{1,0:T(8,128)(2,1)} %refs_11_.3) | copy-start | bytes 4718596
  18.7 7.7 %collective-permute-start.4 = (bf16[128,512]{1,0:T(8,128)(2,1)S(1)}, bf16[128,512]{1,0:T(8,128)(2,1)S(1)}, u32[]{:S(2)}, u32[]{:S(2)}) collective-permute-start(bf16[128,512]{1,0:T(8,128)(2,1)S(1)} %get-tuple-element.69), channel_id=1, source_target_pairs={{0,8},{2,10},{4,12},{6,14},{8,0},{10,2},{12,4},{14,6},{1,9},{3,11}... | collective-permute-start | bytes 393224 | tf_op jit(solution)/shard_map/ppermute | solution.py:785
  26.5 6.4 %collective-permute-start.7 = (bf16[128,512]{1,0:T(8,128)(2,1)S(1)}, bf16[128,512]{1,0:T(8,128)(2,1)S(1)}, u32[]{:S(2)}, u32[]{:S(2)}) collective-permute-start(bf16[128,512]{1,0:T(8,128)(2,1)S(1)} %get-tuple-element.90), channel_id=1, source_target_pairs={{0,2},{2,0},{4,6},{6,4},{8,10},{10,8},{12,14},{14,12},{1,3},{3,1},... | collective-permute-start | bytes 393224 | tf_op jit(solution)/shard_map/ppermute | solution.py:785
  27.3 7.1 %collective-permute-start.5 = (bf16[128,512]{1,0:T(8,128)(2,1)S(1)}, bf16[128,512]{1,0:T(8,128)(2,1)S(1)}, u32[]{:S(2)}, u32[]{:S(2)}) collective-permute-start(bf16[128,512]{1,0:T(8,128)(2,1)S(1)} %get-tuple-element.85), channel_id=1, source_target_pairs={{0,4},{2,6},{4,0},{6,2},{8,12},{10,14},{12,8},{14,10},{1,5},{3,7},... | collective-permute-start | bytes 393224 | tf_op jit(solution)/shard_map/ppermute | solution.py:785
  27.5 7.5 %collective-permute-start.6 = (bf16[128,512]{1,0:T(8,128)(2,1)S(1)}, bf16[128,512]{1,0:T(8,128)(2,1)S(1)}, u32[]{:S(2)}, u32[]{:S(2)}) collective-permute-start(bf16[128,512]{1,0:T(8,128)(2,1)S(1)} %get-tuple-element.86), channel_id=1, source_target_pairs={{0,6},{2,4},{4,2},{6,0},{8,14},{10,12},{12,10},{14,8},{1,7},{3,5},... | collective-permute-start | bytes 393224 | tf_op jit(solution)/shard_map/ppermute | solution.py:785
  30.1 2.9 %copy-start.6 = (f32[2048]{0:T(1024)S(1)}, f32[2048]{0:T(1024)}, u32[]{:S(2)}) copy-start(f32[2048]{0:T(1024)} %param.20) | copy-start | bytes 24580

commit v9 on v7

--- a/solution.py
+++ b/solution.py
@@ -852,7 +852,8 @@
     first = inner(0, *tied([age], total))
     joined = join(*tied([before_cluster(total, pre)], first[0]), local, pre)
     later = [inner(turn, *tied([age], joined[0])) for turn in range(1, groups)]
-    entering = exchanged(joined, (1, 2, 3))
+    entering = exchanged(joined, (2, 1, 3))
+    (entering[1],) = tied(entering[1:2], entering[2])
     output = None
     for turn, found in enumerate((first, *later)):
         mine = entering[turn * share : (turn + 1) * share]

time: 36.2 us -> 36.2 us (level)
  no operation moved by 1% of the time
where the time goes in v9:
time: 36.2 us; the launch traced here: 35.8 us
  Pallas kernels  17.4 us (48%)
  starting transfers between devices  11.9 us (33%)
  waiting for transfers between devices  6.32 us (17%)
    ppermute x7, starting transfers between devices, moved(): lax.ppermute(value, 'seq', [(i, hop(i)) for i in range(count) if 0 <= hop...  8.92 us
    pallas_call x2, Pallas kernels, intra(): pl.pallas_call(functools.partial(intra_kernel, pieces, heads, head_dim),...  5.67 us
    ppermute x7, waiting for transfers between devices, moved(): lax.ppermute(value, 'seq', [(i, hop(i)) for i in range(count) if 0 <= hop...  5.43 us
    pallas_call x2, Pallas kernels, late(): pl.pallas_call(functools.partial(late_kernel, k, bool(with_c)), out_shape...  3.45 us
    pallas_call x1, Pallas kernels, conv(): pl.pallas_call(conv_kernel, out_shape=(shape((tok, 2 * heads), BF16), sha...  2.96 us
    ppermute x1, starting transfers between devices, on_device(): lax.ppermute(ends, 'seq', [(i, (i + 1) % count) for i in range(count)])  2.95 us
    pallas_call x2, Pallas kernels, final(): pl.pallas_call(functools.partial(final_kernel, turn, groups), out_shape=j...  2.8 us
    pallas_call x1, Pallas kernels, pack(): pl.pallas_call(pack_kernel, out_shape=jax.ShapeDtypeStruct((4, sum(widths...  0.91 us
  transfers between devices with their start and end apart: 8, of which 4 were waited for; matrix products, arithmetic and copies ran while one was open for 0% of the time, Pallas kernels for 40%

profile of v9, /device:TPU:0, one launch (start us, length us, event | category | flops | bytes accessed | tf_op | source)
XLA Modules:
  0.0 35.8 jit_solution(15860527471395215015)
XLA Ops:
  0.0 0.0 copy-start
  0.0 0.0 copy-start.3
  0.0 0.0 copy-start.4
  0.0 0.0 copy-start.9
  0.0 0.0 copy-start.7
  0.0 0.0 copy-start.10
  0.0 0.0 copy-start.5
  0.0 0.9 %pack.1 = bf16[4,2560]{1,0:T(4,128)(2,1)S(1)} custom-call(bf16[384,2048]{1,0:T(8,128)(2,1)} %refs_6_.3, bf16[384,256]{1,0:T(8,128)(2,1)} %b_ref.3, bf16[384,256]{1,0:T(8,128)(2,1)} %refs_7_.1), custom_call_target="tpu_custom_call" | custom-call | tf_op jit(solution)/shard_map/pack/pallas_call | solution.py:149
  0.9 3.0 %collective-permute-start = (bf16[4,2560]{1,0:T(4,128)(2,1)S(1)}, bf16[4,2560]{1,0:T(4,128)(2,1)S(1)}, u32[]{:S(2)}, u32[]{:S(2)}) collective-permute-start(bf16[4,2560]{1,0:T(4,128)(2,1)S(1)} %pack.1), channel_id=1, source_target_pairs={{0,2},{2,4},{4,6},{6,8},{8,10},{10,12},{12,14},{14,0},{1,3},{3,5},... | collective-permute-start | bytes 61448 | tf_op jit(solution)/shard_map/ppermute | solution.py:828
  3.9 0.0 copy-done
  3.9 0.0 copy-done.3
  3.9 0.0 copy-done.4
  3.9 0.0 copy-done.9
  3.9 0.0 copy-done.7
  3.9 0.0 copy-done.10
  3.9 0.0 copy-done.5
  3.9 3.0 %conv.1 = (bf16[384,64]{1,0:T(8,128)(2,1)S(1)}, bf16[8,64]{1,0:T(8,128)(2,1)S(1)}, s32[384,128]{1,0:T(8,128)S(1)}, f32[2,8,512]{2,1,0:T(8,128)S(1)}, f32[8,256]{...) custom-call(s32[4]{0:T(128)S(1)} %copy-done.9, f32[32,384]{1,0:T(8,128)S(1)} %bitcast.3, ...), custom_call_target="tpu_custom_call" | custom-call | flops 12582912 | bytes 3145728 | tf_op jit(solution)/shard_map/conv/pallas_call | solution.py:277
  6.9 0.9 %state.1 = (f32[2,128,512]{2,1,0:T(8,128)S(1)}, f32[2,2,128,512]{3,2,1,0:T(8,128)S(1)}, f32[2,8,512]{2,1,0:T(8,128)S(1)}, f32[2,8,512]{2,1,0:T(8,128)S(1)}) custom-call(bf16[384,64]{1,0:T(8,128)(2,1)S(1)} %get-tuple-element.52.tab_ref.refs_2_, bf16[8,64]{1,0:T(8,128)(2,1)S(1)} %get-tuple-element.53.d_ref.refs_3_, ...), custom_call_target="tpu_custom_call" | custom-call | flops 201326592 | bytes 1572864 | tf_op jit(solution)/shard_map/state/pallas_call | solution.py:336
  7.8 0.9 %collective-permute-done.tail_ref.refs_0_ = bf16[4,2560]{1,0:T(4,128)(2,1)S(1)} collective-permute-done((bf16[4,2560]{1,0:T(4,128)(2,1)S(1)}, bf16[4,2560]{1,0:T(4,128)(2,1)S(1)}, u32[]{:S(2)}, u32[]{:S(2)}) %collective-permute-start) | collective-permute-done | bytes 20512 | tf_op jit(solution)/shard_map/ppermute | solution.py:828
  8.7 0.0 copy-start.2
  8.7 0.0 copy-start.8
  8.7 0.3 head.1
  9.0 0.8 %collective-permute-start.1 = (bf16[520,128]{1,0:T(8,128)(2,1)S(1)}, bf16[520,128]{1,0:T(8,128)(2,1)S(1)}, u32[]{:S(2)}, u32[]{:S(2)}) collective-permute-start(bf16[520,128]{1,0:T(8,128)(2,1)S(1)} %get-tuple-element.69), channel_id=1, source_target_pairs={{0,2},{2,0},{4,6},{6,4},{8,10},{10,8},{12,14},{14,12},{1,3},{3,1},... | collective-permute-start | bytes 399368 | tf_op jit(solution)/shard_map/ppermute | solution.py:780
  9.8 1.6 %collective-permute-start.2 = (bf16[520,128]{1,0:T(8,128)(2,1)S(1)}, bf16[520,128]{1,0:T(8,128)(2,1)S(1)}, u32[]{:S(2)}, u32[]{:S(2)}) collective-permute-start(bf16[520,128]{1,0:T(8,128)(2,1)S(1)} %get-tuple-element.70), channel_id=1, source_target_pairs={{0,4},{2,6},{4,0},{6,2},{8,12},{10,14},{12,8},{14,10},{1,5},{3,7},... | collective-permute-start | bytes 399368 | tf_op jit(solution)/shard_map/ppermute | solution.py:780
  11.4 1.1 %late.1 = (bf16[1,384,512]{2,1,0:T(8,128)(2,1)S(1)}, bf16[1,2,128,512]{3,2,1,0:T(8,128)(2,1)S(1)}, bf16[520,128]{1,0:T(8,128)(2,1)S(1)}) custom-call(bf16[4,2560]{1,0:T(4,128)(2,1)S(1)} %collective-permute-done.tail_ref.refs_0_, s32[384,128]{1,0:T(8,128)S(1)} %get-tuple-element.83.age_ref.refs_1_.refs_5_, ...), custom_call_target="tpu_custom_call" | custom-call | flops 103809024 | bytes 1572864 | tf_op jit(solution)/shard_map/late/pallas_call | solution.py:517
  12.5 1.3 %collective-permute-start.3 = (bf16[520,128]{1,0:T(8,128)(2,1)S(1)}, bf16[520,128]{1,0:T(8,128)(2,1)S(1)}, u32[]{:S(2)}, u32[]{:S(2)}) collective-permute-start(bf16[520,128]{1,0:T(8,128)(2,1)S(1)} %get-tuple-element.71), channel_id=1, source_target_pairs={{0,6},{2,4},{4,2},{6,0},{8,14},{10,12},{12,10},{14,8},{1,7},{3,5},... | collective-permute-start | bytes 399368 | tf_op jit(solution)/shard_map/ppermute | solution.py:780
  13.8 0.0 copy-done.2
  13.8 0.0 copy-done.8
  13.8 2.3 %own.1 = (bf16[384,256]{1,0:T(8,128)(2,1)S(1)}, bf16[2,2,128,512]{3,2,1,0:T(8,128)(2,1)S(1)}, bf16[384,128]{1,0:T(8,128)(2,1)S(1)}, f32[384,128]{1,0:T(8,128)S(1...) custom-call(bf16[4,2560]{1,0:T(4,128)(2,1)S(1)} %collective-permute-, ...), custom_call_target="tpu_custom_call" | custom-call | flops 103809024 | bytes 1572864 | tf_op jit(solution)/shard_map/own/pallas_call | solution.py:517
  16.1 0.0 collective-permute-done.1.refs_1_
  16.1 0.0 collective-permute-done.2.refs_2_
  16.2 2.3 %collective-permute-done.3.refs_1_ = bf16[520,128]{1,0:T(8,128)(2,1)S(1)} collective-permute-done((bf16[520,128]{1,0:T(8,128)(2,1)S(1)}, bf16[520,128]{1,0:T(8,128)(2,1)S(1)}, u32[]{:S(2)}, u32[]{:S(2)}) %collective-permute-start.3) | collective-permute-done | bytes 133152 | tf_op jit(solution)/shard_map/ppermute | solution.py:780
  18.5 0.2 cluster_scan.1
  18.7 1.7 %collective-permute-start.4 = (bf16[128,512]{1,0:T(8,128)(2,1)S(1)}, bf16[128,512]{1,0:T(8,128)(2,1)S(1)}, u32[]{:S(2)}, u32[]{:S(2)}) collective-permute-start(bf16[128,512]{1,0:T(8,128)(2,1)S(1)} %get-tuple-element.72), channel_id=1, source_target_pairs={{0,8},{2,10},{4,12},{6,14},{8,0},{10,2},{12,4},{14,6},{1,9},{3,11}... | collective-permute-start | bytes 393224 | tf_op jit(solution)/shard_map/ppermute | solution.py:780
  20.4 0.0 copy-done.1
  20.4 2.8 %intra.2 = (f32[384,512]{1,0:T(8,128)S(1)}, f32[384,512]{1,0:T(8,128)S(1)}, f32[384,512]{1,0:T(8,128)S(1)}, f32[384,512]{1,0:T(8,128)S(1)}) custom-call(bf16[384,256]{1,0:T(8,128)(2,1)S(1)} %get-tuple-element.61.refs_4_.refs_0_, bf16[384,256]{1,0:T(8,128)(2,1)S(1)} %get-tuple-element.64.refs_1_.refs_0_, bf16[384,128]{1,0:T(8,128)(2,1)S(1)} %get-tuple-element.65.refs_2_, ...), custom_call_target="tpu_custom_call" | custom-call | flops 201326592 | bytes 4718592 | tf_op jit(solution)/shard_map/intra/pallas_call | solution.py:699
  23.3 2.9 %collective-permute-done.4.before_ref = bf16[128,512]{1,0:T(8,128)(2,1)S(1)} collective-permute-done((bf16[128,512]{1,0:T(8,128)(2,1)S(1)}, bf16[128,512]{1,0:T(8,128)(2,1)S(1)}, u32[]{:S(2)}, u32[]{:S(2)}) %collective-permute-start.4) | collective-permute-done | bytes 131104 | tf_op jit(solution)/shard_map/ppermute | solution.py:780
  26.2 0.1 join.1
  26.3 0.3 collective-permute-start.5
  26.6 0.9 %collective-permute-start.7 = (bf16[128,512]{1,0:T(8,128)(2,1)S(1)}, bf16[128,512]{1,0:T(8,128)(2,1)S(1)}, u32[]{:S(2)}, u32[]{:S(2)}) collective-permute-start(bf16[128,512]{1,0:T(8,128)(2,1)S(1)} %get-tuple-element.95), channel_id=1, source_target_pairs={{0,2},{2,0},{4,6},{6,4},{8,10},{10,8},{12,14},{14,12},{1,3},{3,1},... | collective-permute-start | bytes 393224 | tf_op jit(solution)/shard_map/ppermute | solution.py:780
  27.5 2.3 %collective-permute-start.6 = (bf16[128,512]{1,0:T(8,128)(2,1)S(1)}, bf16[128,512]{1,0:T(8,128)(2,1)S(1)}, u32[]{:S(2)}, u32[]{:S(2)}) collective-permute-start(bf16[128,512]{1,0:T(8,128)(2,1)S(1)} %get-tuple-element.91), channel_id=1, source_target_pairs={{0,6},{2,4},{4,2},{6,0},{8,14},{10,12},{12,10},{14,8},{1,7},{3,5},... | collective-permute-start | bytes 393224 | tf_op jit(solution)/shard_map/ppermute | solution.py:780
  29.9 2.8 %intra.3 = (f32[384,512]{1,0:T(8,128)S(1)}, f32[384,512]{1,0:T(8,128)S(1)}, f32[384,512]{1,0:T(8,128)S(1)}, f32[384,512]{1,0:T(8,128)S(1)}) custom-call(bf16[384,256]{1,0:T(8,128)(2,1)S(1)} %get-tuple-element.61.refs_4_.refs_0_, bf16[384,256]{1,0:T(8,128)(2,1)S(1)} %get-tuple-element.64.refs_1_.refs_0_, bf16[384,128]{1,0:T(8,128)(2,1)S(1)} %get-tuple-element.65.refs_2_, ...), custom_call_target="tpu_custom_call" | custom-call | flops 201326592 | bytes 4718592 | tf_op jit(solution)/shard_map/intra/pallas_call | solution.py:699
  32.7 0.0 collective-permute-done.5.refs_6_
  32.7 0.2 collective-permute-done.7.refs_7_
  33.0 0.0 copy-done.6
  33.0 1.4 %final.2.refs_8_ = bf16[384,2048]{1,0:T(8,128)(2,1)} custom-call(bf16[384,256]{1,0:T(8,128)(2,1)S(1)} %get-tuple-element.64.refs_1_.refs_0_, f32[1,2048]{1,0:T(1,128)S(1)} %bitcast.5, f32[384,512]{1,0:T(8,128)S(1)} %get-tuple-element.78.refs_2_, f32[384,512]{1,0:T(8,128)S(1)} %get-tuple-element.92.refs_3_, f32[384,512]{1,0:T(8,128)S(1)} %get-tuple-element.93.refs_4_, ...), custom_call_target="tpu_custom_call" | custom-call | flops 100663296 | bytes 3145728 | tf_op jit(solution)/shard_map/final/pallas_call | solution.py:761
  34.4 0.0 collective-permute-done.6.refs_7_
  34.4 1.4 %final.3 = bf16[384,2048]{1,0:T(8,128)(2,1)} custom-call(bf16[384,256]{1,0:T(8,128)(2,1)S(1)} %get-tuple-element.64.refs_1_.refs_0_, f32[1,2048]{1,0:T(1,128)S(1)} %bitcast.6, f32[384,512]{1,0:T(8,128)S(1)} %get-tuple-element.86.refs_2_, f32[384,512]{1,0:T(8,128)S(1)} %get-tuple-element.87.refs_3_, ...), custom_call_target="tpu_custom_call", output_to_operand_aliasing={{}: (8, {})} | custom-call | flops 100663296 | bytes 3145728 | tf_op jit(solution)/shard_map/final/pallas_call | solution.py:761
  (3 shorter events, 0.0 us)
Async XLA Ops:
  0.0 3.9 %copy-start = (bf16[384,2048]{1,0:T(8,128)(2,1)S(1)}, bf16[384,2048]{1,0:T(8,128)(2,1)}, u32[]{:S(2)}) copy-start(bf16[384,2048]{1,0:T(8,128)(2,1)} %refs_6_.3) | copy-start | bytes 4718596
  0.0 3.9 %copy-start.3 = (bf16[384,256]{1,0:T(8,128)(2,1)S(1)}, bf16[384,256]{1,0:T(8,128)(2,1)}, u32[]{:S(2)}) copy-start(bf16[384,256]{1,0:T(8,128)(2,1)} %b_ref.3) | copy-start | bytes 589828
  0.0 3.9 %copy-start.4 = (f32[4,2048]{1,0:T(4,128)S(1)}, f32[4,2048]{1,0:T(4,128)}, u32[]{:S(2)}) copy-start(f32[4,2048]{1,0:T(4,128)} %refs_5_.3) | copy-start | bytes 98308
  0.0 3.9 %copy-start.9 = (s32[4]{0:T(128)S(1)}, s32[4]{0:T(128)}, u32[]{:S(2)}) copy-start(s32[4]{0:T(128)} %refs_14_.1) | copy-start | bytes 52
  0.0 3.9 %copy-start.7 = (f32[4,256]{1,0:T(4,128)S(1)}, f32[4,256]{1,0:T(4,128)}, u32[]{:S(2)}) copy-start(f32[4,256]{1,0:T(4,128)} %taps_b_ref.3) | copy-start | bytes 12292
  0.0 3.9 %copy-start.10 = (f32[32]{0:T(128)S(1)}, f32[32]{0:T(128)}, u32[]{:S(2)}) copy-start(f32[32]{0:T(128)} %param.15) | copy-start | bytes 388
  0.0 3.9 %copy-start.5 = (f32[384,32]{0,1:T(8,128)S(1)}, f32[384,32]{0,1:T(8,128)}, u32[]{:S(2)}) copy-start(f32[384,32]{0,1:T(8,128)} %param.14) | copy-start | bytes 147460
  0.9 7.7 %collective-permute-start = (bf16[4,2560]{1,0:T(4,128)(2,1)S(1)}, bf16[4,2560]{1,0:T(4,128)(2,1)S(1)}, u32[]{:S(2)}, u32[]{:S(2)}) collective-permute-start(bf16[4,2560]{1,0:T(4,128)(2,1)S(1)} %pack.1), channel_id=1, source_target_pairs={{0,2},{2,4},{4,6},{6,8},{8,10},{10,12},{12,14},{14,0},{1,3},{3,5},... | collective-permute-start | bytes 61448 | tf_op jit(solution)/shard_map/ppermute | solution.py:828
  8.7 5.1 %copy-start.2 = (bf16[384,256]{1,0:T(8,128)(2,1)S(1)}, bf16[384,256]{1,0:T(8,128)(2,1)}, u32[]{:S(2)}) copy-start(bf16[384,256]{1,0:T(8,128)(2,1)} %refs_7_.1) | copy-start | bytes 589828
  8.7 5.1 %copy-start.8 = (f32[4,256]{1,0:T(4,128)S(1)}, f32[4,256]{1,0:T(4,128)}, u32[]{:S(2)}) copy-start(f32[4,256]{1,0:T(4,128)} %refs_8_.1) | copy-start | bytes 12292
  9.0 7.1 %collective-permute-start.1 = (bf16[520,128]{1,0:T(8,128)(2,1)S(1)}, bf16[520,128]{1,0:T(8,128)(2,1)S(1)}, u32[]{:S(2)}, u32[]{:S(2)}) collective-permute-start(bf16[520,128]{1,0:T(8,128)(2,1)S(1)} %get-tuple-element.69), channel_id=1, source_target_pairs={{0,2},{2,0},{4,6},{6,4},{8,10},{10,8},{12,14},{14,12},{1,3},{3,1},... | collective-permute-start | bytes 399368 | tf_op jit(solution)/shard_map/ppermute | solution.py:780
  9.8 6.4 %collective-permute-start.2 = (bf16[520,128]{1,0:T(8,128)(2,1)S(1)}, bf16[520,128]{1,0:T(8,128)(2,1)S(1)}, u32[]{:S(2)}, u32[]{:S(2)}) collective-permute-start(bf16[520,128]{1,0:T(8,128)(2,1)S(1)} %get-tuple-element.70), channel_id=1, source_target_pairs={{0,4},{2,6},{4,0},{6,2},{8,12},{10,14},{12,8},{14,10},{1,5},{3,7},... | collective-permute-start | bytes 399368 | tf_op jit(solution)/shard_map/ppermute | solution.py:780
  12.5 6.0 %collective-permute-start.3 = (bf16[520,128]{1,0:T(8,128)(2,1)S(1)}, bf16[520,128]{1,0:T(8,128)(2,1)S(1)}, u32[]{:S(2)}, u32[]{:S(2)}) collective-permute-start(bf16[520,128]{1,0:T(8,128)(2,1)S(1)} %get-tuple-element.71), channel_id=1, source_target_pairs={{0,6},{2,4},{4,2},{6,0},{8,14},{10,12},{12,10},{14,8},{1,7},{3,5},... | collective-permute-start | bytes 399368 | tf_op jit(solution)/shard_map/ppermute | solution.py:780
  13.8 6.6 %copy-start.1 = (bf16[384,2048]{1,0:T(8,128)(2,1)S(1)}, bf16[384,2048]{1,0:T(8,128)(2,1)}, u32[]{:S(2)}) copy-start(bf16[384,2048]{1,0:T(8,128)(2,1)} %refs_11_.3) | copy-start | bytes 4718596
  18.7 7.5 %collective-permute-start.4 = (bf16[128,512]{1,0:T(8,128)(2,1)S(1)}, bf16[128,512]{1,0:T(8,128)(2,1)S(1)}, u32[]{:S(2)}, u32[]{:S(2)}) collective-permute-start(bf16[128,512]{1,0:T(8,128)(2,1)S(1)} %get-tuple-element.72), channel_id=1, source_target_pairs={{0,8},{2,10},{4,12},{6,14},{8,0},{10,2},{12,4},{14,6},{1,9},{3,11}... | collective-permute-start | bytes 393224 | tf_op jit(solution)/shard_map/ppermute | solution.py:780
  26.3 6.4 %collective-permute-start.5 = (bf16[128,512]{1,0:T(8,128)(2,1)S(1)}, bf16[128,512]{1,0:T(8,128)(2,1)S(1)}, u32[]{:S(2)}, u32[]{:S(2)}) collective-permute-start(bf16[128,512]{1,0:T(8,128)(2,1)S(1)} %get-tuple-element.90), channel_id=1, source_target_pairs={{0,4},{2,6},{4,0},{6,2},{8,12},{10,14},{12,8},{14,10},{1,5},{3,7},... | collective-permute-start | bytes 393224 | tf_op jit(solution)/shard_map/ppermute | solution.py:780
  26.6 6.4 %collective-permute-start.7 = (bf16[128,512]{1,0:T(8,128)(2,1)S(1)}, bf16[128,512]{1,0:T(8,128)(2,1)S(1)}, u32[]{:S(2)}, u32[]{:S(2)}) collective-permute-start(bf16[128,512]{1,0:T(8,128)(2,1)S(1)} %get-tuple-element.95), channel_id=1, source_target_pairs={{0,2},{2,0},{4,6},{6,4},{8,10},{10,8},{12,14},{14,12},{1,3},{3,1},... | collective-permute-start | bytes 393224 | tf_op jit(solution)/shard_map/ppermute | solution.py:780
  27.5 6.8 %collective-permute-start.6 = (bf16[128,512]{1,0:T(8,128)(2,1)S(1)}, bf16[128,512]{1,0:T(8,128)(2,1)S(1)}, u32[]{:S(2)}, u32[]{:S(2)}) collective-permute-start(bf16[128,512]{1,0:T(8,128)(2,1)S(1)} %get-tuple-element.91), channel_id=1, source_target_pairs={{0,6},{2,4},{4,2},{6,0},{8,14},{10,12},{12,10},{14,8},{1,7},{3,5},... | collective-permute-start | bytes 393224 | tf_op jit(solution)/shard_map/ppermute | solution.py:780
  29.9 3.1 %copy-start.6 = (f32[2048]{0:T(1024)S(1)}, f32[2048]{0:T(1024)}, u32[]{:S(2)}) copy-start(f32[2048]{0:T(1024)} %param.20) | copy-start | bytes 24580
